TPU v7x, 32 devices: a whole 2x2x4 slice. The times are simulated.
32 devices in a mesh: seq: 16 (over z, y, core), fsdp: 2 (over x).
Axes of the slice: x: 2, y: 2, z: 4, core: 2. Of those that a mesh axis runs over, the one named last changes fastest.
Arguments:
- tokens_in: bfloat16 [2, 2048, 1152], P('fsdp', 'seq'), may hold values from -6 to 6
- condition: float32 [2, 16, 1152], P('fsdp'), may hold values from -6 to 6
- crop_pieces: int32 [2, 16], P('fsdp'), may hold values from 1 to 16, 128 in all within a row
- pad_counts: int32 [2, 16], P('fsdp'), may hold values from 0 to 32, as said below
- head_mask: int32 [2, 16, 16], P('fsdp'), may hold values 0 or 1
- channel_mask: int32 [2, 16, 36], P('fsdp'), may hold values 0 or 1
- keep_mask: int32 [2, 2048], P('fsdp', 'seq'), may hold values 0 or 1
- qkv_weight: bfloat16 [1152, 3456], P('fsdp'), may hold values from -0.1875 to 0.1875
- out_weight: bfloat16 [1152, 1152], P('fsdp'), may hold values from -1.75 to 1.75
- up_weight: bfloat16 [1152, 4608], P('fsdp'), may hold values from -0.1875 to 0.1875
- down_weight: bfloat16 [4608, 1152], P('fsdp'), may hold values from -0.09375 to 0.09375
- ada_weight: bfloat16 [1152, 6912], P(None, 'fsdp'), may hold values from -0.1875 to 0.1875
- cotangent: bfloat16 [2, 2048, 1152], P('fsdp', 'seq'), may hold values from -6 to 6
Outputs:
- block_out: bfloat16 [2, 2048, 1152], P('fsdp', 'seq')
- input_grad: float32 [2, 2048, 1152], P('fsdp', 'seq')
- qkv_grad: float32 [1152, 3456], P('fsdp', 'seq')
- out_grad: float32 [1152, 1152], P('fsdp', 'seq')
- up_grad: float32 [1152, 4608], P('fsdp', 'seq')
- down_grad: float32 [4608, 1152], P('fsdp', 'seq')
- ada_grad: float32 [1152, 6912], P(None, 'fsdp')
Inputs may be any that keep to these rules, and one draw needn't show every extreme that they name: `pad_counts`: in every row some cycle position has no padding and some has 32 padding slots. `crop_pieces`: each row's pieces sum to 128 and the largest is 16.
All inputs are finite; a program needn't handle non-finite values. No bound on the sum of `head_mask` or of `channel_mask` or of `keep_mask` on one device may be relied on, other than what follows from the above.
Results may differ from a plain program's by a relative error of at most 0.02865.
Values may be sent and summed in bfloat16 or wider, within the bound.
No kernel may reach another device: no remote copies, remote signals or barrier semaphores. Data moves between devices by JAX's collectives and lax.ppermute only.
A program may use at most 256 MiB of HBM per device.

v0:
```python
import jax
import jax.numpy as jnp
from jax import lax
from jax.sharding import PartitionSpec as P

D = 1152
H = 16
HD = 72
CHAN_GROUP = 128


highest = lax.Precision.HIGHEST
norm_epsilon = 1e-06
masked_score = -1e30


def normalize(values):
    average = jnp.mean(values, axis=-1, keepdims=True)
    centred = values - average
    spread = jnp.mean(centred * centred, axis=-1, keepdims=True)
    return centred * lax.rsqrt(spread + norm_epsilon)


def modulated(inputs_row, shift_part, scale_part):
    return normalize(inputs_row) * (1.0 + scale_part) + shift_part


def crop_of(slot_index, crop_ends):
    return jnp.sum((slot_index[:, None] >= crop_ends[None, :-1]).astype(jnp.int32), axis=1)


def block_size():
    return 512


def local(
    tokens_in,
    condition,
    crop_pieces,
    pad_counts,
    head_mask,
    channel_mask,
    keep_mask,
    qkv_weight,
    out_weight,
    up_weight,
    down_weight,
    ada_weight,
    cotangent,
):
    cycle_size = lax.axis_size("seq")
    local_rows = tokens_in.shape[1]
    score_scale = HD ** (-0.5)
    crop_count = crop_pieces.shape[1]
    residual = tokens_in[0].astype(jnp.float32)
    crop_ends = jnp.cumsum(crop_pieces[0])
    pads_row = pad_counts[0]
    cycle_slots = jnp.arange(cycle_size, dtype=jnp.int32)
    local_slots = jnp.arange(local_rows, dtype=jnp.int32)
    crop_here = crop_of(local_slots, crop_ends)
    selector = (crop_here[:, None] == jnp.arange(crop_count, dtype=jnp.int32)[None, :]).astype(
        jnp.float32
    )

    def key_layout(offset, key_count):
        positions = offset + jnp.arange(key_count, dtype=jnp.int32)
        slot_index = positions % local_rows
        owners = positions // local_rows
        owner_pads = jnp.sum(
            jnp.where(owners[:, None] == cycle_slots[None, :], pads_row[None, :], 0), axis=1
        )
        same_crop = crop_here[:, None] == crop_of(slot_index, crop_ends)[None, :]
        return same_crop & (slot_index < local_rows - owner_pads)[None, :]

    cond_act = jax.nn.silu(condition[0]).astype(jnp.bfloat16)
    modulation = jnp.dot(
        cond_act,
        lax.all_gather(ada_weight, "fsdp", axis=1, tiled=True),
        preferred_element_type=jnp.float32,
    )
    mod_tokens = jnp.dot(selector, modulation, precision=highest)
    shift_attn = mod_tokens[:, 0:D]
    scale_attn = mod_tokens[:, D : 2 * D]
    gate_attn = mod_tokens[:, 2 * D : 3 * D]
    shift_mlp = mod_tokens[:, 3 * D : 4 * D]
    scale_mlp = mod_tokens[:, 4 * D : 5 * D]
    gate_mlp = mod_tokens[:, 5 * D : 6 * D]
    head_tokens = jnp.dot(selector, head_mask[0].astype(jnp.float32), precision=highest)
    channel_tokens = jnp.repeat(
        jnp.dot(selector, channel_mask[0].astype(jnp.float32), precision=highest),
        CHAN_GROUP,
        axis=1,
    )
    keep_rows = keep_mask[0].astype(jnp.float32)[:, None]

    def front_half(weights):
        normed_in = modulated(residual, shift_attn, scale_attn).astype(jnp.bfloat16)
        projected = jnp.dot(normed_in, weights[0], preferred_element_type=jnp.float32)
        queries = projected[:, 0:D].astype(jnp.bfloat16)
        keys_here = projected[:, D : 2 * D].astype(jnp.bfloat16)
        values_here = projected[:, 2 * D : 3 * D].astype(jnp.bfloat16)
        return (normed_in, queries, keys_here, values_here)

    def online_step(running, keys_part, values_part, offset, queries):
        best_score, row_total, accumulated = running
        key_count = keys_part.shape[0]
        scores = (
            jnp.einsum(
                "qhd,khd->hqk",
                queries.reshape(local_rows, H, HD),
                keys_part.reshape(key_count, H, HD),
                preferred_element_type=jnp.float32,
            )
            * score_scale
        )
        allowed = key_layout(offset, key_count)[None]
        masked = jnp.where(allowed, scores, masked_score)
        new_best = jnp.maximum(best_score, jnp.max(masked, axis=-1))
        weights_exp = jnp.where(allowed, jnp.exp(masked - new_best[..., None]), 0.0)
        factor = jnp.exp(best_score - new_best)
        row_total = row_total * factor + jnp.sum(weights_exp, axis=-1)
        accumulated = accumulated * factor[..., None] + jnp.einsum(
            "hqk,khd->hqd",
            weights_exp.astype(jnp.bfloat16),
            values_part.reshape(key_count, H, HD),
            preferred_element_type=jnp.float32,
        )
        return (new_best, row_total, accumulated)

    def fold_piece(running, key_parts, offset, queries):
        keys_part, values_part = key_parts
        key_count = keys_part.shape[0]
        rows_block = block_size()

        def one_block(online_state, block_index):
            block_start = block_index * rows_block
            keys_block = lax.dynamic_slice_in_dim(keys_part, block_start, rows_block, 0)
            values_block = lax.dynamic_slice_in_dim(values_part, block_start, rows_block, 0)
            return (
                online_step(online_state, keys_block, values_block, offset + block_start, queries),
                None,
            )

        running, ignored = lax.scan(
            one_block, running, jnp.arange(key_count // rows_block, dtype=jnp.int32)
        )
        return running

    def finish(row_total, accumulated):
        return jnp.transpose(accumulated / row_total[..., None], (1, 0, 2))

    def back_half(weights, heads_out):
        merged = (heads_out * head_tokens[:, :, None]).reshape(local_rows, D).astype(jnp.bfloat16)
        attn_proj = jnp.dot(merged, weights[1], preferred_element_type=jnp.float32)
        mid_state = residual + gate_attn * attn_proj
        normed_mid = modulated(mid_state, shift_mlp, scale_mlp).astype(jnp.bfloat16)
        hidden_pre = jnp.dot(normed_mid, weights[2], preferred_element_type=jnp.float32)
        hidden_act = (jax.nn.gelu(hidden_pre, approximate=True) * channel_tokens).astype(
            jnp.bfloat16
        )
        mlp_out = jnp.dot(hidden_act, weights[3], preferred_element_type=jnp.float32)
        block_result = mid_state + gate_mlp * keep_rows * mlp_out
        return (
            merged,
            attn_proj,
            mid_state,
            normed_mid,
            hidden_pre,
            hidden_act,
            mlp_out,
            block_result,
        )

    weights = (
        lax.all_gather(qkv_weight, "fsdp", axis=0, tiled=True),
        lax.all_gather(out_weight, "fsdp", axis=0, tiled=True),
        lax.all_gather(up_weight, "fsdp", axis=0, tiled=True),
        lax.all_gather(down_weight, "fsdp", axis=0, tiled=True),
    )
    normed_in, queries, keys_here, values_here = front_half(weights)
    start_state = (
        jnp.full((H, local_rows), masked_score, jnp.float32),
        jnp.zeros((H, local_rows), jnp.float32),
        jnp.zeros((H, local_rows, HD), jnp.float32),
    )
    best_score, row_total, accumulated = fold_piece(
        start_state,
        (
            lax.all_gather(keys_here, "seq", axis=0, tiled=True),
            lax.all_gather(values_here, "seq", axis=0, tiled=True),
        ),
        jnp.int32(0),
        queries,
    )
    block_out = back_half(weights, finish(row_total, accumulated))[7]
    weights = (
        lax.all_gather(qkv_weight, "fsdp", axis=0, tiled=True),
        lax.all_gather(out_weight, "fsdp", axis=0, tiled=True),
        lax.all_gather(up_weight, "fsdp", axis=0, tiled=True),
        lax.all_gather(down_weight, "fsdp", axis=0, tiled=True),
    )
    normed_in, queries, keys_here, values_here = front_half(weights)
    keys_all, values_all = (
        lax.all_gather(keys_here, "seq", axis=0, tiled=True),
        lax.all_gather(values_here, "seq", axis=0, tiled=True),
    )
    best_score, row_total, accumulated = fold_piece(start_state, (keys_all, values_all), 0, queries)
    heads_out = finish(row_total, accumulated)
    forward_rest = back_half(weights, heads_out)
    merged, attn_proj, mid_state, normed_mid, hidden_pre, hidden_act, mlp_out, block_again = (
        forward_rest
    )
    grad_out = cotangent[0].astype(jnp.float32)
    grad_mlp = (grad_out * gate_mlp * keep_rows).astype(jnp.bfloat16)
    grad_gate_mlp = grad_out * keep_rows * mlp_out
    down_term = jnp.einsum("tf,td->fd", hidden_act, grad_mlp, preferred_element_type=jnp.float32)
    grad_act = jnp.einsum("td,fd->tf", grad_mlp, weights[3], preferred_element_type=jnp.float32)

    def activation(pre_act):
        return jax.nn.gelu(pre_act, approximate=True) * channel_tokens

    ignored, act_pull = jax.vjp(activation, hidden_pre)
    grad_pre = act_pull(grad_act)[0].astype(jnp.bfloat16)
    up_term = jnp.einsum("td,tf->df", normed_mid, grad_pre, preferred_element_type=jnp.float32)
    grad_normed_mid = jnp.einsum(
        "tf,df->td", grad_pre, weights[2], preferred_element_type=jnp.float32
    )
    ignored, mid_pull = jax.vjp(modulated, mid_state, shift_mlp, scale_mlp)
    grad_mid, grad_shift_mlp, grad_scale_mlp = mid_pull(grad_normed_mid)
    grad_mid = grad_mid + grad_out
    grad_attn = (grad_mid * gate_attn).astype(jnp.bfloat16)
    grad_gate_attn = grad_mid * attn_proj
    out_term = jnp.einsum("td,te->de", merged, grad_attn, preferred_element_type=jnp.float32)
    grad_merged = jnp.einsum("te,de->td", grad_attn, weights[1], preferred_element_type=jnp.float32)
    grad_heads = (grad_merged.reshape(local_rows, H, HD) * head_tokens[:, :, None]).astype(
        jnp.bfloat16
    )
    row_dot = jnp.transpose(jnp.sum(grad_heads.astype(jnp.float32) * heads_out, axis=-1))
    query_heads = queries.reshape(local_rows, H, HD)
    total_rows = keys_all.shape[0]
    rows_block = block_size()

    def back_block(grad_queries, block_index):
        block_start = block_index * rows_block
        keys_block = lax.dynamic_slice_in_dim(keys_all, block_start, rows_block, 0).reshape(
            rows_block, H, HD
        )
        values_block = lax.dynamic_slice_in_dim(values_all, block_start, rows_block, 0).reshape(
            rows_block, H, HD
        )
        scores = (
            jnp.einsum("qhd,khd->hqk", query_heads, keys_block, preferred_element_type=jnp.float32)
            * score_scale
        )
        allowed = key_layout(block_start, rows_block)[None]
        probabilities = (
            jnp.exp(jnp.where(allowed, scores - best_score[..., None], masked_score))
            / row_total[..., None]
        )
        grad_probs = jnp.einsum(
            "qhd,khd->hqk", grad_heads, values_block, preferred_element_type=jnp.float32
        )
        grad_scores = (probabilities * (grad_probs - row_dot[..., None])).astype(jnp.bfloat16)
        grad_queries = grad_queries + jnp.einsum(
            "hqk,khd->qhd", grad_scores, keys_block, preferred_element_type=jnp.float32
        )
        grad_keys = (
            jnp.einsum("hqk,qhd->khd", grad_scores, query_heads, preferred_element_type=jnp.float32)
            * score_scale
        )
        grad_values = jnp.einsum(
            "hqk,qhd->khd",
            probabilities.astype(jnp.bfloat16),
            grad_heads,
            preferred_element_type=jnp.float32,
        )
        return (
            grad_queries,
            (grad_keys.reshape(rows_block, D), grad_values.reshape(rows_block, D)),
        )

    def with_key_terms(grad_queries, block_index):
        return back_block(grad_queries, block_index)

    block_steps = jnp.arange(total_rows // rows_block, dtype=jnp.int32)
    query_start = jnp.zeros((local_rows, H, HD), jnp.float32)
    grad_queries, (key_terms, value_terms) = lax.scan(with_key_terms, query_start, block_steps)
    key_terms = key_terms.reshape(total_rows, D)
    value_terms = value_terms.reshape(total_rows, D)
    key_grads, value_grads = (
        lax.psum_scatter(
            key_terms.astype(jnp.bfloat16), "seq", scatter_dimension=0, tiled=True
        ).astype(jnp.float32),
        lax.psum_scatter(
            value_terms.astype(jnp.bfloat16), "seq", scatter_dimension=0, tiled=True
        ).astype(jnp.float32),
    )
    grad_qkv = jnp.concatenate(
        [
            (grad_queries * score_scale).reshape(local_rows, D).astype(jnp.bfloat16),
            key_grads.astype(jnp.bfloat16),
            value_grads.astype(jnp.bfloat16),
        ],
        axis=1,
    )
    qkv_term = jnp.einsum("td,te->de", normed_in, grad_qkv, preferred_element_type=jnp.float32)
    grad_normed_in = jnp.einsum(
        "te,de->td", grad_qkv, weights[0], preferred_element_type=jnp.float32
    )
    ignored, in_pull = jax.vjp(modulated, residual, shift_attn, scale_attn)
    grad_in, grad_shift_attn, grad_scale_attn = in_pull(grad_normed_in)
    input_grad = grad_in + grad_mid
    grad_mod_tokens = jnp.concatenate(
        [
            grad_shift_attn,
            grad_scale_attn,
            grad_gate_attn,
            grad_shift_mlp,
            grad_scale_mlp,
            grad_gate_mlp,
        ],
        axis=1,
    )
    crop_grads = jnp.dot(jnp.transpose(selector), grad_mod_tokens, precision=highest)
    mod_grads = lax.psum(crop_grads.astype(jnp.bfloat16), "seq")
    ada_term = jnp.einsum("cd,ce->de", cond_act, mod_grads, preferred_element_type=jnp.float32)
    ada_grad = lax.psum_scatter(
        ada_term.astype(jnp.bfloat16), "fsdp", scatter_dimension=1, tiled=True
    ).astype(jnp.float32)
    qkv_rows, out_rows, up_rows, down_rows = (
        lax.psum_scatter(
            qkv_term.astype(jnp.bfloat16), "fsdp", scatter_dimension=0, tiled=True
        ).astype(jnp.float32),
        lax.psum_scatter(
            out_term.astype(jnp.bfloat16), "fsdp", scatter_dimension=0, tiled=True
        ).astype(jnp.float32),
        lax.psum_scatter(
            up_term.astype(jnp.bfloat16), "fsdp", scatter_dimension=0, tiled=True
        ).astype(jnp.float32),
        lax.psum_scatter(
            down_term.astype(jnp.bfloat16), "fsdp", scatter_dimension=0, tiled=True
        ).astype(jnp.float32),
    )
    qkv_grad, out_grad, up_grad, down_grad = (
        lax.psum_scatter(
            qkv_rows.astype(jnp.bfloat16), "seq", scatter_dimension=1, tiled=True
        ).astype(jnp.float32),
        lax.psum_scatter(
            out_rows.astype(jnp.bfloat16), "seq", scatter_dimension=1, tiled=True
        ).astype(jnp.float32),
        lax.psum_scatter(
            up_rows.astype(jnp.bfloat16), "seq", scatter_dimension=1, tiled=True
        ).astype(jnp.float32),
        lax.psum_scatter(
            down_rows.astype(jnp.bfloat16), "seq", scatter_dimension=1, tiled=True
        ).astype(jnp.float32),
    )
    return (
        block_out[None].astype(jnp.bfloat16),
        input_grad[None],
        qkv_grad,
        out_grad,
        up_grad,
        down_grad,
        ada_grad,
    )


def solution(mesh):
    in_specs = (
        P("fsdp", "seq", None),
        P("fsdp", None, None),
        P("fsdp", None),
        P("fsdp", None),
        P("fsdp", None, None),
        P("fsdp", None, None),
        P("fsdp", "seq"),
        P("fsdp", None),
        P("fsdp", None),
        P("fsdp", None),
        P("fsdp", None),
        P(None, "fsdp"),
        P("fsdp", "seq", None),
    )
    out_specs = (
        P("fsdp", "seq", None),
        P("fsdp", "seq", None),
        P("fsdp", "seq"),
        P("fsdp", "seq"),
        P("fsdp", "seq"),
        P("fsdp", "seq"),
        P(None, "fsdp"),
    )
    return jax.shard_map(local, mesh=mesh, in_specs=in_specs, out_specs=out_specs, check_vma=False)
```

profile of v0, /device:TPU:2, one launch (start us, length us, event | category | flops | bytes accessed | tf_op | source)
XLA Modules:
  0.0 1917.3 jit_solution(7837935246109193591)
XLA Ops:
  10.0 188.9 %all-gather.8.cloned.1.call-done = bf16[1152,6912]{1,0:T(8,128)(2,1)} async-done(((bf16[1152,3456]{1,0:T(8,128)(2,1)}), bf16[1152,6912]{1,0:T(8,128)(2,1)}) %all-gather.8.cloned.1.call-update) | async-done | bytes 15925264 | tf_op jit(solution)/shard_map/all_gather | solution.py:78
  198.9 7.7 fusion.80
  211.0 88.7 %all-gather.10.cloned.1.call-done = bf16[1152,3456]{1,0:T(8,128)(2,1)} async-done(((bf16[576,3456]{1,0:T(8,128)(2,1)}), bf16[1152,3456]{1,0:T(8,128)(2,1)}) %all-gather.10.cloned.1.call-update) | async-done | bytes 7962640 | tf_op jit(solution)/shard_map/all_gather | solution.py:175
  314.4 45.6 %all-gather.12.cloned.1.call-done = bf16[2048,1152]{1,0:T(8,128)(2,1)} async-done(((bf16[128,1152]{1,0:T(8,128)(2,1)}), bf16[2048,1152]{1,0:T(8,128)(2,1)}) %all-gather.12.cloned.1.call-update) | async-done | bytes 4718608 | tf_op jit(solution)/shard_map/all_gather | solution.py:189
  360.0 6.6 copy.107
  366.6 48.1 %all-gather.14.cloned.1.call-done = bf16[2048,1152]{1,0:T(8,128)(2,1)} async-done(((bf16[128,1152]{1,0:T(8,128)(2,1)}), bf16[2048,1152]{1,0:T(8,128)(2,1)}) %all-gather.14.cloned.1.call-update) | async-done | bytes 4718608 | tf_op jit(solution)/shard_map/all_gather | solution.py:190
  414.7 6.7 copy.109
  421.3 62.3 %while.40 = (s32[]{:T(128)}, f32[16,128]{1,0:T(8,128)S(1)}, f32[16,128]{1,0:T(8,128)S(1)}, f32[16,128,72]{1,2,0:T(8,128)}, s32[128]{0:T(128)}, /*index=5*/s32[4]...) while((s32[]{:T(128)}, f32[16,128]{1,0:T(8,128)S(1)}, ...), condition=%wide.region_9.10_spmd.clone, body=%wide.region_4.9_spmd.clone.sunk | while | flops 316269056 | bytes 38324084 | solution.py:144
  491.6 93.6 %all-gather.18.cloned.1.call-done = bf16[1152,4608]{1,0:T(8,128)(2,1)} async-done(((bf16[576,4608]{1,0:T(8,128)(2,1)}), bf16[1152,4608]{1,0:T(8,128)(2,1)}) %all-gather.18.cloned.1.call-update) | async-done | bytes 10616848 | tf_op jit(solution)/shard_map/all_gather | solution.py:177
  585.3 8.7 multiply_convert_fusion
  594.0 123.8 %all-gather.20.cloned.1.call-done = bf16[4608,1152]{1,0:T(8,128)(2,1)} async-done(((bf16[2304,1152]{1,0:T(8,128)(2,1)}), bf16[4608,1152]{1,0:T(8,128)(2,1)}) %all-gather.20.cloned.1.call-update) | async-done | bytes 10616848 | tf_op jit(solution)/shard_map/all_gather | solution.py:178
  717.8 10.5 fusion.35
  733.4 6.0 fusion.87
  744.5 115.8 %while.41 = (s32[]{:T(128)}, f32[128,16,72]{0,2,1:T(8,128)}, bf16[4,512,1152]{2,1,0:T(8,128)(2,1)}, bf16[4,512,1152]{2,1,0:T(8,128)(2,1)}, s32[4]{0:T(128)S(1)},...) while((s32[]{:T(128)}, f32[128,16,72]{0,2,1:T(8,128)}, ...), condition=%wide.region_18.19_spmd.clone, body=%wide.region_15.18_spmd.clone.sunk | while | flops 765037056 | bytes 59419064 | solution.py:287
  863.9 73.3 %reduce-scatter.30.cloned.1.call-done = bf16[128,1152]{1,0:T(8,128)(2,1)} async-done(((bf16[2048,1152]{1,0:T(8,128)(2,1)}), bf16[128,1152]{1,0:T(8,128)(2,1)}) %reduce-scatter.30.cloned.1.call-update) | async-done | bytes 294928
  938.4 77.8 %reduce-scatter.32.cloned.1.call-done = bf16[128,1152]{1,0:T(8,128)(2,1)} async-done(((bf16[2048,1152]{1,0:T(8,128)(2,1)}), bf16[128,1152]{1,0:T(8,128)(2,1)}) %reduce-scatter.32.cloned.1.call-update) | async-done | bytes 294928
  1024.5 5.7 convolution_convert_fusion.2
  1031.5 5.9 convolution_convert_fusion.1
  1038.4 6.0 constant_dynamic-update-slice_fusion.3
  1054.1 97.0 %reduce-scatter.22.cloned.1.call-done = bf16[576,3456]{1,0:T(8,128)(2,1)} async-done(((bf16[1152,3456]{1,0:T(8,128)(2,1)}), bf16[576,3456]{1,0:T(8,128)(2,1)}) %reduce-scatter.22.cloned.1.call-update) | async-done | bytes 3981328 | tf_op jit(solution)/shard_map/reduce_scatter | solution.py:331
  1151.2 126.1 %reduce-scatter.26.cloned.1.call-done = bf16[576,4608]{1,0:T(8,128)(2,1)} async-done(((bf16[1152,4608]{1,0:T(8,128)(2,1)}), bf16[576,4608]{1,0:T(8,128)(2,1)}) %reduce-scatter.26.cloned.1.call-update) | async-done | bytes 5308432 | tf_op jit(solution)/shard_map/reduce_scatter | solution.py:337
  1277.3 8.2 copy.137
  1285.6 117.4 %reduce-scatter.28.cloned.1.call-done = bf16[2304,1152]{1,0:T(8,128)(2,1)} async-done(((bf16[4608,1152]{1,0:T(8,128)(2,1)}), bf16[2304,1152]{1,0:T(8,128)(2,1)}) %reduce-scatter.28.cloned.1.call-update) | async-done | bytes 5308432 | tf_op jit(solution)/shard_map/reduce_scatter | solution.py:340
  1402.9 8.5 copy.139
  1411.5 127.5 %all-reduce.5.cloned.1.call-done = (bf16[576,3456]{1,0:T(8,128)(2,1)}, bf16[576,1152]{1,0:T(8,128)(2,1)}, bf16[16,6912]{1,0:T(8,128)(2,1)}) async-done(((bf16[576,3456]{1,0:T(8,128)(2,1)}, bf16[576,1152]{1,0:T(8,128)(2,1)}, bf16[16,6912]{1,0:T(8,128)(2,1)}), (bf16[576,3456]{1,0:T(8,128)(2,1)}, bf16[576,1152]{1,0:T(8,128)(2,1)}, bf16[16,6912]{1,0:T(8,128)(2,1)})) %all-reduce.5.cloned.1.call-update) | async-done | bytes 5529616
  1539.1 8.9 convolution_convert_fusion
  1548.0 21.4 %copy.141 = bf16[1152,6912]{0,1:T(8,128)(2,1)} copy(bf16[1152,6912]{1,0:T(8,128)(2,1)} %convolution_convert_fusion) | data formatting | bytes 31850496
  1576.0 49.3 %reduce-scatter.34.cloned.1.call-done = bf16[288,576]{1,0:T(8,128)(2,1)} async-done(((bf16[4608,576]{1,0:T(8,128)(2,1)}), bf16[288,576]{1,0:T(8,128)(2,1)}) %reduce-scatter.34.cloned.1.call-update) | async-done | bytes 331792
  1627.6 80.8 %reduce-scatter.36.cloned.1.call-done = bf16[72,2304]{1,0:T(8,128)(2,1)} async-done(((bf16[1152,2304]{1,0:T(8,128)(2,1)}), bf16[72,2304]{1,0:T(8,128)(2,1)}) %reduce-scatter.36.cloned.1.call-update) | async-done | bytes 331792
  1710.8 177.8 %reduce-scatter.38.cloned.1.call-done = bf16[3456,1152]{1,0:T(8,128)(2,1)} async-done(((bf16[6912,1152]{1,0:T(8,128)(2,1)}), bf16[3456,1152]{1,0:T(8,128)(2,1)}) %reduce-scatter.38.cloned.1.call-update) | async-done | bytes 7962640
  1888.6 11.5 copy.142
  1900.1 10.2 convert_element_type.222
  (358 shorter events, 246.5 us)
Async XLA Ops:
  7.2 191.8 %all-gather.8.cloned.1.call-start = ((), (), s32[]{:S(2)}) async-start(), calls=%async_computation.9 | async-start | bytes 23887872 | tf_op jit(solution)/shard_map/all_gather | solution.py:78
  7.9 191.0 %copy-start.33 = (f32[1,16,1152]{2,1,0:T(8,128)S(1)}, f32[1,16,1152]{2,1,0:T(8,128)}, u32[]{:S(2)}) copy-start(f32[1,16,1152]{2,1,0:T(8,128)} %param.18) | copy-start | bytes 221188
  7.9 291.8 %all-gather.10.cloned.1.call-start = ((), (), s32[]{:S(2)}) async-start(), calls=%async_computation.10 | async-start | bytes 11943936 | tf_op jit(solution)/shard_map/all_gather | solution.py:175
  8.7 351.3 %all-gather.12.cloned.1.call-start = ((), (), s32[]{:S(2)}) async-start(), calls=%async_computation.11 | async-start | bytes 5013504 | tf_op jit(solution)/shard_map/all_gather | solution.py:189
  9.7 199.1 %copy-start.40 = (f32[128]{0:T(128)}, f32[128]{0:T(128)S(1)}, u32[]{:S(2)}) copy-start(f32[128]{0:T(128)S(1)} %broadcast_multiply_fusion.1) | copy-start | bytes 1540
  10.0 196.7 %copy-start.52 = (f32[128]{0:T(128)}, f32[128]{0:T(128)S(1)}, u32[]{:S(2)}) copy-start(f32[128]{0:T(128)S(1)} %fusion.47) | copy-start | bytes 1540
  10.0 198.9 %copy-start.48 = (f32[128]{0:T(128)}, f32[128]{0:T(128)S(1)}, u32[]{:S(2)}) copy-start(f32[128]{0:T(128)S(1)} %fusion.75) | copy-start | bytes 1540
  211.0 93.4 %copy-start.21 = (bf16[128,1152]{1,0:T(8,128)(2,1)}, bf16[128,1152]{1,0:T(8,128)(2,1)S(1)}, u32[]{:S(2)}) copy-start(bf16[128,1152]{1,0:T(8,128)(2,1)S(1)} %fusion.45) | copy-start | bytes 884740
  305.2 109.4 %all-gather.14.cloned.1.call-start = ((), (), s32[]{:S(2)}) async-start(), calls=%async_computation.12 | async-start | bytes 5013504 | tf_op jit(solution)/shard_map/all_gather | solution.py:190
  305.8 179.8 %all-gather.16.cloned.1.call-start = ((), (), s32[]{:S(2)}) async-start(), calls=%async_computation.13 | async-start | bytes 3981312 | tf_op jit(solution)/shard_map/all_gather | solution.py:176
  306.4 278.9 %all-gather.18.cloned.1.call-start = ((), (), s32[]{:S(2)}) async-start(), calls=%async_computation.14 | async-start | bytes 15925248 | tf_op jit(solution)/shard_map/all_gather | solution.py:177
  307.0 410.8 %all-gather.20.cloned.1.call-start = ((), (), s32[]{:S(2)}) async-start(), calls=%async_computation.15 | async-start | bytes 15925248 | tf_op jit(solution)/shard_map/all_gather | solution.py:178
  307.8 629.4 %reduce-scatter.30.cloned.1.call-start = ((), (), s32[]{:S(2)}) async-start(), calls=%async_computation.20 | async-start | bytes 5013504
  366.6 54.7 %copy-start.35 = (s32[1,16]{1,0:T(1,128)S(1)}, s32[1,16]{1,0:T(1,128)}, u32[]{:S(2)}) copy-start(s32[1,16]{1,0:T(1,128)} %param.20) | copy-start | bytes 196
  717.8 10.5 copy-start.2
  717.8 10.5 copy-start.8
  717.8 10.5 copy-start.38
  860.3 155.8 %reduce-scatter.32.cloned.1.call-start = ((), (), s32[]{:S(2)}) async-start(), calls=%async_computation.21 | async-start | bytes 5013504
  861.1 156.2 %copy-start.22 = (bf16[128,1152]{1,0:T(8,128)(2,1)S(1)}, bf16[128,1152]{1,0:T(8,128)(2,1)}, u32[]{:S(2)}) copy-start(bf16[128,1152]{1,0:T(8,128)(2,1)} %copy-done.21) | copy-start | bytes 884740
  861.1 193.0 %reduce-scatter.24.cloned.1.call-start = ((), (), s32[]{:S(2)}) async-start(), calls=%async_computation.17 | async-start | bytes 3981312 | tf_op jit(solution)/shard_map/reduce_scatter | solution.py:334
  863.8 287.4 %reduce-scatter.22.cloned.1.call-start = ((), (), s32[]{:S(2)}) async-start(), calls=%async_computation.16 | async-start | bytes 11943936 | tf_op jit(solution)/shard_map/reduce_scatter | solution.py:331
  1022.8 254.5 %reduce-scatter.26.cloned.1.call-start = ((), (), s32[]{:S(2)}) async-start(), calls=%async_computation.18 | async-start | bytes 15925248 | tf_op jit(solution)/shard_map/reduce_scatter | solution.py:337
  1030.2 372.7 %reduce-scatter.28.cloned.1.call-start = ((), (), s32[]{:S(2)}) async-start(), calls=%async_computation.19 | async-start | bytes 15925248 | tf_op jit(solution)/shard_map/reduce_scatter | solution.py:340
  1037.5 8.6 copy-start.20
  1037.5 8.6 copy-start.25
  1037.5 8.6 copy-start.31
  1037.5 8.5 copy-start.51
  1037.5 501.5 %all-reduce.5.cloned.1.call-start = ((), (), s32[]{:S(2)}) async-start(), calls=%async_computation.25 | async-start | bytes 11059200
  1151.2 474.1 %reduce-scatter.34.cloned.1.call-start = ((), (), s32[]{:S(2)}) async-start(), calls=%async_computation.22 | async-start | bytes 6266880
  1285.5 422.9 %reduce-scatter.36.cloned.1.call-start = ((), (), s32[]{:S(2)}) async-start(), calls=%async_computation.23 | async-start | bytes 5640192
  1411.5 127.6 %copy-start.34 = (f32[1,16,1152]{2,1,0:T(8,128)S(1)}, f32[1,16,1152]{2,1,0:T(8,128)}, u32[]{:S(2)}) copy-start(f32[1,16,1152]{2,1,0:T(8,128)} %param.18) | copy-start | bytes 221188
  1411.5 477.1 %reduce-scatter.38.cloned.1.call-start = ((), (), s32[]{:S(2)}) async-start(), calls=%async_computation.24 | async-start | bytes 23887872
  (55 other events, 165.2 us)
Sparse Core Ops, SparseCore 0:
  9.6 189.3 all-gather.7
  200.5 99.1 all-gather.9
  305.4 54.5 all-gather.11
  362.7 51.9 all-gather.13
  416.1 36.7 all-gather.15
  454.3 130.9 all-gather.17
  586.8 130.9 all-gather.19
  860.4 76.6 reduce-scatter.29
  941.5 74.5 reduce-scatter.31
  1018.3 35.8 reduce-scatter.23
  1056.4 94.6 reduce-scatter.21
  1154.0 123.2 reduce-scatter.25
  1279.6 123.2 reduce-scatter.27
  1407.8 131.1 all-reduce.4
  1542.8 82.3 reduce-scatter.33
  1629.7 78.6 reduce-scatter.35
  1710.7 177.9 reduce-scatter.37
where the time goes:
time: 1930 us; the launch traced here: 1920 us
  waiting for transfers between devices  1520 us (79%)
  matrix products  171 us (9%)
  local copies, waits for them, and re-layouts  145 us (8%)
  other arithmetic  53.8 us (3%)
    unnamed x23, waiting for transfers between devices  591 us
    all_gather x1, waiting for transfers between devices, local(): lax.all_gather(ada_weight, 'fsdp', axis=1, tiled=True)  189 us
    reduce_scatter x1, waiting for transfers between devices, local(): lax.psum_scatter(up_term.astype(jnp.bfloat16), 'fsdp', scatter_dimension=...  126 us
    all_gather x1, waiting for transfers between devices, local(): lax.all_gather(down_weight, 'fsdp', axis=0, tiled=True)  124 us
    reduce_scatter x1, waiting for transfers between devices, local(): lax.psum_scatter(down_term.astype(jnp.bfloat16), 'fsdp', scatter_dimensio...  117 us
    reduce_scatter x1, waiting for transfers between devices, local(): lax.psum_scatter(qkv_term.astype(jnp.bfloat16), 'fsdp', scatter_dimension...  97 us
    all_gather x1, waiting for transfers between devices, local(): lax.all_gather(up_weight, 'fsdp', axis=0, tiled=True)  93.6 us
    all_gather x1, waiting for transfers between devices, local(): lax.all_gather(qkv_weight, 'fsdp', axis=0, tiled=True)  88.7 us
  transfers between devices with their start and end apart: 17, of which 16 were waited for; matrix products, arithmetic and copies ran while one was open for 10% of the time, Pallas kernels for 0%

commit v1 on v0

v1 whole, which is shorter than its diff:
```python
import functools

import jax
import jax.numpy as jnp
from jax import lax
from jax.experimental import pallas as pl
from jax.experimental.pallas import tpu as pltpu
from jax.sharding import PartitionSpec as P

D = 1152
H = 16
HD = 72
CHAN_GROUP = 128
PIECE_MAX = 16

bf16 = jnp.bfloat16
f32 = jnp.float32
highest = lax.Precision.HIGHEST
norm_epsilon = 1e-06
masked_score = -1e30
score_scale = HD ** (-0.5)
VMEM_LIMIT = 48 * 1024 * 1024


def head_window(head):
    start = head * HD
    low = start // 128 * 128
    width = 128 if start + HD - low <= 128 else 256
    return low, min(width, D - low), start - low


def head_lanes(rows, width, first):
    lane = lax.broadcasted_iota(jnp.int32, (rows, width), 1)
    return (lane >= first) & (lane < first + HD)


def dot_nt(a, b):
    return lax.dot_general(a, b, (((1,), (1,)), ((), ())), preferred_element_type=f32)


def dot_nn(a, b):
    return lax.dot_general(a, b, (((1,), (0,)), ((), ())), preferred_element_type=f32)


def dot_tn(a, b):
    return lax.dot_general(a, b, (((0,), (0,)), ((), ())), preferred_element_type=f32)


def attend_kernel(q_ref, kv_ref, bias_ref, mask_ref, out_ref, acc_ref):
    tokens = q_ref.shape[0]
    acc_ref[...] = jnp.zeros_like(acc_ref)
    for head in range(H):
        low, width, first = head_window(head)
        window = pl.ds(low, width)
        lanes = head_lanes(tokens, width, first)
        query = jnp.where(lanes, q_ref[:, window], jnp.zeros((), bf16))
        scores = dot_nt(query, kv_ref[:, window]) * score_scale + bias_ref[...]
        top = jnp.max(scores, axis=1, keepdims=True)
        weights = jnp.exp(scores - top)
        probs = (weights * (1.0 / jnp.sum(weights, axis=1, keepdims=True))).astype(bf16)
        out = dot_nn(probs, kv_ref[:, pl.ds(D + low, width)])
        acc_ref[:, window] += jnp.where(lanes, out, 0.0)
    slots = mask_ref.shape[0]
    for start in range(0, tokens, slots):
        rows = pl.ds(start, slots)
        out_ref[rows, :] = (acc_ref[rows, :] * mask_ref[...]).astype(bf16)


def attend(queries, kv_window, bias, head_slots):
    tokens = queries.shape[0]
    return pl.pallas_call(
        attend_kernel,
        out_shape=jax.ShapeDtypeStruct((tokens, D), bf16),
        in_specs=[pl.BlockSpec(memory_space=pltpu.VMEM)] * 4,
        out_specs=pl.BlockSpec(memory_space=pltpu.VMEM),
        scratch_shapes=[pltpu.VMEM((tokens, D), f32)],
        compiler_params=pltpu.CompilerParams(vmem_limit_bytes=VMEM_LIMIT),
        name="attend",
    )(queries, kv_window, bias, head_slots)


def attend_back_kernel(
    q_ref, kv_ref, bias_ref, grad_ref, dq_ref, dkv_ref, dq_acc, dk_acc, dv_acc
):
    tokens = q_ref.shape[0]
    dq_acc[...] = jnp.zeros_like(dq_acc)
    dk_acc[...] = jnp.zeros_like(dk_acc)
    dv_acc[...] = jnp.zeros_like(dv_acc)
    for head in range(H):
        low, width, first = head_window(head)
        window = pl.ds(low, width)
        lanes = head_lanes(tokens, width, first)
        query = jnp.where(lanes, q_ref[:, window], jnp.zeros((), bf16))
        grad = jnp.where(lanes, grad_ref[:, window], jnp.zeros((), bf16))
        keys = kv_ref[:, window]
        scores = dot_nt(keys, query) * score_scale + bias_ref[...]
        top = jnp.max(scores, axis=0, keepdims=True)
        weights = jnp.exp(scores - top)
        probs = weights * (1.0 / jnp.sum(weights, axis=0, keepdims=True))
        probs_low = probs.astype(bf16)
        grad_probs = dot_nt(kv_ref[:, pl.ds(D + low, width)], grad)
        row_dot = jnp.sum(probs_low.astype(f32) * grad_probs, axis=0, keepdims=True)
        grad_scores = (probs * (grad_probs - row_dot)).astype(bf16)
        dk_acc[:, window] += dot_nn(grad_scores, query)
        dv_acc[:, window] += dot_nn(probs_low, grad)
        dq_acc[:, window] += jnp.where(lanes, dot_tn(grad_scores, keys), 0.0)
    dq_ref[...] = (dq_acc[...] * score_scale).astype(bf16)
    dkv_ref[:, pl.ds(0, D)] = (dk_acc[...] * score_scale).astype(bf16)
    dkv_ref[:, pl.ds(D, D)] = dv_acc[...].astype(bf16)


def attend_back(queries, kv_window, bias_t, grad_heads):
    tokens = queries.shape[0]
    keys = kv_window.shape[0]
    return pl.pallas_call(
        attend_back_kernel,
        out_shape=(
            jax.ShapeDtypeStruct((tokens, D), bf16),
            jax.ShapeDtypeStruct((keys, 2 * D), bf16),
        ),
        in_specs=[pl.BlockSpec(memory_space=pltpu.VMEM)] * 4,
        out_specs=(pl.BlockSpec(memory_space=pltpu.VMEM),) * 2,
        scratch_shapes=[
            pltpu.VMEM((tokens, D), f32),
            pltpu.VMEM((keys, D), f32),
            pltpu.VMEM((keys, D), f32),
        ],
        compiler_params=pltpu.CompilerParams(vmem_limit_bytes=VMEM_LIMIT),
        name="attend_back",
    )(queries, kv_window, bias_t, grad_heads)


def assemble_kernel(place_ref, *refs, count, col_start, cols):
    local_ref, piece_refs, out_ref, sems = refs[0], refs[1 : 1 + count], refs[-2], refs[-1]
    half = out_ref.shape[0] // 2
    rows = half // count
    mine, quarter, column = place_ref[0], place_ref[1], place_ref[2]
    source = local_ref.at[:, pl.ds(pl.multiple_of(col_start + column * cols, 128), cols)]
    copies = [
        pltpu.make_async_copy(
            source, out_ref.at[pl.ds(pl.multiple_of(mine * half, 8), half), :], sems.at[count]
        )
    ]
    for step, piece in enumerate(piece_refs):
        start = (1 - mine) * half + (quarter ^ step) * rows
        copies.append(
            pltpu.make_async_copy(
                piece, out_ref.at[pl.ds(pl.multiple_of(start, 8), rows), :], sems.at[step]
            )
        )
    for copy in copies:
        copy.start()
    for copy in copies:
        copy.wait()


def assemble(place, local_weight, pieces, col_start, cols):
    count = len(pieces)
    return pl.pallas_call(
        functools.partial(assemble_kernel, count=count, col_start=col_start, cols=cols),
        out_shape=jax.ShapeDtypeStruct((2 * local_weight.shape[0], cols), bf16),
        in_specs=[pl.BlockSpec(memory_space=pltpu.SMEM)]
        + [pl.BlockSpec(memory_space=pl.ANY)] * (1 + count),
        out_specs=pl.BlockSpec(memory_space=pl.ANY),
        scratch_shapes=[pltpu.SemaphoreType.DMA((count + 1,))],
        name="assemble",
    )(place, local_weight, *pieces)


def layer_norm(values):
    average = jnp.mean(values, axis=-1, keepdims=True)
    centred = values - average
    spread = jnp.mean(centred * centred, axis=-1, keepdims=True)
    inverse = lax.rsqrt(spread + norm_epsilon)
    return centred * inverse, inverse


def layer_norm_back(grad_normed, normed, inverse):
    mean_grad = jnp.mean(grad_normed, axis=-1, keepdims=True)
    mean_dot = jnp.mean(grad_normed * normed, axis=-1, keepdims=True)
    return (grad_normed - mean_grad - normed * mean_dot) * inverse


def running_ends(pieces):
    index = jnp.arange(pieces.shape[0], dtype=jnp.int32)
    return jnp.sum(jnp.where(index[None, :] <= index[:, None], pieces[None, :], 0), axis=1)


def crop_of(slots, ends):
    return jnp.sum((slots[..., None] >= ends[:-1]).astype(jnp.int32), axis=-1)


def one_hot(crops, count):
    return (crops[..., None] == jnp.arange(count, dtype=jnp.int32)).astype(f32)


def block_order(size):
    def device(block):
        chip, core = block // 2, block % 2
        return 2 * (chip ^ ((chip >> 1) & 1)) + core if size % 8 == 0 else block

    return [device(block) for block in range(size)]


def local(
    tokens_in,
    condition,
    crop_pieces,
    pad_counts,
    head_mask,
    channel_mask,
    keep_mask,
    qkv_weight,
    out_weight,
    up_weight,
    down_weight,
    ada_weight,
    cotangent,
):
    seq = lax.axis_size("seq")
    rows = lax.axis_size("fsdp")
    tokens = tokens_in.shape[1]
    slots = tokens // seq
    crops = crop_pieces.shape[1]
    hidden = up_weight.shape[1]
    hidden_part = hidden // rows
    half = D // rows
    seq_at = lax.axis_index("seq")
    row_at = lax.axis_index("fsdp")
    fast = rows == 2 and seq == 16
    order = block_order(seq)
    if seq % 8 == 0:
        chip = seq_at // 2
        block_at = 2 * (chip ^ ((chip >> 1) & 1)) + seq_at % 2
    else:
        block_at = seq_at

    def flip(value, bit):
        return lax.ppermute(value, "seq", [(i, i ^ bit) for i in range(seq)])

    def cross(value):
        return lax.ppermute(value, "fsdp", [(0, 1), (1, 0)])

    def shift(value, distance):
        pairs = [
            (order[b], order[b + distance]) for b in range(seq) if 0 <= b + distance < seq
        ]
        return lax.ppermute(value, "seq", pairs)

    def reorder(blocks):
        runs, start = [], 0
        while start < seq:
            stop = start + 1
            while stop < seq and order[stop] == order[stop - 1] + 1:
                stop += 1
            runs.append(blocks[order[start] : order[start] + stop - start])
            start = stop
        return jnp.concatenate(runs, axis=0) if len(runs) > 1 else blocks

    def to_slots(value):
        return lax.all_to_all(reorder(value.reshape(seq, slots, -1)), "seq", 0, 0)

    def from_slots(value):
        return reorder(lax.all_to_all(value, "seq", 0, 0)).reshape(tokens, -1)

    def gather_rows(value):
        if rows == 2:
            return jnp.stack([value, cross(value)])
        return lax.all_gather(value, "fsdp", axis=0)

    def sum_rows(parts):
        if rows == 2:
            return parts[0] + cross(parts[1].astype(bf16)).astype(f32)
        total = lax.psum_scatter(parts.astype(bf16), "fsdp", scatter_dimension=0, tiled=True)
        return total.reshape(parts.shape[1:]).astype(f32)

    def pick(low_part, high_part):
        return jnp.where(row_at == 0, low_part, high_part)

    slot_index = block_at * slots + jnp.arange(slots, dtype=jnp.int32)
    ends = running_ends(crop_pieces[0])
    crop_here = crop_of(slot_index, ends)
    selector = one_hot(crop_here, crops)
    pads = pad_counts[0]

    cond_act = jax.nn.silu(condition[0]).astype(bf16)
    extra = jnp.concatenate(
        [channel_mask[0].astype(bf16), crop_pieces[0].astype(bf16)[:, None]], axis=1
    )
    extra = jnp.pad(extra, ((0, 0), (0, 128 - extra.shape[1])))
    packed = gather_rows(jnp.concatenate([cond_act, extra], axis=1))
    groups = channel_mask.shape[2]
    cond_rows = packed[:, :, :D]
    group_rows = packed[:, :, D : D + groups].astype(f32)
    ends_rows = jax.vmap(running_ends)(packed[:, :, D + groups].astype(jnp.int32))
    selector_rows = jax.vmap(lambda own: one_hot(crop_of(slot_index, own), crops))(ends_rows)

    columns = ada_weight.shape[1]
    mod_rows = jnp.dot(
        cond_rows.reshape(rows * crops, D), ada_weight, preferred_element_type=f32
    ).reshape(rows, crops, columns)
    if rows == 2:
        mod_slots = jnp.einsum("rsc,rcm->rsm", selector_rows, mod_rows, precision=highest)
        arrived = cross(mod_slots[1])
        mod_attn = pick(mod_slots[0], arrived)
        mod_mlp = pick(arrived, mod_slots[0])
    else:
        mine = lax.all_to_all(mod_rows, "fsdp", 0, 0)
        mine = jnp.transpose(mine, (1, 0, 2)).reshape(crops, rows * columns)
        mine = jnp.dot(selector, mine, precision=highest)
        mod_attn, mod_mlp = mine[:, : 3 * D], mine[:, 3 * D :]
    shift_attn, scale_attn, gate_attn = (mod_attn[:, i * D : (i + 1) * D] for i in range(3))
    shift_mlp, scale_mlp, gate_mlp = (mod_mlp[:, i * D : (i + 1) * D] for i in range(3))

    place = jnp.stack([row_at, seq_at & 3, row_at]).astype(jnp.int32)

    def fetch(weight, row_start, col_start, shape):
        first = lax.dynamic_slice(weight, (row_start, col_start), shape)
        first = cross(first)
        second = flip(first, 2)
        return (first, flip(first, 1), second, flip(second, 1))

    def whole_rows(weight, col_start, cols):
        if not fast:
            part = weight[:, col_start : col_start + cols]
            return lax.all_gather(part, "fsdp", axis=0, tiled=True)
        quarter = weight.shape[0] // 4
        pieces = fetch(weight, (seq_at & 3) * quarter, col_start, (quarter, cols))
        return assemble(place * jnp.array([1, 1, 0], jnp.int32), weight, pieces, col_start, cols)

    kv_full = whole_rows(qkv_weight, D, 2 * D)
    q_full = whole_rows(qkv_weight, 0, D)
    out_full = whole_rows(out_weight, 0, D)
    if fast:
        quarter = half // 4
        pieces = fetch(
            up_weight, (seq_at & 3) * quarter, (1 - row_at) * hidden_part, (quarter, hidden_part)
        )
        up_part = assemble(place, up_weight, pieces, 0, hidden_part)
    else:
        up_part = lax.all_to_all(up_weight, "fsdp", 1, 0, tiled=True)

    residual = to_slots(tokens_in[0]).astype(f32)
    kept = jnp.broadcast_to(keep_mask[0].astype(bf16)[:, None], (tokens, 128))
    late_in = to_slots(jnp.concatenate([cotangent[0], kept], axis=1))
    grad_out = late_in[:, :, :D].astype(f32)
    keep = late_in[:, :, D : D + 1].astype(f32)

    normed_tokens, inverse_in = layer_norm(residual)
    normed_in = (normed_tokens * (1.0 + scale_attn) + shift_attn).astype(bf16)
    normed_in = normed_in.reshape(tokens, D)

    reach = -(-(PIECE_MAX - 1) // slots)
    paired = reach == 2 and seq % 2 == 0
    core = seq_at % 2
    if paired:
        below, above = shift(normed_in, 2), shift(normed_in, -2)
        passed = flip(jnp.where(core == 0, above, below), 1)
        near = [normed_in, flip(normed_in, 1), below, above, passed]
        near_at = [
            block_at,
            block_at ^ 1,
            block_at - 2,
            block_at + 2,
            block_at - 1 + 2 * core,
        ]
    else:
        near, near_at = [normed_in], [block_at]
        for distance in range(1, reach + 1):
            near += [shift(normed_in, distance), shift(normed_in, -distance)]
            near_at += [block_at - distance, block_at + distance]
    window_in = jnp.concatenate(near, axis=0)
    near_at = jnp.stack(near_at)
    key_slots = near_at[:, None] * slots + jnp.arange(slots, dtype=jnp.int32)[None, :]
    key_crop = jnp.where((near_at >= 0)[:, None] & (near_at < seq)[:, None], crop_of(key_slots, ends), -1)
    key_crop = jnp.where(
        key_slots[:, None, :] < tokens - pads[None, :, None], key_crop[:, None, :], -1
    ).reshape(-1)
    query_crop = jnp.broadcast_to(crop_here[None, :], (seq, slots)).reshape(tokens)
    bias = jnp.where(query_crop[:, None] == key_crop[None, :], 0.0, masked_score).astype(f32)
    bias_t = jnp.where(key_crop[:, None] == query_crop[None, :], 0.0, masked_score).astype(f32)
    head_slots = jnp.repeat(
        jnp.dot(selector, head_mask[0].astype(f32), precision=highest), HD, axis=1
    )

    kv_window = jnp.dot(window_in, kv_full, preferred_element_type=f32).astype(bf16)
    queries = jnp.dot(normed_in, q_full, preferred_element_type=f32).astype(bf16)
    merged = attend(queries, kv_window, bias, head_slots)
    attn_proj = jnp.dot(merged, out_full, preferred_element_type=f32).reshape(seq, slots, D)
    mid_state = residual + gate_attn * attn_proj
    normed, inverse_mid = layer_norm(mid_state)
    normed_mid = (normed * (1.0 + scale_mlp) + shift_mlp).astype(bf16).reshape(tokens, D)

    mid_rows = gather_rows(normed_mid).reshape(rows * tokens, D)
    grad_mlp = (grad_out * gate_mlp * keep).astype(bf16).reshape(tokens, D)
    grad_mlp_rows = gather_rows(grad_mlp).reshape(rows * tokens, D)
    channels = jnp.einsum("rsc,rcg->rsg", selector_rows, group_rows, precision=highest)
    channels = lax.dynamic_slice_in_dim(
        jnp.repeat(channels, CHAN_GROUP, axis=2), row_at * hidden_part, hidden_part, 2
    )
    channels = channels[:, None]
    wide = (rows, seq, slots, hidden_part)
    hidden_pre = jnp.dot(mid_rows, up_part, preferred_element_type=f32).reshape(wide)
    root = 0.7978845608028654
    inner = jnp.tanh(root * (hidden_pre + 0.044715 * hidden_pre * hidden_pre * hidden_pre))
    hidden_act = (0.5 * hidden_pre * (1.0 + inner) * channels).astype(bf16)
    hidden_act = hidden_act.reshape(rows * tokens, hidden_part)
    slope = 0.5 * (1.0 + inner) + 0.5 * hidden_pre * (1.0 - inner * inner) * root * (
        1.0 + 3.0 * 0.044715 * hidden_pre * hidden_pre
    )
    grad_act = lax.dot_general(
        grad_mlp_rows, down_weight, (((1,), (1,)), ((), ())), preferred_element_type=f32
    ).reshape(wide)
    grad_pre = (grad_act * channels * slope).astype(bf16).reshape(rows * tokens, hidden_part)
    grad_parts = lax.dot_general(
        grad_pre, up_part, (((1,), (1,)), ((), ())), preferred_element_type=f32
    )
    grad_normed_mid = sum_rows(grad_parts.reshape(rows, tokens, D)).reshape(seq, slots, D)
    mlp_parts = jnp.dot(hidden_act, down_weight, preferred_element_type=f32)
    mlp_out = sum_rows(mlp_parts.reshape(rows, tokens, D)).reshape(seq, slots, D)
    block_out = from_slots((mid_state + gate_mlp * keep * mlp_out).astype(bf16))

    grad_mid = grad_out + layer_norm_back(
        grad_normed_mid * (1.0 + scale_mlp), normed, inverse_mid
    )
    grad_attn = (grad_mid * gate_attn).astype(bf16).reshape(tokens, D)
    grad_merged = lax.dot_general(
        grad_attn, out_full, (((1,), (1,)), ((), ())), preferred_element_type=f32
    )
    grad_heads = (grad_merged.reshape(seq, slots, D) * head_slots).astype(bf16)
    grad_queries, grad_window = attend_back(
        queries, kv_window, bias_t, grad_heads.reshape(tokens, D)
    )
    parts = grad_window.reshape(-1, tokens, 2 * D)
    grad_kv = parts[0].astype(f32)
    if paired:
        handed = flip(parts[4], 1).astype(f32)
        down_part = (parts[2].astype(f32) + jnp.where(core == 1, handed, 0.0)).astype(bf16)
        up_side = (parts[3].astype(f32) + jnp.where(core == 0, handed, 0.0)).astype(bf16)
        grad_kv = grad_kv + flip(parts[1], 1).astype(f32)
        grad_kv = grad_kv + shift(down_part, -2).astype(f32) + shift(up_side, 2).astype(f32)
    else:
        for distance in range(1, reach + 1):
            grad_kv = grad_kv + shift(parts[2 * distance - 1], -distance).astype(f32)
            grad_kv = grad_kv + shift(parts[2 * distance], distance).astype(f32)
    grad_kv = grad_kv.astype(bf16)

    contract = (((1,), (1,)), ((), ()))
    grad_normed_in = lax.dot_general(grad_queries, q_full, contract, preferred_element_type=f32)
    grad_normed_in = grad_normed_in + lax.dot_general(
        grad_kv, kv_full, contract, preferred_element_type=f32
    )
    grad_normed_in = grad_normed_in.reshape(seq, slots, D)
    input_grad = grad_mid + layer_norm_back(
        grad_normed_in * (1.0 + scale_attn), normed_tokens, inverse_in
    )
    input_grad = from_slots(input_grad.astype(bf16)).astype(f32)

    def by_crop(parts_list):
        return jnp.dot(
            jnp.transpose(selector), jnp.concatenate(parts_list, axis=1), precision=highest
        ).astype(bf16)

    def all_sum(value):
        if not fast:
            return lax.psum(value, "seq")
        for bit in (1, 2, 4, 8):
            value = (value.astype(f32) + flip(value, bit).astype(f32)).astype(bf16)
        return value

    early = all_sum(
        by_crop(
            [
                jnp.sum(grad_mid * attn_proj, axis=0),
                jnp.sum(grad_normed_mid, axis=0),
                jnp.sum(grad_normed_mid * normed, axis=0),
                jnp.sum(grad_out * keep * mlp_out, axis=0),
            ]
        )
    )
    late = all_sum(
        by_crop(
            [jnp.sum(grad_normed_in, axis=0), jnp.sum(grad_normed_in * normed_tokens, axis=0)]
        )
    )
    mod_grads = jnp.concatenate([late, early], axis=1)
    if rows == 2:
        own = pick(mod_grads[:, : 3 * D], mod_grads[:, 3 * D :])
        other = cross(pick(mod_grads[:, 3 * D :], mod_grads[:, : 3 * D]))
        mod_grads = jnp.stack([own, other])
    else:
        split = jnp.transpose(mod_grads.reshape(crops, rows, columns), (1, 0, 2))
        mod_grads = lax.all_to_all(split, "fsdp", 0, 0)
    ada_grad = lax.dot_general(
        cond_rows.reshape(rows * crops, D),
        mod_grads.reshape(rows * crops, columns),
        (((0,), (0,)), ((), ())),
        preferred_element_type=f32,
    )

    def term(acts, grads):
        return lax.dot_general(
            acts, grads, (((0,), (0,)), ((), ())), preferred_element_type=f32
        ).astype(bf16)

    if not fast:

        def both(value):
            value = lax.psum_scatter(value, "fsdp", scatter_dimension=0, tiled=True)
            return lax.psum_scatter(value, "seq", scatter_dimension=1, tiled=True).astype(f32)

        grad_qkv = jnp.concatenate([grad_queries, grad_kv], axis=1)
        qkv_grad = both(term(normed_in, grad_qkv))
        out_grad = both(term(merged, grad_attn))
        up_cols = lax.all_to_all(term(mid_rows, grad_pre), "fsdp", 0, 1, tiled=True)
        up_grad = lax.psum_scatter(up_cols, "seq", scatter_dimension=1, tiled=True).astype(f32)
        down_cols = term(hidden_act, grad_mlp_rows)
        down_grad = lax.psum_scatter(
            down_cols, "seq", scatter_dimension=1, tiled=True
        ).astype(f32)
    else:

        def pooled(grads, acts, chunks):
            grads = grads.reshape(chunks, 2, grads.shape[0] // (2 * chunks), grads.shape[1])
            mine = lax.dynamic_index_in_dim(grads, core, 1, keepdims=False)
            other = lax.dynamic_index_in_dim(grads, 1 - core, 1, keepdims=False)
            grads = jnp.concatenate([mine, flip(other, 1)], axis=2)
            acts = jnp.concatenate([acts, flip(acts, 1)], axis=0)
            result = lax.dot_general(
                grads.reshape(-1, grads.shape[2]),
                acts,
                (((1,), (0,)), ((), ())),
                preferred_element_type=f32,
            ).astype(bf16)
            return result.reshape(chunks, -1, acts.shape[1])

        bits = {2: 8, 1: 4, 0: 2}

        def scatter(value, axes):
            axes = list(axes)
            for position, axis in enumerate(axes):
                bit = bits[axis]
                at = (seq_at // bit) % 2
                where = 2 - axis
                keep_part = lax.dynamic_index_in_dim(value, at, where, keepdims=True)
                send_part = lax.dynamic_index_in_dim(value, 1 - at, where, keepdims=True)
                value = keep_part.astype(f32) + flip(send_part, bit).astype(f32)
                if position < len(axes) - 1:
                    value = value.astype(bf16)
            return value[0, 0, 0]

        def own_half(value):
            return pick(value[:, :half], value[:, half:])

        def two_rows(acts):
            sent = pick(acts[:, half:], acts[:, :half])
            return jnp.concatenate([own_half(acts), cross(sent)], axis=0)

        def two_grads(grads):
            return jnp.concatenate([grads, cross(grads)], axis=1)

        down_value = pooled(jnp.transpose(grad_mlp_rows), hidden_act, 8)
        down_grad = scatter(down_value.reshape(2, 2, 2, *down_value.shape[1:]), (0, 1, 2))
        down_grad = jnp.transpose(down_grad)

        up_value = pooled(jnp.transpose(grad_pre), mid_rows, 4)
        chunk = up_value.shape[1]
        up_value = up_value.reshape(2, 2, chunk, 2, half)
        up_value = jnp.transpose(up_value, (3, 0, 1, 2, 4))
        up_mine = scatter(up_value, (1, 0, 2)).astype(bf16)
        pairs = []
        for place_seq in range(seq):
            for place_row in range(2):
                high = (place_seq // 8) % 2
                target_seq = (place_seq & 7) | (place_row * 8)
                pairs.append((place_seq * 2 + place_row, target_seq * 2 + high))
        up_grad = jnp.transpose(lax.ppermute(up_mine, ("seq", "fsdp"), pairs)).astype(f32)

        out_value = pooled(two_grads(jnp.transpose(grad_attn)), two_rows(merged), 8)
        out_grad = scatter(out_value.reshape(2, 2, 2, *out_value.shape[1:]), (0, 1, 2))
        out_grad = jnp.transpose(out_grad)

        grad_qkv = jnp.concatenate([grad_queries, grad_kv], axis=1)
        qkv_value = pooled(two_grads(jnp.transpose(grad_qkv)), two_rows(normed_in), 8)
        qkv_grad = scatter(qkv_value.reshape(2, 2, 2, *qkv_value.shape[1:]), (0, 1, 2))
        qkv_grad = jnp.transpose(qkv_grad)

    return (
        block_out[None],
        input_grad[None],
        qkv_grad,
        out_grad,
        up_grad,
        down_grad,
        ada_grad,
    )


def solution(mesh):
    in_specs = (
        P("fsdp", "seq", None),
        P("fsdp", None, None),
        P("fsdp", None),
        P("fsdp", None),
        P("fsdp", None, None),
        P("fsdp", None, None),
        P("fsdp", "seq"),
        P("fsdp", None),
        P("fsdp", None),
        P("fsdp", None),
        P("fsdp", None),
        P(None, "fsdp"),
        P("fsdp", "seq", None),
    )
    out_specs = (
        P("fsdp", "seq", None),
        P("fsdp", "seq", None),
        P("fsdp", "seq"),
        P("fsdp", "seq"),
        P("fsdp", "seq"),
        P("fsdp", "seq"),
        P(None, "fsdp"),
    )
    return jax.shard_map(local, mesh=mesh, in_specs=in_specs, out_specs=out_specs, check_vma=False)
```

time: 1930 us -> 932 us (0.48)
  waiting for transfers between devices: 1520 us -> 160 us
  Pallas kernels: 0 us -> 505 us
  matrix products: 171 us -> 59 us
  starting transfers between devices: 0.68 us -> 91.3 us
  local copies, waits for them, and re-layouts: 145 us -> 60.6 us
    unnamed x23 -> x0, waiting for transfers between devices: 591 us -> none
    all_gather x7 -> x0, waiting for transfers between devices: 589 us -> none  [the longest x1 189 us: local(): lax.all_gather(ada_weight, 'fsdp', axis=1, tiled=True)]
    pallas_call x0 -> x6, Pallas kernels: none -> 505 us  [the longest x4 490 us: assemble(): pl.pallas_call(functools.partial(assemble_kernel, count=count, col_start=...]
    reduce_scatter x4 -> x0, waiting for transfers between devices: 344 us -> none  [the longest x1 126 us: local(): lax.psum_scatter(up_term.astype(jnp.bfloat16), 'fsdp', scatter_dimension=...]
    ppermute x0 -> x64, waiting for transfers between devices: none -> 151 us  [the longest x44 99.2 us: flip(): return lax.ppermute(value, 'seq', [(i, i ^ bit) for i in range(seq)])]
    dot_general x46 -> x21, matrix products: 171 us -> 59 us  [the longest x4 13.2 us: pooled(): lax.dot_general(grads.reshape(-1, grads.shape[2]), acts, (((1,), (0,)), (...]
    ppermute x0 -> x64, starting transfers between devices: none -> 71.7 us  [the longest x44 41.3 us: flip(): return lax.ppermute(value, 'seq', [(i, i ^ bit) for i in range(seq)])]
    unnamed x133 -> x191, local copies, waits for them, and re-layouts: 82.1 us -> 17.6 us
  transfers between devices with their start and end apart: 17 -> 68, of which waited for: 16 -> 25; matrix products, arithmetic and copies ran while one was open for 10% -> 17% of each run, Pallas kernels for 0% -> 55%
where the time goes in v1:
time: 932 us; the launch traced here: 925 us
  Pallas kernels  505 us (54%)
  waiting for transfers between devices  160 us (17%)
  starting transfers between devices  91.3 us (10%)
  local copies, waits for them, and re-layouts  60.6 us (7%)
  matrix products  59 us (6%)
  other arithmetic  46.6 us (5%)
    pallas_call x4, Pallas kernels, assemble(): pl.pallas_call(functools.partial(assemble_kernel, count=count, col_start=...  490 us
    ppermute x44, waiting for transfers between devices, flip(): return lax.ppermute(value, 'seq', [(i, i ^ bit) for i in range(seq)])  99.2 us
    ppermute x44, starting transfers between devices, flip(): return lax.ppermute(value, 'seq', [(i, i ^ bit) for i in range(seq)])  41.3 us
    ppermute x15, waiting for transfers between devices, cross(): return lax.ppermute(value, 'fsdp', [(0, 1), (1, 0)])  35.2 us
  transfers between devices with their start and end apart: 68, of which 25 were waited for; matrix products, arithmetic and copies ran while one was open for 17% of the time, Pallas kernels for 55%

profile of v1, /device:TPU:2, one launch (start us, length us, event | category | flops | bytes accessed | tf_op | source)
XLA Modules:
  0.0 925.4 jit_solution(14173400731746868195)
XLA Ops:
  11.9 6.6 all-to-all-start
  35.5 4.5 fusion
  41.9 11.6 %collective-permute-done.1 = f32[8,3456]{1,0:T(8,128)S(1)} collective-permute-done((f32[8,3456]{1,0:T(8,128)S(1)}, f32[8,3456]{1,0:T(8,128)S(1)}, u32[]{:S(2)}, u32[]{:S(2)}) %collective-permute-start.1) | collective-permute-done | bytes 110624 | tf_op jit(solution)/shard_map/ppermute | solution.py:242
  56.5 4.8 all-to-all-start.1
  63.8 8.6 all-to-all-done.1
  101.4 6.6 collective-permute-done.12.refs_3_
  108.8 82.2 %assemble.4 = bf16[1152,1152]{1,0:T(8,128)(2,1)} custom-call(s32[3]{0:T(128)} %get-tuple-element.23.place_ref, bf16[576,3456]{1,0:T(8,128)(2,1)} %refs_0_.5, bf16[144,1152]{1,0:T(8,128)(2,1)} %copy-done.54, bf16[144,1152]{1,0:T(8,128)(2,1)} %copy-done.56, bf16[144,1152]{1,0:T(8,128)(2,1)} %copy-done.55, bf16[144,1152]{1,0:T(8,128)(2,1)} %copy-done.57), custom_call_target="tpu_custom_call" | custom-call | tf_op jit(solution)/shard_map/assemble/pallas_call | solution.py:159
  191.7 82.3 %assemble.6 = bf16[1152,1152]{1,0:T(8,128)(2,1)} custom-call(s32[3]{0:T(128)} %get-tuple-element.23.place_ref, bf16[576,1152]{1,0:T(8,128)(2,1)} %refs_0_.6, bf16[144,1152]{1,0:T(8,128)(2,1)} %collective-permute-done.14.refs_1_, bf16[144,1152]{1,0:T(8,128)(2,1)} %collective-permute-done.15.refs_2_, bf16[144,1152]{1,0:T(8,128)(2,1)} %copy-done.58, ...), custom_call_target="tpu_custom_call" | custom-call | tf_op jit(solution)/shard_map/assemble/pallas_call | solution.py:159
  277.9 162.6 %assemble.5 = bf16[1152,2304]{1,0:T(8,128)(2,1)} custom-call(s32[3]{0:T(128)} %get-tuple-element.23.place_ref, bf16[576,3456]{1,0:T(8,128)(2,1)} %refs_0_.5, bf16[144,2304]{1,0:T(8,128)(2,1)} %collective-permute-done.10.refs_1_, bf16[144,2304]{1,0:T(8,128)(2,1)} %collective-permute-done.11.refs_2_, bf16[144,2304]{1,0:T(8,128)(2,1)} %collective-permute-done.12.refs_3_, ...), custom_call_target="tpu_custom_call" | custom-call | tf_op jit(solution)/shard_map/assemble/pallas_call | solution.py:159
  440.6 7.0 convolution_convert_fusion.2.kv_ref
  447.6 5.0 attend.1
  458.9 162.8 %assemble.7 = bf16[1152,2304]{1,0:T(8,128)(2,1)} custom-call(s32[3]{0:T(128)} %get-tuple-element.24.place_ref, bf16[576,4608]{1,0:T(8,128)(2,1)} %refs_0_.7, bf16[144,2304]{1,0:T(8,128)(2,1)} %collective-permute-done.19.refs_1_, bf16[144,2304]{1,0:T(8,128)(2,1)} %copy-done.40, bf16[144,2304]{1,0:T(8,128)(2,1)} %collective-permute-done.21.refs_3_, ...), custom_call_target="tpu_custom_call" | custom-call | tf_op jit(solution)/shard_map/assemble/pallas_call | solution.py:159
  622.8 5.7 multiply_convert_fusion
  628.7 6.1 fusion.165
  653.9 4.8 collective-permute-done.23
  662.9 10.6 %attend_back.1 = (bf16[128,1152]{1,0:T(8,128)(2,1)S(1)}, bf16[640,2304]{1,0:T(8,128)(2,1)S(1)}) custom-call(bf16[128,1152]{1,0:T(8,128)(2,1)S(1)} %convolution_convert_fusion.6.q_ref, bf16[640,2304]{1,0:T(8,128)(2,1)} %copy-done, f32[640,128]{1,0:T(8,128)S(1)} %copy-done.2, bf16[128,1152]{1,0:T(8,128)(2,1)S(1)} %fusion.32.grad_ref), custom_call_target="tpu_custom_call" | custom-call | tf_op jit(solution)/shard_map/attend_back/pallas_call | solution.py:115
  689.9 4.7 convolution_convert_fusion
  694.6 7.4 reshape_reshape.14
  701.9 5.0 constant_dynamic-slice_fusion.7
  714.5 6.5 collective-permute-done.62
  723.9 4.6 collective-permute-start.29
  733.1 6.7 collective-permute-done.28
  750.2 21.9 %collective-permute-done.56 = bf16[16,2304]{1,0:T(8,128)(2,1)S(1)} collective-permute-done((bf16[16,2304]{1,0:T(8,128)(2,1)S(1)}, bf16[16,2304]{1,0:T(8,128)(2,1)S(1)}, u32[]{:S(2)}, u32[]{:S(2)}) %collective-permute-start.56) | collective-permute-done | bytes 73760 | tf_op jit(solution)/shard_map/ppermute | solution.py:239
  784.4 7.5 collective-permute-done.37
  798.4 9.2 convolution_bitcast_fusion
  818.1 21.3 %collective-permute-done.41 = bf16[2,2,1,72,576]{4,3,2,1,0:T(8,128)(2,1)} collective-permute-done((bf16[2,2,1,72,576]{4,3,2,1,0:T(8,128)(2,1)}, bf16[2,2,1,72,576]{4,3,2,1,0:T(8,128)(2,1)}, u32[]{:S(2)}, u32[]{:S(2)}) %collective-permute-start.41) | collective-permute-done | bytes 331808 | tf_op jit(solution)/shard_map/ppermute | solution.py:239
  864.9 8.4 collective-permute-done.48
  877.8 7.5 collective-permute-done.34
  890.0 5.2 collective-permute-done.49
  896.0 8.5 collective-permute-done.35
  904.7 6.8 collective-permute-start.36
  912.5 11.8 %collective-permute-done.36 = bf16[1,1,1,216,576]{4,3,2,1,0:T(8,128)(2,1)S(1)} collective-permute-done((bf16[1,1,1,216,576]{4,3,2,1,0:T(8,128)(2,1)S(1)}, bf16[1,1,1,216,576]{4,3,2,1,0:T(8,128)(2,1)S(1)}, u32[]{:S(2)}, u32[]{:S(2)}) %collective-permute-start.36) | collective-permute-done | bytes 248864 | tf_op jit(solution)/shard_map/ppermute | solution.py:239
  (462 shorter events, 208.3 us)
Async XLA Ops:
  3.2 31.8 %collective-permute-start = (bf16[16,1280]{1,0:T(8,128)(2,1)S(1)}, bf16[16,1280]{1,0:T(8,128)(2,1)S(1)}, u32[]{:S(2)}, u32[]{:S(2)}) collective-permute-start(bf16[16,1280]{1,0:T(8,128)(2,1)S(1)} %get-tuple-element.64), channel_id=1, source_target_pairs={{0,1},{1,0},{2,3},{3,2},{4,5},{5,4},{6,7},{7,6},{8,9},{9,8},{10,11... | collective-permute-start | bytes 122888 | tf_op jit(solution)/shard_map/ppermute | solution.py:242
  11.9 44.7 %all-to-all-start = ((bf16[16,8,1152]{2,1,0:T(8,128)(2,1)}), bf16[16,8,1152]{2,1,0:T(8,128)(2,1)S(1)}, u32[]{:S(2)}, u32[]{:S(2)}) async-start(bf16[16,8,1152]{2,1,0:T(8,128)(2,1)} %constant_dynamic-update-slice_fusion), calls=%async_computation | async-start | bytes 589824 | tf_op jit(solution)/shard_map/all_to_all | solution.py:261
  19.6 56.9 %collective-permute-start.10 = (bf16[144,2304]{1,0:T(8,128)(2,1)S(1)}, bf16[144,2304]{1,0:T(8,128)(2,1)}, u32[]{:S(2)}, u32[]{:S(2)}) collective-permute-start(bf16[144,2304]{1,0:T(8,128)(2,1)S(1)} %constant_dynamic-slice_fusion.20), channel_id=1, source_target_pairs={{0,1},{1,0},{2,3},{3,2},{4,5},{5,4},{6,7},{7,6},{8,9},{9,8},{10,11... | collective-permute-start | bytes 1990664 | tf_op jit(solution)/shard_map/ppermute | solution.py:242
  22.2 32.6 %collective-permute-start.2 = (bf16[144,1152]{1,0:T(8,128)(2,1)S(1)}, bf16[144,1152]{1,0:T(8,128)(2,1)S(1)}, u32[]{:S(2)}, u32[]{:S(2)}) collective-permute-start(bf16[144,1152]{1,0:T(8,128)(2,1)S(1)} %constant_dynamic-slice_fusion.19), channel_id=1, source_target_pairs={{0,1},{1,0},{2,3},{3,2},{4,5},{5,4},{6,7},{7,6},{8,9},{9,8},{10,11... | collective-permute-start | bytes 995336 | tf_op jit(solution)/shard_map/ppermute | solution.py:242
  24.5 49.5 %collective-permute-start.14 = (bf16[144,1152]{1,0:T(8,128)(2,1)}, bf16[144,1152]{1,0:T(8,128)(2,1)}, u32[]{:S(2)}, u32[]{:S(2)}) collective-permute-start(bf16[144,1152]{1,0:T(8,128)(2,1)} %constant_dynamic-slice_fusion.18), channel_id=1, source_target_pairs={{0,1},{1,0},{2,3},{3,2},{4,5},{5,4},{6,7},{7,6},{8,9},{9,8},{10,11... | collective-permute-start | bytes 995336 | tf_op jit(solution)/shard_map/ppermute | solution.py:242
  56.5 26.2 %collective-permute-start.3 = (bf16[144,1152]{1,0:T(8,128)(2,1)S(1)}, bf16[144,1152]{1,0:T(8,128)(2,1)S(1)}, u32[]{:S(2)}, u32[]{:S(2)}) collective-permute-start(bf16[144,1152]{1,0:T(8,128)(2,1)S(1)} %collective-permute-done.2.refs_1_), channel_id=1, source_target_pairs={{0,2},{2,0},{4,6},{6,4},{8,10},{10,8},{12,14},{14,12},{16,18},{18,... | collective-permute-start | bytes 995336 | tf_op jit(solution)/shard_map/ppermute | solution.py:239
  84.3 23.8 %collective-permute-start.12 = (bf16[144,2304]{1,0:T(8,128)(2,1)}, bf16[144,2304]{1,0:T(8,128)(2,1)}, u32[]{:S(2)}, u32[]{:S(2)}) collective-permute-start(bf16[144,2304]{1,0:T(8,128)(2,1)} %collective-permute-done.10.refs_1_), channel_id=1, source_target_pairs={{0,4},{2,6},{4,0},{6,2},{8,12},{10,14},{12,8},{14,10},{16,20},{18,... | collective-permute-start | bytes 1990664 | tf_op jit(solution)/shard_map/ppermute | solution.py:239
  88.6 102.4 %collective-permute-start.15 = (bf16[144,1152]{1,0:T(8,128)(2,1)}, bf16[144,1152]{1,0:T(8,128)(2,1)}, u32[]{:S(2)}, u32[]{:S(2)}) collective-permute-start(bf16[144,1152]{1,0:T(8,128)(2,1)} %collective-permute-done.14.refs_1_), channel_id=1, source_target_pairs={{0,2},{2,0},{4,6},{6,4},{8,10},{10,8},{12,14},{14,12},{16,18},{18,... | collective-permute-start | bytes 995336 | tf_op jit(solution)/shard_map/ppermute | solution.py:239
  93.7 97.8 %collective-permute-start.17 = (bf16[144,1152]{1,0:T(8,128)(2,1)S(1)}, bf16[144,1152]{1,0:T(8,128)(2,1)}, u32[]{:S(2)}, u32[]{:S(2)}) collective-permute-start(bf16[144,1152]{1,0:T(8,128)(2,1)S(1)} %collective-permute-done.16.refs_3_), channel_id=1, source_target_pairs={{0,2},{2,0},{4,6},{6,4},{8,10},{10,8},{12,14},{14,12},{16,18},{18,... | collective-permute-start | bytes 995336 | tf_op jit(solution)/shard_map/ppermute | solution.py:239
  99.0 179.0 %collective-permute-start.11 = (bf16[144,2304]{1,0:T(8,128)(2,1)}, bf16[144,2304]{1,0:T(8,128)(2,1)}, u32[]{:S(2)}, u32[]{:S(2)}) collective-permute-start(bf16[144,2304]{1,0:T(8,128)(2,1)} %collective-permute-done.10.refs_1_), channel_id=1, source_target_pairs={{0,2},{2,0},{4,6},{6,4},{8,10},{10,8},{12,14},{14,12},{16,18},{18,... | collective-permute-start | bytes 1990664 | tf_op jit(solution)/shard_map/ppermute | solution.py:239
  99.0 178.7 %collective-permute-start.21 = (bf16[144,2304]{1,0:T(8,128)(2,1)}, bf16[144,2304]{1,0:T(8,128)(2,1)}, u32[]{:S(2)}, u32[]{:S(2)}) collective-permute-start(bf16[144,2304]{1,0:T(8,128)(2,1)} %collective-permute-done.19.refs_1_), channel_id=1, source_target_pairs={{0,4},{2,6},{4,0},{6,2},{8,12},{10,14},{12,8},{14,10},{16,20},{18,... | collective-permute-start | bytes 1990664 | tf_op jit(solution)/shard_map/ppermute | solution.py:239
  108.0 169.9 %collective-permute-start.13 = (bf16[144,2304]{1,0:T(8,128)(2,1)}, bf16[144,2304]{1,0:T(8,128)(2,1)}, u32[]{:S(2)}, u32[]{:S(2)}) collective-permute-start(bf16[144,2304]{1,0:T(8,128)(2,1)} %collective-permute-done.12.refs_3_), channel_id=1, source_target_pairs={{0,2},{2,0},{4,6},{6,4},{8,10},{10,8},{12,14},{14,12},{16,18},{18,... | collective-permute-start | bytes 1990664 | tf_op jit(solution)/shard_map/ppermute | solution.py:239
  191.1 443.8 %collective-permute-start.24 = (bf16[128,1152]{1,0:T(8,128)(2,1)}, bf16[128,1152]{1,0:T(8,128)(2,1)}, u32[]{:S(2)}, u32[]{:S(2)}) collective-permute-start(bf16[128,1152]{1,0:T(8,128)(2,1)} %get-tuple-element.47), channel_id=1, source_target_pairs={{0,1},{1,0},{2,3},{3,2},{4,5},{5,4},{6,7},{7,6},{8,9},{9,8},{10,11... | collective-permute-start | bytes 884744 | tf_op jit(solution)/shard_map/ppermute | solution.py:242
  191.5 84.2 %collective-permute-start.9 = (bf16[128,1152]{1,0:T(8,128)(2,1)}, bf16[128,1152]{1,0:T(8,128)(2,1)}, u32[]{:S(2)}, u32[]{:S(2)}) collective-permute-start(bf16[128,1152]{1,0:T(8,128)(2,1)} %get-tuple-element.54), channel_id=1, source_target_pairs={{0,2},{2,0},{4,6},{6,4},{8,10},{10,8},{12,14},{14,12},{16,18},{18,... | collective-permute-start | bytes 884744 | tf_op jit(solution)/shard_map/ppermute | solution.py:239
  275.7 182.2 %collective-permute-start.20 = (bf16[144,2304]{1,0:T(8,128)(2,1)}, bf16[144,2304]{1,0:T(8,128)(2,1)S(1)}, u32[]{:S(2)}, u32[]{:S(2)}) collective-permute-start(bf16[144,2304]{1,0:T(8,128)(2,1)} %collective-permute-done.19.refs_1_), channel_id=1, source_target_pairs={{0,2},{2,0},{4,6},{6,4},{8,10},{10,8},{12,14},{14,12},{16,18},{18,... | collective-permute-start | bytes 1990664 | tf_op jit(solution)/shard_map/ppermute | solution.py:239
  277.7 180.2 %collective-permute-start.22 = (bf16[144,2304]{1,0:T(8,128)(2,1)}, bf16[144,2304]{1,0:T(8,128)(2,1)S(1)}, u32[]{:S(2)}, u32[]{:S(2)}) collective-permute-start(bf16[144,2304]{1,0:T(8,128)(2,1)} %collective-permute-done.21.refs_3_), channel_id=1, source_target_pairs={{0,2},{2,0},{4,6},{6,4},{8,10},{10,8},{12,14},{14,12},{16,18},{18,... | collective-permute-start | bytes 1990664 | tf_op jit(solution)/shard_map/ppermute | solution.py:239
  454.7 168.1 %collective-permute-start.18 = (bf16[128,1152]{1,0:T(8,128)(2,1)S(1)}, bf16[128,1152]{1,0:T(8,128)(2,1)S(1)}, u32[]{:S(2)}, u32[]{:S(2)}) collective-permute-start(bf16[128,1152]{1,0:T(8,128)(2,1)S(1)} %fusion.185), channel_id=1, source_target_pairs={{0,1},{1,0},{2,3},{3,2},{4,5},{5,4},{6,7},{7,6},{8,9},{9,8},{10,11... | collective-permute-start | bytes 884744 | tf_op jit(solution)/shard_map/ppermute | solution.py:242
  456.5 165.1 %collective-permute-start.39 = (bf16[128,576]{1,0:T(8,128)(2,1)S(1)}, bf16[128,576]{1,0:T(8,128)(2,1)S(1)}, u32[]{:S(2)}, u32[]{:S(2)}) collective-permute-start(bf16[128,576]{1,0:T(8,128)(2,1)S(1)} %get-tuple-element.51), channel_id=1, source_target_pairs={{0,1},{1,0},{2,3},{3,2},{4,5},{5,4},{6,7},{7,6},{8,9},{9,8},{10,11... | collective-permute-start | bytes 442376 | tf_op jit(solution)/shard_map/ppermute | solution.py:242
  457.8 395.8 %collective-permute-start.33 = (bf16[256,576]{1,0:T(8,128)(2,1)}, bf16[256,576]{1,0:T(8,128)(2,1)}, u32[]{:S(2)}, u32[]{:S(2)}) collective-permute-start(bf16[256,576]{1,0:T(8,128)(2,1)} %pad_maximum_fusion.4), channel_id=1, source_target_pairs={{0,2},{2,0},{4,6},{6,4},{8,10},{10,8},{12,14},{14,12},{16,18},{18,... | collective-permute-start | bytes 884744 | tf_op jit(solution)/shard_map/ppermute | solution.py:239
  622.4 189.8 %collective-permute-start.40 = (bf16[256,576]{1,0:T(8,128)(2,1)}, bf16[256,576]{1,0:T(8,128)(2,1)}, u32[]{:S(2)}, u32[]{:S(2)}) collective-permute-start(bf16[256,576]{1,0:T(8,128)(2,1)} %pad_maximum_fusion.5), channel_id=1, source_target_pairs={{0,2},{2,0},{4,6},{6,4},{8,10},{10,8},{12,14},{14,12},{16,18},{18,... | collective-permute-start | bytes 884744 | tf_op jit(solution)/shard_map/ppermute | solution.py:239
  628.5 95.4 %collective-permute-start.51 = (bf16[256,2304]{1,0:T(8,128)(2,1)}, bf16[256,2304]{1,0:T(8,128)(2,1)}, u32[]{:S(2)}, u32[]{:S(2)}) collective-permute-start(bf16[256,2304]{1,0:T(8,128)(2,1)} %bitcast.41), channel_id=1, source_target_pairs={{0,2},{2,0},{4,6},{6,4},{8,10},{10,8},{12,14},{14,12},{16,18},{18,... | collective-permute-start | bytes 3538952 | tf_op jit(solution)/shard_map/ppermute | solution.py:239
  652.8 35.1 %collective-permute-start.45 = (bf16[256,1152]{1,0:T(8,128)(2,1)}, bf16[256,1152]{1,0:T(8,128)(2,1)}, u32[]{:S(2)}, u32[]{:S(2)}) collective-permute-start(bf16[256,1152]{1,0:T(8,128)(2,1)} %bitcast.83), channel_id=1, source_target_pairs={{0,2},{2,0},{4,6},{6,4},{8,10},{10,8},{12,14},{14,12},{16,18},{18,... | collective-permute-start | bytes 1769480 | tf_op jit(solution)/shard_map/ppermute | solution.py:239
  679.3 30.6 %all-to-all-start.2 = ((bf16[16,8,1152]{2,1,0:T(8,128)(2,1)}), bf16[16,8,1152]{2,1,0:T(8,128)(2,1)S(1)}, u32[]{:S(2)}, u32[]{:S(2)}) async-start(bf16[16,8,1152]{2,1,0:T(8,128)(2,1)} %get-tuple-element.34), calls=%async_computation.2 | async-start | bytes 589824 | tf_op jit(solution)/shard_map/all_to_all | solution.py:264
  708.2 24.9 %collective-permute-start.26 = (bf16[128,2304]{1,0:T(8,128)(2,1)}, bf16[128,2304]{1,0:T(8,128)(2,1)}, u32[]{:S(2)}, u32[]{:S(2)}) collective-permute-start(bf16[128,2304]{1,0:T(8,128)(2,1)} %get-tuple-element.29), channel_id=1, source_target_pairs={{0,2},{2,0},{4,6},{6,4},{8,10},{10,8},{12,14},{14,12},{16,18},{18,... | collective-permute-start | bytes 1769480 | tf_op jit(solution)/shard_map/ppermute | solution.py:239
  733.1 74.5 %collective-permute-start.46 = (bf16[2,1,2,288,576]{4,3,2,1,0:T(8,128)(2,1)}, bf16[2,1,2,288,576]{4,3,2,1,0:T(8,128)(2,1)}, u32[]{:S(2)}, u32[]{:S(2)}) collective-permute-start(bf16[2,1,2,288,576]{4,3,2,1,0:T(8,128)(2,1)} %bitcast.254), channel_id=1, source_target_pairs={{0,8},{2,10},{4,12},{6,14},{8,0},{10,2},{12,4},{14,6},{16,24},{18,... | collective-permute-start | bytes 3981320 | tf_op jit(solution)/shard_map/ppermute | solution.py:239
  739.8 102.4 %collective-permute-start.52 = (bf16[2,2,1,72,2304]{4,3,2,1,0:T(8,128)(2,1)}, bf16[2,2,1,72,2304]{4,3,2,1,0:T(8,128)(2,1)}, u32[]{:S(2)}, u32[]{:S(2)}) collective-permute-start(bf16[2,2,1,72,2304]{4,3,2,1,0:T(8,128)(2,1)} %constant_dynamic-slice_fusion.2), channel_id=1, source_target_pairs={{0,4},{2,6},{4,0},{6,2},{8,12},{10,14},{12,8},{14,10},{16,20},{18,... | collective-permute-start | bytes 3981320 | tf_op jit(solution)/shard_map/ppermute | solution.py:239
  778.8 32.5 %all-to-all-start.3 = ((bf16[16,8,1152]{2,1,0:T(8,128)(2,1)}), bf16[16,8,1152]{2,1,0:T(8,128)(2,1)S(1)}, u32[]{:S(2)}, u32[]{:S(2)}) async-start(bf16[16,8,1152]{2,1,0:T(8,128)(2,1)} %get-tuple-element.44), calls=%async_computation.3 | async-start | bytes 589824 | tf_op jit(solution)/shard_map/all_to_all | solution.py:264
  812.3 37.9 %collective-permute-start.47 = (bf16[2,1,1,288,576]{4,3,2,1,0:T(8,128)(2,1)}, bf16[2,1,1,288,576]{4,3,2,1,0:T(8,128)(2,1)}, u32[]{:S(2)}, u32[]{:S(2)}) collective-permute-start(bf16[2,1,1,288,576]{4,3,2,1,0:T(8,128)(2,1)} %constant_dynamic-slice_fusion.5), channel_id=1, source_target_pairs={{0,4},{2,6},{4,0},{6,2},{8,12},{10,14},{12,8},{14,10},{16,20},{18,... | collective-permute-start | bytes 1990664 | tf_op jit(solution)/shard_map/ppermute | solution.py:239
  818.0 35.6 %collective-permute-start.31 = (bf16[8,216,256]{2,1,0:T(8,128)(2,1)S(1)}, bf16[8,216,256]{2,1,0:T(8,128)(2,1)S(1)}, u32[]{:S(2)}, u32[]{:S(2)}) collective-permute-start(bf16[8,216,256]{2,1,0:T(8,128)(2,1)S(1)} %get-tuple-element.32), channel_id=1, source_target_pairs={{0,2},{2,0},{4,6},{6,4},{8,10},{10,8},{12,14},{14,12},{16,18},{18,... | collective-permute-start | bytes 2654216 | tf_op jit(solution)/shard_map/ppermute | solution.py:239
  844.8 31.7 %collective-permute-start.53 = (bf16[2,1,1,72,2304]{4,3,2,1,0:T(8,128)(2,1)}, bf16[2,1,1,72,2304]{4,3,2,1,0:T(8,128)(2,1)}, u32[]{:S(2)}, u32[]{:S(2)}) collective-permute-start(bf16[2,1,1,72,2304]{4,3,2,1,0:T(8,128)(2,1)} %constant_dynamic-slice_fusion.1), channel_id=1, source_target_pairs={{0,8},{2,10},{4,12},{6,14},{8,0},{10,2},{12,4},{14,6},{16,24},{18,... | collective-permute-start | bytes 1990664 | tf_op jit(solution)/shard_map/ppermute | solution.py:239
  860.9 24.5 %collective-permute-start.34 = (bf16[2,2,1,216,576]{4,3,2,1,0:T(8,128)(2,1)S(1)}, bf16[2,2,1,216,576]{4,3,2,1,0:T(8,128)(2,1)S(1)}, u32[]{:S(2)}, u32[]{:S(2)}) collective-permute-start(bf16[2,2,1,216,576]{4,3,2,1,0:T(8,128)(2,1)S(1)} %constant_dynamic-slice_fusion.15), channel_id=1, source_target_pairs={{0,4},{2,6},{4,0},{6,2},{8,12},{10,14},{12,8},{14,10},{16,20},{18,... | collective-permute-start | bytes 2985992 | tf_op jit(solution)/shard_map/ppermute | solution.py:239
  887.5 24.1 %collective-permute-start.54 = (bf16[1,1,1,72,2304]{4,3,2,1,0:T(8,128)(2,1)S(1)}, bf16[1,1,1,72,2304]{4,3,2,1,0:T(8,128)(2,1)S(1)}, u32[]{:S(2)}, u32[]{:S(2)}) collective-permute-start(bf16[1,1,1,72,2304]{4,3,2,1,0:T(8,128)(2,1)S(1)} %constant_dynamic-slice_fusion), channel_id=1, source_target_pairs={{0,16},{2,18},{4,20},{6,22},{8,24},{10,26},{12,28},{14,30},{16,0},... | collective-permute-start | bytes 995336 | tf_op jit(solution)/shard_map/ppermute | solution.py:239
  (122 other events, 2611.5 us)

commit v2 on v1

v2 whole, which is shorter than its diff:
```python
import functools

import jax
import jax.numpy as jnp
import numpy as np
from jax import lax
from jax.experimental import pallas as pl
from jax.experimental.pallas import tpu as pltpu
from jax.sharding import PartitionSpec as P

D = 1152
H = 16
HD = 72
CHAN_GROUP = 128
PIECE_MAX = 16
PERIOD = 16

bf16 = jnp.bfloat16
f32 = jnp.float32
highest = lax.Precision.HIGHEST
norm_epsilon = 1e-06
masked_score = -1e30
score_scale = HD ** (-0.5)
VMEM_LIMIT = 56 * 1024 * 1024
VMEM_SPEC = pl.BlockSpec(memory_space=pltpu.VMEM)


def params():
    return pltpu.CompilerParams(vmem_limit_bytes=VMEM_LIMIT)


def dot_nt(a, b):
    return lax.dot_general(a, b, (((1,), (1,)), ((), ())), preferred_element_type=f32)


def dot_nn(a, b):
    return lax.dot_general(a, b, (((1,), (0,)), ((), ())), preferred_element_type=f32)


def dot_tn(a, b):
    return lax.dot_general(a, b, (((0,), (0,)), ((), ())), preferred_element_type=f32)


def source_inputs(sources):
    arrays = [source[0] for source in sources]
    specs = [pl.BlockSpec(source[1], source[2]) for source in sources]
    parts = [(source[3], source[4]) for source in sources]
    return arrays, specs, parts


def fill(target_ref, place_ref, refs, parts):
    half = target_ref.shape[0] // 2
    mine, quarter = place_ref[0], place_ref[1]
    for ref, (step, column) in zip(refs, parts):
        rows, cols = ref.shape
        if step == "all":
            start = 0
        elif step is None:
            start = pl.multiple_of(mine * half, 16)
        else:
            start = pl.multiple_of((1 - mine) * half + (quarter ^ step) * rows, 16)
        target_ref[pl.ds(start, rows), pl.ds(column, cols)] = ref[...]


def whole(shape):
    return pl.BlockSpec(shape, lambda i, place: (0,) * len(shape))


def staged_call(kernel, place, sources, inputs, out_shapes, scratch, name):
    arrays, specs, parts = source_inputs(sources)
    return pl.pallas_call(
        functools.partial(kernel, parts=parts),
        out_shape=out_shapes,
        grid_spec=pltpu.PrefetchScalarGridSpec(
            num_scalar_prefetch=1,
            grid=(1,),
            in_specs=specs + [whole(value.shape) for value in inputs],
            out_specs=[whole(out.shape) for out in out_shapes],
            scratch_shapes=scratch,
        ),
        compiler_params=params(),
        name=name,
    )(place, *arrays, *inputs)


def shaped(*shape, dtype=f32):
    return jax.ShapeDtypeStruct(shape, dtype)


def normalized(values):
    centred = values - jnp.mean(values, axis=1, keepdims=True)
    inverse = lax.rsqrt(jnp.mean(centred * centred, axis=1, keepdims=True) + norm_epsilon)
    return centred * inverse, inverse


def normalized_back(grad, normed, inverse):
    mean_grad = jnp.mean(grad, axis=1, keepdims=True)
    mean_dot = jnp.mean(grad * normed, axis=1, keepdims=True)
    return (grad - mean_grad - normed * mean_dot) * inverse


def norm_in_kernel(tokens_ref, shift_ref, scale_ref, out_ref):
    for start in range(0, tokens_ref.shape[0], PERIOD):
        rows = pl.ds(start, PERIOD)
        normed, ignored = normalized(tokens_ref[rows, :].astype(f32))
        out_ref[rows, :] = (normed * (1.0 + scale_ref[...]) + shift_ref[...]).astype(bf16)


def norm_in(tokens, shift, scale):
    return pl.pallas_call(
        norm_in_kernel,
        out_shape=shaped(*tokens.shape, dtype=bf16),
        in_specs=[VMEM_SPEC] * 3,
        out_specs=VMEM_SPEC,
        compiler_params=params(),
        name="norm_in",
    )(tokens, shift, scale)


def project_kernel(place_ref, *refs, parts):
    count = len(parts)
    weight_ref, window_ref = refs[-2], refs[-1]
    q_ref, kv_ref = refs[-4], refs[-3]
    window_parts = refs[count:-4]
    fill(weight_ref, place_ref, refs[:count], parts)
    tokens = q_ref.shape[0]
    for index, part in enumerate(window_parts):
        window_ref[pl.ds(index * tokens, tokens), :] = part[...]
    for start in range(0, 2 * D, 768):
        kv_ref[:, pl.ds(start, 768)] = dot_nn(
            window_ref[...], weight_ref[:, pl.ds(D + start, 768)]
        ).astype(bf16)
    for start in range(0, D, 384):
        q_ref[:, pl.ds(start, 384)] = dot_nn(
            window_parts[0][...], weight_ref[:, pl.ds(start, 384)]
        ).astype(bf16)


def project(place, sources, window_parts):
    tokens = window_parts[0].shape[0]
    keys = tokens * len(window_parts)
    return staged_call(
        project_kernel,
        place,
        sources,
        window_parts,
        [shaped(tokens, D, dtype=bf16), shaped(keys, 2 * D, dtype=bf16)],
        [pltpu.VMEM((D, 3 * D), bf16), pltpu.VMEM((keys, D), bf16)],
        "project",
    )


def head_window(head):
    start = head * HD
    low = start // 128 * 128
    width = 128 if start + HD - low <= 128 else 256
    return low, min(width, D - low), start - low


def head_lanes(rows, width, first):
    lane = lax.broadcasted_iota(jnp.int32, (rows, width), 1)
    return (lane >= first) & (lane < first + HD)


def attend_kernel(place_ref, *refs, parts):
    count = len(parts)
    q_ref, kv_ref, bias_ref, mask_ref, tokens_ref, gate_ref, shift_ref, scale_ref = refs[
        count : count + 8
    ]
    merged_ref, proj_ref, mid_ref, normed_ref, acc_ref, weight_ref = refs[count + 8 :]
    tokens = q_ref.shape[0]
    fill(weight_ref, place_ref, refs[:count], parts)
    acc_ref[...] = jnp.zeros_like(acc_ref)
    for head in range(H):
        low, width, first = head_window(head)
        window = pl.ds(low, width)
        lanes = head_lanes(tokens, width, first)
        query = jnp.where(lanes, q_ref[:, window], jnp.zeros((), bf16))
        scores = dot_nt(query, kv_ref[:, window]) * score_scale + bias_ref[...]
        top = jnp.max(scores, axis=1, keepdims=True)
        weights = jnp.exp(scores - top)
        probs = (weights * (1.0 / jnp.sum(weights, axis=1, keepdims=True))).astype(bf16)
        out = dot_nn(probs, kv_ref[:, pl.ds(D + low, width)])
        acc_ref[:, window] += jnp.where(lanes, out, 0.0)
    for start in range(0, tokens, PERIOD):
        rows = pl.ds(start, PERIOD)
        merged_ref[rows, :] = (acc_ref[rows, :] * mask_ref[...]).astype(bf16)
    proj_ref[...] = dot_nn(merged_ref[...], weight_ref[...])
    for start in range(0, tokens, PERIOD):
        rows = pl.ds(start, PERIOD)
        mid = tokens_ref[rows, :].astype(f32) + gate_ref[...] * proj_ref[rows, :]
        mid_ref[rows, :] = mid
        normed, ignored = normalized(mid)
        normed_ref[rows, :] = (normed * (1.0 + scale_ref[...]) + shift_ref[...]).astype(bf16)


def attend(place, sources, *inputs):
    tokens = inputs[0].shape[0]
    return staged_call(
        attend_kernel,
        place,
        sources,
        inputs,
        [
            shaped(tokens, D, dtype=bf16),
            shaped(tokens, D),
            shaped(tokens, D),
            shaped(tokens, D, dtype=bf16),
        ],
        [pltpu.VMEM((tokens, D), f32), pltpu.VMEM((D, D), bf16)],
        "attend",
    )


def attend_back_kernel(
    q_ref, kv_ref, bias_ref, grad_ref, dq_ref, dkv_ref, dq_acc, dk_acc, dv_acc
):
    tokens = q_ref.shape[0]
    dq_acc[...] = jnp.zeros_like(dq_acc)
    dk_acc[...] = jnp.zeros_like(dk_acc)
    dv_acc[...] = jnp.zeros_like(dv_acc)
    for head in range(H):
        low, width, first = head_window(head)
        window = pl.ds(low, width)
        lanes = head_lanes(tokens, width, first)
        query = jnp.where(lanes, q_ref[:, window], jnp.zeros((), bf16))
        grad = jnp.where(lanes, grad_ref[:, window], jnp.zeros((), bf16))
        keys = kv_ref[:, window]
        scores = dot_nt(keys, query) * score_scale + bias_ref[...]
        top = jnp.max(scores, axis=0, keepdims=True)
        weights = jnp.exp(scores - top)
        probs = weights * (1.0 / jnp.sum(weights, axis=0, keepdims=True))
        probs_low = probs.astype(bf16)
        grad_probs = dot_nt(kv_ref[:, pl.ds(D + low, width)], grad)
        row_dot = jnp.sum(probs_low.astype(f32) * grad_probs, axis=0, keepdims=True)
        grad_scores = (probs * (grad_probs - row_dot)).astype(bf16)
        dk_acc[:, window] += dot_nn(grad_scores, query)
        dv_acc[:, window] += dot_nn(probs_low, grad)
        dq_acc[:, window] += jnp.where(lanes, dot_tn(grad_scores, keys), 0.0)
    dq_ref[...] = (dq_acc[...] * score_scale).astype(bf16)
    for index in range(dkv_ref.shape[0]):
        rows = pl.ds(index * tokens, tokens)
        dkv_ref[index, :, pl.ds(0, D)] = (dk_acc[rows, :] * score_scale).astype(bf16)
        dkv_ref[index, :, pl.ds(D, D)] = dv_acc[rows, :].astype(bf16)


def attend_back(queries, kv_window, bias_t, grad_heads):
    tokens = queries.shape[0]
    keys = kv_window.shape[0]
    return pl.pallas_call(
        attend_back_kernel,
        out_shape=(
            shaped(tokens, D, dtype=bf16),
            shaped(keys // tokens, tokens, 2 * D, dtype=bf16),
        ),
        in_specs=[VMEM_SPEC] * 4,
        out_specs=(VMEM_SPEC,) * 2,
        scratch_shapes=[
            pltpu.VMEM((tokens, D), f32),
            pltpu.VMEM((keys, D), f32),
            pltpu.VMEM((keys, D), f32),
        ],
        compiler_params=params(),
        name="attend_back",
    )(queries, kv_window, bias_t, grad_heads)


def feed_kernel(place_ref, *refs, parts, own_rows):
    count = len(parts)
    mid_ref, grad_ref, channel_ref, down_ref = refs[count : count + 4]
    act_ref, pre_ref, grad_own, grad_low, out_own, out_low = refs[count + 4 : count + 10]
    weight_ref, grad_acc, out_acc = refs[count + 10 :]
    step, steps = pl.program_id(0), pl.num_programs(0)
    rows, cols = act_ref.shape
    groups = channel_ref.shape[0]
    tokens = rows // groups

    @pl.when(step == 0)
    def _():
        grad_acc[...] = jnp.zeros_like(grad_acc)
        out_acc[...] = jnp.zeros_like(out_acc)

    fill(weight_ref, place_ref, refs[:count], parts)
    root = 0.7978845608028654
    for group in range(groups):
        span = pl.ds(group * tokens, tokens)
        channels = jnp.concatenate([channel_ref[group]] * (tokens // PERIOD), axis=0)
        pre = dot_nn(mid_ref[span, :], weight_ref[...])
        grad_act = dot_nt(grad_ref[span, :], down_ref[...])
        square = pre * pre
        inner = jnp.tanh(root * (pre + 0.044715 * (square * pre)))
        half_sum = 0.5 + 0.5 * inner
        act_ref[span, :] = (pre * half_sum * channels).astype(bf16)
        slope = half_sum + (0.5 * pre) * (1.0 - inner * inner) * (
            root + (3.0 * 0.044715 * root) * square
        )
        pre_ref[span, :] = (grad_act * channels * slope).astype(bf16)
    grad_acc[...] += dot_nt(pre_ref[...], weight_ref[...])
    out_acc[...] += dot_nn(act_ref[...], down_ref[...])

    @pl.when(step == steps - 1)
    def _():
        skip = rows - grad_low.shape[0]
        grad_own[...] = grad_acc[pl.ds(0, own_rows), :]
        out_own[...] = out_acc[pl.ds(0, own_rows), :]
        grad_low[...] = grad_acc[pl.ds(skip, rows - skip), :].astype(bf16)
        out_low[...] = out_acc[pl.ds(skip, rows - skip), :].astype(bf16)


def feed(place, sources, mid_rows, grad_rows, channels, down, chunk, tokens, low_rows):
    arrays, specs, parts = source_inputs(sources)
    rows = mid_rows.shape[0]
    width = down.shape[0]
    by_chunk = pl.BlockSpec((rows, chunk), lambda i, place: (0, i))
    own, low = (tokens, D), (low_rows, D)
    return pl.pallas_call(
        functools.partial(feed_kernel, parts=parts, own_rows=tokens),
        out_shape=[
            shaped(rows, width, dtype=bf16),
            shaped(rows, width, dtype=bf16),
            shaped(*own),
            shaped(*low, dtype=bf16),
            shaped(*own),
            shaped(*low, dtype=bf16),
        ],
        grid_spec=pltpu.PrefetchScalarGridSpec(
            num_scalar_prefetch=1,
            grid=(width // chunk,),
            in_specs=specs
            + [
                whole((rows, D)),
                whole((rows, D)),
                pl.BlockSpec(
                    (channels.shape[0], PERIOD, chunk), lambda i, place: (0, 0, i)
                ),
                pl.BlockSpec((chunk, D), lambda i, place: (i, 0)),
            ],
            out_specs=[by_chunk, by_chunk, whole(own), whole(low), whole(own), whole(low)],
            scratch_shapes=[
                pltpu.VMEM((D, chunk), bf16),
                pltpu.VMEM((rows, D), f32),
                pltpu.VMEM((rows, D), f32),
            ],
        ),
        compiler_params=params(),
        name="feed",
    )(place, *arrays, mid_rows, grad_rows, channels, down)


def mid_back_kernel(place_ref, *refs, parts):
    count = len(parts)
    own_ref, other_ref, mid_ref, proj_ref, late_ref, scale_ref, gate_ref, mask_ref = refs[
        count : count + 8
    ]
    grad_mid_ref, grad_attn_ref, heads_ref, sums_ref, weight_ref, merged_ref = refs[count + 8 :]
    tokens = own_ref.shape[0]
    fill(weight_ref, place_ref, refs[:count], parts)
    gate_sum = jnp.zeros((PERIOD, D), f32)
    shift_sum = jnp.zeros((PERIOD, D), f32)
    scale_sum = jnp.zeros((PERIOD, D), f32)
    for start in range(0, tokens, PERIOD):
        rows = pl.ds(start, PERIOD)
        normed, inverse = normalized(mid_ref[rows, :])
        grad = own_ref[rows, :] + other_ref[rows, :].astype(f32)
        grad_mid = late_ref[rows, pl.ds(0, D)].astype(f32) + normalized_back(
            grad * (1.0 + scale_ref[...]), normed, inverse
        )
        grad_mid_ref[rows, :] = grad_mid
        grad_attn_ref[rows, :] = (grad_mid * gate_ref[...]).astype(bf16)
        gate_sum += grad_mid * proj_ref[rows, :]
        shift_sum += grad
        scale_sum += grad * normed
    sums_ref[0] = gate_sum
    sums_ref[1] = shift_sum
    sums_ref[2] = scale_sum
    merged_ref[...] = dot_nt(grad_attn_ref[...], weight_ref[...])
    for start in range(0, tokens, PERIOD):
        rows = pl.ds(start, PERIOD)
        heads_ref[rows, :] = (merged_ref[rows, :] * mask_ref[...]).astype(bf16)


def mid_back(place, sources, *inputs):
    tokens = inputs[0].shape[0]
    return staged_call(
        mid_back_kernel,
        place,
        sources,
        inputs,
        [
            shaped(tokens, D),
            shaped(tokens, D, dtype=bf16),
            shaped(tokens, D, dtype=bf16),
            shaped(3, PERIOD, D),
        ],
        [pltpu.VMEM((D, D), bf16), pltpu.VMEM((tokens, D), f32)],
        "mid_back",
    )


def in_back_kernel(place_ref, *refs, parts):
    count = len(parts)
    dq_ref, dkv_ref, tokens_ref, scale_ref, grad_mid_ref = refs[count : count + 5]
    grad_in_ref, sums_ref, weight_ref, grad_ref = refs[count + 5 :]
    tokens = dq_ref.shape[0]
    fill(weight_ref, place_ref, refs[:count], parts)
    grad_ref[...] = dot_nt(dkv_ref[...], weight_ref[:, pl.ds(D, 2 * D)]) + dot_nt(
        dq_ref[...], weight_ref[:, pl.ds(0, D)]
    )
    shift_sum = jnp.zeros((PERIOD, D), f32)
    scale_sum = jnp.zeros((PERIOD, D), f32)
    for start in range(0, tokens, PERIOD):
        rows = pl.ds(start, PERIOD)
        normed, inverse = normalized(tokens_ref[rows, :].astype(f32))
        grad = grad_ref[rows, :]
        back = normalized_back(grad * (1.0 + scale_ref[...]), normed, inverse)
        grad_in_ref[rows, :] = (grad_mid_ref[rows, :] + back).astype(bf16)
        shift_sum += grad
        scale_sum += grad * normed
    sums_ref[0] = shift_sum
    sums_ref[1] = scale_sum


def in_back(place, sources, *inputs):
    tokens = inputs[0].shape[0]
    return staged_call(
        in_back_kernel,
        place,
        sources,
        inputs,
        [shaped(tokens, D, dtype=bf16), shaped(2, PERIOD, D)],
        [pltpu.VMEM((D, 3 * D), bf16), pltpu.VMEM((tokens, D), f32)],
        "in_back",
    )


def term_kernel(place_ref, *refs, pairs, chunk, plan):
    acc_ref = refs[-1]
    for index in range(pairs):
        value = None
        grads, acts = refs[2 * index], refs[2 * index + 1]
        width = acts.shape[1]
        for start in range(0, width, 576):
            span = pl.ds(start, 576)
            value = dot_tn(grads[...], acts[:, span])
            acc_ref[:, span] = value if index == 0 else acc_ref[:, span] + value
    core = place_ref[2]
    outs = refs[2 * pairs : -1]
    for out_index, (first, count, axis) in enumerate(plan):
        send_ref, keep_ref = outs[2 * out_index], outs[2 * out_index + 1]
        at = place_ref[3 + axis]
        width = send_ref.shape[-1]
        for target, side in ((send_ref, 1 - at), (keep_ref, at)):
            blocks = target.shape[0]
            for block in range(blocks):
                pieces = acc_ref.shape[1] // width
                lane, rest = block // (blocks // pieces), block % (blocks // pieces)
                if axis == 0:
                    line = rest * 4 + side * 2 + core
                else:
                    line = (rest // 2) * 8 + side * 4 + (rest % 2) * 2 + core
                start = pl.multiple_of(line * chunk + first, 8)
                target[block] = acc_ref[pl.ds(start, count), pl.ds(lane * width, width)].astype(
                    bf16
                )


def term(place, pairs, plan, blocks, width):
    columns = pairs[0][0].shape[1]
    rows = pairs[0][1].shape[1]
    chunk = columns // (4 * blocks * width // rows)
    flat = [value for pair in pairs for value in pair]
    outs = []
    for first, count, axis in plan:
        outs += [shaped(blocks, count, width, dtype=bf16)] * 2
    return pl.pallas_call(
        functools.partial(term_kernel, pairs=len(pairs), chunk=chunk, plan=plan),
        out_shape=outs,
        in_specs=[pl.BlockSpec(memory_space=pltpu.SMEM)] + [VMEM_SPEC] * len(flat),
        out_specs=[VMEM_SPEC] * len(outs),
        scratch_shapes=[pltpu.VMEM((columns, rows), f32)],
        compiler_params=params(),
        name="term",
    )(place, *flat)


def running_ends(pieces):
    index = jnp.arange(pieces.shape[0], dtype=jnp.int32)
    return jnp.sum(jnp.where(index[None, :] <= index[:, None], pieces[None, :], 0), axis=1)


def crop_of(slots, ends):
    return jnp.sum((slots[..., None] >= ends[:-1]).astype(jnp.int32), axis=-1)


def one_hot(crops, count):
    return (crops[..., None] == jnp.arange(count, dtype=jnp.int32)).astype(f32)


def block_order(size):
    def device(block):
        chip, core = block // 2, block % 2
        return 2 * (chip ^ ((chip >> 1) & 1)) + core if size % 8 == 0 else block

    return [device(block) for block in range(size)]


def local(
    tokens_in,
    condition,
    crop_pieces,
    pad_counts,
    head_mask,
    channel_mask,
    keep_mask,
    qkv_weight,
    out_weight,
    up_weight,
    down_weight,
    ada_weight,
    cotangent,
):
    seq = lax.axis_size("seq")
    rows = lax.axis_size("fsdp")
    tokens = tokens_in.shape[1]
    slots = tokens // seq
    repeats = PERIOD // slots
    crops = crop_pieces.shape[1]
    hidden = up_weight.shape[1]
    hidden_part = hidden // rows
    half = D // rows
    seq_at = lax.axis_index("seq")
    row_at = lax.axis_index("fsdp")
    fast = rows == 2 and seq == 16
    order = block_order(seq)
    core = seq_at % 2
    if seq % 8 == 0:
        chip = seq_at // 2
        block_at = 2 * (chip ^ ((chip >> 1) & 1)) + core
    else:
        block_at = seq_at
    place = jnp.stack(
        [row_at, seq_at & 3, core, (seq_at // 2) % 2, (seq_at // 4) % 2]
    ).astype(jnp.int32)

    def flip(value, bit):
        return lax.ppermute(value, "seq", [(i, i ^ bit) for i in range(seq)])

    def cross(value):
        return lax.ppermute(value, "fsdp", [(0, 1), (1, 0)])

    def shift(value, distance):
        pairs = [
            (order[b], order[b + distance]) for b in range(seq) if 0 <= b + distance < seq
        ]
        return lax.ppermute(value, "seq", pairs)

    swap_rows = jnp.asarray(
        np.kron(np.eye(seq)[np.array(order)], np.eye(slots)), bf16
    )

    def to_slots(value):
        moved = jnp.dot(swap_rows, value, preferred_element_type=f32).astype(bf16)
        moved = lax.all_to_all(moved.reshape(seq, slots, -1), "seq", 0, 0)
        return moved.reshape(tokens, -1)

    def from_slots(value, dtype):
        value = lax.all_to_all(value.reshape(seq, slots, -1), "seq", 0, 0)
        value = value.reshape(tokens, -1)
        return jnp.dot(swap_rows, value, preferred_element_type=f32).astype(dtype)

    def after(value, *earlier):
        return lax.optimization_barrier((value, *earlier))[0]

    def gather_rows(value):
        if rows == 2:
            return jnp.stack([value, cross(value)])
        return lax.all_gather(value, "fsdp", axis=0)

    def pick(low_part, high_part):
        return jnp.where(row_at == 0, low_part, high_part)

    def tiled(value):
        return jnp.concatenate([value] * repeats, axis=-2) if repeats > 1 else value

    slot_index = block_at * slots + jnp.arange(slots, dtype=jnp.int32)
    ends = running_ends(crop_pieces[0])
    crop_here = crop_of(slot_index, ends)
    selector = one_hot(crop_here, crops)
    pads = pad_counts[0]

    cond_act = jax.nn.silu(condition[0]).astype(bf16)
    extra = jnp.concatenate(
        [channel_mask[0].astype(bf16), crop_pieces[0].astype(bf16)[:, None]], axis=1
    )
    extra = jnp.pad(extra, ((0, 0), (0, 128 - extra.shape[1])))
    packed = gather_rows(jnp.concatenate([cond_act, extra], axis=1))
    groups = channel_mask.shape[2]
    cond_rows = packed[:, :, :D].reshape(rows * crops, D)
    group_rows = packed[:, :, D : D + groups].astype(f32)
    ends_rows = jax.vmap(running_ends)(packed[:, :, D + groups].astype(jnp.int32))
    selector_rows = jax.vmap(lambda own: one_hot(crop_of(slot_index, own), crops))(ends_rows)

    columns = ada_weight.shape[1]
    mod_rows = jnp.dot(cond_rows, ada_weight, preferred_element_type=f32)
    mod_rows = mod_rows.reshape(rows, crops, columns)
    if rows == 2:
        mod_slots = jnp.einsum("rsc,rcm->rsm", selector_rows, mod_rows, precision=highest)
        arrived = cross(mod_slots[1])
        mod_attn = pick(mod_slots[0], arrived)
        mod_mlp = pick(arrived, mod_slots[0])
    else:
        mine = lax.all_to_all(mod_rows, "fsdp", 0, 0)
        mine = jnp.transpose(mine, (1, 0, 2)).reshape(crops, rows * columns)
        mine = jnp.dot(selector, mine, precision=highest)
        mod_attn, mod_mlp = mine[:, : 3 * D], mine[:, 3 * D :]
    mod_attn, mod_mlp = tiled(mod_attn), tiled(mod_mlp)
    shift_attn, scale_attn, gate_attn = (mod_attn[:, i * D : (i + 1) * D] for i in range(3))
    shift_mlp, scale_mlp, gate_mlp = (mod_mlp[:, i * D : (i + 1) * D] for i in range(3))

    def block(at):
        return lambda i, place: (0, at)

    if fast:
        quarter = half // 4
        chunk = 768

        def fetch(weight, column, cols, *earlier):
            part = lax.dynamic_slice(weight, ((seq_at & 3) * quarter, column), (quarter, cols))
            first = cross(after(part, *earlier))
            second = flip(first, 2)
            return (first, flip(first, 1), second, flip(second, 1))

        other_part = (1 - row_at) * hidden_part
        k_pieces = fetch(qkv_weight, D, D, packed)
        v_pieces = fetch(qkv_weight, 2 * D, D, k_pieces[0], mod_slots)
        q_pieces = fetch(qkv_weight, 0, D, k_pieces[0], mod_slots)
        out_pieces = fetch(out_weight, 0, D, v_pieces[0])
        up_low = fetch(up_weight, other_part, hidden_part // 2, q_pieces[0])
        up_high = fetch(
            up_weight, other_part + hidden_part // 2, hidden_part // 2, out_pieces[0]
        )
        qkv_sources = [(qkv_weight, (half, 3 * D), block(0), None, 0)]
        for column, pieces in ((0, q_pieces), (D, k_pieces), (2 * D, v_pieces)):
            qkv_sources += [
                (piece, (quarter, D), block(0), step, column)
                for step, piece in enumerate(pieces)
            ]
        out_sources = [(out_weight, (half, D), block(0), None, 0)]
        out_sources += [
            (piece, (quarter, D), block(0), step, 0) for step, piece in enumerate(out_pieces)
        ]
        chunks = hidden_part // chunk
        up_sources = [
            (up_weight, (half, chunk), lambda i, place: (0, place[0] * chunks + i), None, 0)
        ]
        up_sources += [
            (
                jnp.concatenate([low, high], axis=1),
                (quarter, chunk),
                lambda i, place: (0, i),
                step,
                0,
            )
            for step, (low, high) in enumerate(zip(up_low, up_high))
        ]
        low_rows = tokens
    else:
        chunk = hidden_part
        qkv_full = lax.all_gather(qkv_weight, "fsdp", axis=0, tiled=True)
        out_full = lax.all_gather(out_weight, "fsdp", axis=0, tiled=True)
        up_part = lax.all_to_all(up_weight, "fsdp", 1, 0, tiled=True)
        qkv_sources = [(qkv_full, (D, 3 * D), block(0), "all", 0)]
        out_sources = [(out_full, (D, D), block(0), "all", 0)]
        up_sources = [(up_part, (D, hidden_part), block(0), "all", 0)]
        low_rows = rows * tokens

    tokens_here = to_slots(tokens_in[0])
    kept = jnp.broadcast_to(keep_mask[0].astype(bf16)[:, None], (tokens, 128))
    normed_in = norm_in(tokens_here, shift_attn, scale_attn)

    reach = -(-(PIECE_MAX - 1) // slots)
    paired = reach == 2 and seq % 2 == 0
    if paired:
        below, above = shift(normed_in, 2), shift(normed_in, -2)
        passed = flip(jnp.where(core == 0, above, below), 1)
        near = [normed_in, flip(normed_in, 1), below, above, passed]
        near_at = [
            block_at,
            block_at ^ 1,
            block_at - 2,
            block_at + 2,
            block_at - 1 + 2 * core,
        ]
    else:
        near, near_at = [normed_in], [block_at]
        for distance in range(1, reach + 1):
            near += [shift(normed_in, distance), shift(normed_in, -distance)]
            near_at += [block_at - distance, block_at + distance]
    late_in = to_slots(after(jnp.concatenate([cotangent[0], kept], axis=1), normed_in))
    near_at = jnp.stack(near_at)
    key_slots = near_at[:, None] * slots + jnp.arange(slots, dtype=jnp.int32)[None, :]
    inside = (near_at >= 0) & (near_at < seq)
    key_crop = jnp.where(inside[:, None], crop_of(key_slots, ends), -1)
    key_crop = jnp.where(
        key_slots[:, None, :] < tokens - pads[None, :, None], key_crop[:, None, :], -1
    ).reshape(-1)
    query_crop = jnp.broadcast_to(crop_here[None, :], (seq, slots)).reshape(tokens)
    bias = jnp.where(query_crop[:, None] == key_crop[None, :], 0.0, masked_score).astype(f32)
    bias_t = jnp.where(key_crop[:, None] == query_crop[None, :], 0.0, masked_score).astype(f32)
    head_slots = tiled(
        jnp.repeat(jnp.dot(selector, head_mask[0].astype(f32), precision=highest), HD, axis=1)
    )

    def by_slot(value):
        return value.reshape(tokens // PERIOD, PERIOD, -1)

    queries, kv_window = project(place, qkv_sources, near)
    grad_mlp = by_slot(late_in[:, :D].astype(f32)) * gate_mlp
    grad_mlp = (grad_mlp * by_slot(late_in[:, D : D + 1].astype(f32))).reshape(tokens, D)
    grad_mlp_rows = gather_rows(grad_mlp.astype(bf16)).reshape(rows * tokens, D)
    queries = after(queries, grad_mlp)
    merged, attn_proj, mid_state, normed_mid = attend(
        place,
        out_sources,
        queries,
        kv_window,
        bias,
        head_slots,
        tokens_here,
        gate_attn,
        shift_mlp,
        scale_mlp,
    )

    mid_rows = gather_rows(normed_mid).reshape(rows * tokens, D)
    channels = jnp.einsum("rsc,rcg->rsg", selector_rows, group_rows, precision=highest)
    channels = lax.dynamic_slice_in_dim(
        jnp.repeat(tiled(channels), CHAN_GROUP, axis=2), row_at * hidden_part, hidden_part, 2
    )
    hidden_act, grad_pre, grad_own, grad_low, out_own, out_low = feed(
        place,
        up_sources,
        mid_rows,
        grad_mlp_rows,
        channels,
        down_weight,
        chunk,
        tokens,
        low_rows,
    )

    def own_sum(own, low):
        if rows == 2:
            return own, cross(low)
        low = low.reshape(rows, tokens, D)
        low = lax.psum_scatter(low, "fsdp", scatter_dimension=0, tiled=True)
        return jnp.zeros_like(own), low.reshape(tokens, D)

    grad_own, grad_other = own_sum(grad_own, grad_low)
    out_own, out_other = own_sum(out_own, out_low)
    mlp_out = out_own + out_other.astype(f32)
    kept_out = by_slot(mlp_out * late_in[:, D : D + 1].astype(f32))
    block_out = (by_slot(mid_state) + gate_mlp * kept_out).reshape(tokens, D)
    block_out = block_out.astype(bf16)
    gate_mlp_sum = jnp.sum(by_slot(late_in[:, :D].astype(f32)) * kept_out, axis=0)

    if fast:

        def pooled(grads, acts):
            return [(grads, acts), (flip(grads, 1), flip(acts, 1))]

        down_pairs = pooled(grad_mlp_rows, hidden_act)
        up_pairs = pooled(grad_pre, mid_rows)
        down_sent, down_kept = term(place, down_pairs, [(0, D // seq, 0)], 4, hidden_part)
        grad_own = after(grad_own, down_sent)

    grad_mid, grad_attn, grad_heads, mid_sums = mid_back(
        place,
        out_sources,
        grad_own,
        grad_other,
        mid_state,
        attn_proj,
        late_in,
        scale_mlp,
        gate_attn,
        head_slots,
    )
    if fast:

        def own_half(value):
            return pick(value[:, :half], value[:, half:])

        def other_half(value):
            return pick(value[:, half:], value[:, :half])

        crossing = jnp.concatenate(
            [other_half(merged), other_half(normed_in), grad_attn], axis=1
        )
        crossed = cross(crossing)
        grad_heads = after(grad_heads, crossing, up_pairs)
    grad_queries, parts = attend_back(queries, kv_window, bias_t, grad_heads)
    grad_kv = parts[0].astype(f32)
    if paired:
        handed = flip(parts[4], 1).astype(f32)
        down_part = (parts[2].astype(f32) + jnp.where(core == 1, handed, 0.0)).astype(bf16)
        up_side = (parts[3].astype(f32) + jnp.where(core == 0, handed, 0.0)).astype(bf16)
        grad_kv = grad_kv + flip(parts[1], 1).astype(f32)
        if fast:
            block_out, ignored, ignored = lax.optimization_barrier(
                (block_out, down_part, up_side)
            )
            up_ready, ignored, ignored = lax.optimization_barrier(
                (up_pairs, down_part, up_side)
            )
            up_sent, up_kept = term(place, up_ready, [(0, hidden // seq, 0)], 4, half)
            grad_kv = after(grad_kv, up_sent)
        grad_kv = grad_kv + shift(down_part, -2).astype(f32) + shift(up_side, 2).astype(f32)
    else:
        for distance in range(1, reach + 1):
            grad_kv = grad_kv + shift(parts[2 * distance - 1], -distance).astype(f32)
            grad_kv = grad_kv + shift(parts[2 * distance], distance).astype(f32)
    grad_kv = grad_kv.astype(bf16)
    block_out = from_slots(block_out, bf16)
    input_grad, in_sums = in_back(
        place, qkv_sources, grad_queries, grad_kv, tokens_here, scale_attn, grad_mid
    )
    input_grad = from_slots(input_grad, f32)

    def by_crop(sums):
        sums = sums.reshape(-1, repeats, slots, D)
        sums = jnp.sum(sums, axis=1) if repeats > 1 else sums[:, 0]
        return jnp.einsum("sc,nsd->cnd", selector, sums, precision=highest).astype(bf16)

    def all_sum(value):
        if not fast:
            return lax.psum(value, "seq")
        for bit in (1, 2, 4, 8):
            value = (value.astype(f32) + flip(value, bit).astype(f32)).astype(bf16)
        return value

    mod_grads = jnp.concatenate([in_sums, mid_sums, gate_mlp_sum[None]], axis=0)
    mod_grads = all_sum(by_crop(mod_grads).reshape(crops, 6 * D))
    if rows == 2:
        own = pick(mod_grads[:, : 3 * D], mod_grads[:, 3 * D :])
        other = cross(pick(mod_grads[:, 3 * D :], mod_grads[:, : 3 * D]))
        mod_grads = jnp.concatenate([own, other], axis=0)
    else:
        split = jnp.transpose(mod_grads.reshape(crops, rows, columns), (1, 0, 2))
        mod_grads = lax.all_to_all(split, "fsdp", 0, 0).reshape(rows * crops, columns)
    ada_grad = lax.dot_general(
        cond_rows, mod_grads, (((0,), (0,)), ((), ())), preferred_element_type=f32
    )

    if not fast:

        def product(acts, grads):
            return lax.dot_general(
                acts, grads, (((0,), (0,)), ((), ())), preferred_element_type=f32
            ).astype(bf16)

        def both(value):
            value = lax.psum_scatter(value, "fsdp", scatter_dimension=0, tiled=True)
            return lax.psum_scatter(value, "seq", scatter_dimension=1, tiled=True).astype(f32)

        grad_qkv = jnp.concatenate([grad_queries, grad_kv], axis=1)
        qkv_grad = both(product(normed_in, grad_qkv))
        out_grad = both(product(merged, grad_attn))
        up_cols = lax.all_to_all(product(mid_rows, grad_pre), "fsdp", 0, 1, tiled=True)
        up_grad = lax.psum_scatter(up_cols, "seq", scatter_dimension=1, tiled=True).astype(f32)
        down_cols = product(hidden_act, grad_mlp_rows)
        down_grad = lax.psum_scatter(
            down_cols, "seq", scatter_dimension=1, tiled=True
        ).astype(f32)
    else:

        def scatter(sent, kept, bits):
            value = kept.astype(f32) + flip(sent, bits[0]).astype(f32)
            shape = value.shape[1:]
            value = value.reshape(2, 2, *shape).astype(bf16)
            at = (seq_at // bits[2]) % 2
            send = lax.dynamic_index_in_dim(value, 1 - at, 1, keepdims=False)
            keep = lax.dynamic_index_in_dim(value, at, 1, keepdims=False)
            value = (keep.astype(f32) + flip(send, bits[2]).astype(f32)).astype(bf16)
            at = (seq_at // bits[1]) % 2
            send = lax.dynamic_index_in_dim(value, 1 - at, 0, keepdims=False)
            keep = lax.dynamic_index_in_dim(value, at, 0, keepdims=False)
            return keep.astype(f32) + flip(send, bits[1]).astype(f32)

        down_grad = jnp.transpose(scatter(down_sent, down_kept, (2, 8, 4)))
        up_mine = scatter(up_sent, up_kept, (2, 8, 4)).astype(bf16)
        pairs = []
        for place_seq in range(seq):
            for place_row in range(2):
                high = (place_seq // 8) % 2
                target_seq = (place_seq & 7) | (place_row * 8)
                pairs.append((place_seq * 2 + place_row, target_seq * 2 + high))
        up_grad = jnp.transpose(lax.ppermute(up_mine, ("seq", "fsdp"), pairs)).astype(f32)

        out_acts = jnp.concatenate([own_half(merged), crossed[:, :half]], axis=0)
        out_grads = jnp.concatenate([grad_attn, crossed[:, D:]], axis=0)
        out_sent, out_kept = term(
            place,
            pooled(out_grads, out_acts),
            [(0, D // seq, 0)],
            4,
            half,
        )
        out_grad = jnp.transpose(scatter(out_sent, out_kept, (2, 8, 4)))

        q_crossed, kv_crossed = cross(grad_queries), cross(grad_kv)
        qkv_grads = jnp.concatenate(
            [
                jnp.concatenate([grad_queries, q_crossed], axis=0),
                jnp.concatenate([grad_kv, kv_crossed], axis=0),
            ],
            axis=1,
        )
        qkv_acts = jnp.concatenate([own_half(normed_in), crossed[:, half:D]], axis=0)
        first = 3 * D // seq // 16 * 8
        sent_a, kept_a, sent_b, kept_b = term(
            place,
            pooled(qkv_grads, qkv_acts),
            [(0, first, 0), (first, 3 * D // seq - first, 1)],
            4,
            half,
        )
        qkv_grad = jnp.transpose(
            jnp.concatenate(
                [
                    scatter(sent_a, kept_a, (2, 8, 4)),
                    scatter(sent_b, kept_b, (4, 8, 2)),
                ],
                axis=0,
            )
        )

    return (
        block_out[None],
        input_grad[None],
        qkv_grad,
        out_grad,
        up_grad,
        down_grad,
        ada_grad,
    )


def solution(mesh):
    in_specs = (
        P("fsdp", "seq", None),
        P("fsdp", None, None),
        P("fsdp", None),
        P("fsdp", None),
        P("fsdp", None, None),
        P("fsdp", None, None),
        P("fsdp", "seq"),
        P("fsdp", None),
        P("fsdp", None),
        P("fsdp", None),
        P("fsdp", None),
        P(None, "fsdp"),
        P("fsdp", "seq", None),
    )
    out_specs = (
        P("fsdp", "seq", None),
        P("fsdp", "seq", None),
        P("fsdp", "seq"),
        P("fsdp", "seq"),
        P("fsdp", "seq"),
        P("fsdp", "seq"),
        P(None, "fsdp"),
    )
    return jax.shard_map(local, mesh=mesh, in_specs=in_specs, out_specs=out_specs, check_vma=False)
```

time: 932 us -> 419 us (0.45)
  Pallas kernels: 505 us -> 94.9 us
  matrix products: 59 us -> 17.8 us
  local copies, waits for them, and re-layouts: 60.6 us -> 22.5 us
  waiting for transfers between devices: 160 us -> 141 us
  other arithmetic: 46.6 us -> 34.1 us
  starting transfers between devices: 91.3 us -> 101 us
    pallas_call x6 -> x11, Pallas kernels: 505 us -> 94.9 us  [the longest x4 35.4 us: staged_call(): pl.pallas_call(functools.partial(kernel, parts=parts), out_shape=out_shap...]
    dot_general x18 -> x7, matrix products: 58.4 us -> 17.1 us  [the longest x1 8.15 us: local(): lax.dot_general(cond_rows, mod_grads, (((0,), (0,)), ((), ())), preferred...]
    ppermute x15 -> x16, waiting for transfers between devices: 35.2 us -> 22.2 us  [cross(): return lax.ppermute(value, 'fsdp', [(0, 1), (1, 0)])]
    dynamic_slice x21 -> x4, local copies, waits for them, and re-layouts: 19.5 us -> 6.62 us  [the longest x3 5.87 us: fetch(): lax.dynamic_slice(weight, ((seq_at & 3) * quarter, column), (quarter, cols))]
    ppermute x4, waiting for transfers between devices: 11.8 us -> 0.01 us  [shift(): return lax.ppermute(value, 'seq', pairs)]
    ppermute x44 -> x49, starting transfers between devices: 41.3 us -> 46.2 us  [flip(): return lax.ppermute(value, 'seq', [(i, i ^ bit) for i in range(seq)])]
    ppermute x44 -> x49, waiting for transfers between devices: 99.2 us -> 96 us  [flip(): return lax.ppermute(value, 'seq', [(i, i ^ bit) for i in range(seq)])]
  transfers between devices with their start and end apart: 68 -> 74, of which waited for: 25 -> 25; matrix products, arithmetic and copies ran while one was open for 17% -> 15% of each run, Pallas kernels for 55% -> 16%
where the time goes in v2:
time: 419 us; the launch traced here: 413 us
  waiting for transfers between devices  141 us (34%)
  starting transfers between devices  101 us (24%)
  Pallas kernels  94.9 us (23%)
  other arithmetic  34.1 us (8%)
  local copies, waits for them, and re-layouts  22.5 us (5%)
  matrix products  17.8 us (4%)
    ppermute x49, waiting for transfers between devices, flip(): return lax.ppermute(value, 'seq', [(i, i ^ bit) for i in range(seq)])  96 us
    ppermute x49, starting transfers between devices, flip(): return lax.ppermute(value, 'seq', [(i, i ^ bit) for i in range(seq)])  46.2 us
    pallas_call x4, Pallas kernels, staged_call(): pl.pallas_call(functools.partial(kernel, parts=parts), out_shape=out_shap...  35.4 us
    pallas_call x4, Pallas kernels, term(): pl.pallas_call(functools.partial(term_kernel, pairs=len(pairs), chunk=chu...  30.2 us
    ppermute x16, waiting for transfers between devices, cross(): return lax.ppermute(value, 'fsdp', [(0, 1), (1, 0)])  22.2 us
    all_to_all x2, waiting for transfers between devices, from_slots(): value = lax.all_to_all(value.reshape(seq, slots, -1), 'seq', 0, 0)  17.1 us
    ppermute x16, starting transfers between devices, cross(): return lax.ppermute(value, 'fsdp', [(0, 1), (1, 0)])  17 us
    pallas_call x1, Pallas kernels, feed(): pl.pallas_call(functools.partial(feed_kernel, parts=parts, own_rows=token...  14.8 us
  transfers between devices with their start and end apart: 74, of which 25 were waited for; matrix products, arithmetic and copies ran while one was open for 15% of the time, Pallas kernels for 16%

profile of v2, /device:TPU:2, one launch (start us, length us, event | category | flops | bytes accessed | tf_op | source)
XLA Modules:
  0.0 413.0 jit_solution(9041956749685899745)
XLA Ops:
  6.2 5.9 %all-to-all-start = ((bf16[16,8,1152]{2,1,0:T(8,128)(2,1)}), bf16[16,8,1152]{2,1,0:T(8,128)(2,1)S(1)}, u32[]{:S(2)}, u32[]{:S(2)}) async-start(bf16[16,8,1152]{2,1,0:T(8,128)(2,1)} %fusion.2), calls=%async_computation | async-start | bytes 589824 | tf_op jit(solution)/shard_map/all_to_all | solution.py:563
  19.5 4.6 %fusion = f32[2,16,3456]{2,1,0:T(8,128)S(1)} fusion(bf16[2,16,1152]{2,1,0:T(8,128)(2,1)S(1)} %fusion.30, bf16[1152,3456]{1,0:T(8,128)(2,1)} %param.25), kind=kOutput, calls=%fused_computation | convolution fusion | flops 254803968 | bytes 8478720 | tf_op jit(solution)/shard_map/dot_general | solution.py:604
  38.3 3.8 collective-permute-start.19
  50.0 7.8 %all-to-all-start.1 = ((bf16[16,8,1280]{2,1,0:T(8,128)(2,1)}), bf16[16,8,1280]{2,1,0:T(8,128)(2,1)S(1)}, u32[]{:S(2)}, u32[]{:S(2)}) async-start(bf16[16,8,1280]{2,1,0:T(8,128)(2,1)} %fusion.4), calls=%async_computation.1 | async-start | bytes 655360 | tf_op jit(solution)/shard_map/all_to_all | solution.py:563
  64.8 7.2 %collective-permute-done.9.refs_3_ = bf16[144,1152]{1,0:T(8,128)(2,1)S(1)} collective-permute-done((bf16[144,1152]{1,0:T(8,128)(2,1)S(1)}, bf16[144,1152]{1,0:T(8,128)(2,1)S(1)}, u32[]{:S(2)}, u32[]{:S(2)}) %collective-permute-start.9) | collective-permute-done | bytes 331808 | tf_op jit(solution)/shard_map/ppermute | solution.py:546
  73.5 5.6 %collective-permute-done.15.refs_11_ = bf16[144,1152]{1,0:T(8,128)(2,1)S(1)} collective-permute-done((bf16[144,1152]{1,0:T(8,128)(2,1)S(1)}, bf16[144,1152]{1,0:T(8,128)(2,1)S(1)}, u32[]{:S(2)}, u32[]{:S(2)}) %collective-permute-start.15) | collective-permute-done | bytes 331808 | tf_op jit(solution)/shard_map/ppermute | solution.py:546
  89.9 11.1 %project.1 = (bf16[128,1152]{1,0:T(8,128)(2,1)}, bf16[640,2304]{1,0:T(8,128)(2,1)}) custom-call(s32[5]{0:T(128)} %stack.68.place_ref, bf16[576,3456]{1,0:T(8,128)(2,1)} %refs_0_.9, bf16[144,1152]{1,0:T(8,128)(2,1)} %copy-done.16, bf16[144,1152]{1,0:T(8,128)(2,1)} %copy-done.19, bf16[144,1152]{1,0:T(8,128)(2,1)} %copy-done.20, bf16[144,1152]{1,0:T(8,128)(2,1)} %copy-done.24, ...), custom_call_target="tpu_custom_call" | custom-call | tf_op jit(solution)/shard_map/project/pallas_call | solution.py:71
  103.6 10.3 %attend.1 = (bf16[128,1152]{1,0:T(8,128)(2,1)}, f32[128,1152]{1,0:T(8,128)}, f32[128,1152]{1,0:T(8,128)}, bf16[128,1152]{1,0:T(8,128)(2,1)}) custom-call(s32[5]{0:T(128)} %stack.68.place_ref, bf16[576,1152]{1,0:T(8,128)(2,1)} %refs_0_.8, bf16[144,1152]{1,0:T(8,128)(2,1)} %collective-permute-done.3.refs_1_, bf16[144,1152]{1,0:T(8,128)(2,1)} %copy-done.28, ...), custom_call_target="tpu_custom_call" | custom-call | tf_op jit(solution)/shard_map/attend/pallas_call | solution.py:71
  117.2 6.0 %collective-permute-done.30 = bf16[128,1152]{1,0:T(8,128)(2,1)S(1)} collective-permute-done((bf16[128,1152]{1,0:T(8,128)(2,1)}, bf16[128,1152]{1,0:T(8,128)(2,1)S(1)}, u32[]{:S(2)}, u32[]{:S(2)}) %collective-permute-start.30) | collective-permute-done | bytes 294944 | tf_op jit(solution)/shard_map/ppermute | solution.py:549
  125.0 14.8 %feed.1 = (bf16[256,2304]{1,0:T(8,128)(2,1)}, bf16[256,2304]{1,0:T(8,128)(2,1)}, f32[128,1152]{1,0:T(8,128)}, bf16[128,1152]{1,0:T(8,128)(2,1)}, f32[128,1152]{1,0:T(8,128)}, /*index=5*/bf16[128,1152]{1,0:T(8,128)(2,1)}) custom-call(s32[5]{0:T(128)} %stack.68.place_ref, bf16[576,4608]{1,0:T(8,128)(2,1)} %refs_0_.7, ...), custom_call_target="tpu_custom_call" | custom-call | tf_op jit(solution)/shard_map/feed/pallas_call | solution.py:316
  146.7 10.1 %term.4 = (bf16[4,72,2304]{2,1,0:T(8,128)(2,1)}, bf16[4,72,2304]{2,1,0:T(8,128)(2,1)}) custom-call(s32[5]{0:T(128)} %stack.68.place_ref, bf16[256,1152]{1,0:T(8,128)(2,1)} %bitcast.206, bf16[256,2304]{1,0:T(8,128)(2,1)} %get-tuple-element.68.refs_1_, bf16[256,1152]{1,0:T(8,128)(2,1)} %copy-done.41, bf16[256,2304]{1,0:T(8,128)(2,1)} %copy-done.32), custom_call_target="tpu_custom_call" | custom-call | tf_op jit(solution)/shard_map/term/pallas_call | solution.py:475
  157.5 5.4 %mid_back.1 = (f32[128,1152]{1,0:T(8,128)}, bf16[128,1152]{1,0:T(8,128)(2,1)}, bf16[128,1152]{1,0:T(8,128)(2,1)}, f32[3,16,1152]{2,1,0:T(8,128)}) custom-call(s32[5]{0:T(128)} %stack.68.place_ref, bf16[576,1152]{1,0:T(8,128)(2,1)} %refs_0_.8, bf16[144,1152]{1,0:T(8,128)(2,1)} %collective-permute-done.3.refs_1_, bf16[144,1152]{1,0:T(8,128)(2,1)} %copy-done.28, ...), custom_call_target="tpu_custom_call" | custom-call | tf_op jit(solution)/shard_map/mid_back/pallas_call | solution.py:71
  166.2 12.4 %attend_back.1 = (bf16[128,1152]{1,0:T(8,128)(2,1)}, bf16[5,128,2304]{2,1,0:T(8,128)(2,1)}) custom-call(bf16[128,1152]{1,0:T(8,128)(2,1)} %get-tuple-element.59.refs_5_.q_ref, bf16[640,2304]{1,0:T(8,128)(2,1)} %get-tuple-element.60.refs_6_.kv_ref, f32[640,128]{1,0:T(8,128)} %compare_select_fusion.bias_ref, bf16[128,1152]{1,0:T(8,128)(2,1)} %get-tuple-element.77.grad_ref), custom_call_target="tpu_custom_call" | custom-call | tf_op jit(solution)/shard_map/attend_back/pallas_call | solution.py:250
  182.7 7.9 %collective-permute-done.32 = bf16[128,1152]{1,0:T(8,128)(2,1)S(1)} collective-permute-done((bf16[128,1152]{1,0:T(8,128)(2,1)S(1)}, bf16[128,1152]{1,0:T(8,128)(2,1)S(1)}, u32[]{:S(2)}, u32[]{:S(2)}) %collective-permute-start.32) | collective-permute-done | bytes 294944 | tf_op jit(solution)/shard_map/ppermute | solution.py:549
  202.9 6.4 %all-to-all-start.2 = ((bf16[16,8,1152]{2,1,0:T(8,128)(2,1)}), bf16[16,8,1152]{2,1,0:T(8,128)(2,1)S(1)}, u32[]{:S(2)}, u32[]{:S(2)}) async-start(bf16[16,8,1152]{2,1,0:T(8,128)(2,1)} %bitcast.39), calls=%async_computation.2 | async-start | bytes 589824 | tf_op jit(solution)/shard_map/all_to_all | solution.py:567
  209.3 10.2 %term.5 = (bf16[4,288,576]{2,1,0:T(8,128)(2,1)}, bf16[4,288,576]{2,1,0:T(8,128)(2,1)}) custom-call(s32[5]{0:T(128)} %stack.68.place_ref, bf16[256,2304]{1,0:T(8,128)(2,1)} %get-tuple-element.81.refs_0_, bf16[256,1152]{1,0:T(8,128)(2,1)} %bitcast.203, bf16[256,2304]{1,0:T(8,128)(2,1)} %copy-done.31, bf16[256,1152]{1,0:T(8,128)(2,1)} %copy-done.40), custom_call_target="tpu_custom_call" | custom-call | tf_op jit(solution)/shard_map/term/pallas_call | solution.py:475
  223.3 17.1 %all-to-all-done.2 = bf16[16,8,1152]{2,1,0:T(8,128)(2,1)S(1)} async-done(((bf16[16,8,1152]{2,1,0:T(8,128)(2,1)}), bf16[16,8,1152]{2,1,0:T(8,128)(2,1)S(1)}, u32[]{:S(2)}, u32[]{:S(2)}) %all-to-all-start.2) | async-done | bytes 294944 | tf_op jit(solution)/shard_map/all_to_all | solution.py:567
  246.1 8.5 %in_back.1 = (bf16[128,1152]{1,0:T(8,128)(2,1)}, f32[2,16,1152]{2,1,0:T(8,128)}) custom-call(s32[5]{0:T(128)} %stack.68.place_ref, bf16[576,3456]{1,0:T(8,128)(2,1)} %refs_0_.9, bf16[144,1152]{1,0:T(8,128)(2,1)} %copy-done.16, bf16[144,1152]{1,0:T(8,128)(2,1)} %copy-done.19, bf16[144,1152]{1,0:T(8,128)(2,1)} %copy-done.20, bf16[144,1152]{1,0:T(8,128)(2,1)} %copy-done.24, ...), custom_call_target="tpu_custom_call" | custom-call | tf_op jit(solution)/shard_map/in_back/pallas_call | solution.py:71
  254.6 5.8 %all-to-all-start.3 = ((bf16[16,8,1152]{2,1,0:T(8,128)(2,1)}), bf16[16,8,1152]{2,1,0:T(8,128)(2,1)S(1)}, u32[]{:S(2)}, u32[]{:S(2)}) async-start(bf16[16,8,1152]{2,1,0:T(8,128)(2,1)} %bitcast.233), calls=%async_computation.3 | async-start | bytes 589824 | tf_op jit(solution)/shard_map/all_to_all | solution.py:567
  270.0 11.6 %collective-permute-done.55 = bf16[4,72,576]{2,1,0:T(8,128)(2,1)S(1)} collective-permute-done((bf16[4,72,576]{2,1,0:T(8,128)(2,1)S(1)}, bf16[4,72,576]{2,1,0:T(8,128)(2,1)S(1)}, u32[]{:S(2)}, u32[]{:S(2)}) %collective-permute-start.55) | collective-permute-done | bytes 331808 | tf_op jit(solution)/shard_map/ppermute | solution.py:546
  282.8 4.7 %collective-permute-done.66 = bf16[16,6912]{1,0:T(8,128)(2,1)S(1)} collective-permute-done((bf16[16,6912]{1,0:T(8,128)(2,1)S(1)}, bf16[16,6912]{1,0:T(8,128)(2,1)S(1)}, u32[]{:S(2)}, u32[]{:S(2)}) %collective-permute-start.66) | collective-permute-done | bytes 221216 | tf_op jit(solution)/shard_map/ppermute | solution.py:546
  288.8 5.2 %collective-permute-done.56 = bf16[2,72,576]{2,1,0:T(8,128)(2,1)S(1)} collective-permute-done((bf16[2,72,576]{2,1,0:T(8,128)(2,1)S(1)}, bf16[2,72,576]{2,1,0:T(8,128)(2,1)S(1)}, u32[]{:S(2)}, u32[]{:S(2)}) %collective-permute-start.56) | collective-permute-done | bytes 165920 | tf_op jit(solution)/shard_map/ppermute | solution.py:546
  304.5 14.5 %collective-permute-done.67 = bf16[16,6912]{1,0:T(8,128)(2,1)S(1)} collective-permute-done((bf16[16,6912]{1,0:T(8,128)(2,1)S(1)}, bf16[16,6912]{1,0:T(8,128)(2,1)S(1)}, u32[]{:S(2)}, u32[]{:S(2)}) %collective-permute-start.67) | collective-permute-done | bytes 221216 | tf_op jit(solution)/shard_map/ppermute | solution.py:546
  325.3 4.0 collective-permute-done.68
  331.6 12.3 %collective-permute-done.59 = bf16[2,288,576]{2,1,0:T(8,128)(2,1)S(1)} collective-permute-done((bf16[2,288,576]{2,1,0:T(8,128)(2,1)S(1)}, bf16[2,288,576]{2,1,0:T(8,128)(2,1)S(1)}, u32[]{:S(2)}, u32[]{:S(2)}) %collective-permute-start.59) | collective-permute-done | bytes 663584 | tf_op jit(solution)/shard_map/ppermute | solution.py:546
  345.9 8.1 %fusion.23 = f32[1152,3456]{1,0:T(8,128)} fusion(bf16[32,1152]{1,0:T(8,128)(2,1)S(1)} %bitcast.227, bf16[16,3456]{1,0:T(8,128)(2,1)S(1)} %collective-permute-done.69, bf16[16,3456]{1,0:T(8,128)(2,1)S(1)} %get-tuple-element.140), kind=kOutput, calls=%fused_computation.87 | convolution fusion | flops 255246336 | bytes 16220160 | tf_op jit(solution)/shard_map/dot_general | solution.py:851
  354.0 7.5 %collective-permute-done.60 = bf16[288,576]{1,0:T(8,128)(2,1)S(1)} collective-permute-done((bf16[288,576]{1,0:T(8,128)(2,1)S(1)}, bf16[288,576]{1,0:T(8,128)(2,1)S(1)}, u32[]{:S(2)}, u32[]{:S(2)}) %collective-permute-start.60) | collective-permute-done | bytes 331808 | tf_op jit(solution)/shard_map/ppermute | solution.py:546
  364.9 6.5 %term.6 = (bf16[4,104,576]{2,1,0:T(8,128)(2,1)}, bf16[4,104,576]{2,1,0:T(8,128)(2,1)}, bf16[4,112,576]{2,1,0:T(8,128)(2,1)}, bf16[4,112,576]{2,1,0:T(8,128)(2,1)}) custom-call(s32[5]{0:T(128)} %stack.68.place_ref, bf16[256,3456]{1,0:T(8,128)(2,1)} %copy-done.2, bf16[256,576]{1,0:T(8,128)(2,1)} %pad_maximum_fusion.8.refs_1_, bf16[256,3456]{1,0:T(8,128)(2,1)} %copy-done.12, ...), custom_call_target="tpu_custom_call" | custom-call | tf_op jit(solution)/shard_map/term/pallas_call | solution.py:475
  377.3 5.3 %collective-permute-done.61 = bf16[288,576]{1,0:T(8,128)(2,1)S(1)} collective-permute-done((bf16[288,576]{1,0:T(8,128)(2,1)S(1)}, bf16[288,576]{1,0:T(8,128)(2,1)S(1)}, u32[]{:S(2)}, u32[]{:S(2)}) %collective-permute-start.61) | collective-permute-done | bytes 331808 | tf_op jit(solution)/shard_map/ppermute | solution.py:898
  384.5 5.0 %collective-permute-start.48 = (bf16[2,104,576]{2,1,0:T(8,128)(2,1)S(1)}, bf16[2,104,576]{2,1,0:T(8,128)(2,1)S(1)}, u32[]{:S(2)}, u32[]{:S(2)}) collective-permute-start(bf16[2,104,576]{2,1,0:T(8,128)(2,1)S(1)} %dynamic-slice_bitcast_fusion.5), channel_id=1, source_target_pairs={{0,8},{2,10},{4,12},{6,14},{8,0},{10,2},{12,4},{14,6},{16,24},{18,... | collective-permute-start | bytes 718856 | tf_op jit(solution)/shard_map/ppermute | solution.py:546
  391.5 4.1 collective-permute-done.48
  402.3 7.0 %collective-permute-done.49 = bf16[104,576]{1,0:T(8,128)(2,1)S(1)} collective-permute-done((bf16[104,576]{1,0:T(8,128)(2,1)S(1)}, bf16[104,576]{1,0:T(8,128)(2,1)S(1)}, u32[]{:S(2)}, u32[]{:S(2)}) %collective-permute-start.49) | collective-permute-done | bytes 119840 | tf_op jit(solution)/shard_map/ppermute | solution.py:546
  (367 shorter events, 154.2 us)
Async XLA Ops:
  2.9 23.3 %collective-permute-start.1 = (bf16[144,1152]{1,0:T(8,128)(2,1)S(1)}, bf16[144,1152]{1,0:T(8,128)(2,1)S(1)}, u32[]{:S(2)}, u32[]{:S(2)}) collective-permute-start(bf16[144,1152]{1,0:T(8,128)(2,1)S(1)} %get-tuple-element.53), channel_id=1, source_target_pairs={{0,1},{1,0},{2,3},{3,2},{4,5},{5,4},{6,7},{7,6},{8,9},{9,8},{10,11... | collective-permute-start | bytes 995336 | tf_op jit(solution)/shard_map/ppermute | solution.py:549
  6.2 27.3 %all-to-all-start = ((bf16[16,8,1152]{2,1,0:T(8,128)(2,1)}), bf16[16,8,1152]{2,1,0:T(8,128)(2,1)S(1)}, u32[]{:S(2)}, u32[]{:S(2)}) async-start(bf16[16,8,1152]{2,1,0:T(8,128)(2,1)} %fusion.2), calls=%async_computation | async-start | bytes 589824 | tf_op jit(solution)/shard_map/all_to_all | solution.py:563
  28.3 17.9 %collective-permute-start.11 = (bf16[144,1152]{1,0:T(8,128)(2,1)S(1)}, bf16[144,1152]{1,0:T(8,128)(2,1)S(1)}, u32[]{:S(2)}, u32[]{:S(2)}) collective-permute-start(bf16[144,1152]{1,0:T(8,128)(2,1)S(1)} %collective-permute-done.1.refs_5_), channel_id=1, source_target_pairs={{0,2},{2,0},{4,6},{6,4},{8,10},{10,8},{12,14},{14,12},{16,18},{18,... | collective-permute-start | bytes 995336 | tf_op jit(solution)/shard_map/ppermute | solution.py:546
  28.3 18.5 %collective-permute-start.12 = (bf16[144,1152]{1,0:T(8,128)(2,1)S(1)}, bf16[144,1152]{1,0:T(8,128)(2,1)S(1)}, u32[]{:S(2)}, u32[]{:S(2)}) collective-permute-start(bf16[144,1152]{1,0:T(8,128)(2,1)S(1)} %collective-permute-done.1.refs_5_), channel_id=1, source_target_pairs={{0,4},{2,6},{4,0},{6,2},{8,12},{10,14},{12,8},{14,10},{16,20},{18,... | collective-permute-start | bytes 995336 | tf_op jit(solution)/shard_map/ppermute | solution.py:546
  36.2 21.6 %collective-permute-start.18 = (bf16[128,1152]{1,0:T(8,128)(2,1)}, bf16[128,1152]{1,0:T(8,128)(2,1)}, u32[]{:S(2)}, u32[]{:S(2)}) collective-permute-start(bf16[128,1152]{1,0:T(8,128)(2,1)} %norm_in.1.refs_13_), channel_id=1, source_target_pairs={{0,2},{2,0},{4,6},{6,4},{8,10},{10,8},{12,14},{14,12},{16,18},{18,... | collective-permute-start | bytes 884744 | tf_op jit(solution)/shard_map/ppermute | solution.py:546
  38.3 20.0 %collective-permute-start.19 = (bf16[128,1152]{1,0:T(8,128)(2,1)}, bf16[128,1152]{1,0:T(8,128)(2,1)S(1)}, u32[]{:S(2)}, u32[]{:S(2)}) collective-permute-start(bf16[128,1152]{1,0:T(8,128)(2,1)} %norm_in.1.refs_13_), channel_id=1, source_target_pairs={{0,4},{2,6},{4,12},{6,14},{12,8},{14,10},{8,16},{10,18},{16,20},{1... | collective-permute-start | bytes 884744 | tf_op jit(solution)/shard_map/ppermute | solution.py:555
  50.0 30.8 %all-to-all-start.1 = ((bf16[16,8,1280]{2,1,0:T(8,128)(2,1)}), bf16[16,8,1280]{2,1,0:T(8,128)(2,1)S(1)}, u32[]{:S(2)}, u32[]{:S(2)}) async-start(bf16[16,8,1280]{2,1,0:T(8,128)(2,1)} %fusion.4), calls=%async_computation.1 | async-start | bytes 655360 | tf_op jit(solution)/shard_map/all_to_all | solution.py:563
  60.1 19.0 %collective-permute-start.15 = (bf16[144,1152]{1,0:T(8,128)(2,1)S(1)}, bf16[144,1152]{1,0:T(8,128)(2,1)S(1)}, u32[]{:S(2)}, u32[]{:S(2)}) collective-permute-start(bf16[144,1152]{1,0:T(8,128)(2,1)S(1)} %collective-permute-done.2.refs_9_), channel_id=1, source_target_pairs={{0,4},{2,6},{4,0},{6,2},{8,12},{10,14},{12,8},{14,10},{16,20},{18,... | collective-permute-start | bytes 995336 | tf_op jit(solution)/shard_map/ppermute | solution.py:546
  81.0 21.4 %collective-permute-start.4 = (bf16[144,1152]{1,0:T(8,128)(2,1)}, bf16[144,1152]{1,0:T(8,128)(2,1)S(1)}, u32[]{:S(2)}, u32[]{:S(2)}) collective-permute-start(bf16[144,1152]{1,0:T(8,128)(2,1)} %collective-permute-done.3.refs_1_), channel_id=1, source_target_pairs={{0,2},{2,0},{4,6},{6,4},{8,10},{10,8},{12,14},{14,12},{16,18},{18,... | collective-permute-start | bytes 995336 | tf_op jit(solution)/shard_map/ppermute | solution.py:546
  81.5 20.8 %collective-permute-start.26 = (bf16[144,1152]{1,0:T(8,128)(2,1)}, bf16[144,1152]{1,0:T(8,128)(2,1)S(1)}, u32[]{:S(2)}, u32[]{:S(2)}) collective-permute-start(bf16[144,1152]{1,0:T(8,128)(2,1)} %collective-permute-done.22), channel_id=1, source_target_pairs={{0,4},{2,6},{4,0},{6,2},{8,12},{10,14},{12,8},{14,10},{16,20},{18,... | collective-permute-start | bytes 995336 | tf_op jit(solution)/shard_map/ppermute | solution.py:546
  86.8 28.7 %collective-permute-start.27 = (bf16[144,1152]{1,0:T(8,128)(2,1)}, bf16[144,1152]{1,0:T(8,128)(2,1)S(1)}, u32[]{:S(2)}, u32[]{:S(2)}) collective-permute-start(bf16[144,1152]{1,0:T(8,128)(2,1)} %collective-permute-done.23), channel_id=1, source_target_pairs={{0,4},{2,6},{4,0},{6,2},{8,12},{10,14},{12,8},{14,10},{16,20},{18,... | collective-permute-start | bytes 995336 | tf_op jit(solution)/shard_map/ppermute | solution.py:546
  102.5 21.6 %collective-permute-start.28 = (bf16[144,1152]{1,0:T(8,128)(2,1)S(1)}, bf16[144,1152]{1,0:T(8,128)(2,1)S(1)}, u32[]{:S(2)}, u32[]{:S(2)}) collective-permute-start(bf16[144,1152]{1,0:T(8,128)(2,1)S(1)} %collective-permute-done.26), channel_id=1, source_target_pairs={{0,2},{2,0},{4,6},{6,4},{8,10},{10,8},{12,14},{14,12},{16,18},{18,... | collective-permute-start | bytes 995336 | tf_op jit(solution)/shard_map/ppermute | solution.py:546
  139.9 25.1 %collective-permute-start.36 = (bf16[256,2304]{1,0:T(8,128)(2,1)}, bf16[256,2304]{1,0:T(8,128)(2,1)S(1)}, u32[]{:S(2)}, u32[]{:S(2)}) collective-permute-start(bf16[256,2304]{1,0:T(8,128)(2,1)} %get-tuple-element.81.refs_0_), channel_id=1, source_target_pairs={{0,2},{2,0},{4,6},{6,4},{8,10},{10,8},{12,14},{14,12},{16,18},{18,... | collective-permute-start | bytes 3538952 | tf_op jit(solution)/shard_map/ppermute | solution.py:546
  140.5 24.5 %collective-permute-start.37 = (bf16[256,1152]{1,0:T(8,128)(2,1)S(1)}, bf16[256,1152]{1,0:T(8,128)(2,1)S(1)}, u32[]{:S(2)}, u32[]{:S(2)}) collective-permute-start(bf16[256,1152]{1,0:T(8,128)(2,1)S(1)} %bitcast.204), channel_id=1, source_target_pairs={{0,2},{2,0},{4,6},{6,4},{8,10},{10,8},{12,14},{14,12},{16,18},{18,... | collective-permute-start | bytes 1769480 | tf_op jit(solution)/shard_map/ppermute | solution.py:546
  191.5 27.9 %collective-permute-start.44 = (bf16[128,2304]{1,0:T(8,128)(2,1)}, bf16[128,2304]{1,0:T(8,128)(2,1)S(1)}, u32[]{:S(2)}, u32[]{:S(2)}) collective-permute-start(bf16[128,2304]{1,0:T(8,128)(2,1)} %concatenate.92), channel_id=1, source_target_pairs={{0,1},{1,0},{2,3},{3,2},{4,5},{5,4},{6,7},{7,6},{8,9},{9,8},{10,11... | collective-permute-start | bytes 1769480 | tf_op jit(solution)/shard_map/ppermute | solution.py:549
  192.8 74.0 %collective-permute-start.62 = (bf16[4,72,2304]{2,1,0:T(8,128)(2,1)}, bf16[4,72,2304]{2,1,0:T(8,128)(2,1)S(1)}, u32[]{:S(2)}, u32[]{:S(2)}) collective-permute-start(bf16[4,72,2304]{2,1,0:T(8,128)(2,1)} %get-tuple-element.69), channel_id=1, source_target_pairs={{0,4},{2,6},{4,0},{6,2},{8,12},{10,14},{12,8},{14,10},{16,20},{18,... | collective-permute-start | bytes 3981320 | tf_op jit(solution)/shard_map/ppermute | solution.py:546
  193.9 108.1 %collective-permute-start.42 = (bf16[128,1152]{1,0:T(8,128)(2,1)}, bf16[128,1152]{1,0:T(8,128)(2,1)}, u32[]{:S(2)}, u32[]{:S(2)}) collective-permute-start(bf16[128,1152]{1,0:T(8,128)(2,1)} %get-tuple-element.80.refs_13_), channel_id=1, source_target_pairs={{0,1},{1,0},{2,3},{3,2},{4,5},{5,4},{6,7},{7,6},{8,9},{9,8},{10,11... | collective-permute-start | bytes 884744 | tf_op jit(solution)/shard_map/ppermute | solution.py:549
  198.0 45.3 %collective-permute-start.41 = (bf16[128,2304]{1,0:T(8,128)(2,1)}, bf16[128,2304]{1,0:T(8,128)(2,1)}, u32[]{:S(2)}, u32[]{:S(2)}) collective-permute-start(bf16[128,2304]{1,0:T(8,128)(2,1)} %get-tuple-element.125), channel_id=1, source_target_pairs={{0,4},{2,6},{4,12},{6,14},{12,8},{14,10},{8,16},{10,18},{16,20},{1... | collective-permute-start | bytes 1769480 | tf_op jit(solution)/shard_map/ppermute | solution.py:555
  201.6 41.9 %collective-permute-start.40 = (bf16[128,2304]{1,0:T(8,128)(2,1)}, bf16[128,2304]{1,0:T(8,128)(2,1)}, u32[]{:S(2)}, u32[]{:S(2)}) collective-permute-start(bf16[128,2304]{1,0:T(8,128)(2,1)} %get-tuple-element.126), channel_id=1, source_target_pairs={{4,0},{6,2},{12,4},{14,6},{8,12},{10,14},{16,8},{18,10},{20,16},{2... | collective-permute-start | bytes 1769480 | tf_op jit(solution)/shard_map/ppermute | solution.py:555
  202.9 37.6 %all-to-all-start.2 = ((bf16[16,8,1152]{2,1,0:T(8,128)(2,1)}), bf16[16,8,1152]{2,1,0:T(8,128)(2,1)S(1)}, u32[]{:S(2)}, u32[]{:S(2)}) async-start(bf16[16,8,1152]{2,1,0:T(8,128)(2,1)} %bitcast.39), calls=%async_computation.2 | async-start | bytes 589824 | tf_op jit(solution)/shard_map/all_to_all | solution.py:567
  219.5 101.3 %collective-permute-start.58 = (bf16[4,288,576]{2,1,0:T(8,128)(2,1)}, bf16[4,288,576]{2,1,0:T(8,128)(2,1)}, u32[]{:S(2)}, u32[]{:S(2)}) collective-permute-start(bf16[4,288,576]{2,1,0:T(8,128)(2,1)} %get-tuple-element.85), channel_id=1, source_target_pairs={{0,4},{2,6},{4,0},{6,2},{8,12},{10,14},{12,8},{14,10},{16,20},{18,... | collective-permute-start | bytes 3981320 | tf_op jit(solution)/shard_map/ppermute | solution.py:546
  243.3 19.1 %collective-permute-start.53 = (bf16[256,1152]{1,0:T(8,128)(2,1)S(1)}, bf16[256,1152]{1,0:T(8,128)(2,1)}, u32[]{:S(2)}, u32[]{:S(2)}) collective-permute-start(bf16[256,1152]{1,0:T(8,128)(2,1)S(1)} %pad_maximum_fusion.6.refs_0_), channel_id=1, source_target_pairs={{0,2},{2,0},{4,6},{6,4},{8,10},{10,8},{12,14},{14,12},{16,18},{18,... | collective-permute-start | bytes 1769480 | tf_op jit(solution)/shard_map/ppermute | solution.py:546
  243.5 18.3 %collective-permute-start.54 = (bf16[256,576]{1,0:T(8,128)(2,1)}, bf16[256,576]{1,0:T(8,128)(2,1)}, u32[]{:S(2)}, u32[]{:S(2)}) collective-permute-start(bf16[256,576]{1,0:T(8,128)(2,1)} %pad_maximum_fusion.9.refs_1_), channel_id=1, source_target_pairs={{0,2},{2,0},{4,6},{6,4},{8,10},{10,8},{12,14},{14,12},{16,18},{18,... | collective-permute-start | bytes 884744 | tf_op jit(solution)/shard_map/ppermute | solution.py:546
  254.6 41.6 %all-to-all-start.3 = ((bf16[16,8,1152]{2,1,0:T(8,128)(2,1)}), bf16[16,8,1152]{2,1,0:T(8,128)(2,1)S(1)}, u32[]{:S(2)}, u32[]{:S(2)}) async-start(bf16[16,8,1152]{2,1,0:T(8,128)(2,1)} %bitcast.233), calls=%async_computation.3 | async-start | bytes 589824 | tf_op jit(solution)/shard_map/all_to_all | solution.py:567
  261.9 101.7 %collective-permute-start.46 = (bf16[256,576]{1,0:T(8,128)(2,1)}, bf16[256,576]{1,0:T(8,128)(2,1)}, u32[]{:S(2)}, u32[]{:S(2)}) collective-permute-start(bf16[256,576]{1,0:T(8,128)(2,1)} %pad_maximum_fusion.8.refs_1_), channel_id=1, source_target_pairs={{0,2},{2,0},{4,6},{6,4},{8,10},{10,8},{12,14},{14,12},{16,18},{18,... | collective-permute-start | bytes 884744 | tf_op jit(solution)/shard_map/ppermute | solution.py:546
  262.4 40.6 %collective-permute-start.43 = (bf16[128,2304]{1,0:T(8,128)(2,1)S(1)}, bf16[128,2304]{1,0:T(8,128)(2,1)}, u32[]{:S(2)}, u32[]{:S(2)}) collective-permute-start(bf16[128,2304]{1,0:T(8,128)(2,1)S(1)} %copy-done.3), channel_id=1, source_target_pairs={{0,1},{1,0},{2,3},{3,2},{4,5},{5,4},{6,7},{7,6},{8,9},{9,8},{10,11... | collective-permute-start | bytes 1769480 | tf_op jit(solution)/shard_map/ppermute | solution.py:549
  300.3 24.3 %collective-permute-start.63 = (bf16[2,72,2304]{2,1,0:T(8,128)(2,1)S(1)}, bf16[2,72,2304]{2,1,0:T(8,128)(2,1)S(1)}, u32[]{:S(2)}, u32[]{:S(2)}) collective-permute-start(bf16[2,72,2304]{2,1,0:T(8,128)(2,1)S(1)} %dynamic-slice_bitcast_fusion.1), channel_id=1, source_target_pairs={{0,8},{2,10},{4,12},{6,14},{8,0},{10,2},{12,4},{14,6},{16,24},{18,... | collective-permute-start | bytes 1990664 | tf_op jit(solution)/shard_map/ppermute | solution.py:546
  304.4 59.2 %collective-permute-start.45 = (bf16[256,3456]{1,0:T(8,128)(2,1)S(1)}, bf16[256,3456]{1,0:T(8,128)(2,1)S(1)}, u32[]{:S(2)}, u32[]{:S(2)}) collective-permute-start(bf16[256,3456]{1,0:T(8,128)(2,1)S(1)} %maximum_maximum_fusion.refs_0_), channel_id=1, source_target_pairs={{0,2},{2,0},{4,6},{6,4},{8,10},{10,8},{12,14},{14,12},{16,18},{18,... | collective-permute-start | bytes 5308424 | tf_op jit(solution)/shard_map/ppermute | solution.py:546
  322.6 21.3 %collective-permute-start.59 = (bf16[2,288,576]{2,1,0:T(8,128)(2,1)S(1)}, bf16[2,288,576]{2,1,0:T(8,128)(2,1)S(1)}, u32[]{:S(2)}, u32[]{:S(2)}) collective-permute-start(bf16[2,288,576]{2,1,0:T(8,128)(2,1)S(1)} %dynamic-slice_bitcast_fusion), channel_id=1, source_target_pairs={{0,8},{2,10},{4,12},{6,14},{8,0},{10,2},{12,4},{14,6},{16,24},{18,... | collective-permute-start | bytes 1990664 | tf_op jit(solution)/shard_map/ppermute | solution.py:546
  324.8 48.1 %collective-permute-start.64 = (bf16[72,2304]{1,0:T(8,128)(2,1)S(1)}, bf16[72,2304]{1,0:T(8,128)(2,1)S(1)}, u32[]{:S(2)}, u32[]{:S(2)}) collective-permute-start(bf16[72,2304]{1,0:T(8,128)(2,1)S(1)} %dynamic-slice_bitcast_fusion.3), channel_id=1, source_target_pairs={{0,16},{2,18},{4,20},{6,22},{8,24},{10,26},{12,28},{14,30},{16,0},... | collective-permute-start | bytes 995336 | tf_op jit(solution)/shard_map/ppermute | solution.py:546
  344.2 17.4 %collective-permute-start.60 = (bf16[288,576]{1,0:T(8,128)(2,1)S(1)}, bf16[288,576]{1,0:T(8,128)(2,1)S(1)}, u32[]{:S(2)}, u32[]{:S(2)}) collective-permute-start(bf16[288,576]{1,0:T(8,128)(2,1)S(1)} %dynamic-slice_bitcast_fusion.2), channel_id=1, source_target_pairs={{0,16},{2,18},{4,20},{6,22},{8,24},{10,26},{12,28},{14,30},{16,0},... | collective-permute-start | bytes 995336 | tf_op jit(solution)/shard_map/ppermute | solution.py:546
  361.7 20.9 %collective-permute-start.61 = (bf16[288,576]{1,0:T(8,128)(2,1)S(1)}, bf16[288,576]{1,0:T(8,128)(2,1)S(1)}, u32[]{:S(2)}, u32[]{:S(2)}) collective-permute-start(bf16[288,576]{1,0:T(8,128)(2,1)S(1)} %fusion.12), channel_id=1, source_target_pairs={{0,0},{1,16},{2,2},{3,18},{4,4},{5,20},{6,6},{7,22},{8,8},{9,24},{... | collective-permute-start | bytes 995336 | tf_op jit(solution)/shard_map/ppermute | solution.py:898
  (105 other events, 1152.7 us)

commit v3 on v2

--- a/solution.py
+++ b/solution.py
@@ -23,6 +23,7 @@
 score_scale = HD ** (-0.5)
 VMEM_LIMIT = 56 * 1024 * 1024
 VMEM_SPEC = pl.BlockSpec(memory_space=pltpu.VMEM)
+COST = pl.CostEstimate(flops=1, transcendentals=0, bytes_accessed=1)
 
 
 def params():
@@ -50,7 +51,7 @@
 
 def fill(target_ref, place_ref, refs, parts):
     half = target_ref.shape[0] // 2
-    mine, quarter = place_ref[0], place_ref[1]
+    mine = place_ref[0]
     for ref, (step, column) in zip(refs, parts):
         rows, cols = ref.shape
         if step == "all":
@@ -58,7 +59,8 @@
         elif step is None:
             start = pl.multiple_of(mine * half, 16)
         else:
-            start = pl.multiple_of((1 - mine) * half + (quarter ^ step) * rows, 16)
+            quarter = place_ref[step[0]] ^ step[1]
+            start = pl.multiple_of((1 - mine) * half + quarter * rows, 16)
         target_ref[pl.ds(start, rows), pl.ds(column, cols)] = ref[...]
 
 
@@ -79,6 +81,7 @@
             scratch_shapes=scratch,
         ),
         compiler_params=params(),
+        cost_estimate=COST,
         name=name,
     )(place, *arrays, *inputs)
 
@@ -99,22 +102,31 @@
     return (grad - mean_grad - normed * mean_dot) * inverse
 
 
-def norm_in_kernel(tokens_ref, shift_ref, scale_ref, out_ref):
+def slot_rows(value):
+    repeats = PERIOD // value.shape[0]
+    return jnp.concatenate([value] * repeats, axis=0) if repeats > 1 else value
+
+
+def norm_in_kernel(place_ref, tokens_ref, own_ref, other_ref, out_ref):
+    first = place_ref[0] == 0
+    shift = slot_rows(jnp.where(first, own_ref[:, pl.ds(0, D)], other_ref[:, pl.ds(0, D)]))
+    scale = slot_rows(jnp.where(first, own_ref[:, pl.ds(D, D)], other_ref[:, pl.ds(D, D)]))
     for start in range(0, tokens_ref.shape[0], PERIOD):
         rows = pl.ds(start, PERIOD)
-        normed, ignored = normalized(tokens_ref[rows, :].astype(f32))
-        out_ref[rows, :] = (normed * (1.0 + scale_ref[...]) + shift_ref[...]).astype(bf16)
-
-
-def norm_in(tokens, shift, scale):
+        normed, ignored = normalized(tokens_ref[rows, pl.ds(0, D)].astype(f32))
+        out_ref[rows, :] = (normed * (1.0 + scale) + shift).astype(bf16)
+
+
+def norm_in(place, tokens, own, other):
     return pl.pallas_call(
         norm_in_kernel,
-        out_shape=shaped(*tokens.shape, dtype=bf16),
-        in_specs=[VMEM_SPEC] * 3,
+        out_shape=shaped(tokens.shape[0], D, dtype=bf16),
+        in_specs=[pl.BlockSpec(memory_space=pltpu.SMEM)] + [VMEM_SPEC] * 3,
         out_specs=VMEM_SPEC,
         compiler_params=params(),
+        cost_estimate=COST,
         name="norm_in",
-    )(tokens, shift, scale)
+    )(place, tokens, own, other)
 
 
 def project_kernel(place_ref, *refs, parts):
@@ -188,7 +200,7 @@
     proj_ref[...] = dot_nn(merged_ref[...], weight_ref[...])
     for start in range(0, tokens, PERIOD):
         rows = pl.ds(start, PERIOD)
-        mid = tokens_ref[rows, :].astype(f32) + gate_ref[...] * proj_ref[rows, :]
+        mid = tokens_ref[rows, pl.ds(0, D)].astype(f32) + gate_ref[...] * proj_ref[rows, :]
         mid_ref[rows, :] = mid
         normed, ignored = normalized(mid)
         normed_ref[rows, :] = (normed * (1.0 + scale_ref[...]) + shift_ref[...]).astype(bf16)
@@ -213,9 +225,10 @@
 
 
 def attend_back_kernel(
-    q_ref, kv_ref, bias_ref, grad_ref, dq_ref, dkv_ref, dq_acc, dk_acc, dv_acc
+    q_ref, kv_ref, bias_ref, grad_ref, dq_ref, *refs
 ):
     tokens = q_ref.shape[0]
+    dkv_refs, (dq_acc, dk_acc, dv_acc) = refs[:-3], refs[-3:]
     dq_acc[...] = jnp.zeros_like(dq_acc)
     dk_acc[...] = jnp.zeros_like(dk_acc)
     dv_acc[...] = jnp.zeros_like(dv_acc)
@@ -238,38 +251,40 @@
         dv_acc[:, window] += dot_nn(probs_low, grad)
         dq_acc[:, window] += jnp.where(lanes, dot_tn(grad_scores, keys), 0.0)
     dq_ref[...] = (dq_acc[...] * score_scale).astype(bf16)
-    for index in range(dkv_ref.shape[0]):
+    for index, dkv_ref in enumerate(dkv_refs):
         rows = pl.ds(index * tokens, tokens)
-        dkv_ref[index, :, pl.ds(0, D)] = (dk_acc[rows, :] * score_scale).astype(bf16)
-        dkv_ref[index, :, pl.ds(D, D)] = dv_acc[rows, :].astype(bf16)
+        dkv_ref[:, pl.ds(0, D)] = (dk_acc[rows, :] * score_scale).astype(bf16)
+        dkv_ref[:, pl.ds(D, D)] = dv_acc[rows, :].astype(bf16)
 
 
 def attend_back(queries, kv_window, bias_t, grad_heads):
     tokens = queries.shape[0]
     keys = kv_window.shape[0]
+    outs = [shaped(tokens, D, dtype=bf16)]
+    outs += [shaped(tokens, 2 * D, dtype=bf16)] * (keys // tokens)
     return pl.pallas_call(
         attend_back_kernel,
-        out_shape=(
-            shaped(tokens, D, dtype=bf16),
-            shaped(keys // tokens, tokens, 2 * D, dtype=bf16),
-        ),
+        out_shape=outs,
         in_specs=[VMEM_SPEC] * 4,
-        out_specs=(VMEM_SPEC,) * 2,
+        out_specs=[VMEM_SPEC] * len(outs),
         scratch_shapes=[
             pltpu.VMEM((tokens, D), f32),
             pltpu.VMEM((keys, D), f32),
             pltpu.VMEM((keys, D), f32),
         ],
         compiler_params=params(),
+        cost_estimate=COST,
         name="attend_back",
     )(queries, kv_window, bias_t, grad_heads)
 
 
-def feed_kernel(place_ref, *refs, parts, own_rows):
+def feed_kernel(place_ref, *refs, parts, arrays):
     count = len(parts)
-    mid_ref, grad_ref, channel_ref, down_ref = refs[count : count + 4]
-    act_ref, pre_ref, grad_own, grad_low, out_own, out_low = refs[count + 4 : count + 10]
-    weight_ref, grad_acc, out_acc = refs[count + 10 :]
+    mid_refs, grad_refs = refs[count : count + arrays], refs[count + arrays : count + 2 * arrays]
+    channel_ref, down_ref = refs[count + 2 * arrays : count + 2 * arrays + 2]
+    act_ref, pre_ref, grad_own, grad_low, out_own, out_low = refs[-9:-3]
+    weight_ref, grad_acc, out_acc = refs[-3:]
+    own_rows = grad_own.shape[0]
     step, steps = pl.program_id(0), pl.num_programs(0)
     rows, cols = act_ref.shape
     groups = channel_ref.shape[0]
@@ -284,9 +299,11 @@
     root = 0.7978845608028654
     for group in range(groups):
         span = pl.ds(group * tokens, tokens)
+        source, at = (group, 0) if arrays > 1 else (0, group * tokens)
+        part = pl.ds(at, tokens)
         channels = jnp.concatenate([channel_ref[group]] * (tokens // PERIOD), axis=0)
-        pre = dot_nn(mid_ref[span, :], weight_ref[...])
-        grad_act = dot_nt(grad_ref[span, :], down_ref[...])
+        pre = dot_nn(mid_refs[source][part, :], weight_ref[...])
+        grad_act = dot_nt(grad_refs[source][part, :], down_ref[...])
         square = pre * pre
         inner = jnp.tanh(root * (pre + 0.044715 * (square * pre)))
         half_sum = 0.5 + 0.5 * inner
@@ -307,14 +324,14 @@
         out_low[...] = out_acc[pl.ds(skip, rows - skip), :].astype(bf16)
 
 
-def feed(place, sources, mid_rows, grad_rows, channels, down, chunk, tokens, low_rows):
+def feed(place, sources, mids, grads, channels, down, chunk, tokens, low_rows):
     arrays, specs, parts = source_inputs(sources)
-    rows = mid_rows.shape[0]
+    rows = sum(mid.shape[0] for mid in mids)
     width = down.shape[0]
     by_chunk = pl.BlockSpec((rows, chunk), lambda i, place: (0, i))
     own, low = (tokens, D), (low_rows, D)
     return pl.pallas_call(
-        functools.partial(feed_kernel, parts=parts, own_rows=tokens),
+        functools.partial(feed_kernel, parts=parts, arrays=len(mids)),
         out_shape=[
             shaped(rows, width, dtype=bf16),
             shaped(rows, width, dtype=bf16),
@@ -327,9 +344,8 @@
             num_scalar_prefetch=1,
             grid=(width // chunk,),
             in_specs=specs
+            + [whole(value.shape) for value in (*mids, *grads)]
             + [
-                whole((rows, D)),
-                whole((rows, D)),
                 pl.BlockSpec(
                     (channels.shape[0], PERIOD, chunk), lambda i, place: (0, 0, i)
                 ),
@@ -343,8 +359,9 @@
             ],
         ),
         compiler_params=params(),
+        cost_estimate=COST,
         name="feed",
-    )(place, *arrays, mid_rows, grad_rows, channels, down)
+    )(place, *arrays, *mids, *grads, channels, down)
 
 
 def mid_back_kernel(place_ref, *refs, parts):
@@ -352,7 +369,16 @@
     own_ref, other_ref, mid_ref, proj_ref, late_ref, scale_ref, gate_ref, mask_ref = refs[
         count : count + 8
     ]
-    grad_mid_ref, grad_attn_ref, heads_ref, sums_ref, weight_ref, merged_ref = refs[count + 8 :]
+    attn_ref, normed_ref = refs[count + 8 : count + 10]
+    grad_mid_ref, own_pack_ref, pack_ref, heads_ref, sums_ref, weight_ref, merged_ref = refs[
+        count + 10 :
+    ]
+    first = place_ref[0] == 0
+    half = D // 2
+    for index, ref in enumerate((attn_ref, normed_ref)):
+        low, high = ref[:, pl.ds(0, half)], ref[:, pl.ds(half, half)]
+        own_pack_ref[:, pl.ds(index * half, half)] = jnp.where(first, low, high)
+        pack_ref[:, pl.ds(index * half, half)] = jnp.where(first, high, low)
     tokens = own_ref.shape[0]
     fill(weight_ref, place_ref, refs[:count], parts)
     gate_sum = jnp.zeros((PERIOD, D), f32)
@@ -362,18 +388,20 @@
         rows = pl.ds(start, PERIOD)
         normed, inverse = normalized(mid_ref[rows, :])
         grad = own_ref[rows, :] + other_ref[rows, :].astype(f32)
-        grad_mid = late_ref[rows, pl.ds(0, D)].astype(f32) + normalized_back(
+        grad_mid = late_ref[rows, pl.ds(D, D)].astype(f32) + normalized_back(
             grad * (1.0 + scale_ref[...]), normed, inverse
         )
         grad_mid_ref[rows, :] = grad_mid
-        grad_attn_ref[rows, :] = (grad_mid * gate_ref[...]).astype(bf16)
+        grad_attn = (grad_mid * gate_ref[...]).astype(bf16)
+        own_pack_ref[rows, pl.ds(D, D)] = grad_attn
+        pack_ref[rows, pl.ds(D, D)] = grad_attn
         gate_sum += grad_mid * proj_ref[rows, :]
         shift_sum += grad
         scale_sum += grad * normed
     sums_ref[0] = gate_sum
     sums_ref[1] = shift_sum
     sums_ref[2] = scale_sum
-    merged_ref[...] = dot_nt(grad_attn_ref[...], weight_ref[...])
+    merged_ref[...] = dot_nt(pack_ref[:, pl.ds(D, D)], weight_ref[...])
     for start in range(0, tokens, PERIOD):
         rows = pl.ds(start, PERIOD)
         heads_ref[rows, :] = (merged_ref[rows, :] * mask_ref[...]).astype(bf16)
@@ -388,7 +416,8 @@
         inputs,
         [
             shaped(tokens, D),
-            shaped(tokens, D, dtype=bf16),
+            shaped(tokens, 2 * D, dtype=bf16),
+            shaped(tokens, 2 * D, dtype=bf16),
             shaped(tokens, D, dtype=bf16),
             shaped(3, PERIOD, D),
         ],
@@ -410,7 +439,7 @@
     scale_sum = jnp.zeros((PERIOD, D), f32)
     for start in range(0, tokens, PERIOD):
         rows = pl.ds(start, PERIOD)
-        normed, inverse = normalized(tokens_ref[rows, :].astype(f32))
+        normed, inverse = normalized(tokens_ref[rows, pl.ds(0, D)].astype(f32))
         grad = grad_ref[rows, :]
         back = normalized_back(grad * (1.0 + scale_ref[...]), normed, inverse)
         grad_in_ref[rows, :] = (grad_mid_ref[rows, :] + back).astype(bf16)
@@ -433,54 +462,75 @@
     )
 
 
-def term_kernel(place_ref, *refs, pairs, chunk, plan):
-    acc_ref = refs[-1]
-    for index in range(pairs):
-        value = None
-        grads, acts = refs[2 * index], refs[2 * index + 1]
-        width = acts.shape[1]
+def term_kernel(place_ref, *refs, layout, outputs):
+    joined = refs[-3 * len(layout) :]
+    place_at = {0: place_ref[3], 1: place_ref[4]}
+    core = place_ref[2]
+    first_out = len(refs) - 3 * len(layout) - 2 * outputs
+    for index, (pieces, chunk, plan) in enumerate(layout):
+        grads_ref, acts_ref, acc_ref = joined[3 * index : 3 * index + 3]
+        for target, ref_at, column, cols, row_to, col_to in pieces:
+            value = refs[ref_at][:, pl.ds(column, cols)]
+            into = grads_ref if target == 0 else acts_ref
+            into[pl.ds(row_to, value.shape[0]), pl.ds(col_to, cols)] = value
+        width = acts_ref.shape[1]
         for start in range(0, width, 576):
             span = pl.ds(start, 576)
-            value = dot_tn(grads[...], acts[:, span])
-            acc_ref[:, span] = value if index == 0 else acc_ref[:, span] + value
-    core = place_ref[2]
-    outs = refs[2 * pairs : -1]
-    for out_index, (first, count, axis) in enumerate(plan):
-        send_ref, keep_ref = outs[2 * out_index], outs[2 * out_index + 1]
-        at = place_ref[3 + axis]
-        width = send_ref.shape[-1]
-        for target, side in ((send_ref, 1 - at), (keep_ref, at)):
-            blocks = target.shape[0]
-            for block in range(blocks):
-                pieces = acc_ref.shape[1] // width
-                lane, rest = block // (blocks // pieces), block % (blocks // pieces)
-                if axis == 0:
-                    line = rest * 4 + side * 2 + core
-                else:
-                    line = (rest // 2) * 8 + side * 4 + (rest % 2) * 2 + core
-                start = pl.multiple_of(line * chunk + first, 8)
-                target[block] = acc_ref[pl.ds(start, count), pl.ds(lane * width, width)].astype(
-                    bf16
-                )
-
-
-def term(place, pairs, plan, blocks, width):
-    columns = pairs[0][0].shape[1]
-    rows = pairs[0][1].shape[1]
-    chunk = columns // (4 * blocks * width // rows)
-    flat = [value for pair in pairs for value in pair]
-    outs = []
-    for first, count, axis in plan:
-        outs += [shaped(blocks, count, width, dtype=bf16)] * 2
+            acc_ref[:, span] = dot_tn(grads_ref[...], acts_ref[:, span])
+        for out_index, (first, count, into_row, axis) in enumerate(plan):
+            at = place_at[axis]
+            for side_at, side in ((0, 1 - at), (1, at)):
+                out_ref = refs[first_out + 2 * out_index + side_at]
+                blocks, lanes = out_ref.shape[0], out_ref.shape[2]
+                lane_blocks = width // lanes
+                for block in range(blocks):
+                    lane, rest = divmod(block, blocks // lane_blocks)
+                    if axis == 0:
+                        line = rest * 4 + side * 2 + core
+                    else:
+                        line = (rest // 2) * 8 + side * 4 + (rest % 2) * 2 + core
+                    start = pl.multiple_of(line * chunk + first, 8)
+                    out_ref[block, pl.ds(into_row, count), :] = acc_ref[
+                        pl.ds(start, count), pl.ds(lane * lanes, lanes)
+                    ].astype(bf16)
+
+
+def term(place, weights, width):
+    arrays, layout, scratch, rows_out = [], [], [], [0, 0]
+    for grads, acts in weights:
+        pieces, shapes = [], []
+        for target, value in ((0, grads), (1, acts)):
+            row_to = 0
+            for group in value:
+                col_to = 0
+                for array, column, cols in group:
+                    pieces.append((target, len(arrays), column, cols, row_to, col_to))
+                    arrays.append(array)
+                    col_to += cols
+                row_to += group[0][0].shape[0]
+            shapes.append((row_to, col_to))
+        (depth, columns), (_, rows) = shapes
+        chunk = columns // (16 * width // rows)
+        first = chunk // 16 * 8
+        plan = [(0, first, rows_out[0], 0), (first, chunk - first, rows_out[1], 1)]
+        rows_out = [rows_out[0] + first, rows_out[1] + chunk - first]
+        layout.append((pieces, chunk, plan))
+        scratch += [
+            pltpu.VMEM((depth, columns), bf16),
+            pltpu.VMEM((depth, rows), bf16),
+            pltpu.VMEM((columns, rows), f32),
+        ]
+    outs = [shaped(4, rows_out[axis], width, dtype=bf16) for axis in (0, 0, 1, 1)]
     return pl.pallas_call(
-        functools.partial(term_kernel, pairs=len(pairs), chunk=chunk, plan=plan),
+        functools.partial(term_kernel, layout=layout, outputs=2),
         out_shape=outs,
-        in_specs=[pl.BlockSpec(memory_space=pltpu.SMEM)] + [VMEM_SPEC] * len(flat),
+        in_specs=[pl.BlockSpec(memory_space=pltpu.SMEM)] + [VMEM_SPEC] * len(arrays),
         out_specs=[VMEM_SPEC] * len(outs),
-        scratch_shapes=[pltpu.VMEM((columns, rows), f32)],
+        scratch_shapes=scratch,
         compiler_params=params(),
+        cost_estimate=COST,
         name="term",
-    )(place, *flat)
+    )(place, *arrays)
 
 
 def running_ends(pieces):
@@ -539,7 +589,14 @@
     else:
         block_at = seq_at
     place = jnp.stack(
-        [row_at, seq_at & 3, core, (seq_at // 2) % 2, (seq_at // 4) % 2]
+        [
+            row_at,
+            seq_at & 3,
+            core,
+            (seq_at // 2) % 2,
+            (seq_at // 4) % 2,
+            (seq_at // 4) % 2 * 2 + core,
+        ]
     ).astype(jnp.int32)
 
     def flip(value, bit):
@@ -570,6 +627,10 @@
 
     def after(value, *earlier):
         return lax.optimization_barrier((value, *earlier))[0]
+
+    def fetch_first(weight, column, cols, bit, *earlier):
+        row = after(((seq_at // bit) % 2 * 2 + core) * (half // 4), *earlier)
+        return cross(lax.dynamic_slice(weight, (row, column), (half // 4, cols)))
 
     def gather_rows(value):
         if rows == 2:
@@ -601,67 +662,58 @@
     selector_rows = jax.vmap(lambda own: one_hot(crop_of(slot_index, own), crops))(ends_rows)
 
     columns = ada_weight.shape[1]
+    quarter = half // 4
+    if fast:
+        k_first = fetch_first(qkv_weight, D, D, 2, seq_at)
+        v_first = fetch_first(qkv_weight, 2 * D, D, 4, k_first)
+        k_second = flip(k_first, 2)
+        cond_rows = after(cond_rows, k_first)
     mod_rows = jnp.dot(cond_rows, ada_weight, preferred_element_type=f32)
     mod_rows = mod_rows.reshape(rows, crops, columns)
     if rows == 2:
         mod_slots = jnp.einsum("rsc,rcm->rsm", selector_rows, mod_rows, precision=highest)
+        if fast:
+            mod_slots = after(mod_slots, v_first, k_second)
         arrived = cross(mod_slots[1])
         mod_attn = pick(mod_slots[0], arrived)
         mod_mlp = pick(arrived, mod_slots[0])
+        norm_mods = (mod_slots[0], arrived)
     else:
         mine = lax.all_to_all(mod_rows, "fsdp", 0, 0)
         mine = jnp.transpose(mine, (1, 0, 2)).reshape(crops, rows * columns)
         mine = jnp.dot(selector, mine, precision=highest)
         mod_attn, mod_mlp = mine[:, : 3 * D], mine[:, 3 * D :]
+        norm_mods = (mod_attn, mod_attn)
     mod_attn, mod_mlp = tiled(mod_attn), tiled(mod_mlp)
-    shift_attn, scale_attn, gate_attn = (mod_attn[:, i * D : (i + 1) * D] for i in range(3))
+    ignored, scale_attn, gate_attn = (mod_attn[:, i * D : (i + 1) * D] for i in range(3))
     shift_mlp, scale_mlp, gate_mlp = (mod_mlp[:, i * D : (i + 1) * D] for i in range(3))
 
     def block(at):
         return lambda i, place: (0, at)
 
     if fast:
-        quarter = half // 4
         chunk = 768
 
-        def fetch(weight, column, cols, *earlier):
-            part = lax.dynamic_slice(weight, ((seq_at & 3) * quarter, column), (quarter, cols))
-            first = cross(after(part, *earlier))
-            second = flip(first, 2)
+        def spread(first, second):
             return (first, flip(first, 1), second, flip(second, 1))
 
         other_part = (1 - row_at) * hidden_part
-        k_pieces = fetch(qkv_weight, D, D, packed)
-        v_pieces = fetch(qkv_weight, 2 * D, D, k_pieces[0], mod_slots)
-        q_pieces = fetch(qkv_weight, 0, D, k_pieces[0], mod_slots)
-        out_pieces = fetch(out_weight, 0, D, v_pieces[0])
-        up_low = fetch(up_weight, other_part, hidden_part // 2, q_pieces[0])
-        up_high = fetch(
-            up_weight, other_part + hidden_part // 2, hidden_part // 2, out_pieces[0]
-        )
+        q_first = fetch_first(qkv_weight, 0, D, 2, arrived)
+        out_first = fetch_first(out_weight, 0, D, 4, q_first)
+        up_first_piece = fetch_first(up_weight, other_part, hidden_part, 2, out_first)
+        v_second, q_second, out_second = flip(v_first, 4), flip(q_first, 2), flip(out_first, 4)
+        k_pieces, v_pieces = spread(k_first, k_second), spread(v_first, v_second)
+        q_pieces, out_pieces = spread(q_first, q_second), spread(out_first, out_second)
         qkv_sources = [(qkv_weight, (half, 3 * D), block(0), None, 0)]
-        for column, pieces in ((0, q_pieces), (D, k_pieces), (2 * D, v_pieces)):
+        for at, column, pieces in ((1, 0, q_pieces), (1, D, k_pieces), (5, 2 * D, v_pieces)):
             qkv_sources += [
-                (piece, (quarter, D), block(0), step, column)
+                (piece, (quarter, D), block(0), (at, step), column)
                 for step, piece in enumerate(pieces)
             ]
         out_sources = [(out_weight, (half, D), block(0), None, 0)]
         out_sources += [
-            (piece, (quarter, D), block(0), step, 0) for step, piece in enumerate(out_pieces)
-        ]
-        chunks = hidden_part // chunk
-        up_sources = [
-            (up_weight, (half, chunk), lambda i, place: (0, place[0] * chunks + i), None, 0)
-        ]
-        up_sources += [
-            (
-                jnp.concatenate([low, high], axis=1),
-                (quarter, chunk),
-                lambda i, place: (0, i),
-                step,
-                0,
-            )
-            for step, (low, high) in enumerate(zip(up_low, up_high))
+            (piece, (quarter, D), block(0), (5, step), 0)
+            for step, piece in enumerate(out_pieces)
         ]
         low_rows = tokens
     else:
@@ -674,14 +726,18 @@
         up_sources = [(up_part, (D, hidden_part), block(0), "all", 0)]
         low_rows = rows * tokens
 
-    tokens_here = to_slots(tokens_in[0])
     kept = jnp.broadcast_to(keep_mask[0].astype(bf16)[:, None], (tokens, 128))
-    normed_in = norm_in(tokens_here, shift_attn, scale_attn)
+    tokens_here = to_slots(jnp.concatenate([tokens_in[0], cotangent[0], kept], axis=1))
+    if fast:
+        tokens_here = after(tokens_here, v_second)
+    normed_in = norm_in(place, tokens_here, *norm_mods)
 
     reach = -(-(PIECE_MAX - 1) // slots)
     paired = reach == 2 and seq % 2 == 0
     if paired:
         below, above = shift(normed_in, 2), shift(normed_in, -2)
+        if fast:
+            above = after(above, q_second)
         passed = flip(jnp.where(core == 0, above, below), 1)
         near = [normed_in, flip(normed_in, 1), below, above, passed]
         near_at = [
@@ -696,8 +752,7 @@
         for distance in range(1, reach + 1):
             near += [shift(normed_in, distance), shift(normed_in, -distance)]
             near_at += [block_at - distance, block_at + distance]
-    late_in = to_slots(after(jnp.concatenate([cotangent[0], kept], axis=1), normed_in))
-    near_at = jnp.stack(near_at)
+    near_at = after(jnp.stack(near_at), normed_in)
     key_slots = near_at[:, None] * slots + jnp.arange(slots, dtype=jnp.int32)[None, :]
     inside = (near_at >= 0) & (near_at < seq)
     key_crop = jnp.where(inside[:, None], crop_of(key_slots, ends), -1)
@@ -714,10 +769,22 @@
     def by_slot(value):
         return value.reshape(tokens // PERIOD, PERIOD, -1)
 
+    if fast:
+        near[-1] = after(near[-1], out_second)
     queries, kv_window = project(place, qkv_sources, near)
-    grad_mlp = by_slot(late_in[:, :D].astype(f32)) * gate_mlp
-    grad_mlp = (grad_mlp * by_slot(late_in[:, D : D + 1].astype(f32))).reshape(tokens, D)
-    grad_mlp_rows = gather_rows(grad_mlp.astype(bf16)).reshape(rows * tokens, D)
+    if fast:
+        up_second_piece = flip(after(up_first_piece, queries), 2)
+    grad_out = by_slot(tokens_here[:, D : 2 * D].astype(f32))
+    keep = by_slot(tokens_here[:, 2 * D : 2 * D + 1].astype(f32))
+    grad_mlp = grad_out * gate_mlp * keep
+    grad_mlp = grad_mlp.reshape(tokens, D).astype(bf16)
+
+    def row_list(value):
+        if rows == 2:
+            return [value, cross(value)]
+        return [lax.all_gather(value, "fsdp", axis=0, tiled=True)]
+
+    grad_mlps = row_list(grad_mlp)
     queries = after(queries, grad_mlp)
     merged, attn_proj, mid_state, normed_mid = attend(
         place,
@@ -732,7 +799,20 @@
         scale_mlp,
     )
 
-    mid_rows = gather_rows(normed_mid).reshape(rows * tokens, D)
+    mids = row_list(normed_mid)
+    if fast:
+        up_pieces = spread(up_first_piece, after(up_second_piece, merged))
+        chunks = hidden_part // chunk
+        up_sources = [
+            (up_weight, (half, chunk), lambda i, place: (0, place[0] * chunks + i), None, 0)
+        ]
+        up_sources += [
+            (piece, (quarter, chunk), lambda i, place: (0, i), (1, step), 0)
+            for step, piece in enumerate(up_pieces)
+        ]
+        grad_mlps_side = [flip(value, 1) for value in grad_mlps]
+        mids_side = [flip(value, 1) for value in mids]
+        mids[1] = after(mids[1], grad_mlps_side)
     channels = jnp.einsum("rsc,rcg->rsg", selector_rows, group_rows, precision=highest)
     channels = lax.dynamic_slice_in_dim(
         jnp.repeat(tiled(channels), CHAN_GROUP, axis=2), row_at * hidden_part, hidden_part, 2
@@ -740,8 +820,8 @@
     hidden_act, grad_pre, grad_own, grad_low, out_own, out_low = feed(
         place,
         up_sources,
-        mid_rows,
-        grad_mlp_rows,
+        mids,
+        grad_mlps,
         channels,
         down_weight,
         chunk,
@@ -759,99 +839,148 @@
     grad_own, grad_other = own_sum(grad_own, grad_low)
     out_own, out_other = own_sum(out_own, out_low)
     mlp_out = out_own + out_other.astype(f32)
-    kept_out = by_slot(mlp_out * late_in[:, D : D + 1].astype(f32))
+    kept_out = by_slot(mlp_out) * keep
     block_out = (by_slot(mid_state) + gate_mlp * kept_out).reshape(tokens, D)
     block_out = block_out.astype(bf16)
-    gate_mlp_sum = jnp.sum(by_slot(late_in[:, :D].astype(f32)) * kept_out, axis=0)
-
-    if fast:
-
-        def pooled(grads, acts):
-            return [(grads, acts), (flip(grads, 1), flip(acts, 1))]
-
-        down_pairs = pooled(grad_mlp_rows, hidden_act)
-        up_pairs = pooled(grad_pre, mid_rows)
-        down_sent, down_kept = term(place, down_pairs, [(0, D // seq, 0)], 4, hidden_part)
-        grad_own = after(grad_own, down_sent)
-
-    grad_mid, grad_attn, grad_heads, mid_sums = mid_back(
+    gate_mlp_sum = jnp.sum(grad_out * kept_out, axis=0)
+
+    if fast:
+
+        def columns_of(array, column=0, cols=None):
+            return [(array, column, array.shape[1] if cols is None else cols)]
+
+        act_side, pre_side = flip(hidden_act, 1), flip(grad_pre, 1)
+        down_parts = term(
+            place,
+            [
+                (
+                    [columns_of(value) for value in (*grad_mlps, *grad_mlps_side)],
+                    [columns_of(value) for value in (hidden_act, act_side)],
+                )
+            ],
+            hidden_part,
+        )
+        grad_own = after(grad_own, down_parts)
+        down_first = (flip(down_parts[0], 2), flip(down_parts[2], 4))
+
+    grad_mid, own_pack, pack, grad_heads, mid_sums = mid_back(
         place,
         out_sources,
         grad_own,
         grad_other,
         mid_state,
         attn_proj,
-        late_in,
+        tokens_here,
         scale_mlp,
         gate_attn,
         head_slots,
-    )
-    if fast:
-
-        def own_half(value):
-            return pick(value[:, :half], value[:, half:])
-
-        def other_half(value):
-            return pick(value[:, half:], value[:, :half])
-
-        crossing = jnp.concatenate(
-            [other_half(merged), other_half(normed_in), grad_attn], axis=1
+        merged,
+        normed_in,
+    )
+    if fast:
+
+        crossed = cross(pack)
+        own_side = flip(own_pack, 1)
+        grad_heads = after(grad_heads, pack, own_side, pre_side, mids_side)
+    grad_queries, *parts = attend_back(queries, kv_window, bias_t, grad_heads)
+    if fast:
+        parts[4], down_first = lax.optimization_barrier((parts[4], down_first))
+    if paired:
+        handed = flip(parts[4], 1)
+        near_side = flip(parts[1], 1)
+        zero = jnp.zeros((), bf16)
+        down_part = parts[2] + jnp.where(core == 1, handed, zero)
+        up_side = parts[3] + jnp.where(core == 0, handed, zero)
+        from_above, from_below = shift(down_part, -2), shift(up_side, 2)
+        arrivals = [near_side, from_above, from_below]
+    else:
+        arrivals = []
+        for distance in range(1, reach + 1):
+            arrivals += [
+                shift(parts[2 * distance - 1], -distance),
+                shift(parts[2 * distance], distance),
+            ]
+    if fast:
+        q_crossed = cross(grad_queries)
+        q_side = flip(grad_queries, 1)
+        crossed_side = flip(crossed, 1)
+        down_first, ignored = lax.optimization_barrier((down_first, (down_part, up_side)))
+
+        def reduced(kept, arrived_part):
+            value = (kept.astype(f32) + arrived_part.astype(f32)).astype(bf16)
+            return value.reshape(2, value.shape[0] // 2, *value.shape[1:])
+
+        def second_step(values):
+            steps = []
+            for value, bit in zip(values, (4, 2)):
+                at = (seq_at // bit) % 2
+                send = lax.dynamic_index_in_dim(value, 1 - at, 1, keepdims=False)
+                keep_part = lax.dynamic_index_in_dim(value, at, 1, keepdims=False)
+                steps.append((send, keep_part, bit))
+            return steps
+
+        def third_step(kept_parts, arrived_parts):
+            value = jnp.concatenate(
+                [
+                    (kept_part.astype(f32) + arrived_part.astype(f32)).astype(bf16)
+                    for kept_part, arrived_part in zip(kept_parts, arrived_parts)
+                ],
+                axis=1,
+            )
+            at = (seq_at // 8) % 2
+            send = lax.dynamic_index_in_dim(value, 1 - at, 0, keepdims=False)
+            return send, lax.dynamic_index_in_dim(value, at, 0, keepdims=False)
+
+        down_values = [reduced(down_parts[1], down_first[0]), reduced(down_parts[3], down_first[1])]
+        down_steps = second_step(down_values)
+        down_second = [flip(send, bit) for send, ignored, bit in down_steps]
+        up_parts = term(
+            place,
+            [
+                (
+                    [columns_of(value) for value in (grad_pre, pre_side)],
+                    [columns_of(value) for value in (*mids, *mids_side)],
+                ),
+                (
+                    [columns_of(value, D, D) for value in (own_pack, crossed, own_side, crossed_side)],
+                    [
+                        columns_of(value, 0, half)
+                        for value in (own_pack, crossed, own_side, crossed_side)
+                    ],
+                ),
+            ],
+            half,
         )
-        crossed = cross(crossing)
-        grad_heads = after(grad_heads, crossing, up_pairs)
-    grad_queries, parts = attend_back(queries, kv_window, bias_t, grad_heads)
+        up_first = (flip(up_parts[0], 2), flip(up_parts[2], 4))
+        arrivals[0] = after(arrivals[0], up_parts, q_crossed, q_side, out_other)
     grad_kv = parts[0].astype(f32)
-    if paired:
-        handed = flip(parts[4], 1).astype(f32)
-        down_part = (parts[2].astype(f32) + jnp.where(core == 1, handed, 0.0)).astype(bf16)
-        up_side = (parts[3].astype(f32) + jnp.where(core == 0, handed, 0.0)).astype(bf16)
-        grad_kv = grad_kv + flip(parts[1], 1).astype(f32)
-        if fast:
-            block_out, ignored, ignored = lax.optimization_barrier(
-                (block_out, down_part, up_side)
-            )
-            up_ready, ignored, ignored = lax.optimization_barrier(
-                (up_pairs, down_part, up_side)
-            )
-            up_sent, up_kept = term(place, up_ready, [(0, hidden // seq, 0)], 4, half)
-            grad_kv = after(grad_kv, up_sent)
-        grad_kv = grad_kv + shift(down_part, -2).astype(f32) + shift(up_side, 2).astype(f32)
-    else:
-        for distance in range(1, reach + 1):
-            grad_kv = grad_kv + shift(parts[2 * distance - 1], -distance).astype(f32)
-            grad_kv = grad_kv + shift(parts[2 * distance], distance).astype(f32)
+    for arrival in arrivals:
+        grad_kv = grad_kv + arrival.astype(f32)
     grad_kv = grad_kv.astype(bf16)
-    block_out = from_slots(block_out, bf16)
+    if fast:
+        grad_queries, down_second = lax.optimization_barrier((grad_queries, down_second))
     input_grad, in_sums = in_back(
         place, qkv_sources, grad_queries, grad_kv, tokens_here, scale_attn, grad_mid
     )
-    input_grad = from_slots(input_grad, f32)
+
+    if fast:
+        kv_crossed = cross(grad_kv)
+        down_second = after(down_second, in_sums)
+        down_send, down_keep = third_step([step[1] for step in down_steps], down_second)
+        down_last = flip(down_send, 8)
+        kv_crossed, in_sums, down_last = lax.optimization_barrier(
+            (kv_crossed, in_sums, down_last)
+        )
+        up_first, grad_kv, q_crossed_late, ignored = lax.optimization_barrier(
+            (up_first, grad_kv, q_crossed, kv_crossed)
+        )
 
     def by_crop(sums):
         sums = sums.reshape(-1, repeats, slots, D)
         sums = jnp.sum(sums, axis=1) if repeats > 1 else sums[:, 0]
         return jnp.einsum("sc,nsd->cnd", selector, sums, precision=highest).astype(bf16)
 
-    def all_sum(value):
-        if not fast:
-            return lax.psum(value, "seq")
-        for bit in (1, 2, 4, 8):
-            value = (value.astype(f32) + flip(value, bit).astype(f32)).astype(bf16)
-        return value
-
     mod_grads = jnp.concatenate([in_sums, mid_sums, gate_mlp_sum[None]], axis=0)
-    mod_grads = all_sum(by_crop(mod_grads).reshape(crops, 6 * D))
-    if rows == 2:
-        own = pick(mod_grads[:, : 3 * D], mod_grads[:, 3 * D :])
-        other = cross(pick(mod_grads[:, 3 * D :], mod_grads[:, : 3 * D]))
-        mod_grads = jnp.concatenate([own, other], axis=0)
-    else:
-        split = jnp.transpose(mod_grads.reshape(crops, rows, columns), (1, 0, 2))
-        mod_grads = lax.all_to_all(split, "fsdp", 0, 0).reshape(rows * crops, columns)
-    ada_grad = lax.dot_general(
-        cond_rows, mod_grads, (((0,), (0,)), ((), ())), preferred_element_type=f32
-    )
-
     if not fast:
 
         def product(acts, grads):
@@ -865,30 +994,63 @@
 
         grad_qkv = jnp.concatenate([grad_queries, grad_kv], axis=1)
         qkv_grad = both(product(normed_in, grad_qkv))
-        out_grad = both(product(merged, grad_attn))
-        up_cols = lax.all_to_all(product(mid_rows, grad_pre), "fsdp", 0, 1, tiled=True)
+        out_grad = both(product(merged, own_pack[:, D:]))
+        up_cols = lax.all_to_all(product(mids[0], grad_pre), "fsdp", 0, 1, tiled=True)
         up_grad = lax.psum_scatter(up_cols, "seq", scatter_dimension=1, tiled=True).astype(f32)
-        down_cols = product(hidden_act, grad_mlp_rows)
+        down_cols = product(hidden_act, grad_mlps[0])
         down_grad = lax.psum_scatter(
             down_cols, "seq", scatter_dimension=1, tiled=True
         ).astype(f32)
     else:
 
-        def scatter(sent, kept, bits):
-            value = kept.astype(f32) + flip(sent, bits[0]).astype(f32)
-            shape = value.shape[1:]
-            value = value.reshape(2, 2, *shape).astype(bf16)
-            at = (seq_at // bits[2]) % 2
-            send = lax.dynamic_index_in_dim(value, 1 - at, 1, keepdims=False)
-            keep = lax.dynamic_index_in_dim(value, at, 1, keepdims=False)
-            value = (keep.astype(f32) + flip(send, bits[2]).astype(f32)).astype(bf16)
-            at = (seq_at // bits[1]) % 2
-            send = lax.dynamic_index_in_dim(value, 1 - at, 0, keepdims=False)
-            keep = lax.dynamic_index_in_dim(value, at, 0, keepdims=False)
-            return keep.astype(f32) + flip(send, bits[1]).astype(f32)
-
-        down_grad = jnp.transpose(scatter(down_sent, down_kept, (2, 8, 4)))
-        up_mine = scatter(up_sent, up_kept, (2, 8, 4)).astype(bf16)
+        kv_side = flip(grad_kv, 1)
+        kv_crossed_side, q_crossed_side = flip(kv_crossed, 1), flip(q_crossed_late, 1)
+
+        def joined(first_part, second_part):
+            return columns_of(first_part) + columns_of(second_part)
+
+        up_steps = second_step([reduced(up_parts[1], up_first[0]), reduced(up_parts[3], up_first[1])])
+        up_second = [flip(send, bit) for send, ignored, bit in up_steps]
+        qkv_parts = term(
+            place,
+            [
+                (
+                    [
+                        joined(grad_queries, grad_kv),
+                        joined(q_crossed, kv_crossed),
+                        joined(q_side, kv_side),
+                        joined(q_crossed_side, kv_crossed_side),
+                    ],
+                    [
+                        columns_of(value, half, half)
+                        for value in (own_pack, crossed, own_side, crossed_side)
+                    ],
+                )
+            ],
+            half,
+        )
+        qkv_first = (flip(qkv_parts[0], 2), flip(qkv_parts[2], 4))
+        qkv_steps = second_step(
+            [reduced(qkv_parts[1], qkv_first[0]), reduced(qkv_parts[3], qkv_first[1])]
+        )
+        qkv_second = [flip(send, bit) for send, ignored, bit in qkv_steps]
+        up_second, block_out, input_grad, mod_grads, ignored = lax.optimization_barrier(
+            (up_second, block_out, input_grad, mod_grads, qkv_parts)
+        )
+        up_send, up_keep = third_step([step[1] for step in up_steps], up_second)
+        qkv_send, qkv_keep = third_step([step[1] for step in qkv_steps], qkv_second)
+        up_last, ignored = lax.optimization_barrier(
+            (flip(up_send, 8), [send for send, ignored, ignored in qkv_steps])
+        )
+        down_grad = jnp.transpose(down_keep.astype(f32) + down_last.astype(f32))
+        qkv_grad = jnp.transpose(qkv_keep.astype(f32) + flip(qkv_send, 8).astype(f32))
+        mixed = up_keep.astype(f32) + up_last.astype(f32)
+        up_rows, out_rows = hidden // seq, D // seq
+        up_low, out_low = up_rows // 16 * 8, out_rows // 16 * 8
+        parted = up_low + out_low
+        rest = parted + up_rows - up_low
+        up_mine = jnp.concatenate([mixed[:up_low], mixed[parted:rest]], axis=0).astype(bf16)
+        out_grad = jnp.transpose(jnp.concatenate([mixed[up_low:parted], mixed[rest:]], axis=0))
         pairs = []
         for place_seq in range(seq):
             for place_row in range(2):
@@ -896,45 +1058,35 @@
                 target_seq = (place_seq & 7) | (place_row * 8)
                 pairs.append((place_seq * 2 + place_row, target_seq * 2 + high))
         up_grad = jnp.transpose(lax.ppermute(up_mine, ("seq", "fsdp"), pairs)).astype(f32)
-
-        out_acts = jnp.concatenate([own_half(merged), crossed[:, :half]], axis=0)
-        out_grads = jnp.concatenate([grad_attn, crossed[:, D:]], axis=0)
-        out_sent, out_kept = term(
-            place,
-            pooled(out_grads, out_acts),
-            [(0, D // seq, 0)],
-            4,
-            half,
+    mod_grads = by_crop(mod_grads).reshape(crops, 6 * D)
+    if fast:
+        share = columns // 2
+        quarters = [mod_grads[:, i * share : (i + 1) * share] for i in range(4)]
+        first_core = core == 0
+        kept_sum = [jnp.where(first_core, quarters[i], quarters[i + 1]) for i in (0, 2)]
+        sent_sum = [jnp.where(first_core, quarters[i + 1], quarters[i]) for i in (0, 2)]
+        kept_sum, sent_sum = (jnp.stack(value) for value in (kept_sum, sent_sum))
+        mod_grads = (kept_sum.astype(f32) + flip(sent_sum, 1).astype(f32)).astype(bf16)
+        for bit, ahead in ((2, [send for send, ignored, ignored in qkv_steps]), (4, qkv_send), (8, ())):
+            mod_grads = (mod_grads.astype(f32) + flip(mod_grads, bit).astype(f32)).astype(bf16)
+            mod_grads = after(mod_grads, ahead)
+        own = pick(mod_grads[0], mod_grads[1])
+        other = cross(pick(mod_grads[1], mod_grads[0]))
+        own = jnp.concatenate([own, other], axis=0)
+        other = flip(own, 1)
+        mod_grads = jnp.concatenate(
+            [jnp.where(first_core, own, other), jnp.where(first_core, other, own)], axis=1
         )
-        out_grad = jnp.transpose(scatter(out_sent, out_kept, (2, 8, 4)))
-
-        q_crossed, kv_crossed = cross(grad_queries), cross(grad_kv)
-        qkv_grads = jnp.concatenate(
-            [
-                jnp.concatenate([grad_queries, q_crossed], axis=0),
-                jnp.concatenate([grad_kv, kv_crossed], axis=0),
-            ],
-            axis=1,
-        )
-        qkv_acts = jnp.concatenate([own_half(normed_in), crossed[:, half:D]], axis=0)
-        first = 3 * D // seq // 16 * 8
-        sent_a, kept_a, sent_b, kept_b = term(
-            place,
-            pooled(qkv_grads, qkv_acts),
-            [(0, first, 0), (first, 3 * D // seq - first, 1)],
-            4,
-            half,
-        )
-        qkv_grad = jnp.transpose(
-            jnp.concatenate(
-                [
-                    scatter(sent_a, kept_a, (2, 8, 4)),
-                    scatter(sent_b, kept_b, (4, 8, 2)),
-                ],
-                axis=0,
-            )
-        )
-
+    else:
+        mod_grads = lax.psum(mod_grads, "seq")
+        split = jnp.transpose(mod_grads.reshape(crops, rows, columns), (1, 0, 2))
+        mod_grads = lax.all_to_all(split, "fsdp", 0, 0).reshape(rows * crops, columns)
+    ada_grad = lax.dot_general(
+        cond_rows, mod_grads, (((0,), (0,)), ((), ())), preferred_element_type=f32
+    )
+
+    both_out = from_slots(jnp.concatenate([block_out, input_grad], axis=1), f32)
+    block_out, input_grad = both_out[:, :D].astype(bf16), both_out[:, D:]
     return (
         block_out[None],
         input_grad[None],

time: 419 us -> 346 us (0.83)
  the two profiles are of different devices: /device:TPU:2 before, /device:TPU:0 now
where the time goes in v3:
time: 346 us; the launch traced here: 341 us
  waiting for transfers between devices  108 us (31%)
  Pallas kernels  92.1 us (27%)
  starting transfers between devices  73.7 us (21%)
  other arithmetic  27.3 us (8%)
  local copies, waits for them, and re-layouts  20.9 us (6%)
  matrix products  16.4 us (5%)
    ppermute x51, waiting for transfers between devices, flip(): return lax.ppermute(value, 'seq', [(i, i ^ bit) for i in range(seq)])  76.2 us
    pallas_call x4, Pallas kernels, staged_call(): pl.pallas_call(functools.partial(kernel, parts=parts), out_shape=out_shap...  36.4 us
    ppermute x51, starting transfers between devices, flip(): return lax.ppermute(value, 'seq', [(i, i ^ bit) for i in range(seq)])  34.6 us
    ppermute x15, waiting for transfers between devices, cross(): return lax.ppermute(value, 'fsdp', [(0, 1), (1, 0)])  32.2 us
    pallas_call x3, Pallas kernels, term(): pl.pallas_call(functools.partial(term_kernel, layout=layout, outputs=2),...  25.8 us
    ppermute x15, starting transfers between devices, cross(): return lax.ppermute(value, 'fsdp', [(0, 1), (1, 0)])  16.2 us
    pallas_call x1, Pallas kernels, feed(): pl.pallas_call(functools.partial(feed_kernel, parts=parts, arrays=len(mid...  14.7 us
    pallas_call x1, Pallas kernels, attend_back(): pl.pallas_call(attend_back_kernel, out_shape=outs, in_specs=[VMEM_SPEC] *...  13.1 us
  transfers between devices with their start and end apart: 73, of which 23 were waited for; matrix products, arithmetic and copies ran while one was open for 16% of the time, Pallas kernels for 23%

profile of v3, /device:TPU:0, one launch (start us, length us, event | category | flops | bytes accessed | tf_op | source)
XLA Modules:
  0.0 341.1 jit_solution(7165748495098742132)
XLA Ops:
  1.8 3.0 collective-permute-start.1
  7.8 5.9 %all-to-all-start = ((bf16[16,8,2432]{2,1,0:T(8,128)(2,1)}), bf16[16,8,2432]{2,1,0:T(8,128)(2,1)S(1)}, u32[]{:S(2)}, u32[]{:S(2)}) async-start(bf16[16,8,2432]{2,1,0:T(8,128)(2,1)} %fusion), calls=%async_computation | async-start | bytes 1245184 | tf_op jit(solution)/shard_map/all_to_all | solution.py:620
  15.4 2.7 collective-permute-done
  22.3 4.5 %fusion.66 = f32[32,3456]{1,0:T(8,128)S(1)} fusion(bf16[32,1152]{1,0:T(8,128)(2,1)S(1)} %bitcast.208, bf16[1152,3456]{1,0:T(8,128)(2,1)} %param.25), kind=kOutput, calls=%fused_computation.179 | convolution fusion | flops 254803968 | bytes 8478720 | tf_op jit(solution)/shard_map/dot_general | solution.py:671
  29.2 3.0 collective-permute-done.3.refs_7_
  40.1 8.4 %collective-permute-done.5.refs_1_ = bf16[144,1152]{1,0:T(8,128)(2,1)S(1)} collective-permute-done((bf16[144,1152]{1,0:T(8,128)(2,1)S(1)}, bf16[144,1152]{1,0:T(8,128)(2,1)S(1)}, u32[]{:S(2)}, u32[]{:S(2)}) %collective-permute-start.5) | collective-permute-done | bytes 331808 | tf_op jit(solution)/shard_map/ppermute | solution.py:606
  56.5 5.4 %collective-permute-start.18 = (bf16[128,1152]{1,0:T(8,128)(2,1)}, bf16[128,1152]{1,0:T(8,128)(2,1)}, u32[]{:S(2)}, u32[]{:S(2)}) collective-permute-start(bf16[128,1152]{1,0:T(8,128)(2,1)} %norm_in.1.refs_13_.refs_14_), channel_id=1, source_target_pairs={{0,4},{2,6},{4,12},{6,14},{12,8},{14,10},{8,16},{10,18},{16,20},{1... | collective-permute-start | bytes 884744 | tf_op jit(solution)/shard_map/ppermute | solution.py:612
  69.1 7.1 %collective-permute-done.21.refs_3_ = bf16[144,1152]{1,0:T(8,128)(2,1)} collective-permute-done((bf16[144,1152]{1,0:T(8,128)(2,1)}, bf16[144,1152]{1,0:T(8,128)(2,1)}, u32[]{:S(2)}, u32[]{:S(2)}) %collective-permute-start.21) | collective-permute-done | bytes 331808 | tf_op jit(solution)/shard_map/ppermute | solution.py:603
  78.7 11.1 %project.1 = (bf16[128,1152]{1,0:T(8,128)(2,1)}, bf16[640,2304]{1,0:T(8,128)(2,1)}) custom-call(s32[6]{0:T(128)} %stack.72.place_ref, bf16[576,3456]{1,0:T(8,128)(2,1)} %refs_0_.9, bf16[144,1152]{1,0:T(8,128)(2,1)} %copy-done.15, bf16[144,1152]{1,0:T(8,128)(2,1)} %copy-done.20, bf16[144,1152]{1,0:T(8,128)(2,1)} %copy-done.16, bf16[144,1152]{1,0:T(8,128)(2,1)} %copy-done.21, ...), custom_call_target="tpu_custom_call" | custom-call | flops 1 | bytes 1 | tf_op jit(solution)/shard_map/project/pallas_call | solution.py:73
  93.9 10.6 %attend.1 = (bf16[128,1152]{1,0:T(8,128)(2,1)}, f32[128,1152]{1,0:T(8,128)}, f32[128,1152]{1,0:T(8,128)}, bf16[128,1152]{1,0:T(8,128)(2,1)}) custom-call(s32[6]{0:T(128)} %stack.72.place_ref, bf16[576,1152]{1,0:T(8,128)(2,1)} %refs_0_.8, bf16[144,1152]{1,0:T(8,128)(2,1)} %collective-permute-done.6.refs_1_, bf16[144,1152]{1,0:T(8,128)(2,1)} %copy-done.22, ...), custom_call_target="tpu_custom_call" | custom-call | flops 1 | bytes 1 | tf_op jit(solution)/shard_map/attend/pallas_call | solution.py:73
  110.1 7.6 %collective-permute-done.26.refs_6_.refs_3_ = bf16[128,1152]{1,0:T(8,128)(2,1)S(1)} collective-permute-done((bf16[128,1152]{1,0:T(8,128)(2,1)S(1)}, bf16[128,1152]{1,0:T(8,128)(2,1)S(1)}, u32[]{:S(2)}, u32[]{:S(2)}) %collective-permute-start.26) | collective-permute-done | bytes 294944 | tf_op jit(solution)/shard_map/ppermute | solution.py:606
  118.4 14.7 %feed.1 = (bf16[256,2304]{1,0:T(8,128)(2,1)}, bf16[256,2304]{1,0:T(8,128)(2,1)}, f32[128,1152]{1,0:T(8,128)}, bf16[128,1152]{1,0:T(8,128)(2,1)}, f32[128,1152]{1,0:T(8,128)}, /*index=5*/bf16[128,1152]{1,0:T(8,128)(2,1)}) custom-call(s32[6]{0:T(128)} %stack.72.place_ref, bf16[576,4608]{1,0:T(8,128)(2,1)} %refs_0_.7, ...), custom_call_target="tpu_custom_call" | custom-call | flops 1 | bytes 1 | tf_op jit(solution)/shard_map/feed/pallas_call | solution.py:333
  137.3 7.7 %term.3 = (bf16[4,32,2304]{2,1,0:T(8,128)(2,1)}, bf16[4,32,2304]{2,1,0:T(8,128)(2,1)}, bf16[4,40,2304]{2,1,0:T(8,128)(2,1)}, bf16[4,40,2304]{2,1,0:T(8,128)(2,1)}) custom-call(s32[6]{0:T(128)} %stack.72.place_ref, bf16[128,1152]{1,0:T(8,128)(2,1)} %copy-done.8, bf16[128,1152]{1,0:T(8,128)(2,1)} %copy-done.31, bf16[128,1152]{1,0:T(8,128)(2,1)} %copy-done.63, ...), custom_call_target="tpu_custom_call" | custom-call | flops 1 | bytes 1 | tf_op jit(solution)/shard_map/term/pallas_call | solution.py:524
  146.0 6.2 %mid_back.1 = (f32[128,1152]{1,0:T(8,128)}, bf16[128,2304]{1,0:T(8,128)(2,1)}, bf16[128,2304]{1,0:T(8,128)(2,1)}, bf16[128,1152]{1,0:T(8,128)(2,1)}, f32[3,16,1152]{2,1,0:T(8,128)}) custom-call(s32[6]{0:T(128)} %stack.72.place_ref, bf16[576,1152]{1,0:T(8,128)(2,1)} %refs_0_.8, bf16[144,1152]{1,0:T(8,128)(2,1)} %collective-permute-done.6.refs_1_, ...), custom_call_target="tpu_custom_call" | custom-call | flops 1 | bytes 1 | tf_op jit(solution)/shard_map/mid_back/pallas_call | solution.py:73
  155.9 13.1 %attend_back.1 = (bf16[128,1152]{1,0:T(8,128)(2,1)}, bf16[128,2304]{1,0:T(8,128)(2,1)}, bf16[128,2304]{1,0:T(8,128)(2,1)}, bf16[128,2304]{1,0:T(8,128)(2,1)}, bf...) custom-call(bf16[128,1152]{1,0:T(8,128)(2,1)} %get-tuple-element.99.refs_5_.q_ref, ...), custom_call_target="tpu_custom_call" | custom-call | flops 1 | bytes 1 | tf_op jit(solution)/shard_map/attend_back/pallas_call | solution.py:265
  176.6 3.3 collective-permute-done.43
  181.2 4.6 %collective-permute-done.41.refs_2_ = bf16[128,1152]{1,0:T(8,128)(2,1)S(1)} collective-permute-done((bf16[128,1152]{1,0:T(8,128)(2,1)}, bf16[128,1152]{1,0:T(8,128)(2,1)S(1)}, u32[]{:S(2)}, u32[]{:S(2)}) %collective-permute-start.41) | collective-permute-done | bytes 294944 | tf_op jit(solution)/shard_map/ppermute | solution.py:606
  185.9 4.2 %collective-permute-start.48 = (bf16[128,2304]{1,0:T(8,128)(2,1)}, bf16[128,2304]{1,0:T(8,128)(2,1)}, u32[]{:S(2)}, u32[]{:S(2)}) collective-permute-start(bf16[128,2304]{1,0:T(8,128)(2,1)} %get-tuple-element.172), channel_id=1, source_target_pairs={{0,4},{2,6},{4,12},{6,14},{12,8},{14,10},{8,16},{10,18},{16,20},{1... | collective-permute-start | bytes 1769480 | tf_op jit(solution)/shard_map/ppermute | solution.py:612
  192.6 10.6 %term.4 = (bf16[4,176,576]{2,1,0:T(8,128)(2,1)}, bf16[4,176,576]{2,1,0:T(8,128)(2,1)}, bf16[4,184,576]{2,1,0:T(8,128)(2,1)}, bf16[4,184,576]{2,1,0:T(8,128)(2,1)}) custom-call(s32[6]{0:T(128)} %stack.72.place_ref, bf16[256,2304]{1,0:T(8,128)(2,1)} %get-tuple-element.106.refs_0_, bf16[256,2304]{1,0:T(8,128)(2,1)} %copy-done.25, ...), custom_call_target="tpu_custom_call" | custom-call | flops 1 | bytes 1 | tf_op jit(solution)/shard_map/term/pallas_call | solution.py:524
  204.6 6.8 %collective-permute-start.38 = (bf16[4,176,576]{2,1,0:T(8,128)(2,1)}, bf16[4,176,576]{2,1,0:T(8,128)(2,1)}, u32[]{:S(2)}, u32[]{:S(2)}) collective-permute-start(bf16[4,176,576]{2,1,0:T(8,128)(2,1)} %get-tuple-element.120), channel_id=1, source_target_pairs={{0,4},{2,6},{4,0},{6,2},{8,12},{10,14},{12,8},{14,10},{16,20},{18,... | collective-permute-start | bytes 2433032 | tf_op jit(solution)/shard_map/ppermute | solution.py:603
  214.1 8.5 %in_back.1 = (bf16[128,1152]{1,0:T(8,128)(2,1)}, f32[2,16,1152]{2,1,0:T(8,128)}) custom-call(s32[6]{0:T(128)} %stack.72.place_ref, bf16[576,3456]{1,0:T(8,128)(2,1)} %refs_0_.9, bf16[144,1152]{1,0:T(8,128)(2,1)} %copy-done.15, bf16[144,1152]{1,0:T(8,128)(2,1)} %copy-done.20, bf16[144,1152]{1,0:T(8,128)(2,1)} %copy-done.16, bf16[144,1152]{1,0:T(8,128)(2,1)} %copy-done.21, ...), custom_call_target="tpu_custom_call" | custom-call | flops 1 | bytes 1 | tf_op jit(solution)/shard_map/in_back/pallas_call | solution.py:73
  228.8 10.8 %collective-permute-done.52 = bf16[72,2304]{1,0:T(8,128)(2,1)} collective-permute-done((bf16[72,2304]{1,0:T(8,128)(2,1)}, bf16[72,2304]{1,0:T(8,128)(2,1)}, u32[]{:S(2)}, u32[]{:S(2)}) %collective-permute-start.52) | collective-permute-done | bytes 331808 | tf_op jit(solution)/shard_map/ppermute | solution.py:603
  249.2 7.5 %term.5 = (bf16[4,104,576]{2,1,0:T(8,128)(2,1)}, bf16[4,104,576]{2,1,0:T(8,128)(2,1)}, bf16[4,112,576]{2,1,0:T(8,128)(2,1)}, bf16[4,112,576]{2,1,0:T(8,128)(2,1)}) custom-call(s32[6]{0:T(128)} %stack.72.place_ref, bf16[128,1152]{1,0:T(8,128)(2,1)} %get-tuple-element.138.refs_13_.refs_0_, bf16[128,2304]{1,0:T(8,128)(2,1)} %copy-done.5, ...), custom_call_target="tpu_custom_call" | custom-call | flops 1 | bytes 1 | tf_op jit(solution)/shard_map/term/pallas_call | solution.py:524
  264.4 4.1 %all-to-all-start.1 = ((bf16[16,8,2304]{2,1,0:T(8,128)(2,1)}), bf16[16,8,2304]{2,1,0:T(8,128)(2,1)S(1)}, u32[]{:S(2)}, u32[]{:S(2)}) async-start(bf16[16,8,2304]{2,1,0:T(8,128)(2,1)} %maximum_bitcast_fusion), calls=%async_computation.1 | async-start | bytes 1179648 | tf_op jit(solution)/shard_map/all_to_all | solution.py:624
  268.5 5.9 %collective-permute-done.66 = bf16[2,16,1728]{2,1,0:T(8,128)(2,1)S(1)} collective-permute-done((bf16[2,16,1728]{2,1,0:T(8,128)(2,1)}, bf16[2,16,1728]{2,1,0:T(8,128)(2,1)S(1)}, u32[]{:S(2)}, u32[]{:S(2)}) %collective-permute-start.66) | collective-permute-done | bytes 110624 | tf_op jit(solution)/shard_map/ppermute | solution.py:603
  276.4 6.0 %collective-permute-done.60 = bf16[4,112,576]{2,1,0:T(8,128)(2,1)S(1)} collective-permute-done((bf16[4,112,576]{2,1,0:T(8,128)(2,1)}, bf16[4,112,576]{2,1,0:T(8,128)(2,1)S(1)}, u32[]{:S(2)}, u32[]{:S(2)}) %collective-permute-start.60) | collective-permute-done | bytes 516128 | tf_op jit(solution)/shard_map/ppermute | solution.py:603
  283.4 5.6 %collective-permute-done.63 = bf16[360,576]{1,0:T(8,128)(2,1)} collective-permute-done((bf16[360,576]{1,0:T(8,128)(2,1)}, bf16[360,576]{1,0:T(8,128)(2,1)}, u32[]{:S(2)}, u32[]{:S(2)}) %collective-permute-start.63) | collective-permute-done | bytes 414752 | tf_op jit(solution)/shard_map/ppermute | solution.py:603
  291.1 13.1 %collective-permute-done.67 = bf16[2,16,1728]{2,1,0:T(8,128)(2,1)S(1)} collective-permute-done((bf16[2,16,1728]{2,1,0:T(8,128)(2,1)S(1)}, bf16[2,16,1728]{2,1,0:T(8,128)(2,1)S(1)}, u32[]{:S(2)}, u32[]{:S(2)}) %collective-permute-start.67) | collective-permute-done | bytes 110624 | tf_op jit(solution)/shard_map/ppermute | solution.py:603
  305.3 2.9 collective-permute-start.62
  308.2 16.2 %collective-permute-done.68 = bf16[2,16,1728]{2,1,0:T(8,128)(2,1)S(1)} collective-permute-done((bf16[2,16,1728]{2,1,0:T(8,128)(2,1)S(1)}, bf16[2,16,1728]{2,1,0:T(8,128)(2,1)S(1)}, u32[]{:S(2)}, u32[]{:S(2)}) %collective-permute-start.68) | collective-permute-done | bytes 110624 | tf_op jit(solution)/shard_map/ppermute | solution.py:603
  325.4 3.2 collective-permute-done.69
  330.9 8.1 %fusion.34 = f32[1152,3456]{1,0:T(8,128)} fusion(bf16[32,1152]{1,0:T(8,128)(2,1)S(1)} %bitcast.209, bf16[32,1728]{1,0:T(8,128)(2,1)S(1)} %get-tuple-element.178, bf16[32,1728]{1,0:T(8,128)(2,1)S(1)} %get-tuple-element.177), kind=kOutput, calls=%fused_computation.95 | convolution fusion | flops 255246336 | bytes 16220160 | tf_op jit(solution)/shard_map/dot_general | solution.py:1084
  (387 shorter events, 106.2 us)
Async XLA Ops:
  1.8 16.9 %collective-permute-start.1 = (bf16[144,1152]{1,0:T(8,128)(2,1)S(1)}, bf16[144,1152]{1,0:T(8,128)(2,1)S(1)}, u32[]{:S(2)}, u32[]{:S(2)}) collective-permute-start(bf16[144,1152]{1,0:T(8,128)(2,1)S(1)} %constant_dynamic-slice_fusion.3), channel_id=1, source_target_pairs={{0,1},{1,0},{2,3},{3,2},{4,5},{5,4},{6,7},{7,6},{8,9},{9,8},{10,11... | collective-permute-start | bytes 995336 | tf_op jit(solution)/shard_map/ppermute | solution.py:606
  7.8 44.4 %all-to-all-start = ((bf16[16,8,2432]{2,1,0:T(8,128)(2,1)}), bf16[16,8,2432]{2,1,0:T(8,128)(2,1)S(1)}, u32[]{:S(2)}, u32[]{:S(2)}) async-start(bf16[16,8,2432]{2,1,0:T(8,128)(2,1)} %fusion), calls=%async_computation | async-start | bytes 1245184 | tf_op jit(solution)/shard_map/all_to_all | solution.py:620
  35.5 31.8 %collective-permute-start.12 = (bf16[144,1152]{1,0:T(8,128)(2,1)S(1)}, bf16[144,1152]{1,0:T(8,128)(2,1)S(1)}, u32[]{:S(2)}, u32[]{:S(2)}) collective-permute-start(bf16[144,1152]{1,0:T(8,128)(2,1)S(1)} %collective-permute-done.1.refs_5_), channel_id=1, source_target_pairs={{0,2},{2,0},{4,6},{6,4},{8,10},{10,8},{12,14},{14,12},{16,18},{18,... | collective-permute-start | bytes 995336 | tf_op jit(solution)/shard_map/ppermute | solution.py:603
  35.5 16.7 %collective-permute-start.15 = (bf16[144,1152]{1,0:T(8,128)(2,1)S(1)}, bf16[144,1152]{1,0:T(8,128)(2,1)S(1)}, u32[]{:S(2)}, u32[]{:S(2)}) collective-permute-start(bf16[144,1152]{1,0:T(8,128)(2,1)S(1)} %collective-permute-done.2.refs_9_), channel_id=1, source_target_pairs={{0,8},{2,10},{4,12},{6,14},{8,0},{10,2},{12,4},{14,6},{16,24},{18,... | collective-permute-start | bytes 995336 | tf_op jit(solution)/shard_map/ppermute | solution.py:603
  65.4 24.4 %collective-permute-start.7 = (bf16[144,2304]{1,0:T(8,128)(2,1)S(1)}, bf16[144,2304]{1,0:T(8,128)(2,1)}, u32[]{:S(2)}, u32[]{:S(2)}) collective-permute-start(bf16[144,2304]{1,0:T(8,128)(2,1)S(1)} %dynamic_slice.85), channel_id=1, source_target_pairs={{0,1},{1,0},{2,3},{3,2},{4,5},{5,4},{6,7},{7,6},{8,9},{9,8},{10,11... | collective-permute-start | bytes 1990664 | tf_op jit(solution)/shard_map/ppermute | solution.py:606
  89.8 17.3 %collective-permute-start.22 = (bf16[144,2304]{1,0:T(8,128)(2,1)}, bf16[144,2304]{1,0:T(8,128)(2,1)}, u32[]{:S(2)}, u32[]{:S(2)}) collective-permute-start(bf16[144,2304]{1,0:T(8,128)(2,1)} %collective-permute-done.7.refs_1_), channel_id=1, source_target_pairs={{0,4},{2,6},{4,0},{6,2},{8,12},{10,14},{12,8},{14,10},{16,20},{18,... | collective-permute-start | bytes 1990664 | tf_op jit(solution)/shard_map/ppermute | solution.py:603
  91.4 16.9 %collective-permute-start.28 = (bf16[128,1152]{1,0:T(8,128)(2,1)S(1)}, bf16[128,1152]{1,0:T(8,128)(2,1)S(1)}, u32[]{:S(2)}, u32[]{:S(2)}) collective-permute-start(bf16[128,1152]{1,0:T(8,128)(2,1)S(1)} %fusion.12.refs_7_.refs_0_), channel_id=1, source_target_pairs={{0,1},{1,0},{2,3},{3,2},{4,5},{5,4},{6,7},{7,6},{8,9},{9,8},{10,11... | collective-permute-start | bytes 884744 | tf_op jit(solution)/shard_map/ppermute | solution.py:606
  133.2 22.7 %collective-permute-start.30 = (bf16[256,2304]{1,0:T(8,128)(2,1)}, bf16[256,2304]{1,0:T(8,128)(2,1)S(1)}, u32[]{:S(2)}, u32[]{:S(2)}) collective-permute-start(bf16[256,2304]{1,0:T(8,128)(2,1)} %get-tuple-element.106.refs_0_), channel_id=1, source_target_pairs={{0,2},{2,0},{4,6},{6,4},{8,10},{10,8},{12,14},{14,12},{16,18},{18,... | collective-permute-start | bytes 3538952 | tf_op jit(solution)/shard_map/ppermute | solution.py:603
  145.0 24.9 %collective-permute-start.45 = (bf16[4,40,2304]{2,1,0:T(8,128)(2,1)}, bf16[4,40,2304]{2,1,0:T(8,128)(2,1)}, u32[]{:S(2)}, u32[]{:S(2)}) collective-permute-start(bf16[4,40,2304]{2,1,0:T(8,128)(2,1)} %get-tuple-element.111), channel_id=1, source_target_pairs={{0,8},{2,10},{4,12},{6,14},{8,0},{10,2},{12,4},{14,6},{16,24},{18,... | collective-permute-start | bytes 2211848 | tf_op jit(solution)/shard_map/ppermute | solution.py:603
  152.7 16.3 %collective-permute-start.44 = (bf16[4,32,2304]{2,1,0:T(8,128)(2,1)S(1)}, bf16[4,32,2304]{2,1,0:T(8,128)(2,1)S(1)}, u32[]{:S(2)}, u32[]{:S(2)}) collective-permute-start(bf16[4,32,2304]{2,1,0:T(8,128)(2,1)S(1)} %copy-done.73), channel_id=1, source_target_pairs={{0,4},{2,6},{4,0},{6,2},{8,12},{10,14},{12,8},{14,10},{16,20},{18,... | collective-permute-start | bytes 1769480 | tf_op jit(solution)/shard_map/ppermute | solution.py:603
  154.8 17.1 %collective-permute-start.35 = (bf16[128,2304]{1,0:T(8,128)(2,1)}, bf16[128,2304]{1,0:T(8,128)(2,1)S(1)}, u32[]{:S(2)}, u32[]{:S(2)}) collective-permute-start(bf16[128,2304]{1,0:T(8,128)(2,1)} %get-tuple-element.118), channel_id=1, source_target_pairs={{0,1},{1,0},{2,3},{3,2},{4,5},{5,4},{6,7},{7,6},{8,9},{9,8},{10,11... | collective-permute-start | bytes 1769480 | tf_op jit(solution)/shard_map/ppermute | solution.py:606
  170.9 14.9 %collective-permute-start.41 = (bf16[128,1152]{1,0:T(8,128)(2,1)}, bf16[128,1152]{1,0:T(8,128)(2,1)S(1)}, u32[]{:S(2)}, u32[]{:S(2)}) collective-permute-start(bf16[128,1152]{1,0:T(8,128)(2,1)} %get-tuple-element.138.refs_13_.refs_0_), channel_id=1, source_target_pairs={{0,1},{1,0},{2,3},{3,2},{4,5},{5,4},{6,7},{7,6},{8,9},{9,8},{10,11... | collective-permute-start | bytes 884744 | tf_op jit(solution)/shard_map/ppermute | solution.py:606
  171.9 18.1 %collective-permute-start.42 = (bf16[128,1152]{1,0:T(8,128)(2,1)}, bf16[128,1152]{1,0:T(8,128)(2,1)S(1)}, u32[]{:S(2)}, u32[]{:S(2)}) collective-permute-start(bf16[128,1152]{1,0:T(8,128)(2,1)} %get-tuple-element.138.refs_13_.refs_0_), channel_id=1, source_target_pairs={{0,2},{2,0},{4,6},{6,4},{8,10},{10,8},{12,14},{14,12},{16,18},{18,... | collective-permute-start | bytes 884744 | tf_op jit(solution)/shard_map/ppermute | solution.py:603
  171.9 31.3 %collective-permute-start.40 = (bf16[128,2304]{1,0:T(8,128)(2,1)}, bf16[128,2304]{1,0:T(8,128)(2,1)S(1)}, u32[]{:S(2)}, u32[]{:S(2)}) collective-permute-start(bf16[128,2304]{1,0:T(8,128)(2,1)} %get-tuple-element.125), channel_id=1, source_target_pairs={{0,2},{2,0},{4,6},{6,4},{8,10},{10,8},{12,14},{14,12},{16,18},{18,... | collective-permute-start | bytes 1769480 | tf_op jit(solution)/shard_map/ppermute | solution.py:603
  172.5 19.3 %collective-permute-start.37 = (bf16[128,2304]{1,0:T(8,128)(2,1)S(1)}, bf16[128,2304]{1,0:T(8,128)(2,1)S(1)}, u32[]{:S(2)}, u32[]{:S(2)}) collective-permute-start(bf16[128,2304]{1,0:T(8,128)(2,1)S(1)} %collective-permute-done.35.refs_7_.refs_11_.refs_9_), channel_id=1, source_target_pairs={{0,2},{2,0},{4,6},{6,4},{8,10},{10,8},{12,14},{14,12},{16,18},{18,... | collective-permute-start | bytes 1769480 | tf_op jit(solution)/shard_map/ppermute | solution.py:603
  179.9 31.4 %collective-permute-start.47 = (bf16[128,2304]{1,0:T(8,128)(2,1)}, bf16[128,2304]{1,0:T(8,128)(2,1)}, u32[]{:S(2)}, u32[]{:S(2)}) collective-permute-start(bf16[128,2304]{1,0:T(8,128)(2,1)} %get-tuple-element.171), channel_id=1, source_target_pairs={{4,0},{6,2},{12,4},{14,6},{8,12},{10,14},{16,8},{18,10},{20,16},{2... | collective-permute-start | bytes 1769480 | tf_op jit(solution)/shard_map/ppermute | solution.py:612
  185.9 25.5 %collective-permute-start.48 = (bf16[128,2304]{1,0:T(8,128)(2,1)}, bf16[128,2304]{1,0:T(8,128)(2,1)}, u32[]{:S(2)}, u32[]{:S(2)}) collective-permute-start(bf16[128,2304]{1,0:T(8,128)(2,1)} %get-tuple-element.172), channel_id=1, source_target_pairs={{0,4},{2,6},{4,12},{6,14},{12,8},{14,10},{8,16},{10,18},{16,20},{1... | collective-permute-start | bytes 1769480 | tf_op jit(solution)/shard_map/ppermute | solution.py:612
  190.0 21.3 %collective-permute-start.51 = (bf16[2,40,2304]{2,1,0:T(8,128)(2,1)S(1)}, bf16[2,40,2304]{2,1,0:T(8,128)(2,1)}, u32[]{:S(2)}, u32[]{:S(2)}) collective-permute-start(bf16[2,40,2304]{2,1,0:T(8,128)(2,1)S(1)} %dynamic-slice_bitcast_fusion.2), channel_id=1, source_target_pairs={{0,4},{2,6},{4,0},{6,2},{8,12},{10,14},{12,8},{14,10},{16,20},{18,... | collective-permute-start | bytes 1105928 | tf_op jit(solution)/shard_map/ppermute | solution.py:603
  203.2 36.4 %collective-permute-start.39 = (bf16[4,184,576]{2,1,0:T(8,128)(2,1)}, bf16[4,184,576]{2,1,0:T(8,128)(2,1)}, u32[]{:S(2)}, u32[]{:S(2)}) collective-permute-start(bf16[4,184,576]{2,1,0:T(8,128)(2,1)} %get-tuple-element.121), channel_id=1, source_target_pairs={{0,8},{2,10},{4,12},{6,14},{8,0},{10,2},{12,4},{14,6},{16,24},{18,... | collective-permute-start | bytes 2543624 | tf_op jit(solution)/shard_map/ppermute | solution.py:603
  204.6 35.1 %collective-permute-start.38 = (bf16[4,176,576]{2,1,0:T(8,128)(2,1)}, bf16[4,176,576]{2,1,0:T(8,128)(2,1)}, u32[]{:S(2)}, u32[]{:S(2)}) collective-permute-start(bf16[4,176,576]{2,1,0:T(8,128)(2,1)} %get-tuple-element.120), channel_id=1, source_target_pairs={{0,4},{2,6},{4,0},{6,2},{8,12},{10,14},{12,8},{14,10},{16,20},{18,... | collective-permute-start | bytes 2433032 | tf_op jit(solution)/shard_map/ppermute | solution.py:603
  212.9 26.7 %collective-permute-start.49 = (bf16[128,2304]{1,0:T(8,128)(2,1)S(1)}, bf16[128,2304]{1,0:T(8,128)(2,1)S(1)}, u32[]{:S(2)}, u32[]{:S(2)}) collective-permute-start(bf16[128,2304]{1,0:T(8,128)(2,1)S(1)} %add_convert_fusion.4.refs_14_.refs_1_), channel_id=1, source_target_pairs={{0,1},{1,0},{2,3},{3,2},{4,5},{5,4},{6,7},{7,6},{8,9},{9,8},{10,11... | collective-permute-start | bytes 1769480 | tf_op jit(solution)/shard_map/ppermute | solution.py:606
  224.6 15.1 %collective-permute-start.52 = (bf16[72,2304]{1,0:T(8,128)(2,1)}, bf16[72,2304]{1,0:T(8,128)(2,1)}, u32[]{:S(2)}, u32[]{:S(2)}) collective-permute-start(bf16[72,2304]{1,0:T(8,128)(2,1)} %fusion.28), channel_id=1, source_target_pairs={{0,16},{2,18},{4,20},{6,22},{8,24},{10,26},{12,28},{14,30},{16,0},... | collective-permute-start | bytes 995336 | tf_op jit(solution)/shard_map/ppermute | solution.py:603
  241.8 17.0 %collective-permute-start.54 = (bf16[2,184,576]{2,1,0:T(8,128)(2,1)S(1)}, bf16[2,184,576]{2,1,0:T(8,128)(2,1)S(1)}, u32[]{:S(2)}, u32[]{:S(2)}) collective-permute-start(bf16[2,184,576]{2,1,0:T(8,128)(2,1)S(1)} %dynamic-slice_bitcast_fusion), channel_id=1, source_target_pairs={{0,4},{2,6},{4,0},{6,2},{8,12},{10,14},{12,8},{14,10},{16,20},{18,... | collective-permute-start | bytes 1271816 | tf_op jit(solution)/shard_map/ppermute | solution.py:603
  256.7 17.7 %collective-permute-start.58 = (bf16[4,104,576]{2,1,0:T(8,128)(2,1)}, bf16[4,104,576]{2,1,0:T(8,128)(2,1)S(1)}, u32[]{:S(2)}, u32[]{:S(2)}) collective-permute-start(bf16[4,104,576]{2,1,0:T(8,128)(2,1)} %get-tuple-element.154), channel_id=1, source_target_pairs={{0,4},{2,6},{4,0},{6,2},{8,12},{10,14},{12,8},{14,10},{16,20},{18,... | collective-permute-start | bytes 1437704 | tf_op jit(solution)/shard_map/ppermute | solution.py:603
  256.8 25.6 %collective-permute-start.60 = (bf16[4,112,576]{2,1,0:T(8,128)(2,1)}, bf16[4,112,576]{2,1,0:T(8,128)(2,1)S(1)}, u32[]{:S(2)}, u32[]{:S(2)}) collective-permute-start(bf16[4,112,576]{2,1,0:T(8,128)(2,1)} %get-tuple-element.156), channel_id=1, source_target_pairs={{0,8},{2,10},{4,12},{6,14},{8,0},{10,2},{12,4},{14,6},{16,24},{18,... | collective-permute-start | bytes 1548296 | tf_op jit(solution)/shard_map/ppermute | solution.py:603
  260.6 28.4 %collective-permute-start.63 = (bf16[360,576]{1,0:T(8,128)(2,1)}, bf16[360,576]{1,0:T(8,128)(2,1)}, u32[]{:S(2)}, u32[]{:S(2)}) collective-permute-start(bf16[360,576]{1,0:T(8,128)(2,1)} %fusion.22), channel_id=1, source_target_pairs={{0,16},{2,18},{4,20},{6,22},{8,24},{10,26},{12,28},{14,30},{16,0},... | collective-permute-start | bytes 1244168 | tf_op jit(solution)/shard_map/ppermute | solution.py:603
  264.4 74.6 %all-to-all-start.1 = ((bf16[16,8,2304]{2,1,0:T(8,128)(2,1)}), bf16[16,8,2304]{2,1,0:T(8,128)(2,1)S(1)}, u32[]{:S(2)}, u32[]{:S(2)}) async-start(bf16[16,8,2304]{2,1,0:T(8,128)(2,1)} %maximum_bitcast_fusion), calls=%async_computation.1 | async-start | bytes 1179648 | tf_op jit(solution)/shard_map/all_to_all | solution.py:624
  274.6 29.7 %collective-permute-start.59 = (bf16[2,104,576]{2,1,0:T(8,128)(2,1)S(1)}, bf16[2,104,576]{2,1,0:T(8,128)(2,1)S(1)}, u32[]{:S(2)}, u32[]{:S(2)}) collective-permute-start(bf16[2,104,576]{2,1,0:T(8,128)(2,1)S(1)} %dynamic-slice_bitcast_fusion.5), channel_id=1, source_target_pairs={{0,8},{2,10},{4,12},{6,14},{8,0},{10,2},{12,4},{14,6},{16,24},{18,... | collective-permute-start | bytes 718856 | tf_op jit(solution)/shard_map/ppermute | solution.py:603
  282.5 21.8 %collective-permute-start.61 = (bf16[2,112,576]{2,1,0:T(8,128)(2,1)S(1)}, bf16[2,112,576]{2,1,0:T(8,128)(2,1)S(1)}, u32[]{:S(2)}, u32[]{:S(2)}) collective-permute-start(bf16[2,112,576]{2,1,0:T(8,128)(2,1)S(1)} %dynamic-slice_bitcast_fusion.4), channel_id=1, source_target_pairs={{0,4},{2,6},{4,0},{6,2},{8,12},{10,14},{12,8},{14,10},{16,20},{18,... | collective-permute-start | bytes 774152 | tf_op jit(solution)/shard_map/ppermute | solution.py:603
  290.4 34.1 %collective-permute-start.64 = (bf16[288,576]{1,0:T(8,128)(2,1)S(1)}, bf16[288,576]{1,0:T(8,128)(2,1)S(1)}, u32[]{:S(2)}, u32[]{:S(2)}) collective-permute-start(bf16[288,576]{1,0:T(8,128)(2,1)S(1)} %pad_maximum_fusion.1), channel_id=1, source_target_pairs={{0,0},{1,16},{2,2},{3,18},{4,4},{5,20},{6,6},{7,22},{8,8},{9,24},{... | collective-permute-start | bytes 995336 | tf_op jit(solution)/shard_map/ppermute | solution.py:1060
  304.5 19.9 %collective-permute-start.68 = (bf16[2,16,1728]{2,1,0:T(8,128)(2,1)S(1)}, bf16[2,16,1728]{2,1,0:T(8,128)(2,1)S(1)}, u32[]{:S(2)}, u32[]{:S(2)}) collective-permute-start(bf16[2,16,1728]{2,1,0:T(8,128)(2,1)S(1)} %add_convert_fusion.8), channel_id=1, source_target_pairs={{0,16},{2,18},{4,20},{6,22},{8,24},{10,26},{12,28},{14,30},{16,0},... | collective-permute-start | bytes 331784 | tf_op jit(solution)/shard_map/ppermute | solution.py:603
  305.3 24.7 %collective-permute-start.62 = (bf16[216,576]{1,0:T(8,128)(2,1)S(1)}, bf16[216,576]{1,0:T(8,128)(2,1)S(1)}, u32[]{:S(2)}, u32[]{:S(2)}) collective-permute-start(bf16[216,576]{1,0:T(8,128)(2,1)S(1)} %fusion.31), channel_id=1, source_target_pairs={{0,16},{2,18},{4,20},{6,22},{8,24},{10,26},{12,28},{14,30},{16,0},... | collective-permute-start | bytes 746504 | tf_op jit(solution)/shard_map/ppermute | solution.py:603
  (118 other events, 980.9 us)

commit v4 on v3

--- a/solution.py
+++ b/solution.py
@@ -59,8 +59,8 @@
         elif step is None:
             start = pl.multiple_of(mine * half, 16)
         else:
-            quarter = place_ref[step[0]] ^ step[1]
-            start = pl.multiple_of((1 - mine) * half + quarter * rows, 16)
+            part = place_ref[step[0]] ^ step[1]
+            start = pl.multiple_of((1 - mine) * half + part * rows, 16)
         target_ref[pl.ds(start, rows), pl.ds(column, cols)] = ref[...]
 
 
@@ -107,22 +107,34 @@
     return jnp.concatenate([value] * repeats, axis=0) if repeats > 1 else value
 
 
-def norm_in_kernel(place_ref, tokens_ref, own_ref, other_ref, out_ref):
-    first = place_ref[0] == 0
-    shift = slot_rows(jnp.where(first, own_ref[:, pl.ds(0, D)], other_ref[:, pl.ds(0, D)]))
-    scale = slot_rows(jnp.where(first, own_ref[:, pl.ds(D, D)], other_ref[:, pl.ds(D, D)]))
+def mod_attn(place_ref, own_ref, other_ref, index):
+    columns = pl.ds(index * D, D)
+    return slot_rows(jnp.where(place_ref[6] == 0, own_ref[:, columns], other_ref[:, columns]))
+
+
+def mod_mlp(place_ref, own_ref, other_ref, index):
+    return mod_attn(place_ref, other_ref, own_ref, index)
+
+
+def norm_in_kernel(place_ref, tokens_ref, own_ref, other_ref, out_ref, grad_ref):
+    shift = mod_attn(place_ref, own_ref, other_ref, 0)
+    scale = 1.0 + mod_attn(place_ref, own_ref, other_ref, 1)
+    gate = mod_mlp(place_ref, own_ref, other_ref, 2)
     for start in range(0, tokens_ref.shape[0], PERIOD):
         rows = pl.ds(start, PERIOD)
         normed, ignored = normalized(tokens_ref[rows, pl.ds(0, D)].astype(f32))
-        out_ref[rows, :] = (normed * (1.0 + scale) + shift).astype(bf16)
+        out_ref[rows, :] = (normed * scale + shift).astype(bf16)
+        keep = tokens_ref[rows, pl.ds(2 * D, 128)].astype(f32)[:, :1]
+        grad = tokens_ref[rows, pl.ds(D, D)].astype(f32)
+        grad_ref[rows, :] = (grad * gate * keep).astype(bf16)
 
 
 def norm_in(place, tokens, own, other):
     return pl.pallas_call(
         norm_in_kernel,
-        out_shape=shaped(tokens.shape[0], D, dtype=bf16),
+        out_shape=[shaped(tokens.shape[0], D, dtype=bf16)] * 2,
         in_specs=[pl.BlockSpec(memory_space=pltpu.SMEM)] + [VMEM_SPEC] * 3,
-        out_specs=VMEM_SPEC,
+        out_specs=[VMEM_SPEC] * 2,
         compiler_params=params(),
         cost_estimate=COST,
         name="norm_in",
@@ -176,10 +188,11 @@
 
 def attend_kernel(place_ref, *refs, parts):
     count = len(parts)
-    q_ref, kv_ref, bias_ref, mask_ref, tokens_ref, gate_ref, shift_ref, scale_ref = refs[
-        count : count + 8
-    ]
-    merged_ref, proj_ref, mid_ref, normed_ref, acc_ref, weight_ref = refs[count + 8 :]
+    q_ref, kv_ref, bias_ref, mask_ref, tokens_ref, own_ref, other_ref = refs[count : count + 7]
+    merged_ref, proj_ref, mid_ref, normed_ref, acc_ref, weight_ref = refs[count + 7 :]
+    gate = mod_attn(place_ref, own_ref, other_ref, 2)
+    shift = mod_mlp(place_ref, own_ref, other_ref, 0)
+    scale = 1.0 + mod_mlp(place_ref, own_ref, other_ref, 1)
     tokens = q_ref.shape[0]
     fill(weight_ref, place_ref, refs[:count], parts)
     acc_ref[...] = jnp.zeros_like(acc_ref)
@@ -200,10 +213,10 @@
     proj_ref[...] = dot_nn(merged_ref[...], weight_ref[...])
     for start in range(0, tokens, PERIOD):
         rows = pl.ds(start, PERIOD)
-        mid = tokens_ref[rows, pl.ds(0, D)].astype(f32) + gate_ref[...] * proj_ref[rows, :]
+        mid = tokens_ref[rows, pl.ds(0, D)].astype(f32) + gate * proj_ref[rows, :]
         mid_ref[rows, :] = mid
         normed, ignored = normalized(mid)
-        normed_ref[rows, :] = (normed * (1.0 + scale_ref[...]) + shift_ref[...]).astype(bf16)
+        normed_ref[rows, :] = (normed * scale + shift).astype(bf16)
 
 
 def attend(place, sources, *inputs):
@@ -282,7 +295,7 @@
     count = len(parts)
     mid_refs, grad_refs = refs[count : count + arrays], refs[count + arrays : count + 2 * arrays]
     channel_ref, down_ref = refs[count + 2 * arrays : count + 2 * arrays + 2]
-    act_ref, pre_ref, grad_own, grad_low, out_own, out_low = refs[-9:-3]
+    act_ref, pre_ref, grad_own, out_own, low_ref = refs[-8:-3]
     weight_ref, grad_acc, out_acc = refs[-3:]
     own_rows = grad_own.shape[0]
     step, steps = pl.program_id(0), pl.num_programs(0)
@@ -317,11 +330,11 @@
 
     @pl.when(step == steps - 1)
     def _():
-        skip = rows - grad_low.shape[0]
+        skip = rows - low_ref.shape[0]
         grad_own[...] = grad_acc[pl.ds(0, own_rows), :]
         out_own[...] = out_acc[pl.ds(0, own_rows), :]
-        grad_low[...] = grad_acc[pl.ds(skip, rows - skip), :].astype(bf16)
-        out_low[...] = out_acc[pl.ds(skip, rows - skip), :].astype(bf16)
+        low_ref[:, pl.ds(0, D)] = grad_acc[pl.ds(skip, rows - skip), :].astype(bf16)
+        low_ref[:, pl.ds(D, D)] = out_acc[pl.ds(skip, rows - skip), :].astype(bf16)
 
 
 def feed(place, sources, mids, grads, channels, down, chunk, tokens, low_rows):
@@ -329,14 +342,13 @@
     rows = sum(mid.shape[0] for mid in mids)
     width = down.shape[0]
     by_chunk = pl.BlockSpec((rows, chunk), lambda i, place: (0, i))
-    own, low = (tokens, D), (low_rows, D)
+    own, low = (tokens, D), (low_rows, 2 * D)
     return pl.pallas_call(
         functools.partial(feed_kernel, parts=parts, arrays=len(mids)),
         out_shape=[
             shaped(rows, width, dtype=bf16),
             shaped(rows, width, dtype=bf16),
             shaped(*own),
-            shaped(*low, dtype=bf16),
             shaped(*own),
             shaped(*low, dtype=bf16),
         ],
@@ -351,7 +363,7 @@
                 ),
                 pl.BlockSpec((chunk, D), lambda i, place: (i, 0)),
             ],
-            out_specs=[by_chunk, by_chunk, whole(own), whole(low), whole(own), whole(low)],
+            out_specs=[by_chunk, by_chunk, whole(own), whole(own), whole(low)],
             scratch_shapes=[
                 pltpu.VMEM((D, chunk), bf16),
                 pltpu.VMEM((rows, D), f32),
@@ -366,13 +378,15 @@
 
 def mid_back_kernel(place_ref, *refs, parts):
     count = len(parts)
-    own_ref, other_ref, mid_ref, proj_ref, late_ref, scale_ref, gate_ref, mask_ref = refs[
-        count : count + 8
+    own_ref, out_ref, other_ref, mid_ref, proj_ref, late_ref = refs[count : count + 6]
+    mod_own, mod_other, mask_ref, attn_ref, normed_ref = refs[count + 6 : count + 11]
+    grad_mid_ref, own_pack_ref, pack_ref, heads_ref, block_ref, sums_ref = refs[
+        count + 11 : count + 17
     ]
-    attn_ref, normed_ref = refs[count + 8 : count + 10]
-    grad_mid_ref, own_pack_ref, pack_ref, heads_ref, sums_ref, weight_ref, merged_ref = refs[
-        count + 10 :
-    ]
+    weight_ref, merged_ref = refs[count + 17 :]
+    scale = 1.0 + mod_mlp(place_ref, mod_own, mod_other, 1)
+    gate = mod_attn(place_ref, mod_own, mod_other, 2)
+    out_gate = mod_mlp(place_ref, mod_own, mod_other, 2)
     first = place_ref[0] == 0
     half = D // 2
     for index, ref in enumerate((attn_ref, normed_ref)):
@@ -381,26 +395,26 @@
         pack_ref[:, pl.ds(index * half, half)] = jnp.where(first, high, low)
     tokens = own_ref.shape[0]
     fill(weight_ref, place_ref, refs[:count], parts)
-    gate_sum = jnp.zeros((PERIOD, D), f32)
-    shift_sum = jnp.zeros((PERIOD, D), f32)
-    scale_sum = jnp.zeros((PERIOD, D), f32)
+    sums = [jnp.zeros((PERIOD, D), f32) for ignored in range(4)]
     for start in range(0, tokens, PERIOD):
         rows = pl.ds(start, PERIOD)
         normed, inverse = normalized(mid_ref[rows, :])
-        grad = own_ref[rows, :] + other_ref[rows, :].astype(f32)
-        grad_mid = late_ref[rows, pl.ds(D, D)].astype(f32) + normalized_back(
-            grad * (1.0 + scale_ref[...]), normed, inverse
-        )
+        grad = own_ref[rows, :] + other_ref[rows, pl.ds(0, D)].astype(f32)
+        grad_out = late_ref[rows, pl.ds(D, D)].astype(f32)
+        grad_mid = grad_out + normalized_back(grad * scale, normed, inverse)
         grad_mid_ref[rows, :] = grad_mid
-        grad_attn = (grad_mid * gate_ref[...]).astype(bf16)
+        grad_attn = (grad_mid * gate).astype(bf16)
         own_pack_ref[rows, pl.ds(D, D)] = grad_attn
         pack_ref[rows, pl.ds(D, D)] = grad_attn
-        gate_sum += grad_mid * proj_ref[rows, :]
-        shift_sum += grad
-        scale_sum += grad * normed
-    sums_ref[0] = gate_sum
-    sums_ref[1] = shift_sum
-    sums_ref[2] = scale_sum
+        out = out_ref[rows, :] + other_ref[rows, pl.ds(D, D)].astype(f32)
+        out = out * late_ref[rows, pl.ds(2 * D, 128)].astype(f32)[:, :1]
+        block_ref[rows, :] = (mid_ref[rows, :] + out_gate * out).astype(bf16)
+        for index, value in enumerate(
+            (grad_mid * proj_ref[rows, :], grad, grad * normed, grad_out * out)
+        ):
+            sums[index] += value
+    for index in range(4):
+        sums_ref[index] = sums[index]
     merged_ref[...] = dot_nt(pack_ref[:, pl.ds(D, D)], weight_ref[...])
     for start in range(0, tokens, PERIOD):
         rows = pl.ds(start, PERIOD)
@@ -419,7 +433,8 @@
             shaped(tokens, 2 * D, dtype=bf16),
             shaped(tokens, 2 * D, dtype=bf16),
             shaped(tokens, D, dtype=bf16),
-            shaped(3, PERIOD, D),
+            shaped(tokens, D, dtype=bf16),
+            shaped(4, PERIOD, D),
         ],
         [pltpu.VMEM((D, D), bf16), pltpu.VMEM((tokens, D), f32)],
         "mid_back",
@@ -428,21 +443,24 @@
 
 def in_back_kernel(place_ref, *refs, parts):
     count = len(parts)
-    dq_ref, dkv_ref, tokens_ref, scale_ref, grad_mid_ref = refs[count : count + 5]
-    grad_in_ref, sums_ref, weight_ref, grad_ref = refs[count + 5 :]
+    dq_ref, dkv_ref, tokens_ref, mod_own, mod_other = refs[count : count + 5]
+    grad_mid_ref, block_ref = refs[count + 5 : count + 7]
+    both_ref, sums_ref, weight_ref, grad_ref = refs[count + 7 :]
     tokens = dq_ref.shape[0]
     fill(weight_ref, place_ref, refs[:count], parts)
     grad_ref[...] = dot_nt(dkv_ref[...], weight_ref[:, pl.ds(D, 2 * D)]) + dot_nt(
         dq_ref[...], weight_ref[:, pl.ds(0, D)]
     )
+    scale = 1.0 + mod_attn(place_ref, mod_own, mod_other, 1)
     shift_sum = jnp.zeros((PERIOD, D), f32)
     scale_sum = jnp.zeros((PERIOD, D), f32)
+    both_ref[:, pl.ds(0, D)] = block_ref[...]
     for start in range(0, tokens, PERIOD):
         rows = pl.ds(start, PERIOD)
         normed, inverse = normalized(tokens_ref[rows, pl.ds(0, D)].astype(f32))
         grad = grad_ref[rows, :]
-        back = normalized_back(grad * (1.0 + scale_ref[...]), normed, inverse)
-        grad_in_ref[rows, :] = (grad_mid_ref[rows, :] + back).astype(bf16)
+        back = normalized_back(grad * scale, normed, inverse)
+        both_ref[rows, pl.ds(D, D)] = (grad_mid_ref[rows, :] + back).astype(bf16)
         shift_sum += grad
         scale_sum += grad * normed
     sums_ref[0] = shift_sum
@@ -456,7 +474,7 @@
         place,
         sources,
         inputs,
-        [shaped(tokens, D, dtype=bf16), shaped(2, PERIOD, D)],
+        [shaped(tokens, 2 * D, dtype=bf16), shaped(2, PERIOD, D)],
         [pltpu.VMEM((D, 3 * D), bf16), pltpu.VMEM((tokens, D), f32)],
         "in_back",
     )
@@ -531,6 +549,28 @@
         cost_estimate=COST,
         name="term",
     )(place, *arrays)
+
+
+def outer_kernel(left_ref, right_ref, out_ref):
+    out_ref[...] = dot_tn(left_ref[...], right_ref[...])
+
+
+def outer(left, right):
+    depth, rows = left.shape
+    columns = right.shape[1]
+    return pl.pallas_call(
+        outer_kernel,
+        out_shape=shaped(rows, columns),
+        grid=(rows // 128,),
+        in_specs=[
+            pl.BlockSpec((depth, 128), lambda i: (0, i)),
+            pl.BlockSpec((depth, columns), lambda i: (0, 0)),
+        ],
+        out_specs=pl.BlockSpec((128, columns), lambda i: (i, 0)),
+        compiler_params=params(),
+        cost_estimate=COST,
+        name="outer",
+    )(left, right)
 
 
 def running_ends(pieces):
@@ -596,6 +636,8 @@
             (seq_at // 2) % 2,
             (seq_at // 4) % 2,
             (seq_at // 4) % 2 * 2 + core,
+            row_at if fast else jnp.zeros_like(row_at),
+            (seq_at // 8) % 2,
         ]
     ).astype(jnp.int32)
 
@@ -620,17 +662,24 @@
         moved = lax.all_to_all(moved.reshape(seq, slots, -1), "seq", 0, 0)
         return moved.reshape(tokens, -1)
 
-    def from_slots(value, dtype):
+    def from_slots(value, dtype, *earlier):
         value = lax.all_to_all(value.reshape(seq, slots, -1), "seq", 0, 0)
+        value = after(value, *earlier) if earlier else value
         value = value.reshape(tokens, -1)
         return jnp.dot(swap_rows, value, preferred_element_type=f32).astype(dtype)
 
     def after(value, *earlier):
         return lax.optimization_barrier((value, *earlier))[0]
 
-    def fetch_first(weight, column, cols, bit, *earlier):
-        row = after(((seq_at // bit) % 2 * 2 + core) * (half // 4), *earlier)
-        return cross(lax.dynamic_slice(weight, (row, column), (half // 4, cols)))
+    def fetch_first(slices, bit, *earlier):
+        count = 2 if bit is None else 4
+        part = core if bit is None else (seq_at // bit) % 2 * 2 + core
+        row = after(part * (half // count), *earlier)
+        parts = [
+            lax.dynamic_slice(weight, (row, column), (half // count, cols))
+            for weight, column, cols in slices
+        ]
+        return cross(jnp.concatenate(parts, axis=1) if len(parts) > 1 else parts[0])
 
     def gather_rows(value):
         if rows == 2:
@@ -664,30 +713,24 @@
     columns = ada_weight.shape[1]
     quarter = half // 4
     if fast:
-        k_first = fetch_first(qkv_weight, D, D, 2, seq_at)
-        v_first = fetch_first(qkv_weight, 2 * D, D, 4, k_first)
+        k_first = fetch_first([(qkv_weight, D, D), (out_weight, 0, D)], 2, seq_at)
         k_second = flip(k_first, 2)
-        cond_rows = after(cond_rows, k_first)
     mod_rows = jnp.dot(cond_rows, ada_weight, preferred_element_type=f32)
     mod_rows = mod_rows.reshape(rows, crops, columns)
     if rows == 2:
         mod_slots = jnp.einsum("rsc,rcm->rsm", selector_rows, mod_rows, precision=highest)
         if fast:
-            mod_slots = after(mod_slots, v_first, k_second)
+            mod_slots = after(mod_slots, k_first)
         arrived = cross(mod_slots[1])
-        mod_attn = pick(mod_slots[0], arrived)
-        mod_mlp = pick(arrived, mod_slots[0])
-        norm_mods = (mod_slots[0], arrived)
+        mods = (mod_slots[0], arrived)
     else:
         mine = lax.all_to_all(mod_rows, "fsdp", 0, 0)
         mine = jnp.transpose(mine, (1, 0, 2)).reshape(crops, rows * columns)
         mine = jnp.dot(selector, mine, precision=highest)
-        mod_attn, mod_mlp = mine[:, : 3 * D], mine[:, 3 * D :]
-        norm_mods = (mod_attn, mod_attn)
-    mod_attn, mod_mlp = tiled(mod_attn), tiled(mod_mlp)
-    ignored, scale_attn, gate_attn = (mod_attn[:, i * D : (i + 1) * D] for i in range(3))
-    shift_mlp, scale_mlp, gate_mlp = (mod_mlp[:, i * D : (i + 1) * D] for i in range(3))
-
+        mods = (mine[:, : 3 * D], mine[:, 3 * D :])
+
+    kept = jnp.broadcast_to(keep_mask[0].astype(bf16)[:, None], (tokens, 128))
+    tokens_here = to_slots(jnp.concatenate([tokens_in[0], cotangent[0], kept], axis=1))
     def block(at):
         return lambda i, place: (0, at)
 
@@ -698,22 +741,26 @@
             return (first, flip(first, 1), second, flip(second, 1))
 
         other_part = (1 - row_at) * hidden_part
-        q_first = fetch_first(qkv_weight, 0, D, 2, arrived)
-        out_first = fetch_first(out_weight, 0, D, 4, q_first)
-        up_first_piece = fetch_first(up_weight, other_part, hidden_part, 2, out_first)
-        v_second, q_second, out_second = flip(v_first, 4), flip(q_first, 2), flip(out_first, 4)
+        v_first = fetch_first([(qkv_weight, 2 * D, D)], 4, mod_slots)
+        q_first = fetch_first([(qkv_weight, 0, D)], None, arrived)
+        tokens_here = after(tokens_here, k_second)
+        normed_in, grad_mlp = norm_in(place, tokens_here, *mods)
+        up_first_piece = fetch_first(
+            [(up_weight, other_part, hidden_part)], 2, q_first, normed_in
+        )
+        v_second = flip(v_first, 4)
         k_pieces, v_pieces = spread(k_first, k_second), spread(v_first, v_second)
-        q_pieces, out_pieces = spread(q_first, q_second), spread(out_first, out_second)
+        q_pieces = (q_first, flip(q_first, 1))
         qkv_sources = [(qkv_weight, (half, 3 * D), block(0), None, 0)]
-        for at, column, pieces in ((1, 0, q_pieces), (1, D, k_pieces), (5, 2 * D, v_pieces)):
+        for at, column, pieces in ((2, 0, q_pieces), (1, D, k_pieces), (5, 2 * D, v_pieces)):
             qkv_sources += [
-                (piece, (quarter, D), block(0), (at, step), column)
+                (piece, (piece.shape[0], D), block(0), (at, step), column)
                 for step, piece in enumerate(pieces)
             ]
         out_sources = [(out_weight, (half, D), block(0), None, 0)]
         out_sources += [
-            (piece, (quarter, D), block(0), (5, step), 0)
-            for step, piece in enumerate(out_pieces)
+            (piece, (quarter, D), block(1), (1, step), 0)
+            for step, piece in enumerate(k_pieces)
         ]
         low_rows = tokens
     else:
@@ -726,18 +773,15 @@
         up_sources = [(up_part, (D, hidden_part), block(0), "all", 0)]
         low_rows = rows * tokens
 
-    kept = jnp.broadcast_to(keep_mask[0].astype(bf16)[:, None], (tokens, 128))
-    tokens_here = to_slots(jnp.concatenate([tokens_in[0], cotangent[0], kept], axis=1))
-    if fast:
-        tokens_here = after(tokens_here, v_second)
-    normed_in = norm_in(place, tokens_here, *norm_mods)
+    if not fast:
+        normed_in, grad_mlp = norm_in(place, tokens_here, *mods)
 
     reach = -(-(PIECE_MAX - 1) // slots)
     paired = reach == 2 and seq % 2 == 0
     if paired:
         below, above = shift(normed_in, 2), shift(normed_in, -2)
         if fast:
-            above = after(above, q_second)
+            above = after(above, v_second, q_first)
         passed = flip(jnp.where(core == 0, above, below), 1)
         near = [normed_in, flip(normed_in, 1), below, above, passed]
         near_at = [
@@ -766,18 +810,9 @@
         jnp.repeat(jnp.dot(selector, head_mask[0].astype(f32), precision=highest), HD, axis=1)
     )
 
-    def by_slot(value):
-        return value.reshape(tokens // PERIOD, PERIOD, -1)
-
-    if fast:
-        near[-1] = after(near[-1], out_second)
     queries, kv_window = project(place, qkv_sources, near)
     if fast:
         up_second_piece = flip(after(up_first_piece, queries), 2)
-    grad_out = by_slot(tokens_here[:, D : 2 * D].astype(f32))
-    keep = by_slot(tokens_here[:, 2 * D : 2 * D + 1].astype(f32))
-    grad_mlp = grad_out * gate_mlp * keep
-    grad_mlp = grad_mlp.reshape(tokens, D).astype(bf16)
 
     def row_list(value):
         if rows == 2:
@@ -785,7 +820,6 @@
         return [lax.all_gather(value, "fsdp", axis=0, tiled=True)]
 
     grad_mlps = row_list(grad_mlp)
-    queries = after(queries, grad_mlp)
     merged, attn_proj, mid_state, normed_mid = attend(
         place,
         out_sources,
@@ -794,14 +828,12 @@
         bias,
         head_slots,
         tokens_here,
-        gate_attn,
-        shift_mlp,
-        scale_mlp,
+        *mods,
     )
 
     mids = row_list(normed_mid)
     if fast:
-        up_pieces = spread(up_first_piece, after(up_second_piece, merged))
+        up_pieces = spread(up_first_piece, after(up_second_piece, mids[1]))
         chunks = hidden_part // chunk
         up_sources = [
             (up_weight, (half, chunk), lambda i, place: (0, place[0] * chunks + i), None, 0)
@@ -817,7 +849,7 @@
     channels = lax.dynamic_slice_in_dim(
         jnp.repeat(tiled(channels), CHAN_GROUP, axis=2), row_at * hidden_part, hidden_part, 2
     )
-    hidden_act, grad_pre, grad_own, grad_low, out_own, out_low = feed(
+    hidden_act, grad_pre, grad_own, out_own, low = feed(
         place,
         up_sources,
         mids,
@@ -829,20 +861,13 @@
         low_rows,
     )
 
-    def own_sum(own, low):
-        if rows == 2:
-            return own, cross(low)
-        low = low.reshape(rows, tokens, D)
+    if rows == 2:
+        low = cross(low)
+    else:
+        low = low.reshape(rows, tokens, 2 * D)
         low = lax.psum_scatter(low, "fsdp", scatter_dimension=0, tiled=True)
-        return jnp.zeros_like(own), low.reshape(tokens, D)
-
-    grad_own, grad_other = own_sum(grad_own, grad_low)
-    out_own, out_other = own_sum(out_own, out_low)
-    mlp_out = out_own + out_other.astype(f32)
-    kept_out = by_slot(mlp_out) * keep
-    block_out = (by_slot(mid_state) + gate_mlp * kept_out).reshape(tokens, D)
-    block_out = block_out.astype(bf16)
-    gate_mlp_sum = jnp.sum(grad_out * kept_out, axis=0)
+        low = low.reshape(tokens, 2 * D)
+        grad_own, out_own = jnp.zeros_like(grad_own), jnp.zeros_like(out_own)
 
     if fast:
 
@@ -863,16 +888,16 @@
         grad_own = after(grad_own, down_parts)
         down_first = (flip(down_parts[0], 2), flip(down_parts[2], 4))
 
-    grad_mid, own_pack, pack, grad_heads, mid_sums = mid_back(
+    grad_mid, own_pack, pack, grad_heads, block_out, mid_sums = mid_back(
         place,
         out_sources,
         grad_own,
-        grad_other,
+        out_own,
+        low,
         mid_state,
         attn_proj,
         tokens_here,
-        scale_mlp,
-        gate_attn,
+        *mods,
         head_slots,
         merged,
         normed_in,
@@ -952,25 +977,22 @@
             half,
         )
         up_first = (flip(up_parts[0], 2), flip(up_parts[2], 4))
-        arrivals[0] = after(arrivals[0], up_parts, q_crossed, q_side, out_other)
+        arrivals[0] = after(arrivals[0], up_parts, q_side)
     grad_kv = parts[0].astype(f32)
     for arrival in arrivals:
         grad_kv = grad_kv + arrival.astype(f32)
     grad_kv = grad_kv.astype(bf16)
     if fast:
         grad_queries, down_second = lax.optimization_barrier((grad_queries, down_second))
-    input_grad, in_sums = in_back(
-        place, qkv_sources, grad_queries, grad_kv, tokens_here, scale_attn, grad_mid
-    )
-
+    both_out, in_sums = in_back(
+        place, qkv_sources, grad_queries, grad_kv, tokens_here, *mods, grad_mid, block_out
+    )
     if fast:
         kv_crossed = cross(grad_kv)
         down_second = after(down_second, in_sums)
         down_send, down_keep = third_step([step[1] for step in down_steps], down_second)
         down_last = flip(down_send, 8)
-        kv_crossed, in_sums, down_last = lax.optimization_barrier(
-            (kv_crossed, in_sums, down_last)
-        )
+        kv_crossed, in_sums = lax.optimization_barrier((kv_crossed, in_sums))
         up_first, grad_kv, q_crossed_late, ignored = lax.optimization_barrier(
             (up_first, grad_kv, q_crossed, kv_crossed)
         )
@@ -980,7 +1002,7 @@
         sums = jnp.sum(sums, axis=1) if repeats > 1 else sums[:, 0]
         return jnp.einsum("sc,nsd->cnd", selector, sums, precision=highest).astype(bf16)
 
-    mod_grads = jnp.concatenate([in_sums, mid_sums, gate_mlp_sum[None]], axis=0)
+    mod_grads = jnp.concatenate([in_sums, mid_sums], axis=0)
     if not fast:
 
         def product(acts, grads):
@@ -1034,15 +1056,14 @@
             [reduced(qkv_parts[1], qkv_first[0]), reduced(qkv_parts[3], qkv_first[1])]
         )
         qkv_second = [flip(send, bit) for send, ignored, bit in qkv_steps]
-        up_second, block_out, input_grad, mod_grads, ignored = lax.optimization_barrier(
-            (up_second, block_out, input_grad, mod_grads, qkv_parts)
+        up_second, mod_grads, down_last, ignored = lax.optimization_barrier(
+            (up_second, mod_grads, down_last, qkv_parts)
         )
+        qkv_sends = [step[0] for step in qkv_steps]
         up_send, up_keep = third_step([step[1] for step in up_steps], up_second)
         qkv_send, qkv_keep = third_step([step[1] for step in qkv_steps], qkv_second)
-        up_last, ignored = lax.optimization_barrier(
-            (flip(up_send, 8), [send for send, ignored, ignored in qkv_steps])
-        )
         down_grad = jnp.transpose(down_keep.astype(f32) + down_last.astype(f32))
+        up_last, ignored = lax.optimization_barrier((flip(up_send, 8), qkv_send))
         qkv_grad = jnp.transpose(qkv_keep.astype(f32) + flip(qkv_send, 8).astype(f32))
         mixed = up_keep.astype(f32) + up_last.astype(f32)
         up_rows, out_rows = hidden // seq, D // seq
@@ -1067,7 +1088,7 @@
         sent_sum = [jnp.where(first_core, quarters[i + 1], quarters[i]) for i in (0, 2)]
         kept_sum, sent_sum = (jnp.stack(value) for value in (kept_sum, sent_sum))
         mod_grads = (kept_sum.astype(f32) + flip(sent_sum, 1).astype(f32)).astype(bf16)
-        for bit, ahead in ((2, [send for send, ignored, ignored in qkv_steps]), (4, qkv_send), (8, ())):
+        for bit, ahead in ((8, ()), (2, qkv_sends), (4, qkv_send)):
             mod_grads = (mod_grads.astype(f32) + flip(mod_grads, bit).astype(f32)).astype(bf16)
             mod_grads = after(mod_grads, ahead)
         own = pick(mod_grads[0], mod_grads[1])
@@ -1081,11 +1102,9 @@
         mod_grads = lax.psum(mod_grads, "seq")
         split = jnp.transpose(mod_grads.reshape(crops, rows, columns), (1, 0, 2))
         mod_grads = lax.all_to_all(split, "fsdp", 0, 0).reshape(rows * crops, columns)
-    ada_grad = lax.dot_general(
-        cond_rows, mod_grads, (((0,), (0,)), ((), ())), preferred_element_type=f32
-    )
-
-    both_out = from_slots(jnp.concatenate([block_out, input_grad], axis=1), f32)
+    ada_grad = outer(cond_rows, mod_grads)
+
+    both_out = from_slots(both_out, f32, *(qkv_sends if fast else ()))
     block_out, input_grad = both_out[:, :D].astype(bf16), both_out[:, D:]
     return (
         block_out[None],

time: 346 us -> 320 us (0.925)
  the two profiles are of different devices: /device:TPU:0 before, /device:TPU:2 now
where the time goes in v4:
time: 320 us; the launch traced here: 314 us
  Pallas kernels  102 us (32%)
  waiting for transfers between devices  79.9 us (25%)
  starting transfers between devices  76.4 us (24%)
  other arithmetic  23.6 us (7%)
  local copies, waits for them, and re-layouts  22.3 us (7%)
  matrix products  8.2 us (3%)
    ppermute x46, waiting for transfers between devices, flip(): return lax.ppermute(value, 'seq', [(i, i ^ bit) for i in range(seq)])  40.3 us
    pallas_call x4, Pallas kernels, staged_call(): pl.pallas_call(functools.partial(kernel, parts=parts), out_shape=out_shap...  37.1 us
    ppermute x46, starting transfers between devices, flip(): return lax.ppermute(value, 'seq', [(i, i ^ bit) for i in range(seq)])  36.5 us
    pallas_call x3, Pallas kernels, term(): pl.pallas_call(functools.partial(term_kernel, layout=layout, outputs=2),...  25.2 us
    ppermute x13, waiting for transfers between devices, cross(): return lax.ppermute(value, 'fsdp', [(0, 1), (1, 0)])  24 us
    ppermute x13, starting transfers between devices, cross(): return lax.ppermute(value, 'fsdp', [(0, 1), (1, 0)])  15.3 us
    pallas_call x1, Pallas kernels, feed(): pl.pallas_call(functools.partial(feed_kernel, parts=parts, arrays=len(mid...  14.7 us
    pallas_call x1, Pallas kernels, attend_back(): pl.pallas_call(attend_back_kernel, out_shape=outs, in_specs=[VMEM_SPEC] *...  13.1 us
  transfers between devices with their start and end apart: 66, of which 26 were waited for; matrix products, arithmetic and copies ran while one was open for 14% of the time, Pallas kernels for 28%

profile of v4, /device:TPU:2, one launch (start us, length us, event | category | flops | bytes accessed | tf_op | source)
XLA Modules:
  0.0 314.2 jit_solution(17907045876470853310)
XLA Ops:
  7.9 5.9 %all-to-all-start = ((bf16[16,8,2432]{2,1,0:T(8,128)(2,1)}), bf16[16,8,2432]{2,1,0:T(8,128)(2,1)S(1)}, u32[]{:S(2)}, u32[]{:S(2)}) async-start(bf16[16,8,2432]{2,1,0:T(8,128)(2,1)} %fusion.2), calls=%async_computation | async-start | bytes 1245184 | tf_op jit(solution)/shard_map/all_to_all | solution.py:662
  15.7 4.6 %fusion = f32[2,16,3456]{2,1,0:T(8,128)S(1)} fusion(bf16[2,16,1152]{2,1,0:T(8,128)(2,1)S(1)} %fusion.32, bf16[1152,3456]{1,0:T(8,128)(2,1)} %param.25), kind=kOutput, calls=%fused_computation | convolution fusion | flops 254803968 | bytes 8478720 | tf_op jit(solution)/shard_map/dot_general | solution.py:718
  32.0 4.4 %collective-permute-done.8.refs_7_ = bf16[144,1152]{1,0:T(8,128)(2,1)} collective-permute-done((bf16[144,1152]{1,0:T(8,128)(2,1)}, bf16[144,1152]{1,0:T(8,128)(2,1)}, u32[]{:S(2)}, u32[]{:S(2)}) %collective-permute-start.8) | collective-permute-done | bytes 331808 | tf_op jit(solution)/shard_map/ppermute | solution.py:648
  37.8 3.2 %collective-permute-done.6.refs_5_.refs_3_ = bf16[144,2304]{1,0:T(8,128)(2,1)S(1)} collective-permute-done((bf16[144,2304]{1,0:T(8,128)(2,1)S(1)}, bf16[144,2304]{1,0:T(8,128)(2,1)S(1)}, u32[]{:S(2)}, u32[]{:S(2)}) %collective-permute-start.6) | collective-permute-done | bytes 663584 | tf_op jit(solution)/shard_map/ppermute | solution.py:645
  43.4 3.8 %collective-permute-start.13 = (bf16[128,1152]{1,0:T(8,128)(2,1)}, bf16[128,1152]{1,0:T(8,128)(2,1)}, u32[]{:S(2)}, u32[]{:S(2)}) collective-permute-start(bf16[128,1152]{1,0:T(8,128)(2,1)} %get-tuple-element.89.refs_11_.refs_15_), channel_id=1, source_target_pairs={{0,4},{2,6},{4,12},{6,14},{12,8},{14,10},{8,16},{10,18},{16,20},{1... | collective-permute-start | bytes 884744 | tf_op jit(solution)/shard_map/ppermute | solution.py:654
  51.4 5.2 %collective-permute-done.14.refs_14_ = bf16[128,1152]{1,0:T(8,128)(2,1)} collective-permute-done((bf16[128,1152]{1,0:T(8,128)(2,1)}, bf16[128,1152]{1,0:T(8,128)(2,1)}, u32[]{:S(2)}, u32[]{:S(2)}) %collective-permute-start.14) | collective-permute-done | bytes 294944 | tf_op jit(solution)/shard_map/ppermute | solution.py:654
  63.6 11.2 %project.1 = (bf16[128,1152]{1,0:T(8,128)(2,1)}, bf16[640,2304]{1,0:T(8,128)(2,1)}) custom-call(s32[8]{0:T(128)} %stack.77.place_ref, bf16[576,3456]{1,0:T(8,128)(2,1)} %refs_0_.9, bf16[288,1152]{1,0:T(8,128)(2,1)} %copy-done.8, bf16[288,1152]{1,0:T(8,128)(2,1)} %copy-done.9, bf16[144,2304]{1,0:T(8,128)(2,1)} %copy-done.1, bf16[144,2304]{1,0:T(8,128)(2,1)} %copy-done.3, ...), custom_call_target="tpu_custom_call" | custom-call | flops 1 | bytes 1 | tf_op jit(solution)/shard_map/project/pallas_call | solution.py:73
  77.5 10.5 %attend.1 = (bf16[128,1152]{1,0:T(8,128)(2,1)}, f32[128,1152]{1,0:T(8,128)}, f32[128,1152]{1,0:T(8,128)}, bf16[128,1152]{1,0:T(8,128)(2,1)}) custom-call(s32[8]{0:T(128)} %stack.77.place_ref, bf16[576,1152]{1,0:T(8,128)(2,1)} %refs_0_.8, bf16[144,2304]{1,0:T(8,128)(2,1)} %copy-done.1, bf16[144,2304]{1,0:T(8,128)(2,1)} %copy-done.3, ...), custom_call_target="tpu_custom_call" | custom-call | flops 1 | bytes 1 | tf_op jit(solution)/shard_map/attend/pallas_call | solution.py:73
  90.1 8.0 %collective-permute-done.19.refs_6_.refs_3_ = bf16[128,1152]{1,0:T(8,128)(2,1)S(1)} collective-permute-done((bf16[128,1152]{1,0:T(8,128)(2,1)}, bf16[128,1152]{1,0:T(8,128)(2,1)S(1)}, u32[]{:S(2)}, u32[]{:S(2)}) %collective-permute-start.19) | collective-permute-done | bytes 294944 | tf_op jit(solution)/shard_map/ppermute | solution.py:648
  99.3 4.3 %collective-permute-done.22.refs_8_.refs_1_ = bf16[128,1152]{1,0:T(8,128)(2,1)S(1)} collective-permute-done((bf16[128,1152]{1,0:T(8,128)(2,1)S(1)}, bf16[128,1152]{1,0:T(8,128)(2,1)S(1)}, u32[]{:S(2)}, u32[]{:S(2)}) %collective-permute-start.22) | collective-permute-done | bytes 294944 | tf_op jit(solution)/shard_map/ppermute | solution.py:648
  106.0 14.7 %feed.1 = (bf16[256,2304]{1,0:T(8,128)(2,1)}, bf16[256,2304]{1,0:T(8,128)(2,1)}, f32[128,1152]{1,0:T(8,128)}, f32[128,1152]{1,0:T(8,128)}, bf16[128,2304]{1,0:T(8,128)(2,1)}) custom-call(s32[8]{0:T(128)} %stack.77.place_ref, bf16[576,4608]{1,0:T(8,128)(2,1)} %refs_0_.7, bf16[144,2304]{1,0:T(8,128)(2,1)} %collective-permute-done.16.refs_1_, ...), custom_call_target="tpu_custom_call" | custom-call | flops 1 | bytes 1 | tf_op jit(solution)/shard_map/feed/pallas_call | solution.py:346
  124.9 7.7 %term.3 = (bf16[4,32,2304]{2,1,0:T(8,128)(2,1)}, bf16[4,32,2304]{2,1,0:T(8,128)(2,1)}, bf16[4,40,2304]{2,1,0:T(8,128)(2,1)}, bf16[4,40,2304]{2,1,0:T(8,128)(2,1)}) custom-call(s32[8]{0:T(128)} %stack.77.place_ref, bf16[128,1152]{1,0:T(8,128)(2,1)} %get-tuple-element.98.refs_7_.refs_0_, bf16[128,1152]{1,0:T(8,128)(2,1)} %copy-done.23, ...), custom_call_target="tpu_custom_call" | custom-call | flops 1 | bytes 1 | tf_op jit(solution)/shard_map/term/pallas_call | solution.py:542
  133.6 3.2 %collective-permute-done.25.refs_7_ = bf16[128,2304]{1,0:T(8,128)(2,1)S(1)} collective-permute-done((bf16[128,2304]{1,0:T(8,128)(2,1)}, bf16[128,2304]{1,0:T(8,128)(2,1)S(1)}, u32[]{:S(2)}, u32[]{:S(2)}) %collective-permute-start.25) | collective-permute-done | bytes 589856 | tf_op jit(solution)/shard_map/ppermute | solution.py:648
  137.6 6.7 %mid_back.1 = (f32[128,1152]{1,0:T(8,128)}, bf16[128,2304]{1,0:T(8,128)(2,1)}, bf16[128,2304]{1,0:T(8,128)(2,1)}, bf16[128,1152]{1,0:T(8,128)(2,1)}, bf16[128,1152]{1,0:T(8,128)(2,1)}, /*index=5*/f32[4,16,1152]{2,1,0:T(8,128)}) custom-call(s32[8]{0:T(128)} %stack.77.place_ref, bf16[576,1152]{1,0:T(8,128)(2,1)} %refs_0_.8, bf16[144,2304]{1,0:T(8,128)(2,1)} %copy-done.1, ...), custom_call_target="tpu_custom_call" | custom-call | flops 1 | bytes 1 | tf_op jit(solution)/shard_map/mid_back/pallas_call | solution.py:73
  147.1 13.1 %attend_back.1 = (bf16[128,1152]{1,0:T(8,128)(2,1)}, bf16[128,2304]{1,0:T(8,128)(2,1)}, bf16[128,2304]{1,0:T(8,128)(2,1)}, bf16[128,2304]{1,0:T(8,128)(2,1)}, bf...) custom-call(bf16[128,1152]{1,0:T(8,128)(2,1)} %get-tuple-element.91.refs_5_.q_ref, ...), custom_call_target="tpu_custom_call" | custom-call | flops 1 | bytes 1 | tf_op jit(solution)/shard_map/attend_back/pallas_call | solution.py:278
  164.2 2.7 select_add_fusion
  166.9 3.4 %collective-permute-start.40 = (bf16[128,2304]{1,0:T(8,128)(2,1)}, bf16[128,2304]{1,0:T(8,128)(2,1)S(1)}, u32[]{:S(2)}, u32[]{:S(2)}) collective-permute-start(bf16[128,2304]{1,0:T(8,128)(2,1)} %get-tuple-element.163), channel_id=1, source_target_pairs={{0,4},{2,6},{4,12},{6,14},{12,8},{14,10},{8,16},{10,18},{16,20},{1... | collective-permute-start | bytes 1769480 | tf_op jit(solution)/shard_map/ppermute | solution.py:654
  172.7 2.6 collective-permute-start.34
  176.5 10.2 %term.4 = (bf16[4,176,576]{2,1,0:T(8,128)(2,1)}, bf16[4,176,576]{2,1,0:T(8,128)(2,1)}, bf16[4,184,576]{2,1,0:T(8,128)(2,1)}, bf16[4,184,576]{2,1,0:T(8,128)(2,1)}) custom-call(s32[8]{0:T(128)} %stack.77.place_ref, bf16[256,2304]{1,0:T(8,128)(2,1)} %get-tuple-element.115.refs_0_, bf16[256,2304]{1,0:T(8,128)(2,1)} %copy-done.16, ...), custom_call_target="tpu_custom_call" | custom-call | flops 1 | bytes 1 | tf_op jit(solution)/shard_map/term/pallas_call | solution.py:542
  188.4 6.4 %collective-permute-start.41 = (bf16[4,176,576]{2,1,0:T(8,128)(2,1)}, bf16[4,176,576]{2,1,0:T(8,128)(2,1)S(1)}, u32[]{:S(2)}, u32[]{:S(2)}) collective-permute-start(bf16[4,176,576]{2,1,0:T(8,128)(2,1)} %get-tuple-element.129), channel_id=1, source_target_pairs={{0,4},{2,6},{4,0},{6,2},{8,12},{10,14},{12,8},{14,10},{16,20},{18,... | collective-permute-start | bytes 2433032 | tf_op jit(solution)/shard_map/ppermute | solution.py:645
  200.1 8.7 %in_back.1 = (bf16[128,2304]{1,0:T(8,128)(2,1)}, f32[2,16,1152]{2,1,0:T(8,128)}) custom-call(s32[8]{0:T(128)} %stack.77.place_ref, bf16[576,3456]{1,0:T(8,128)(2,1)} %refs_0_.9, bf16[288,1152]{1,0:T(8,128)(2,1)} %copy-done.8, bf16[288,1152]{1,0:T(8,128)(2,1)} %copy-done.9, bf16[144,2304]{1,0:T(8,128)(2,1)} %copy-done.1, bf16[144,2304]{1,0:T(8,128)(2,1)} %copy-done.3, ...), custom_call_target="tpu_custom_call" | custom-call | flops 1 | bytes 1 | tf_op jit(solution)/shard_map/in_back/pallas_call | solution.py:73
  214.7 2.8 collective-permute-done.42
  224.0 4.5 %all-to-all-start.1 = ((bf16[16,8,2304]{2,1,0:T(8,128)(2,1)}), bf16[16,8,2304]{2,1,0:T(8,128)(2,1)}, u32[]{:S(2)}, u32[]{:S(2)}) async-start(bf16[16,8,2304]{2,1,0:T(8,128)(2,1)} %bitcast.186), calls=%async_computation.1 | async-start | bytes 1179648 | tf_op jit(solution)/shard_map/all_to_all | solution.py:666
  229.5 7.3 %term.5 = (bf16[4,104,576]{2,1,0:T(8,128)(2,1)}, bf16[4,104,576]{2,1,0:T(8,128)(2,1)}, bf16[4,112,576]{2,1,0:T(8,128)(2,1)}, bf16[4,112,576]{2,1,0:T(8,128)(2,1)}) custom-call(s32[8]{0:T(128)} %stack.77.place_ref, bf16[128,1152]{1,0:T(8,128)(2,1)} %get-tuple-element.126.refs_11_.refs_0_, bf16[128,2304]{1,0:T(8,128)(2,1)} %add_convert_fusion.3.refs_12_.refs_1_, ...), custom_call_target="tpu_custom_call" | custom-call | flops 1 | bytes 1 | tf_op jit(solution)/shard_map/term/pallas_call | solution.py:542
  240.3 5.0 %collective-permute-done.55 = bf16[72,2304]{1,0:T(8,128)(2,1)} collective-permute-done((bf16[72,2304]{1,0:T(8,128)(2,1)}, bf16[72,2304]{1,0:T(8,128)(2,1)}, u32[]{:S(2)}, u32[]{:S(2)}) %collective-permute-start.55) | collective-permute-done | bytes 331808 | tf_op jit(solution)/shard_map/ppermute | solution.py:645
  247.7 3.0 collective-permute-start.56
  250.7 11.0 %collective-permute-done.59 = bf16[2,16,1728]{2,1,0:T(8,128)(2,1)S(1)} collective-permute-done((bf16[2,16,1728]{2,1,0:T(8,128)(2,1)S(1)}, bf16[2,16,1728]{2,1,0:T(8,128)(2,1)S(1)}, u32[]{:S(2)}, u32[]{:S(2)}) %collective-permute-start.59) | collective-permute-done | bytes 110624 | tf_op jit(solution)/shard_map/ppermute | solution.py:645
  267.6 4.3 %collective-permute-start.50 = (bf16[2,104,576]{2,1,0:T(8,128)(2,1)}, bf16[2,104,576]{2,1,0:T(8,128)(2,1)}, u32[]{:S(2)}, u32[]{:S(2)}) collective-permute-start(bf16[2,104,576]{2,1,0:T(8,128)(2,1)} %dynamic-slice_bitcast_fusion.5), channel_id=1, source_target_pairs={{0,8},{2,10},{4,12},{6,14},{8,0},{10,2},{12,4},{14,6},{16,24},{18,... | collective-permute-start | bytes 718856 | tf_op jit(solution)/shard_map/ppermute | solution.py:645
  275.8 6.4 %collective-permute-done.61 = bf16[2,16,1728]{2,1,0:T(8,128)(2,1)S(1)} collective-permute-done((bf16[2,16,1728]{2,1,0:T(8,128)(2,1)S(1)}, bf16[2,16,1728]{2,1,0:T(8,128)(2,1)S(1)}, u32[]{:S(2)}, u32[]{:S(2)}) %collective-permute-start.61) | collective-permute-done | bytes 110624 | tf_op jit(solution)/shard_map/ppermute | solution.py:645
  286.2 4.3 %collective-permute-start.57 = (bf16[288,576]{1,0:T(8,128)(2,1)S(1)}, bf16[288,576]{1,0:T(8,128)(2,1)S(1)}, u32[]{:S(2)}, u32[]{:S(2)}) collective-permute-start(bf16[288,576]{1,0:T(8,128)(2,1)S(1)} %pad_maximum_fusion.2), channel_id=1, source_target_pairs={{0,0},{1,16},{2,2},{3,18},{4,4},{5,20},{6,6},{7,22},{8,8},{9,24},{... | collective-permute-start | bytes 995336 | tf_op jit(solution)/shard_map/ppermute | solution.py:1081
  292.7 9.1 %outer.1 = f32[1152,3456]{1,0:T(8,128)} custom-call(bf16[32,1152]{1,0:T(8,128)(2,1)} %bitcast.185, bf16[32,3456]{1,0:T(8,128)(2,1)} %pad_maximum_fusion.3.right_ref), custom_call_target="tpu_custom_call" | custom-call | flops 1 | bytes 1 | tf_op jit(solution)/shard_map/outer/pallas_call | solution.py:561
  302.7 10.4 %collective-permute-done.57 = bf16[288,576]{1,0:T(8,128)(2,1)S(1)} collective-permute-done((bf16[288,576]{1,0:T(8,128)(2,1)S(1)}, bf16[288,576]{1,0:T(8,128)(2,1)S(1)}, u32[]{:S(2)}, u32[]{:S(2)}) %collective-permute-start.57) | collective-permute-done | bytes 331808 | tf_op jit(solution)/shard_map/ppermute | solution.py:1081
  (338 shorter events, 103.7 us)
Async XLA Ops:
  4.6 16.7 %collective-permute-start.1 = (bf16[144,2304]{1,0:T(8,128)(2,1)S(1)}, bf16[144,2304]{1,0:T(8,128)(2,1)S(1)}, u32[]{:S(2)}, u32[]{:S(2)}) collective-permute-start(bf16[144,2304]{1,0:T(8,128)(2,1)S(1)} %pad_maximum_fusion), channel_id=1, source_target_pairs={{0,1},{1,0},{2,3},{3,2},{4,5},{5,4},{6,7},{7,6},{8,9},{9,8},{10,11... | collective-permute-start | bytes 1990664 | tf_op jit(solution)/shard_map/ppermute | solution.py:648
  7.9 29.8 %all-to-all-start = ((bf16[16,8,2432]{2,1,0:T(8,128)(2,1)}), bf16[16,8,2432]{2,1,0:T(8,128)(2,1)S(1)}, u32[]{:S(2)}, u32[]{:S(2)}) async-start(bf16[16,8,2432]{2,1,0:T(8,128)(2,1)} %fusion.2), calls=%async_computation | async-start | bytes 1245184 | tf_op jit(solution)/shard_map/all_to_all | solution.py:662
  23.7 17.2 %collective-permute-start.6 = (bf16[144,2304]{1,0:T(8,128)(2,1)S(1)}, bf16[144,2304]{1,0:T(8,128)(2,1)S(1)}, u32[]{:S(2)}, u32[]{:S(2)}) collective-permute-start(bf16[144,2304]{1,0:T(8,128)(2,1)S(1)} %collective-permute-done.1.refs_3_.refs_1_), channel_id=1, source_target_pairs={{0,4},{2,6},{4,0},{6,2},{8,12},{10,14},{12,8},{14,10},{16,20},{18,... | collective-permute-start | bytes 1990664 | tf_op jit(solution)/shard_map/ppermute | solution.py:645
  28.4 28.2 %collective-permute-start.5 = (bf16[144,2304]{1,0:T(8,128)(2,1)S(1)}, bf16[144,2304]{1,0:T(8,128)(2,1)S(1)}, u32[]{:S(2)}, u32[]{:S(2)}) collective-permute-start(bf16[144,2304]{1,0:T(8,128)(2,1)S(1)} %collective-permute-done.1.refs_3_.refs_1_), channel_id=1, source_target_pairs={{0,2},{2,0},{4,6},{6,4},{8,10},{10,8},{12,14},{14,12},{16,18},{18,... | collective-permute-start | bytes 1990664 | tf_op jit(solution)/shard_map/ppermute | solution.py:645
  30.5 18.8 %collective-permute-start.3 = (bf16[288,1152]{1,0:T(8,128)(2,1)}, bf16[288,1152]{1,0:T(8,128)(2,1)S(1)}, u32[]{:S(2)}, u32[]{:S(2)}) collective-permute-start(bf16[288,1152]{1,0:T(8,128)(2,1)} %constant_dynamic-slice_fusion.1), channel_id=1, source_target_pairs={{0,1},{1,0},{2,3},{3,2},{4,5},{5,4},{6,7},{7,6},{8,9},{9,8},{10,11... | collective-permute-start | bytes 1990664 | tf_op jit(solution)/shard_map/ppermute | solution.py:648
  43.4 15.0 %collective-permute-start.13 = (bf16[128,1152]{1,0:T(8,128)(2,1)}, bf16[128,1152]{1,0:T(8,128)(2,1)}, u32[]{:S(2)}, u32[]{:S(2)}) collective-permute-start(bf16[128,1152]{1,0:T(8,128)(2,1)} %get-tuple-element.89.refs_11_.refs_15_), channel_id=1, source_target_pairs={{0,4},{2,6},{4,12},{6,14},{12,8},{14,10},{8,16},{10,18},{16,20},{1... | collective-permute-start | bytes 884744 | tf_op jit(solution)/shard_map/ppermute | solution.py:654
  56.6 18.1 %collective-permute-start.16 = (bf16[144,2304]{1,0:T(8,128)(2,1)S(1)}, bf16[144,2304]{1,0:T(8,128)(2,1)}, u32[]{:S(2)}, u32[]{:S(2)}) collective-permute-start(bf16[144,2304]{1,0:T(8,128)(2,1)S(1)} %dynamic_slice.85), channel_id=1, source_target_pairs={{0,1},{1,0},{2,3},{3,2},{4,5},{5,4},{6,7},{7,6},{8,9},{9,8},{10,11... | collective-permute-start | bytes 1990664 | tf_op jit(solution)/shard_map/ppermute | solution.py:648
  74.7 23.4 %collective-permute-start.18 = (bf16[144,2304]{1,0:T(8,128)(2,1)}, bf16[144,2304]{1,0:T(8,128)(2,1)S(1)}, u32[]{:S(2)}, u32[]{:S(2)}) collective-permute-start(bf16[144,2304]{1,0:T(8,128)(2,1)} %collective-permute-done.16.refs_1_), channel_id=1, source_target_pairs={{0,4},{2,6},{4,0},{6,2},{8,12},{10,14},{12,8},{14,10},{16,20},{18,... | collective-permute-start | bytes 1990664 | tf_op jit(solution)/shard_map/ppermute | solution.py:645
  90.1 15.1 %collective-permute-start.17 = (bf16[144,2304]{1,0:T(8,128)(2,1)}, bf16[144,2304]{1,0:T(8,128)(2,1)S(1)}, u32[]{:S(2)}, u32[]{:S(2)}) collective-permute-start(bf16[144,2304]{1,0:T(8,128)(2,1)} %collective-permute-done.16.refs_1_), channel_id=1, source_target_pairs={{0,2},{2,0},{4,6},{6,4},{8,10},{10,8},{12,14},{14,12},{16,18},{18,... | collective-permute-start | bytes 1990664 | tf_op jit(solution)/shard_map/ppermute | solution.py:645
  120.9 15.8 %collective-permute-start.25 = (bf16[128,2304]{1,0:T(8,128)(2,1)}, bf16[128,2304]{1,0:T(8,128)(2,1)S(1)}, u32[]{:S(2)}, u32[]{:S(2)}) collective-permute-start(bf16[128,2304]{1,0:T(8,128)(2,1)} %get-tuple-element.108), channel_id=1, source_target_pairs={{0,1},{1,0},{2,3},{3,2},{4,5},{5,4},{6,7},{7,6},{8,9},{9,8},{10,11... | collective-permute-start | bytes 1769480 | tf_op jit(solution)/shard_map/ppermute | solution.py:648
  121.3 25.8 %collective-permute-start.27 = (bf16[256,2304]{1,0:T(8,128)(2,1)}, bf16[256,2304]{1,0:T(8,128)(2,1)S(1)}, u32[]{:S(2)}, u32[]{:S(2)}) collective-permute-start(bf16[256,2304]{1,0:T(8,128)(2,1)} %get-tuple-element.115.refs_0_), channel_id=1, source_target_pairs={{0,2},{2,0},{4,6},{6,4},{8,10},{10,8},{12,14},{14,12},{16,18},{18,... | collective-permute-start | bytes 3538952 | tf_op jit(solution)/shard_map/ppermute | solution.py:645
  132.6 27.7 %collective-permute-start.31 = (bf16[4,40,2304]{2,1,0:T(8,128)(2,1)}, bf16[4,40,2304]{2,1,0:T(8,128)(2,1)S(1)}, u32[]{:S(2)}, u32[]{:S(2)}) collective-permute-start(bf16[4,40,2304]{2,1,0:T(8,128)(2,1)} %get-tuple-element.104), channel_id=1, source_target_pairs={{0,8},{2,10},{4,12},{6,14},{8,0},{10,2},{12,4},{14,6},{16,24},{18,... | collective-permute-start | bytes 2211848 | tf_op jit(solution)/shard_map/ppermute | solution.py:645
  144.3 16.0 %collective-permute-start.30 = (bf16[4,32,2304]{2,1,0:T(8,128)(2,1)S(1)}, bf16[4,32,2304]{2,1,0:T(8,128)(2,1)S(1)}, u32[]{:S(2)}, u32[]{:S(2)}) collective-permute-start(bf16[4,32,2304]{2,1,0:T(8,128)(2,1)S(1)} %copy-done.57), channel_id=1, source_target_pairs={{0,4},{2,6},{4,0},{6,2},{8,12},{10,14},{12,8},{14,10},{16,20},{18,... | collective-permute-start | bytes 1769480 | tf_op jit(solution)/shard_map/ppermute | solution.py:645
  146.8 15.6 %collective-permute-start.36 = (bf16[128,2304]{1,0:T(8,128)(2,1)}, bf16[128,2304]{1,0:T(8,128)(2,1)S(1)}, u32[]{:S(2)}, u32[]{:S(2)}) collective-permute-start(bf16[128,2304]{1,0:T(8,128)(2,1)} %get-tuple-element.113), channel_id=1, source_target_pairs={{0,1},{1,0},{2,3},{3,2},{4,5},{5,4},{6,7},{7,6},{8,9},{9,8},{10,11... | collective-permute-start | bytes 1769480 | tf_op jit(solution)/shard_map/ppermute | solution.py:648
  161.1 25.6 %collective-permute-start.35 = (bf16[128,2304]{1,0:T(8,128)(2,1)}, bf16[128,2304]{1,0:T(8,128)(2,1)S(1)}, u32[]{:S(2)}, u32[]{:S(2)}) collective-permute-start(bf16[128,2304]{1,0:T(8,128)(2,1)} %get-tuple-element.128), channel_id=1, source_target_pairs={{0,2},{2,0},{4,6},{6,4},{8,10},{10,8},{12,14},{14,12},{16,18},{18,... | collective-permute-start | bytes 1769480 | tf_op jit(solution)/shard_map/ppermute | solution.py:645
  166.9 29.3 %collective-permute-start.40 = (bf16[128,2304]{1,0:T(8,128)(2,1)}, bf16[128,2304]{1,0:T(8,128)(2,1)S(1)}, u32[]{:S(2)}, u32[]{:S(2)}) collective-permute-start(bf16[128,2304]{1,0:T(8,128)(2,1)} %get-tuple-element.163), channel_id=1, source_target_pairs={{0,4},{2,6},{4,12},{6,14},{12,8},{14,10},{8,16},{10,18},{16,20},{1... | collective-permute-start | bytes 1769480 | tf_op jit(solution)/shard_map/ppermute | solution.py:654
  170.3 25.9 %collective-permute-start.39 = (bf16[128,2304]{1,0:T(8,128)(2,1)}, bf16[128,2304]{1,0:T(8,128)(2,1)}, u32[]{:S(2)}, u32[]{:S(2)}) collective-permute-start(bf16[128,2304]{1,0:T(8,128)(2,1)} %get-tuple-element.164), channel_id=1, source_target_pairs={{4,0},{6,2},{12,4},{14,6},{8,12},{10,14},{16,8},{18,10},{20,16},{2... | collective-permute-start | bytes 1769480 | tf_op jit(solution)/shard_map/ppermute | solution.py:654
  172.7 23.1 %collective-permute-start.34 = (bf16[2,40,2304]{2,1,0:T(8,128)(2,1)}, bf16[2,40,2304]{2,1,0:T(8,128)(2,1)}, u32[]{:S(2)}, u32[]{:S(2)}) collective-permute-start(bf16[2,40,2304]{2,1,0:T(8,128)(2,1)} %dynamic-slice_bitcast_fusion.2), channel_id=1, source_target_pairs={{0,4},{2,6},{4,0},{6,2},{8,12},{10,14},{12,8},{14,10},{16,20},{18,... | collective-permute-start | bytes 1105928 | tf_op jit(solution)/shard_map/ppermute | solution.py:645
  186.8 25.5 %collective-permute-start.43 = (bf16[128,1152]{1,0:T(8,128)(2,1)S(1)}, bf16[128,1152]{1,0:T(8,128)(2,1)S(1)}, u32[]{:S(2)}, u32[]{:S(2)}) collective-permute-start(bf16[128,1152]{1,0:T(8,128)(2,1)S(1)} %copy-done.21), channel_id=1, source_target_pairs={{0,1},{1,0},{2,3},{3,2},{4,5},{5,4},{6,7},{7,6},{8,9},{9,8},{10,11... | collective-permute-start | bytes 884744 | tf_op jit(solution)/shard_map/ppermute | solution.py:648
  188.4 26.2 %collective-permute-start.41 = (bf16[4,176,576]{2,1,0:T(8,128)(2,1)}, bf16[4,176,576]{2,1,0:T(8,128)(2,1)S(1)}, u32[]{:S(2)}, u32[]{:S(2)}) collective-permute-start(bf16[4,176,576]{2,1,0:T(8,128)(2,1)} %get-tuple-element.129), channel_id=1, source_target_pairs={{0,4},{2,6},{4,0},{6,2},{8,12},{10,14},{12,8},{14,10},{16,20},{18,... | collective-permute-start | bytes 2433032 | tf_op jit(solution)/shard_map/ppermute | solution.py:645
  195.8 21.6 %collective-permute-start.42 = (bf16[4,184,576]{2,1,0:T(8,128)(2,1)}, bf16[4,184,576]{2,1,0:T(8,128)(2,1)S(1)}, u32[]{:S(2)}, u32[]{:S(2)}) collective-permute-start(bf16[4,184,576]{2,1,0:T(8,128)(2,1)} %get-tuple-element.131), channel_id=1, source_target_pairs={{0,8},{2,10},{4,12},{6,14},{8,0},{10,2},{12,4},{14,6},{16,24},{18,... | collective-permute-start | bytes 2543624 | tf_op jit(solution)/shard_map/ppermute | solution.py:645
  212.2 17.3 %collective-permute-start.47 = (bf16[128,2304]{1,0:T(8,128)(2,1)}, bf16[128,2304]{1,0:T(8,128)(2,1)}, u32[]{:S(2)}, u32[]{:S(2)}) collective-permute-start(bf16[128,2304]{1,0:T(8,128)(2,1)} %collective-permute-done.44.refs_3_), channel_id=1, source_target_pairs={{0,2},{2,0},{4,6},{6,4},{8,10},{10,8},{12,14},{14,12},{16,18},{18,... | collective-permute-start | bytes 1769480 | tf_op jit(solution)/shard_map/ppermute | solution.py:645
  219.0 26.3 %collective-permute-start.53 = (bf16[2,176,576]{2,1,0:T(8,128)(2,1)}, bf16[2,176,576]{2,1,0:T(8,128)(2,1)}, u32[]{:S(2)}, u32[]{:S(2)}) collective-permute-start(bf16[2,176,576]{2,1,0:T(8,128)(2,1)} %dynamic-slice_bitcast_fusion.1), channel_id=1, source_target_pairs={{0,8},{2,10},{4,12},{6,14},{8,0},{10,2},{12,4},{14,6},{16,24},{18,... | collective-permute-start | bytes 1216520 | tf_op jit(solution)/shard_map/ppermute | solution.py:645
  219.6 25.7 %collective-permute-start.54 = (bf16[2,184,576]{2,1,0:T(8,128)(2,1)S(1)}, bf16[2,184,576]{2,1,0:T(8,128)(2,1)S(1)}, u32[]{:S(2)}, u32[]{:S(2)}) collective-permute-start(bf16[2,184,576]{2,1,0:T(8,128)(2,1)S(1)} %dynamic-slice_bitcast_fusion), channel_id=1, source_target_pairs={{0,4},{2,6},{4,0},{6,2},{8,12},{10,14},{12,8},{14,10},{16,20},{18,... | collective-permute-start | bytes 1271816 | tf_op jit(solution)/shard_map/ppermute | solution.py:645
  223.0 22.3 %collective-permute-start.55 = (bf16[72,2304]{1,0:T(8,128)(2,1)}, bf16[72,2304]{1,0:T(8,128)(2,1)}, u32[]{:S(2)}, u32[]{:S(2)}) collective-permute-start(bf16[72,2304]{1,0:T(8,128)(2,1)} %fusion.26), channel_id=1, source_target_pairs={{0,16},{2,18},{4,20},{6,22},{8,24},{10,26},{12,28},{14,30},{16,0},... | collective-permute-start | bytes 995336 | tf_op jit(solution)/shard_map/ppermute | solution.py:645
  224.0 48.8 %all-to-all-start.1 = ((bf16[16,8,2304]{2,1,0:T(8,128)(2,1)}), bf16[16,8,2304]{2,1,0:T(8,128)(2,1)}, u32[]{:S(2)}, u32[]{:S(2)}) async-start(bf16[16,8,2304]{2,1,0:T(8,128)(2,1)} %bitcast.186), calls=%async_computation.1 | async-start | bytes 1179648 | tf_op jit(solution)/shard_map/all_to_all | solution.py:666
  236.8 29.8 %collective-permute-start.48 = (bf16[4,104,576]{2,1,0:T(8,128)(2,1)}, bf16[4,104,576]{2,1,0:T(8,128)(2,1)S(1)}, u32[]{:S(2)}, u32[]{:S(2)}) collective-permute-start(bf16[4,104,576]{2,1,0:T(8,128)(2,1)} %get-tuple-element.142), channel_id=1, source_target_pairs={{0,4},{2,6},{4,0},{6,2},{8,12},{10,14},{12,8},{14,10},{16,20},{18,... | collective-permute-start | bytes 1437704 | tf_op jit(solution)/shard_map/ppermute | solution.py:645
  238.8 33.1 %collective-permute-start.49 = (bf16[4,112,576]{2,1,0:T(8,128)(2,1)}, bf16[4,112,576]{2,1,0:T(8,128)(2,1)S(1)}, u32[]{:S(2)}, u32[]{:S(2)}) collective-permute-start(bf16[4,112,576]{2,1,0:T(8,128)(2,1)} %get-tuple-element.144), channel_id=1, source_target_pairs={{0,8},{2,10},{4,12},{6,14},{8,0},{10,2},{12,4},{14,6},{16,24},{18,... | collective-permute-start | bytes 1548296 | tf_op jit(solution)/shard_map/ppermute | solution.py:645
  247.7 36.6 %collective-permute-start.56 = (bf16[360,576]{1,0:T(8,128)(2,1)S(1)}, bf16[360,576]{1,0:T(8,128)(2,1)S(1)}, u32[]{:S(2)}, u32[]{:S(2)}) collective-permute-start(bf16[360,576]{1,0:T(8,128)(2,1)S(1)} %fusion.20), channel_id=1, source_target_pairs={{0,16},{2,18},{4,20},{6,22},{8,24},{10,26},{12,28},{14,30},{16,0},... | collective-permute-start | bytes 1244168 | tf_op jit(solution)/shard_map/ppermute | solution.py:645
  267.6 14.7 %collective-permute-start.50 = (bf16[2,104,576]{2,1,0:T(8,128)(2,1)}, bf16[2,104,576]{2,1,0:T(8,128)(2,1)}, u32[]{:S(2)}, u32[]{:S(2)}) collective-permute-start(bf16[2,104,576]{2,1,0:T(8,128)(2,1)} %dynamic-slice_bitcast_fusion.5), channel_id=1, source_target_pairs={{0,8},{2,10},{4,12},{6,14},{8,0},{10,2},{12,4},{14,6},{16,24},{18,... | collective-permute-start | bytes 718856 | tf_op jit(solution)/shard_map/ppermute | solution.py:645
  283.4 18.4 %collective-permute-start.52 = (bf16[216,576]{1,0:T(8,128)(2,1)S(1)}, bf16[216,576]{1,0:T(8,128)(2,1)S(1)}, u32[]{:S(2)}, u32[]{:S(2)}) collective-permute-start(bf16[216,576]{1,0:T(8,128)(2,1)S(1)} %fusion.29), channel_id=1, source_target_pairs={{0,16},{2,18},{4,20},{6,22},{8,24},{10,26},{12,28},{14,30},{16,0},... | collective-permute-start | bytes 746504 | tf_op jit(solution)/shard_map/ppermute | solution.py:645
  286.2 26.9 %collective-permute-start.57 = (bf16[288,576]{1,0:T(8,128)(2,1)S(1)}, bf16[288,576]{1,0:T(8,128)(2,1)S(1)}, u32[]{:S(2)}, u32[]{:S(2)}) collective-permute-start(bf16[288,576]{1,0:T(8,128)(2,1)S(1)} %pad_maximum_fusion.2), channel_id=1, source_target_pairs={{0,0},{1,16},{2,2},{3,18},{4,4},{5,20},{6,6},{7,22},{8,8},{9,24},{... | collective-permute-start | bytes 995336 | tf_op jit(solution)/shard_map/ppermute | solution.py:1081
  (98 other events, 683.4 us)

commit v5 on v4

--- a/solution.py
+++ b/solution.py
@@ -68,17 +68,51 @@
     return pl.BlockSpec(shape, lambda i, place: (0,) * len(shape))
 
 
+def copies_in(target_ref, place_ref, refs, parts, sems):
+    half = target_ref.shape[0] // 2
+    mine = place_ref[0]
+    copies = []
+    for index, (ref, (source_column, cols, step, column)) in enumerate(zip(refs, parts)):
+        rows = ref.shape[0]
+        if step == "all":
+            start = 0
+        elif step is None:
+            start = pl.multiple_of(mine * half, 16)
+        else:
+            part = place_ref[step[0]] ^ step[1]
+            start = pl.multiple_of((1 - mine) * half + part * rows, 16)
+        copies.append(
+            (
+                column,
+                pltpu.make_async_copy(
+                    ref.at[:, pl.ds(source_column, cols)],
+                    target_ref.at[pl.ds(start, rows), pl.ds(column, cols)],
+                    sems.at[index],
+                ),
+            )
+        )
+    return copies
+
+
+def wait_for(copies, column):
+    for at, copy in copies:
+        if at == column:
+            copy.wait()
+
+
 def staged_call(kernel, place, sources, inputs, out_shapes, scratch, name):
-    arrays, specs, parts = source_inputs(sources)
+    arrays = [source[0] for source in sources]
+    parts = [source[1:] for source in sources]
     return pl.pallas_call(
         functools.partial(kernel, parts=parts),
         out_shape=out_shapes,
         grid_spec=pltpu.PrefetchScalarGridSpec(
             num_scalar_prefetch=1,
             grid=(1,),
-            in_specs=specs + [whole(value.shape) for value in inputs],
+            in_specs=[pl.BlockSpec(memory_space=pl.ANY)] * len(arrays)
+            + [whole(value.shape) for value in inputs],
             out_specs=[whole(out.shape) for out in out_shapes],
-            scratch_shapes=scratch,
+            scratch_shapes=scratch + [pltpu.SemaphoreType.DMA((len(arrays),))],
         ),
         compiler_params=params(),
         cost_estimate=COST,
@@ -143,17 +177,23 @@
 
 def project_kernel(place_ref, *refs, parts):
     count = len(parts)
-    weight_ref, window_ref = refs[-2], refs[-1]
-    q_ref, kv_ref = refs[-4], refs[-3]
-    window_parts = refs[count:-4]
-    fill(weight_ref, place_ref, refs[:count], parts)
+    q_ref, kv_ref, weight_ref, window_ref, sems = refs[-5:]
+    window_parts = refs[count:-5]
+    copies = copies_in(weight_ref, place_ref, refs[:count], parts, sems)
+    for column in (D, 2 * D, 0):
+        for at, copy in copies:
+            if at == column:
+                copy.start()
     tokens = q_ref.shape[0]
     for index, part in enumerate(window_parts):
         window_ref[pl.ds(index * tokens, tokens), :] = part[...]
-    for start in range(0, 2 * D, 768):
-        kv_ref[:, pl.ds(start, 768)] = dot_nn(
-            window_ref[...], weight_ref[:, pl.ds(D + start, 768)]
-        ).astype(bf16)
+    for column in (D, 2 * D):
+        wait_for(copies, column)
+        for start in range(0, D, 384):
+            kv_ref[:, pl.ds(column - D + start, 384)] = dot_nn(
+                window_ref[...], weight_ref[:, pl.ds(column + start, 384)]
+            ).astype(bf16)
+    wait_for(copies, 0)
     for start in range(0, D, 384):
         q_ref[:, pl.ds(start, 384)] = dot_nn(
             window_parts[0][...], weight_ref[:, pl.ds(start, 384)]
@@ -181,6 +221,20 @@
     return low, min(width, D - low), start - low
 
 
+HEAD_GROUPS = ((0, 1), (2, 3), (4, 5), (6, 7), (8,), (9, 10), (11, 12), (13, 14), (15,))
+
+
+def group_window(heads):
+    windows = [head_window(head) for head in heads]
+    return windows[0][0], max(window[1] for window in windows), [window[2] for window in windows]
+
+
+def masked_rows(value, lanes):
+    zero = jnp.zeros((), value.dtype)
+    parts = [jnp.where(lane, value, zero) for lane in lanes]
+    return jnp.concatenate(parts, axis=0) if len(parts) > 1 else parts[0]
+
+
 def head_lanes(rows, width, first):
     lane = lax.broadcasted_iota(jnp.int32, (rows, width), 1)
     return (lane >= first) & (lane < first + HD)
@@ -189,27 +243,34 @@
 def attend_kernel(place_ref, *refs, parts):
     count = len(parts)
     q_ref, kv_ref, bias_ref, mask_ref, tokens_ref, own_ref, other_ref = refs[count : count + 7]
-    merged_ref, proj_ref, mid_ref, normed_ref, acc_ref, weight_ref = refs[count + 7 :]
+    merged_ref, proj_ref, mid_ref, normed_ref, acc_ref, weight_ref, sems = refs[count + 7 :]
     gate = mod_attn(place_ref, own_ref, other_ref, 2)
     shift = mod_mlp(place_ref, own_ref, other_ref, 0)
     scale = 1.0 + mod_mlp(place_ref, own_ref, other_ref, 1)
     tokens = q_ref.shape[0]
-    fill(weight_ref, place_ref, refs[:count], parts)
+    copies = copies_in(weight_ref, place_ref, refs[:count], parts, sems)
+    for ignored, copy in copies:
+        copy.start()
     acc_ref[...] = jnp.zeros_like(acc_ref)
-    for head in range(H):
-        low, width, first = head_window(head)
+    for heads in HEAD_GROUPS:
+        low, width, firsts = group_window(heads)
         window = pl.ds(low, width)
-        lanes = head_lanes(tokens, width, first)
-        query = jnp.where(lanes, q_ref[:, window], jnp.zeros((), bf16))
-        scores = dot_nt(query, kv_ref[:, window]) * score_scale + bias_ref[...]
+        lanes = [head_lanes(tokens, width, first) for first in firsts]
+        bias = jnp.concatenate([bias_ref[...]] * len(heads), axis=0)
+        query = masked_rows(q_ref[:, window], lanes)
+        scores = dot_nt(query, kv_ref[:, window]) * score_scale + bias
         top = jnp.max(scores, axis=1, keepdims=True)
         weights = jnp.exp(scores - top)
         probs = (weights * (1.0 / jnp.sum(weights, axis=1, keepdims=True))).astype(bf16)
         out = dot_nn(probs, kv_ref[:, pl.ds(D + low, width)])
-        acc_ref[:, window] += jnp.where(lanes, out, 0.0)
+        value = acc_ref[:, window]
+        for index, lane in enumerate(lanes):
+            value = value + jnp.where(lane, out[index * tokens : (index + 1) * tokens], 0.0)
+        acc_ref[:, window] = value
     for start in range(0, tokens, PERIOD):
         rows = pl.ds(start, PERIOD)
         merged_ref[rows, :] = (acc_ref[rows, :] * mask_ref[...]).astype(bf16)
+    wait_for(copies, 0)
     proj_ref[...] = dot_nn(merged_ref[...], weight_ref[...])
     for start in range(0, tokens, PERIOD):
         rows = pl.ds(start, PERIOD)
@@ -245,14 +306,15 @@
     dq_acc[...] = jnp.zeros_like(dq_acc)
     dk_acc[...] = jnp.zeros_like(dk_acc)
     dv_acc[...] = jnp.zeros_like(dv_acc)
-    for head in range(H):
-        low, width, first = head_window(head)
+    for heads in HEAD_GROUPS:
+        low, width, firsts = group_window(heads)
         window = pl.ds(low, width)
-        lanes = head_lanes(tokens, width, first)
-        query = jnp.where(lanes, q_ref[:, window], jnp.zeros((), bf16))
-        grad = jnp.where(lanes, grad_ref[:, window], jnp.zeros((), bf16))
+        lanes = [head_lanes(tokens, width, first) for first in firsts]
+        bias = jnp.concatenate([bias_ref[...]] * len(heads), axis=1)
+        query = masked_rows(q_ref[:, window], lanes)
+        grad = masked_rows(grad_ref[:, window], lanes)
         keys = kv_ref[:, window]
-        scores = dot_nt(keys, query) * score_scale + bias_ref[...]
+        scores = dot_nt(keys, query) * score_scale + bias
         top = jnp.max(scores, axis=0, keepdims=True)
         weights = jnp.exp(scores - top)
         probs = weights * (1.0 / jnp.sum(weights, axis=0, keepdims=True))
@@ -262,7 +324,11 @@
         grad_scores = (probs * (grad_probs - row_dot)).astype(bf16)
         dk_acc[:, window] += dot_nn(grad_scores, query)
         dv_acc[:, window] += dot_nn(probs_low, grad)
-        dq_acc[:, window] += jnp.where(lanes, dot_tn(grad_scores, keys), 0.0)
+        back = dot_tn(grad_scores, keys)
+        value = dq_acc[:, window]
+        for index, lane in enumerate(lanes):
+            value = value + jnp.where(lane, back[index * tokens : (index + 1) * tokens], 0.0)
+        dq_acc[:, window] = value
     dq_ref[...] = (dq_acc[...] * score_scale).astype(bf16)
     for index, dkv_ref in enumerate(dkv_refs):
         rows = pl.ds(index * tokens, tokens)
@@ -295,8 +361,8 @@
     count = len(parts)
     mid_refs, grad_refs = refs[count : count + arrays], refs[count + arrays : count + 2 * arrays]
     channel_ref, down_ref = refs[count + 2 * arrays : count + 2 * arrays + 2]
-    act_ref, pre_ref, grad_own, out_own, low_ref = refs[-8:-3]
-    weight_ref, grad_acc, out_acc = refs[-3:]
+    act_ref, pre_ref, grad_own, out_own, low_ref = refs[-12:-7]
+    weight_ref, grad_acc, out_acc, mid_all, grad_all, pre_acc, back_acc = refs[-7:]
     own_rows = grad_own.shape[0]
     step, steps = pl.program_id(0), pl.num_programs(0)
     rows, cols = act_ref.shape
@@ -307,16 +373,20 @@
     def _():
         grad_acc[...] = jnp.zeros_like(grad_acc)
         out_acc[...] = jnp.zeros_like(out_acc)
+        share = rows // arrays
+        for index in range(arrays):
+            part = pl.ds(index * share, share)
+            mid_all[part, :] = mid_refs[index][...]
+            grad_all[part, :] = grad_refs[index][...]
 
     fill(weight_ref, place_ref, refs[:count], parts)
     root = 0.7978845608028654
-    for group in range(groups):
-        span = pl.ds(group * tokens, tokens)
-        source, at = (group, 0) if arrays > 1 else (0, group * tokens)
-        part = pl.ds(at, tokens)
-        channels = jnp.concatenate([channel_ref[group]] * (tokens // PERIOD), axis=0)
-        pre = dot_nn(mid_refs[source][part, :], weight_ref[...])
-        grad_act = dot_nt(grad_refs[source][part, :], down_ref[...])
+    pre_acc[...] = dot_nn(mid_all[...], weight_ref[...])
+    back_acc[...] = dot_nt(grad_all[...], down_ref[...])
+    for group, start in [(g, t) for g in range(groups) for t in range(0, tokens, PERIOD)]:
+        span = pl.ds(group * tokens + start, PERIOD)
+        channels = channel_ref[group]
+        pre, grad_act = pre_acc[span, :], back_acc[span, :]
         square = pre * pre
         inner = jnp.tanh(root * (pre + 0.044715 * (square * pre)))
         half_sum = 0.5 + 0.5 * inner
@@ -368,6 +438,10 @@
                 pltpu.VMEM((D, chunk), bf16),
                 pltpu.VMEM((rows, D), f32),
                 pltpu.VMEM((rows, D), f32),
+                pltpu.VMEM((rows, D), bf16),
+                pltpu.VMEM((rows, D), bf16),
+                pltpu.VMEM((rows, chunk), f32),
+                pltpu.VMEM((rows, chunk), f32),
             ],
         ),
         compiler_params=params(),
@@ -383,7 +457,10 @@
     grad_mid_ref, own_pack_ref, pack_ref, heads_ref, block_ref, sums_ref = refs[
         count + 11 : count + 17
     ]
-    weight_ref, merged_ref = refs[count + 17 :]
+    weight_ref, merged_ref, sems = refs[count + 17 :]
+    copies = copies_in(weight_ref, place_ref, refs[:count], parts, sems)
+    for ignored, copy in copies:
+        copy.start()
     scale = 1.0 + mod_mlp(place_ref, mod_own, mod_other, 1)
     gate = mod_attn(place_ref, mod_own, mod_other, 2)
     out_gate = mod_mlp(place_ref, mod_own, mod_other, 2)
@@ -394,7 +471,6 @@
         own_pack_ref[:, pl.ds(index * half, half)] = jnp.where(first, low, high)
         pack_ref[:, pl.ds(index * half, half)] = jnp.where(first, high, low)
     tokens = own_ref.shape[0]
-    fill(weight_ref, place_ref, refs[:count], parts)
     sums = [jnp.zeros((PERIOD, D), f32) for ignored in range(4)]
     for start in range(0, tokens, PERIOD):
         rows = pl.ds(start, PERIOD)
@@ -415,6 +491,7 @@
             sums[index] += value
     for index in range(4):
         sums_ref[index] = sums[index]
+    wait_for(copies, 0)
     merged_ref[...] = dot_nt(pack_ref[:, pl.ds(D, D)], weight_ref[...])
     for start in range(0, tokens, PERIOD):
         rows = pl.ds(start, PERIOD)
@@ -445,16 +522,23 @@
     count = len(parts)
     dq_ref, dkv_ref, tokens_ref, mod_own, mod_other = refs[count : count + 5]
     grad_mid_ref, block_ref = refs[count + 5 : count + 7]
-    both_ref, sums_ref, weight_ref, grad_ref = refs[count + 7 :]
+    both_ref, sums_ref, weight_ref, grad_ref, sems = refs[count + 7 :]
     tokens = dq_ref.shape[0]
-    fill(weight_ref, place_ref, refs[:count], parts)
-    grad_ref[...] = dot_nt(dkv_ref[...], weight_ref[:, pl.ds(D, 2 * D)]) + dot_nt(
-        dq_ref[...], weight_ref[:, pl.ds(0, D)]
-    )
+    copies = copies_in(weight_ref, place_ref, refs[:count], parts, sems)
+    for column in (D, 2 * D, 0):
+        for at, copy in copies:
+            if at == column:
+                copy.start()
+    both_ref[:, pl.ds(0, D)] = block_ref[...]
+    wait_for(copies, D)
+    grad_ref[...] = dot_nt(dkv_ref[:, pl.ds(0, D)], weight_ref[:, pl.ds(D, D)])
+    wait_for(copies, 2 * D)
+    grad_ref[...] += dot_nt(dkv_ref[:, pl.ds(D, D)], weight_ref[:, pl.ds(2 * D, D)])
+    wait_for(copies, 0)
+    grad_ref[...] += dot_nt(dq_ref[...], weight_ref[:, pl.ds(0, D)])
     scale = 1.0 + mod_attn(place_ref, mod_own, mod_other, 1)
     shift_sum = jnp.zeros((PERIOD, D), f32)
     scale_sum = jnp.zeros((PERIOD, D), f32)
-    both_ref[:, pl.ds(0, D)] = block_ref[...]
     for start in range(0, tokens, PERIOD):
         rows = pl.ds(start, PERIOD)
         normed, inverse = normalized(tokens_ref[rows, pl.ds(0, D)].astype(f32))
@@ -551,8 +635,17 @@
     )(place, *arrays)
 
 
-def outer_kernel(left_ref, right_ref, out_ref):
-    out_ref[...] = dot_tn(left_ref[...], right_ref[...])
+def outer_kernel(left_ref, right_ref, out_ref, value_ref, sems):
+    copies = []
+    for index in range(value_ref.shape[0] // 128):
+        rows = pl.ds(index * 128, 128)
+        value_ref[rows, :] = dot_tn(left_ref[:, rows], right_ref[...])
+        copies.append(
+            pltpu.make_async_copy(value_ref.at[rows, :], out_ref.at[rows, :], sems.at[index])
+        )
+        copies[-1].start()
+    for copy in copies:
+        copy.wait()
 
 
 def outer(left, right):
@@ -561,12 +654,12 @@
     return pl.pallas_call(
         outer_kernel,
         out_shape=shaped(rows, columns),
-        grid=(rows // 128,),
-        in_specs=[
-            pl.BlockSpec((depth, 128), lambda i: (0, i)),
-            pl.BlockSpec((depth, columns), lambda i: (0, 0)),
+        in_specs=[VMEM_SPEC] * 2,
+        out_specs=pl.BlockSpec(memory_space=pl.ANY),
+        scratch_shapes=[
+            pltpu.VMEM((rows, columns), f32),
+            pltpu.SemaphoreType.DMA((rows // 128,)),
         ],
-        out_specs=pl.BlockSpec((128, columns), lambda i: (i, 0)),
         compiler_params=params(),
         cost_estimate=COST,
         name="outer",
@@ -751,25 +844,21 @@
         v_second = flip(v_first, 4)
         k_pieces, v_pieces = spread(k_first, k_second), spread(v_first, v_second)
         q_pieces = (q_first, flip(q_first, 1))
-        qkv_sources = [(qkv_weight, (half, 3 * D), block(0), None, 0)]
+        qkv_sources = [(qkv_weight, column, D, None, column) for column in (0, D, 2 * D)]
         for at, column, pieces in ((2, 0, q_pieces), (1, D, k_pieces), (5, 2 * D, v_pieces)):
             qkv_sources += [
-                (piece, (piece.shape[0], D), block(0), (at, step), column)
-                for step, piece in enumerate(pieces)
+                (piece, 0, D, (at, step), column) for step, piece in enumerate(pieces)
             ]
-        out_sources = [(out_weight, (half, D), block(0), None, 0)]
-        out_sources += [
-            (piece, (quarter, D), block(1), (1, step), 0)
-            for step, piece in enumerate(k_pieces)
-        ]
+        out_sources = [(out_weight, 0, D, None, 0)]
+        out_sources += [(piece, D, D, (1, step), 0) for step, piece in enumerate(k_pieces)]
         low_rows = tokens
     else:
         chunk = hidden_part
         qkv_full = lax.all_gather(qkv_weight, "fsdp", axis=0, tiled=True)
         out_full = lax.all_gather(out_weight, "fsdp", axis=0, tiled=True)
         up_part = lax.all_to_all(up_weight, "fsdp", 1, 0, tiled=True)
-        qkv_sources = [(qkv_full, (D, 3 * D), block(0), "all", 0)]
-        out_sources = [(out_full, (D, D), block(0), "all", 0)]
+        qkv_sources = [(qkv_full, column, D, "all", column) for column in (0, D, 2 * D)]
+        out_sources = [(out_full, 0, D, "all", 0)]
         up_sources = [(up_part, (D, hidden_part), block(0), "all", 0)]
         low_rows = rows * tokens
 
@@ -810,16 +899,18 @@
         jnp.repeat(jnp.dot(selector, head_mask[0].astype(f32), precision=highest), HD, axis=1)
     )
 
-    queries, kv_window = project(place, qkv_sources, near)
-    if fast:
-        up_second_piece = flip(after(up_first_piece, queries), 2)
-
     def row_list(value):
         if rows == 2:
             return [value, cross(value)]
         return [lax.all_gather(value, "fsdp", axis=0, tiled=True)]
 
     grad_mlps = row_list(grad_mlp)
+    if fast:
+        near[-1] = after(near[-1], grad_mlps[1])
+    queries, kv_window = project(place, qkv_sources, near)
+    if fast:
+        up_second_piece = flip(after(up_first_piece, queries), 2)
+
     merged, attn_proj, mid_state, normed_mid = attend(
         place,
         out_sources,

time: 320 us -> 310 us (0.969)
  Pallas kernels: 102 us -> 91.9 us
  starting transfers between devices: 76.4 us -> 80.4 us
    ppermute x46, starting transfers between devices: 36.5 us -> 42.5 us  [flip(): return lax.ppermute(value, 'seq', [(i, i ^ bit) for i in range(seq)])]
    pallas_call x4, Pallas kernels: 37.1 us -> 33.2 us  [staged_call(): pl.pallas_call(functools.partial(kernel, parts=parts), out_shape=out_shap...]
    unnamed x129 -> x125, local copies, waits for them, and re-layouts: 7.54 us -> 7.12 us
  transfers between devices with their start and end apart: 66 -> 66, of which waited for: 26 -> 27; matrix products, arithmetic and copies ran while one was open for 14% -> 14% of each run, Pallas kernels for 28% -> 26%
where the time goes in v5:
time: 310 us; the launch traced here: 306 us
  Pallas kernels  91.9 us (30%)
  starting transfers between devices  80.4 us (26%)
  waiting for transfers between devices  78.7 us (25%)
  other arithmetic  23.6 us (8%)
  local copies, waits for them, and re-layouts  21 us (7%)
  matrix products  8.2 us (3%)
    ppermute x46, starting transfers between devices, flip(): return lax.ppermute(value, 'seq', [(i, i ^ bit) for i in range(seq)])  42.5 us
    ppermute x46, waiting for transfers between devices, flip(): return lax.ppermute(value, 'seq', [(i, i ^ bit) for i in range(seq)])  39.3 us
    pallas_call x4, Pallas kernels, staged_call(): pl.pallas_call(functools.partial(kernel, parts=parts), out_shape=out_shap...  33.2 us
    pallas_call x3, Pallas kernels, term(): pl.pallas_call(functools.partial(term_kernel, layout=layout, outputs=2),...  25.2 us
    ppermute x13, waiting for transfers between devices, cross(): return lax.ppermute(value, 'fsdp', [(0, 1), (1, 0)])  22.5 us
    ppermute x13, starting transfers between devices, cross(): return lax.ppermute(value, 'fsdp', [(0, 1), (1, 0)])  14.1 us
    pallas_call x1, Pallas kernels, feed(): pl.pallas_call(functools.partial(feed_kernel, parts=parts, arrays=len(mid...  12.7 us
    ppermute x1, waiting for transfers between devices, local(): lax.ppermute(up_mine, ('seq', 'fsdp'), pairs)  12.3 us
  transfers between devices with their start and end apart: 66, of which 27 were waited for; matrix products, arithmetic and copies ran while one was open for 14% of the time, Pallas kernels for 26%

profile of v5, /device:TPU:2, one launch (start us, length us, event | category | flops | bytes accessed | tf_op | source)
XLA Modules:
  0.0 305.9 jit_solution(11554936210423767949)
XLA Ops:
  7.9 5.9 %all-to-all-start = ((bf16[16,8,2432]{2,1,0:T(8,128)(2,1)}), bf16[16,8,2432]{2,1,0:T(8,128)(2,1)S(1)}, u32[]{:S(2)}, u32[]{:S(2)}) async-start(bf16[16,8,2432]{2,1,0:T(8,128)(2,1)} %fusion.2), calls=%async_computation | async-start | bytes 1245184 | tf_op jit(solution)/shard_map/all_to_all | solution.py:755
  15.9 4.6 %fusion = f32[2,16,3456]{2,1,0:T(8,128)S(1)} fusion(bf16[2,16,1152]{2,1,0:T(8,128)(2,1)S(1)} %fusion.32, bf16[1152,3456]{1,0:T(8,128)(2,1)} %param.25), kind=kOutput, calls=%fused_computation | convolution fusion | flops 254803968 | bytes 8478720 | tf_op jit(solution)/shard_map/dot_general | solution.py:811
  30.6 6.6 %collective-permute-done.8.refs_9_ = bf16[144,1152]{1,0:T(8,128)(2,1)} collective-permute-done((bf16[144,1152]{1,0:T(8,128)(2,1)S(1)}, bf16[144,1152]{1,0:T(8,128)(2,1)}, u32[]{:S(2)}, u32[]{:S(2)}) %collective-permute-start.8) | collective-permute-done | bytes 331808 | tf_op jit(solution)/shard_map/ppermute | solution.py:741
  41.0 2.5 norm_in.1
  43.5 3.7 %collective-permute-start.13 = (bf16[128,1152]{1,0:T(8,128)(2,1)}, bf16[128,1152]{1,0:T(8,128)(2,1)}, u32[]{:S(2)}, u32[]{:S(2)}) collective-permute-start(bf16[128,1152]{1,0:T(8,128)(2,1)} %get-tuple-element.90.refs_13_.refs_15_), channel_id=1, source_target_pairs={{0,4},{2,6},{4,12},{6,14},{12,8},{14,10},{8,16},{10,18},{16,20},{1... | collective-permute-start | bytes 884744 | tf_op jit(solution)/shard_map/ppermute | solution.py:747
  52.1 4.6 %collective-permute-done.14.refs_16_ = bf16[128,1152]{1,0:T(8,128)(2,1)} collective-permute-done((bf16[128,1152]{1,0:T(8,128)(2,1)}, bf16[128,1152]{1,0:T(8,128)(2,1)}, u32[]{:S(2)}, u32[]{:S(2)}) %collective-permute-start.14) | collective-permute-done | bytes 294944 | tf_op jit(solution)/shard_map/ppermute | solution.py:747
  65.7 10.7 %project.1 = (bf16[128,1152]{1,0:T(8,128)(2,1)}, bf16[640,2304]{1,0:T(8,128)(2,1)}) custom-call(s32[8]{0:T(128)} %stack.77.place_ref, bf16[576,3456]{1,0:T(8,128)(2,1)} %refs_2_.3, bf16[576,3456]{1,0:T(8,128)(2,1)} %refs_2_.3, bf16[576,3456]{1,0:T(8,128)(2,1)} %refs_2_.3, bf16[288,1152]{1,0:T(8,128)(2,1)} %copy-done.8, bf16[288,1152]{1,0:T(8,128)(2,1)} %copy-done.9, ...), custom_call_target="tpu_custom_call" | custom-call | flops 1 | bytes 1 | tf_op jit(solution)/shard_map/project/pallas_call | solution.py:106
  79.4 7.5 %attend.1 = (bf16[128,1152]{1,0:T(8,128)(2,1)}, f32[128,1152]{1,0:T(8,128)}, f32[128,1152]{1,0:T(8,128)}, bf16[128,1152]{1,0:T(8,128)(2,1)}) custom-call(s32[8]{0:T(128)} %stack.77.place_ref, bf16[576,1152]{1,0:T(8,128)(2,1)} %refs_0_.8, bf16[144,2304]{1,0:T(8,128)(2,1)} %copy-done.1, bf16[144,2304]{1,0:T(8,128)(2,1)} %copy-done.3, ...), custom_call_target="tpu_custom_call" | custom-call | flops 1 | bytes 1 | tf_op jit(solution)/shard_map/attend/pallas_call | solution.py:106
  87.7 8.3 %collective-permute-done.20.refs_6_.refs_3_ = bf16[128,1152]{1,0:T(8,128)(2,1)S(1)} collective-permute-done((bf16[128,1152]{1,0:T(8,128)(2,1)}, bf16[128,1152]{1,0:T(8,128)(2,1)S(1)}, u32[]{:S(2)}, u32[]{:S(2)}) %collective-permute-start.20) | collective-permute-done | bytes 294944 | tf_op jit(solution)/shard_map/ppermute | solution.py:741
  99.9 12.7 %feed.1 = (bf16[256,2304]{1,0:T(8,128)(2,1)}, bf16[256,2304]{1,0:T(8,128)(2,1)}, f32[128,1152]{1,0:T(8,128)}, f32[128,1152]{1,0:T(8,128)}, bf16[128,2304]{1,0:T(8,128)(2,1)}) custom-call(s32[8]{0:T(128)} %stack.77.place_ref, bf16[576,4608]{1,0:T(8,128)(2,1)} %refs_0_.7, bf16[144,2304]{1,0:T(8,128)(2,1)} %collective-permute-done.17.refs_1_, ...), custom_call_target="tpu_custom_call" | custom-call | flops 1 | bytes 1 | tf_op jit(solution)/shard_map/feed/pallas_call | solution.py:416
  116.8 7.7 %term.3 = (bf16[4,32,2304]{2,1,0:T(8,128)(2,1)}, bf16[4,32,2304]{2,1,0:T(8,128)(2,1)}, bf16[4,40,2304]{2,1,0:T(8,128)(2,1)}, bf16[4,40,2304]{2,1,0:T(8,128)(2,1)}) custom-call(s32[8]{0:T(128)} %stack.77.place_ref, bf16[128,1152]{1,0:T(8,128)(2,1)} %get-tuple-element.92.refs_7_.refs_0_, bf16[128,1152]{1,0:T(8,128)(2,1)} %copy-done.24, ...), custom_call_target="tpu_custom_call" | custom-call | flops 1 | bytes 1 | tf_op jit(solution)/shard_map/term/pallas_call | solution.py:626
  126.0 2.6 collective-permute-done.25.refs_7_
  129.5 6.9 %mid_back.1 = (f32[128,1152]{1,0:T(8,128)}, bf16[128,2304]{1,0:T(8,128)(2,1)}, bf16[128,2304]{1,0:T(8,128)(2,1)}, bf16[128,1152]{1,0:T(8,128)(2,1)}, bf16[128,1152]{1,0:T(8,128)(2,1)}, /*index=5*/f32[4,16,1152]{2,1,0:T(8,128)}) custom-call(s32[8]{0:T(128)} %stack.77.place_ref, bf16[576,1152]{1,0:T(8,128)(2,1)} %refs_0_.8, bf16[144,2304]{1,0:T(8,128)(2,1)} %copy-done.1, ...), custom_call_target="tpu_custom_call" | custom-call | flops 1 | bytes 1 | tf_op jit(solution)/shard_map/mid_back/pallas_call | solution.py:106
  139.6 11.1 %attend_back.1 = (bf16[128,1152]{1,0:T(8,128)(2,1)}, bf16[128,2304]{1,0:T(8,128)(2,1)}, bf16[128,2304]{1,0:T(8,128)(2,1)}, bf16[128,2304]{1,0:T(8,128)(2,1)}, bf...) custom-call(bf16[128,1152]{1,0:T(8,128)(2,1)} %get-tuple-element.94.refs_5_.q_ref, ...), custom_call_target="tpu_custom_call" | custom-call | flops 1 | bytes 1 | tf_op jit(solution)/shard_map/attend_back/pallas_call | solution.py:344
  156.1 2.7 select_add_fusion
  158.8 2.7 collective-permute-start.40
  163.9 2.6 collective-permute-start.34
  168.3 10.3 %term.4 = (bf16[4,176,576]{2,1,0:T(8,128)(2,1)}, bf16[4,176,576]{2,1,0:T(8,128)(2,1)}, bf16[4,184,576]{2,1,0:T(8,128)(2,1)}, bf16[4,184,576]{2,1,0:T(8,128)(2,1)}) custom-call(s32[8]{0:T(128)} %stack.77.place_ref, bf16[256,2304]{1,0:T(8,128)(2,1)} %get-tuple-element.117.refs_0_, bf16[256,2304]{1,0:T(8,128)(2,1)} %copy-done.15, ...), custom_call_target="tpu_custom_call" | custom-call | flops 1 | bytes 1 | tf_op jit(solution)/shard_map/term/pallas_call | solution.py:626
  179.6 7.2 %collective-permute-start.41 = (bf16[4,176,576]{2,1,0:T(8,128)(2,1)}, bf16[4,176,576]{2,1,0:T(8,128)(2,1)S(1)}, u32[]{:S(2)}, u32[]{:S(2)}) collective-permute-start(bf16[4,176,576]{2,1,0:T(8,128)(2,1)} %get-tuple-element.131), channel_id=1, source_target_pairs={{0,4},{2,6},{4,0},{6,2},{8,12},{10,14},{12,8},{14,10},{16,20},{18,... | collective-permute-start | bytes 2433032 | tf_op jit(solution)/shard_map/ppermute | solution.py:738
  191.3 8.1 %in_back.1 = (bf16[128,2304]{1,0:T(8,128)(2,1)}, f32[2,16,1152]{2,1,0:T(8,128)}) custom-call(s32[8]{0:T(128)} %stack.77.place_ref, bf16[576,3456]{1,0:T(8,128)(2,1)} %refs_2_.3, bf16[576,3456]{1,0:T(8,128)(2,1)} %refs_2_.3, bf16[576,3456]{1,0:T(8,128)(2,1)} %refs_2_.3, bf16[288,1152]{1,0:T(8,128)(2,1)} %copy-done.8, bf16[288,1152]{1,0:T(8,128)(2,1)} %copy-done.9, ...), custom_call_target="tpu_custom_call" | custom-call | flops 1 | bytes 1 | tf_op jit(solution)/shard_map/in_back/pallas_call | solution.py:106
  200.7 3.4 %collective-permute-done.44.refs_3_ = bf16[128,2304]{1,0:T(8,128)(2,1)} collective-permute-done((bf16[128,2304]{1,0:T(8,128)(2,1)}, bf16[128,2304]{1,0:T(8,128)(2,1)}, u32[]{:S(2)}, u32[]{:S(2)}) %collective-permute-start.44) | collective-permute-done | bytes 589856 | tf_op jit(solution)/shard_map/ppermute | solution.py:741
  206.4 3.0 collective-permute-done.42
  217.3 4.5 %all-to-all-start.1 = ((bf16[16,8,2304]{2,1,0:T(8,128)(2,1)}), bf16[16,8,2304]{2,1,0:T(8,128)(2,1)}, u32[]{:S(2)}, u32[]{:S(2)}) async-start(bf16[16,8,2304]{2,1,0:T(8,128)(2,1)} %bitcast.186), calls=%async_computation.1 | async-start | bytes 1179648 | tf_op jit(solution)/shard_map/all_to_all | solution.py:759
  222.8 7.3 %term.5 = (bf16[4,104,576]{2,1,0:T(8,128)(2,1)}, bf16[4,104,576]{2,1,0:T(8,128)(2,1)}, bf16[4,112,576]{2,1,0:T(8,128)(2,1)}, bf16[4,112,576]{2,1,0:T(8,128)(2,1)}) custom-call(s32[8]{0:T(128)} %stack.77.place_ref, bf16[128,1152]{1,0:T(8,128)(2,1)} %get-tuple-element.128.refs_13_.refs_0_, bf16[128,2304]{1,0:T(8,128)(2,1)} %add_convert_fusion.3.refs_14_.refs_1_, ...), custom_call_target="tpu_custom_call" | custom-call | flops 1 | bytes 1 | tf_op jit(solution)/shard_map/term/pallas_call | solution.py:626
  233.5 3.6 %collective-permute-done.55 = bf16[72,2304]{1,0:T(8,128)(2,1)} collective-permute-done((bf16[72,2304]{1,0:T(8,128)(2,1)}, bf16[72,2304]{1,0:T(8,128)(2,1)}, u32[]{:S(2)}, u32[]{:S(2)}) %collective-permute-start.55) | collective-permute-done | bytes 331808 | tf_op jit(solution)/shard_map/ppermute | solution.py:738
  239.5 3.0 collective-permute-start.56
  242.5 11.1 %collective-permute-done.59 = bf16[2,16,1728]{2,1,0:T(8,128)(2,1)S(1)} collective-permute-done((bf16[2,16,1728]{2,1,0:T(8,128)(2,1)S(1)}, bf16[2,16,1728]{2,1,0:T(8,128)(2,1)S(1)}, u32[]{:S(2)}, u32[]{:S(2)}) %collective-permute-start.59) | collective-permute-done | bytes 110624 | tf_op jit(solution)/shard_map/ppermute | solution.py:738
  259.5 4.0 %collective-permute-start.50 = (bf16[2,104,576]{2,1,0:T(8,128)(2,1)}, bf16[2,104,576]{2,1,0:T(8,128)(2,1)}, u32[]{:S(2)}, u32[]{:S(2)}) collective-permute-start(bf16[2,104,576]{2,1,0:T(8,128)(2,1)} %dynamic-slice_bitcast_fusion.5), channel_id=1, source_target_pairs={{0,8},{2,10},{4,12},{6,14},{8,0},{10,2},{12,4},{14,6},{16,24},{18,... | collective-permute-start | bytes 718856 | tf_op jit(solution)/shard_map/ppermute | solution.py:738
  268.4 5.9 %collective-permute-done.61 = bf16[2,16,1728]{2,1,0:T(8,128)(2,1)S(1)} collective-permute-done((bf16[2,16,1728]{2,1,0:T(8,128)(2,1)S(1)}, bf16[2,16,1728]{2,1,0:T(8,128)(2,1)S(1)}, u32[]{:S(2)}, u32[]{:S(2)}) %collective-permute-start.61) | collective-permute-done | bytes 110624 | tf_op jit(solution)/shard_map/ppermute | solution.py:738
  277.9 4.3 %collective-permute-start.57 = (bf16[288,576]{1,0:T(8,128)(2,1)S(1)}, bf16[288,576]{1,0:T(8,128)(2,1)S(1)}, u32[]{:S(2)}, u32[]{:S(2)}) collective-permute-start(bf16[288,576]{1,0:T(8,128)(2,1)S(1)} %pad_maximum_fusion.2), channel_id=1, source_target_pairs={{0,0},{1,16},{2,2},{3,18},{4,4},{5,20},{6,6},{7,22},{8,8},{9,24},{... | collective-permute-start | bytes 995336 | tf_op jit(solution)/shard_map/ppermute | solution.py:1172
  284.4 7.1 %outer.1 = f32[1152,3456]{1,0:T(8,128)} custom-call(bf16[32,1152]{1,0:T(8,128)(2,1)} %bitcast.185, bf16[32,3456]{1,0:T(8,128)(2,1)} %pad_maximum_fusion.3.right_ref), custom_call_target="tpu_custom_call" | custom-call | flops 1 | bytes 1 | tf_op jit(solution)/shard_map/outer/pallas_call | solution.py:654
  292.4 12.3 %collective-permute-done.57 = bf16[288,576]{1,0:T(8,128)(2,1)S(1)} collective-permute-done((bf16[288,576]{1,0:T(8,128)(2,1)S(1)}, bf16[288,576]{1,0:T(8,128)(2,1)S(1)}, u32[]{:S(2)}, u32[]{:S(2)}) %collective-permute-start.57) | collective-permute-done | bytes 331808 | tf_op jit(solution)/shard_map/ppermute | solution.py:1172
  (334 shorter events, 105.5 us)
Async XLA Ops:
  4.6 16.7 %collective-permute-start.1 = (bf16[144,2304]{1,0:T(8,128)(2,1)S(1)}, bf16[144,2304]{1,0:T(8,128)(2,1)S(1)}, u32[]{:S(2)}, u32[]{:S(2)}) collective-permute-start(bf16[144,2304]{1,0:T(8,128)(2,1)S(1)} %pad_maximum_fusion), channel_id=1, source_target_pairs={{0,1},{1,0},{2,3},{3,2},{4,5},{5,4},{6,7},{7,6},{8,9},{9,8},{10,11... | collective-permute-start | bytes 1990664 | tf_op jit(solution)/shard_map/ppermute | solution.py:741
  7.9 30.8 %all-to-all-start = ((bf16[16,8,2432]{2,1,0:T(8,128)(2,1)}), bf16[16,8,2432]{2,1,0:T(8,128)(2,1)S(1)}, u32[]{:S(2)}, u32[]{:S(2)}) async-start(bf16[16,8,2432]{2,1,0:T(8,128)(2,1)} %fusion.2), calls=%async_computation | async-start | bytes 1245184 | tf_op jit(solution)/shard_map/all_to_all | solution.py:755
  23.7 17.2 %collective-permute-start.6 = (bf16[144,2304]{1,0:T(8,128)(2,1)S(1)}, bf16[144,2304]{1,0:T(8,128)(2,1)S(1)}, u32[]{:S(2)}, u32[]{:S(2)}) collective-permute-start(bf16[144,2304]{1,0:T(8,128)(2,1)S(1)} %collective-permute-done.1.refs_5_.refs_1_), channel_id=1, source_target_pairs={{0,4},{2,6},{4,0},{6,2},{8,12},{10,14},{12,8},{14,10},{16,20},{18,... | collective-permute-start | bytes 1990664 | tf_op jit(solution)/shard_map/ppermute | solution.py:738
  29.0 19.9 %collective-permute-start.3 = (bf16[288,1152]{1,0:T(8,128)(2,1)}, bf16[288,1152]{1,0:T(8,128)(2,1)S(1)}, u32[]{:S(2)}, u32[]{:S(2)}) collective-permute-start(bf16[288,1152]{1,0:T(8,128)(2,1)} %constant_dynamic-slice_fusion.1), channel_id=1, source_target_pairs={{0,1},{1,0},{2,3},{3,2},{4,5},{5,4},{6,7},{7,6},{8,9},{9,8},{10,11... | collective-permute-start | bytes 1990664 | tf_op jit(solution)/shard_map/ppermute | solution.py:741
  37.2 13.7 %collective-permute-start.10 = (bf16[144,1152]{1,0:T(8,128)(2,1)}, bf16[144,1152]{1,0:T(8,128)(2,1)}, u32[]{:S(2)}, u32[]{:S(2)}) collective-permute-start(bf16[144,1152]{1,0:T(8,128)(2,1)} %collective-permute-done.8.refs_9_), channel_id=1, source_target_pairs={{0,8},{2,10},{4,12},{6,14},{8,0},{10,2},{12,4},{14,6},{16,24},{18,... | collective-permute-start | bytes 995336 | tf_op jit(solution)/shard_map/ppermute | solution.py:738
  56.7 19.8 %collective-permute-start.17 = (bf16[144,2304]{1,0:T(8,128)(2,1)S(1)}, bf16[144,2304]{1,0:T(8,128)(2,1)}, u32[]{:S(2)}, u32[]{:S(2)}) collective-permute-start(bf16[144,2304]{1,0:T(8,128)(2,1)S(1)} %dynamic_slice.85), channel_id=1, source_target_pairs={{0,1},{1,0},{2,3},{3,2},{4,5},{5,4},{6,7},{7,6},{8,9},{9,8},{10,11... | collective-permute-start | bytes 1990664 | tf_op jit(solution)/shard_map/ppermute | solution.py:741
  76.5 19.4 %collective-permute-start.19 = (bf16[144,2304]{1,0:T(8,128)(2,1)}, bf16[144,2304]{1,0:T(8,128)(2,1)S(1)}, u32[]{:S(2)}, u32[]{:S(2)}) collective-permute-start(bf16[144,2304]{1,0:T(8,128)(2,1)} %collective-permute-done.17.refs_1_), channel_id=1, source_target_pairs={{0,4},{2,6},{4,0},{6,2},{8,12},{10,14},{12,8},{14,10},{16,20},{18,... | collective-permute-start | bytes 1990664 | tf_op jit(solution)/shard_map/ppermute | solution.py:738
  112.8 15.8 %collective-permute-start.25 = (bf16[128,2304]{1,0:T(8,128)(2,1)}, bf16[128,2304]{1,0:T(8,128)(2,1)S(1)}, u32[]{:S(2)}, u32[]{:S(2)}) collective-permute-start(bf16[128,2304]{1,0:T(8,128)(2,1)} %get-tuple-element.110), channel_id=1, source_target_pairs={{0,1},{1,0},{2,3},{3,2},{4,5},{5,4},{6,7},{7,6},{8,9},{9,8},{10,11... | collective-permute-start | bytes 1769480 | tf_op jit(solution)/shard_map/ppermute | solution.py:741
  113.6 26.0 %collective-permute-start.27 = (bf16[256,2304]{1,0:T(8,128)(2,1)}, bf16[256,2304]{1,0:T(8,128)(2,1)S(1)}, u32[]{:S(2)}, u32[]{:S(2)}) collective-permute-start(bf16[256,2304]{1,0:T(8,128)(2,1)} %get-tuple-element.117.refs_0_), channel_id=1, source_target_pairs={{0,2},{2,0},{4,6},{6,4},{8,10},{10,8},{12,14},{14,12},{16,18},{18,... | collective-permute-start | bytes 3538952 | tf_op jit(solution)/shard_map/ppermute | solution.py:738
  124.5 27.7 %collective-permute-start.31 = (bf16[4,40,2304]{2,1,0:T(8,128)(2,1)}, bf16[4,40,2304]{2,1,0:T(8,128)(2,1)S(1)}, u32[]{:S(2)}, u32[]{:S(2)}) collective-permute-start(bf16[4,40,2304]{2,1,0:T(8,128)(2,1)} %get-tuple-element.106), channel_id=1, source_target_pairs={{0,8},{2,10},{4,12},{6,14},{8,0},{10,2},{12,4},{14,6},{16,24},{18,... | collective-permute-start | bytes 2211848 | tf_op jit(solution)/shard_map/ppermute | solution.py:738
  136.5 15.7 %collective-permute-start.30 = (bf16[4,32,2304]{2,1,0:T(8,128)(2,1)S(1)}, bf16[4,32,2304]{2,1,0:T(8,128)(2,1)S(1)}, u32[]{:S(2)}, u32[]{:S(2)}) collective-permute-start(bf16[4,32,2304]{2,1,0:T(8,128)(2,1)S(1)} %copy-done.55), channel_id=1, source_target_pairs={{0,4},{2,6},{4,0},{6,2},{8,12},{10,14},{12,8},{14,10},{16,20},{18,... | collective-permute-start | bytes 1769480 | tf_op jit(solution)/shard_map/ppermute | solution.py:738
  138.9 15.6 %collective-permute-start.36 = (bf16[128,2304]{1,0:T(8,128)(2,1)}, bf16[128,2304]{1,0:T(8,128)(2,1)S(1)}, u32[]{:S(2)}, u32[]{:S(2)}) collective-permute-start(bf16[128,2304]{1,0:T(8,128)(2,1)} %get-tuple-element.115), channel_id=1, source_target_pairs={{0,1},{1,0},{2,3},{3,2},{4,5},{5,4},{6,7},{7,6},{8,9},{9,8},{10,11... | collective-permute-start | bytes 1769480 | tf_op jit(solution)/shard_map/ppermute | solution.py:741
  153.1 25.6 %collective-permute-start.35 = (bf16[128,2304]{1,0:T(8,128)(2,1)}, bf16[128,2304]{1,0:T(8,128)(2,1)S(1)}, u32[]{:S(2)}, u32[]{:S(2)}) collective-permute-start(bf16[128,2304]{1,0:T(8,128)(2,1)} %get-tuple-element.130), channel_id=1, source_target_pairs={{0,2},{2,0},{4,6},{6,4},{8,10},{10,8},{12,14},{14,12},{16,18},{18,... | collective-permute-start | bytes 1769480 | tf_op jit(solution)/shard_map/ppermute | solution.py:738
  158.8 29.5 %collective-permute-start.40 = (bf16[128,2304]{1,0:T(8,128)(2,1)}, bf16[128,2304]{1,0:T(8,128)(2,1)S(1)}, u32[]{:S(2)}, u32[]{:S(2)}) collective-permute-start(bf16[128,2304]{1,0:T(8,128)(2,1)} %get-tuple-element.165), channel_id=1, source_target_pairs={{0,4},{2,6},{4,12},{6,14},{12,8},{14,10},{8,16},{10,18},{16,20},{1... | collective-permute-start | bytes 1769480 | tf_op jit(solution)/shard_map/ppermute | solution.py:747
  161.4 26.8 %collective-permute-start.39 = (bf16[128,2304]{1,0:T(8,128)(2,1)}, bf16[128,2304]{1,0:T(8,128)(2,1)}, u32[]{:S(2)}, u32[]{:S(2)}) collective-permute-start(bf16[128,2304]{1,0:T(8,128)(2,1)} %get-tuple-element.166), channel_id=1, source_target_pairs={{4,0},{6,2},{12,4},{14,6},{8,12},{10,14},{16,8},{18,10},{20,16},{2... | collective-permute-start | bytes 1769480 | tf_op jit(solution)/shard_map/ppermute | solution.py:747
  163.9 23.1 %collective-permute-start.34 = (bf16[2,40,2304]{2,1,0:T(8,128)(2,1)}, bf16[2,40,2304]{2,1,0:T(8,128)(2,1)}, u32[]{:S(2)}, u32[]{:S(2)}) collective-permute-start(bf16[2,40,2304]{2,1,0:T(8,128)(2,1)} %dynamic-slice_bitcast_fusion.2), channel_id=1, source_target_pairs={{0,4},{2,6},{4,0},{6,2},{8,12},{10,14},{12,8},{14,10},{16,20},{18,... | collective-permute-start | bytes 1105928 | tf_op jit(solution)/shard_map/ppermute | solution.py:738
  178.6 25.5 %collective-permute-start.43 = (bf16[128,1152]{1,0:T(8,128)(2,1)S(1)}, bf16[128,1152]{1,0:T(8,128)(2,1)S(1)}, u32[]{:S(2)}, u32[]{:S(2)}) collective-permute-start(bf16[128,1152]{1,0:T(8,128)(2,1)S(1)} %copy-done.21), channel_id=1, source_target_pairs={{0,1},{1,0},{2,3},{3,2},{4,5},{5,4},{6,7},{7,6},{8,9},{9,8},{10,11... | collective-permute-start | bytes 884744 | tf_op jit(solution)/shard_map/ppermute | solution.py:741
  179.6 26.7 %collective-permute-start.41 = (bf16[4,176,576]{2,1,0:T(8,128)(2,1)}, bf16[4,176,576]{2,1,0:T(8,128)(2,1)S(1)}, u32[]{:S(2)}, u32[]{:S(2)}) collective-permute-start(bf16[4,176,576]{2,1,0:T(8,128)(2,1)} %get-tuple-element.131), channel_id=1, source_target_pairs={{0,4},{2,6},{4,0},{6,2},{8,12},{10,14},{12,8},{14,10},{16,20},{18,... | collective-permute-start | bytes 2433032 | tf_op jit(solution)/shard_map/ppermute | solution.py:738
  187.0 22.4 %collective-permute-start.42 = (bf16[4,184,576]{2,1,0:T(8,128)(2,1)}, bf16[4,184,576]{2,1,0:T(8,128)(2,1)S(1)}, u32[]{:S(2)}, u32[]{:S(2)}) collective-permute-start(bf16[4,184,576]{2,1,0:T(8,128)(2,1)} %get-tuple-element.133), channel_id=1, source_target_pairs={{0,8},{2,10},{4,12},{6,14},{8,0},{10,2},{12,4},{14,6},{16,24},{18,... | collective-permute-start | bytes 2543624 | tf_op jit(solution)/shard_map/ppermute | solution.py:738
  190.5 13.7 %collective-permute-start.44 = (bf16[128,2304]{1,0:T(8,128)(2,1)}, bf16[128,2304]{1,0:T(8,128)(2,1)}, u32[]{:S(2)}, u32[]{:S(2)}) collective-permute-start(bf16[128,2304]{1,0:T(8,128)(2,1)} %add_convert_fusion.3.refs_14_.refs_1_), channel_id=1, source_target_pairs={{0,1},{1,0},{2,3},{3,2},{4,5},{5,4},{6,7},{7,6},{8,9},{9,8},{10,11... | collective-permute-start | bytes 1769480 | tf_op jit(solution)/shard_map/ppermute | solution.py:741
  204.1 18.7 %collective-permute-start.47 = (bf16[128,2304]{1,0:T(8,128)(2,1)}, bf16[128,2304]{1,0:T(8,128)(2,1)}, u32[]{:S(2)}, u32[]{:S(2)}) collective-permute-start(bf16[128,2304]{1,0:T(8,128)(2,1)} %collective-permute-done.44.refs_3_), channel_id=1, source_target_pairs={{0,2},{2,0},{4,6},{6,4},{8,10},{10,8},{12,14},{14,12},{16,18},{18,... | collective-permute-start | bytes 1769480 | tf_op jit(solution)/shard_map/ppermute | solution.py:738
  210.9 26.2 %collective-permute-start.53 = (bf16[2,176,576]{2,1,0:T(8,128)(2,1)}, bf16[2,176,576]{2,1,0:T(8,128)(2,1)}, u32[]{:S(2)}, u32[]{:S(2)}) collective-permute-start(bf16[2,176,576]{2,1,0:T(8,128)(2,1)} %dynamic-slice_bitcast_fusion.1), channel_id=1, source_target_pairs={{0,8},{2,10},{4,12},{6,14},{8,0},{10,2},{12,4},{14,6},{16,24},{18,... | collective-permute-start | bytes 1216520 | tf_op jit(solution)/shard_map/ppermute | solution.py:738
  211.5 25.6 %collective-permute-start.54 = (bf16[2,184,576]{2,1,0:T(8,128)(2,1)S(1)}, bf16[2,184,576]{2,1,0:T(8,128)(2,1)S(1)}, u32[]{:S(2)}, u32[]{:S(2)}) collective-permute-start(bf16[2,184,576]{2,1,0:T(8,128)(2,1)S(1)} %dynamic-slice_bitcast_fusion), channel_id=1, source_target_pairs={{0,4},{2,6},{4,0},{6,2},{8,12},{10,14},{12,8},{14,10},{16,20},{18,... | collective-permute-start | bytes 1271816 | tf_op jit(solution)/shard_map/ppermute | solution.py:738
  215.0 22.1 %collective-permute-start.55 = (bf16[72,2304]{1,0:T(8,128)(2,1)}, bf16[72,2304]{1,0:T(8,128)(2,1)}, u32[]{:S(2)}, u32[]{:S(2)}) collective-permute-start(bf16[72,2304]{1,0:T(8,128)(2,1)} %fusion.26), channel_id=1, source_target_pairs={{0,16},{2,18},{4,20},{6,22},{8,24},{10,26},{12,28},{14,30},{16,0},... | collective-permute-start | bytes 995336 | tf_op jit(solution)/shard_map/ppermute | solution.py:738
  217.3 47.1 %all-to-all-start.1 = ((bf16[16,8,2304]{2,1,0:T(8,128)(2,1)}), bf16[16,8,2304]{2,1,0:T(8,128)(2,1)}, u32[]{:S(2)}, u32[]{:S(2)}) async-start(bf16[16,8,2304]{2,1,0:T(8,128)(2,1)} %bitcast.186), calls=%async_computation.1 | async-start | bytes 1179648 | tf_op jit(solution)/shard_map/all_to_all | solution.py:759
  230.1 28.4 %collective-permute-start.48 = (bf16[4,104,576]{2,1,0:T(8,128)(2,1)}, bf16[4,104,576]{2,1,0:T(8,128)(2,1)S(1)}, u32[]{:S(2)}, u32[]{:S(2)}) collective-permute-start(bf16[4,104,576]{2,1,0:T(8,128)(2,1)} %get-tuple-element.144), channel_id=1, source_target_pairs={{0,4},{2,6},{4,0},{6,2},{8,12},{10,14},{12,8},{14,10},{16,20},{18,... | collective-permute-start | bytes 1437704 | tf_op jit(solution)/shard_map/ppermute | solution.py:738
  232.0 31.5 %collective-permute-start.49 = (bf16[4,112,576]{2,1,0:T(8,128)(2,1)}, bf16[4,112,576]{2,1,0:T(8,128)(2,1)S(1)}, u32[]{:S(2)}, u32[]{:S(2)}) collective-permute-start(bf16[4,112,576]{2,1,0:T(8,128)(2,1)} %get-tuple-element.146), channel_id=1, source_target_pairs={{0,8},{2,10},{4,12},{6,14},{8,0},{10,2},{12,4},{14,6},{16,24},{18,... | collective-permute-start | bytes 1548296 | tf_op jit(solution)/shard_map/ppermute | solution.py:738
  239.3 14.2 %collective-permute-start.59 = (bf16[2,16,1728]{2,1,0:T(8,128)(2,1)S(1)}, bf16[2,16,1728]{2,1,0:T(8,128)(2,1)S(1)}, u32[]{:S(2)}, u32[]{:S(2)}) collective-permute-start(bf16[2,16,1728]{2,1,0:T(8,128)(2,1)S(1)} %add_convert_fusion.10), channel_id=1, source_target_pairs={{0,16},{2,18},{4,20},{6,22},{8,24},{10,26},{12,28},{14,30},{16,0},... | collective-permute-start | bytes 331784 | tf_op jit(solution)/shard_map/ppermute | solution.py:738
  239.5 36.8 %collective-permute-start.56 = (bf16[360,576]{1,0:T(8,128)(2,1)S(1)}, bf16[360,576]{1,0:T(8,128)(2,1)S(1)}, u32[]{:S(2)}, u32[]{:S(2)}) collective-permute-start(bf16[360,576]{1,0:T(8,128)(2,1)S(1)} %fusion.20), channel_id=1, source_target_pairs={{0,16},{2,18},{4,20},{6,22},{8,24},{10,26},{12,28},{14,30},{16,0},... | collective-permute-start | bytes 1244168 | tf_op jit(solution)/shard_map/ppermute | solution.py:738
  259.5 14.8 %collective-permute-start.50 = (bf16[2,104,576]{2,1,0:T(8,128)(2,1)}, bf16[2,104,576]{2,1,0:T(8,128)(2,1)}, u32[]{:S(2)}, u32[]{:S(2)}) collective-permute-start(bf16[2,104,576]{2,1,0:T(8,128)(2,1)} %dynamic-slice_bitcast_fusion.5), channel_id=1, source_target_pairs={{0,8},{2,10},{4,12},{6,14},{8,0},{10,2},{12,4},{14,6},{16,24},{18,... | collective-permute-start | bytes 718856 | tf_op jit(solution)/shard_map/ppermute | solution.py:738
  275.5 16.1 %collective-permute-start.52 = (bf16[216,576]{1,0:T(8,128)(2,1)S(1)}, bf16[216,576]{1,0:T(8,128)(2,1)S(1)}, u32[]{:S(2)}, u32[]{:S(2)}) collective-permute-start(bf16[216,576]{1,0:T(8,128)(2,1)S(1)} %fusion.29), channel_id=1, source_target_pairs={{0,16},{2,18},{4,20},{6,22},{8,24},{10,26},{12,28},{14,30},{16,0},... | collective-permute-start | bytes 746504 | tf_op jit(solution)/shard_map/ppermute | solution.py:738
  277.9 26.9 %collective-permute-start.57 = (bf16[288,576]{1,0:T(8,128)(2,1)S(1)}, bf16[288,576]{1,0:T(8,128)(2,1)S(1)}, u32[]{:S(2)}, u32[]{:S(2)}) collective-permute-start(bf16[288,576]{1,0:T(8,128)(2,1)S(1)} %pad_maximum_fusion.2), channel_id=1, source_target_pairs={{0,0},{1,16},{2,2},{3,18},{4,4},{5,20},{6,6},{7,22},{8,8},{9,24},{... | collective-permute-start | bytes 995336 | tf_op jit(solution)/shard_map/ppermute | solution.py:1172
  (96 other events, 714.0 us)

commit v6 on v5

--- a/solution.py
+++ b/solution.py
@@ -576,9 +576,7 @@
             into = grads_ref if target == 0 else acts_ref
             into[pl.ds(row_to, value.shape[0]), pl.ds(col_to, cols)] = value
         width = acts_ref.shape[1]
-        for start in range(0, width, 576):
-            span = pl.ds(start, 576)
-            acc_ref[:, span] = dot_tn(grads_ref[...], acts_ref[:, span])
+        acc_ref[...] = dot_tn(grads_ref[...], acts_ref[...])
         for out_index, (first, count, into_row, axis) in enumerate(plan):
             at = place_at[axis]
             for side_at, side in ((0, 1 - at), (1, at)):
@@ -597,7 +595,7 @@
                     ].astype(bf16)
 
 
-def term(place, weights, width):
+def term(place, weights, width, eighths=4):
     arrays, layout, scratch, rows_out = [], [], [], [0, 0]
     for grads, acts in weights:
         pieces, shapes = [], []
@@ -613,7 +611,7 @@
             shapes.append((row_to, col_to))
         (depth, columns), (_, rows) = shapes
         chunk = columns // (16 * width // rows)
-        first = chunk // 16 * 8
+        first = chunk * eighths // 64 * 8
         plan = [(0, first, rows_out[0], 0), (first, chunk - first, rows_out[1], 1)]
         rows_out = [rows_out[0] + first, rows_out[1] + chunk - first]
         layout.append((pieces, chunk, plan))
@@ -1066,6 +1064,7 @@
                 ),
             ],
             half,
+            5,
         )
         up_first = (flip(up_parts[0], 2), flip(up_parts[2], 4))
         arrivals[0] = after(arrivals[0], up_parts, q_side)
@@ -1158,7 +1157,7 @@
         qkv_grad = jnp.transpose(qkv_keep.astype(f32) + flip(qkv_send, 8).astype(f32))
         mixed = up_keep.astype(f32) + up_last.astype(f32)
         up_rows, out_rows = hidden // seq, D // seq
-        up_low, out_low = up_rows // 16 * 8, out_rows // 16 * 8
+        up_low, out_low = up_rows * 5 // 64 * 8, out_rows * 5 // 64 * 8
         parted = up_low + out_low
         rest = parted + up_rows - up_low
         up_mine = jnp.concatenate([mixed[:up_low], mixed[parted:rest]], axis=0).astype(bf16)

time: 310 us -> 307 us (level)
  waiting for transfers between devices: 78.7 us -> 74.5 us
    ppermute x46, waiting for transfers between devices: 39.3 us -> 35.2 us  [flip(): return lax.ppermute(value, 'seq', [(i, i ^ bit) for i in range(seq)])]
    unnamed x125 -> x117, local copies, waits for them, and re-layouts: 7.12 us -> 5.89 us
where the time goes in v6:
time: 307 us; the launch traced here: 302 us
  Pallas kernels  89.8 us (29%)
  starting transfers between devices  83.5 us (27%)
  waiting for transfers between devices  74.5 us (24%)
  other arithmetic  25.3 us (8%)
  local copies, waits for them, and re-layouts  19 us (6%)
  matrix products  8.19 us (3%)
    ppermute x46, starting transfers between devices, flip(): return lax.ppermute(value, 'seq', [(i, i ^ bit) for i in range(seq)])  45.2 us
    ppermute x46, waiting for transfers between devices, flip(): return lax.ppermute(value, 'seq', [(i, i ^ bit) for i in range(seq)])  35.2 us
    pallas_call x4, Pallas kernels, staged_call(): pl.pallas_call(functools.partial(kernel, parts=parts), out_shape=out_shap...  33.2 us
    pallas_call x3, Pallas kernels, term(): pl.pallas_call(functools.partial(term_kernel, layout=layout, outputs=2),...  23.5 us
    ppermute x13, waiting for transfers between devices, cross(): return lax.ppermute(value, 'fsdp', [(0, 1), (1, 0)])  21.9 us
    ppermute x13, starting transfers between devices, cross(): return lax.ppermute(value, 'fsdp', [(0, 1), (1, 0)])  13.5 us
    ppermute x1, waiting for transfers between devices, local(): lax.ppermute(up_mine, ('seq', 'fsdp'), pairs)  12.9 us
    pallas_call x1, Pallas kernels, feed(): pl.pallas_call(functools.partial(feed_kernel, parts=parts, arrays=len(mid...  12.6 us
  transfers between devices with their start and end apart: 66, of which 27 were waited for; matrix products, arithmetic and copies ran while one was open for 14% of the time, Pallas kernels for 26%

profile of v6, /device:TPU:2, one launch (start us, length us, event | category | flops | bytes accessed | tf_op | source)
XLA Modules:
  0.0 302.4 jit_solution(2315898241815761688)
XLA Ops:
  7.9 5.9 %all-to-all-start = ((bf16[16,8,2432]{2,1,0:T(8,128)(2,1)}), bf16[16,8,2432]{2,1,0:T(8,128)(2,1)S(1)}, u32[]{:S(2)}, u32[]{:S(2)}) async-start(bf16[16,8,2432]{2,1,0:T(8,128)(2,1)} %fusion.2), calls=%async_computation | async-start | bytes 1245184 | tf_op jit(solution)/shard_map/all_to_all | solution.py:753
  15.8 4.6 %fusion = f32[2,16,3456]{2,1,0:T(8,128)S(1)} fusion(bf16[2,16,1152]{2,1,0:T(8,128)(2,1)S(1)} %fusion.32, bf16[1152,3456]{1,0:T(8,128)(2,1)} %param.25), kind=kOutput, calls=%fused_computation | convolution fusion | flops 254803968 | bytes 8478720 | tf_op jit(solution)/shard_map/dot_general | solution.py:809
  30.6 6.6 %collective-permute-done.8.refs_9_ = bf16[144,1152]{1,0:T(8,128)(2,1)} collective-permute-done((bf16[144,1152]{1,0:T(8,128)(2,1)S(1)}, bf16[144,1152]{1,0:T(8,128)(2,1)}, u32[]{:S(2)}, u32[]{:S(2)}) %collective-permute-start.8) | collective-permute-done | bytes 331808 | tf_op jit(solution)/shard_map/ppermute | solution.py:739
  40.9 2.5 norm_in.1
  43.4 3.7 %collective-permute-start.13 = (bf16[128,1152]{1,0:T(8,128)(2,1)}, bf16[128,1152]{1,0:T(8,128)(2,1)}, u32[]{:S(2)}, u32[]{:S(2)}) collective-permute-start(bf16[128,1152]{1,0:T(8,128)(2,1)} %get-tuple-element.90.refs_13_.refs_15_), channel_id=1, source_target_pairs={{0,4},{2,6},{4,12},{6,14},{12,8},{14,10},{8,16},{10,18},{16,20},{1... | collective-permute-start | bytes 884744 | tf_op jit(solution)/shard_map/ppermute | solution.py:745
  52.0 4.4 %collective-permute-done.14.refs_16_ = bf16[128,1152]{1,0:T(8,128)(2,1)} collective-permute-done((bf16[128,1152]{1,0:T(8,128)(2,1)}, bf16[128,1152]{1,0:T(8,128)(2,1)}, u32[]{:S(2)}, u32[]{:S(2)}) %collective-permute-start.14) | collective-permute-done | bytes 294944 | tf_op jit(solution)/shard_map/ppermute | solution.py:745
  65.8 10.7 %project.1 = (bf16[128,1152]{1,0:T(8,128)(2,1)}, bf16[640,2304]{1,0:T(8,128)(2,1)}) custom-call(s32[8]{0:T(128)} %stack.77.place_ref, bf16[576,3456]{1,0:T(8,128)(2,1)} %refs_2_.3, bf16[576,3456]{1,0:T(8,128)(2,1)} %refs_2_.3, bf16[576,3456]{1,0:T(8,128)(2,1)} %refs_2_.3, bf16[288,1152]{1,0:T(8,128)(2,1)} %copy-done.8, bf16[288,1152]{1,0:T(8,128)(2,1)} %copy-done.9, ...), custom_call_target="tpu_custom_call" | custom-call | flops 1 | bytes 1 | tf_op jit(solution)/shard_map/project/pallas_call | solution.py:106
  79.5 7.5 %attend.1 = (bf16[128,1152]{1,0:T(8,128)(2,1)}, f32[128,1152]{1,0:T(8,128)}, f32[128,1152]{1,0:T(8,128)}, bf16[128,1152]{1,0:T(8,128)(2,1)}) custom-call(s32[8]{0:T(128)} %stack.77.place_ref, bf16[576,1152]{1,0:T(8,128)(2,1)} %refs_0_.8, bf16[144,2304]{1,0:T(8,128)(2,1)} %copy-done.1, bf16[144,2304]{1,0:T(8,128)(2,1)} %copy-done.3, ...), custom_call_target="tpu_custom_call" | custom-call | flops 1 | bytes 1 | tf_op jit(solution)/shard_map/attend/pallas_call | solution.py:106
  87.8 8.2 %collective-permute-done.20.refs_6_.refs_3_ = bf16[128,1152]{1,0:T(8,128)(2,1)S(1)} collective-permute-done((bf16[128,1152]{1,0:T(8,128)(2,1)}, bf16[128,1152]{1,0:T(8,128)(2,1)S(1)}, u32[]{:S(2)}, u32[]{:S(2)}) %collective-permute-start.20) | collective-permute-done | bytes 294944 | tf_op jit(solution)/shard_map/ppermute | solution.py:739
  99.1 12.6 %feed.1 = (bf16[256,2304]{1,0:T(8,128)(2,1)}, bf16[256,2304]{1,0:T(8,128)(2,1)}, f32[128,1152]{1,0:T(8,128)}, f32[128,1152]{1,0:T(8,128)}, bf16[128,2304]{1,0:T(8,128)(2,1)}) custom-call(s32[8]{0:T(128)} %stack.77.place_ref, bf16[576,4608]{1,0:T(8,128)(2,1)} %refs_0_.7, bf16[144,2304]{1,0:T(8,128)(2,1)} %collective-permute-done.17.refs_1_, ...), custom_call_target="tpu_custom_call" | custom-call | flops 1 | bytes 1 | tf_op jit(solution)/shard_map/feed/pallas_call | solution.py:416
  115.8 6.6 %term.3 = (bf16[4,32,2304]{2,1,0:T(8,128)(2,1)}, bf16[4,32,2304]{2,1,0:T(8,128)(2,1)}, bf16[4,40,2304]{2,1,0:T(8,128)(2,1)}, bf16[4,40,2304]{2,1,0:T(8,128)(2,1)}) custom-call(s32[8]{0:T(128)} %stack.77.place_ref, bf16[128,1152]{1,0:T(8,128)(2,1)} %get-tuple-element.92.refs_7_.refs_0_, bf16[128,1152]{1,0:T(8,128)(2,1)} %copy-done.24, ...), custom_call_target="tpu_custom_call" | custom-call | flops 1 | bytes 1 | tf_op jit(solution)/shard_map/term/pallas_call | solution.py:624
  123.9 3.8 %collective-permute-done.25.refs_7_ = bf16[128,2304]{1,0:T(8,128)(2,1)S(1)} collective-permute-done((bf16[128,2304]{1,0:T(8,128)(2,1)}, bf16[128,2304]{1,0:T(8,128)(2,1)S(1)}, u32[]{:S(2)}, u32[]{:S(2)}) %collective-permute-start.25) | collective-permute-done | bytes 589856 | tf_op jit(solution)/shard_map/ppermute | solution.py:739
  128.5 6.9 %mid_back.1 = (f32[128,1152]{1,0:T(8,128)}, bf16[128,2304]{1,0:T(8,128)(2,1)}, bf16[128,2304]{1,0:T(8,128)(2,1)}, bf16[128,1152]{1,0:T(8,128)(2,1)}, bf16[128,1152]{1,0:T(8,128)(2,1)}, /*index=5*/f32[4,16,1152]{2,1,0:T(8,128)}) custom-call(s32[8]{0:T(128)} %stack.77.place_ref, bf16[576,1152]{1,0:T(8,128)(2,1)} %refs_0_.8, bf16[144,2304]{1,0:T(8,128)(2,1)} %copy-done.1, ...), custom_call_target="tpu_custom_call" | custom-call | flops 1 | bytes 1 | tf_op jit(solution)/shard_map/mid_back/pallas_call | solution.py:106
  138.7 10.9 %attend_back.1 = (bf16[128,1152]{1,0:T(8,128)(2,1)}, bf16[128,2304]{1,0:T(8,128)(2,1)}, bf16[128,2304]{1,0:T(8,128)(2,1)}, bf16[128,2304]{1,0:T(8,128)(2,1)}, bf...) custom-call(bf16[128,1152]{1,0:T(8,128)(2,1)} %get-tuple-element.94.refs_5_.q_ref, ...), custom_call_target="tpu_custom_call" | custom-call | flops 1 | bytes 1 | tf_op jit(solution)/shard_map/attend_back/pallas_call | solution.py:344
  153.6 2.7 select_add_fusion
  156.3 3.4 %collective-permute-start.40 = (bf16[128,2304]{1,0:T(8,128)(2,1)}, bf16[128,2304]{1,0:T(8,128)(2,1)S(1)}, u32[]{:S(2)}, u32[]{:S(2)}) collective-permute-start(bf16[128,2304]{1,0:T(8,128)(2,1)} %get-tuple-element.165), channel_id=1, source_target_pairs={{0,4},{2,6},{4,12},{6,14},{12,8},{14,10},{8,16},{10,18},{16,20},{1... | collective-permute-start | bytes 1769480 | tf_op jit(solution)/shard_map/ppermute | solution.py:745
  162.2 2.6 collective-permute-start.34
  166.5 9.7 %term.4 = (bf16[4,216,576]{2,1,0:T(8,128)(2,1)}, bf16[4,216,576]{2,1,0:T(8,128)(2,1)}, bf16[4,144,576]{2,1,0:T(8,128)(2,1)}, bf16[4,144,576]{2,1,0:T(8,128)(2,1)}) custom-call(s32[8]{0:T(128)} %stack.77.place_ref, bf16[256,2304]{1,0:T(8,128)(2,1)} %get-tuple-element.117.refs_0_, bf16[256,2304]{1,0:T(8,128)(2,1)} %copy-done.15, ...), custom_call_target="tpu_custom_call" | custom-call | flops 1 | bytes 1 | tf_op jit(solution)/shard_map/term/pallas_call | solution.py:624
  177.4 7.6 %collective-permute-start.41 = (bf16[4,216,576]{2,1,0:T(8,128)(2,1)}, bf16[4,216,576]{2,1,0:T(8,128)(2,1)S(1)}, u32[]{:S(2)}, u32[]{:S(2)}) collective-permute-start(bf16[4,216,576]{2,1,0:T(8,128)(2,1)} %get-tuple-element.131), channel_id=1, source_target_pairs={{0,4},{2,6},{4,0},{6,2},{8,12},{10,14},{12,8},{14,10},{16,20},{18,... | collective-permute-start | bytes 2985992 | tf_op jit(solution)/shard_map/ppermute | solution.py:736
  188.8 8.1 %in_back.1 = (bf16[128,2304]{1,0:T(8,128)(2,1)}, f32[2,16,1152]{2,1,0:T(8,128)}) custom-call(s32[8]{0:T(128)} %stack.77.place_ref, bf16[576,3456]{1,0:T(8,128)(2,1)} %refs_2_.3, bf16[576,3456]{1,0:T(8,128)(2,1)} %refs_2_.3, bf16[576,3456]{1,0:T(8,128)(2,1)} %refs_2_.3, bf16[288,1152]{1,0:T(8,128)(2,1)} %copy-done.8, bf16[288,1152]{1,0:T(8,128)(2,1)} %copy-done.9, ...), custom_call_target="tpu_custom_call" | custom-call | flops 1 | bytes 1 | tf_op jit(solution)/shard_map/in_back/pallas_call | solution.py:106
  202.1 4.2 %collective-permute-done.42 = bf16[4,144,576]{2,1,0:T(8,128)(2,1)S(1)} collective-permute-done((bf16[4,144,576]{2,1,0:T(8,128)(2,1)}, bf16[4,144,576]{2,1,0:T(8,128)(2,1)S(1)}, u32[]{:S(2)}, u32[]{:S(2)}) %collective-permute-start.42) | collective-permute-done | bytes 663584 | tf_op jit(solution)/shard_map/ppermute | solution.py:736
  206.4 2.6 collective-permute-done.41
  213.8 4.9 %all-to-all-start.1 = ((bf16[16,8,2304]{2,1,0:T(8,128)(2,1)}), bf16[16,8,2304]{2,1,0:T(8,128)(2,1)}, u32[]{:S(2)}, u32[]{:S(2)}) async-start(bf16[16,8,2304]{2,1,0:T(8,128)(2,1)} %bitcast.186), calls=%async_computation.1 | async-start | bytes 1179648 | tf_op jit(solution)/shard_map/all_to_all | solution.py:757
  219.8 7.3 %term.5 = (bf16[4,104,576]{2,1,0:T(8,128)(2,1)}, bf16[4,104,576]{2,1,0:T(8,128)(2,1)}, bf16[4,112,576]{2,1,0:T(8,128)(2,1)}, bf16[4,112,576]{2,1,0:T(8,128)(2,1)}) custom-call(s32[8]{0:T(128)} %stack.77.place_ref, bf16[128,1152]{1,0:T(8,128)(2,1)} %get-tuple-element.128.refs_13_.refs_0_, bf16[128,2304]{1,0:T(8,128)(2,1)} %add_convert_fusion.3.refs_14_.refs_1_, ...), custom_call_target="tpu_custom_call" | custom-call | flops 1 | bytes 1 | tf_op jit(solution)/shard_map/term/pallas_call | solution.py:624
  230.5 2.5 collective-permute-done.53
  240.9 7.1 %collective-permute-done.59 = bf16[2,16,1728]{2,1,0:T(8,128)(2,1)S(1)} collective-permute-done((bf16[2,16,1728]{2,1,0:T(8,128)(2,1)S(1)}, bf16[2,16,1728]{2,1,0:T(8,128)(2,1)S(1)}, u32[]{:S(2)}, u32[]{:S(2)}) %collective-permute-start.59) | collective-permute-done | bytes 110624 | tf_op jit(solution)/shard_map/ppermute | solution.py:736
  248.1 2.2 collective-permute-start.60
  254.0 4.8 %collective-permute-start.50 = (bf16[2,104,576]{2,1,0:T(8,128)(2,1)}, bf16[2,104,576]{2,1,0:T(8,128)(2,1)}, u32[]{:S(2)}, u32[]{:S(2)}) collective-permute-start(bf16[2,104,576]{2,1,0:T(8,128)(2,1)} %dynamic-slice_bitcast_fusion.5), channel_id=1, source_target_pairs={{0,8},{2,10},{4,12},{6,14},{8,0},{10,2},{12,4},{14,6},{16,24},{18,... | collective-permute-start | bytes 718856 | tf_op jit(solution)/shard_map/ppermute | solution.py:736
  264.2 6.0 %collective-permute-done.61 = bf16[2,16,1728]{2,1,0:T(8,128)(2,1)S(1)} collective-permute-done((bf16[2,16,1728]{2,1,0:T(8,128)(2,1)S(1)}, bf16[2,16,1728]{2,1,0:T(8,128)(2,1)S(1)}, u32[]{:S(2)}, u32[]{:S(2)}) %collective-permute-start.61) | collective-permute-done | bytes 110624 | tf_op jit(solution)/shard_map/ppermute | solution.py:736
  274.0 4.1 %collective-permute-start.57 = (bf16[288,576]{1,0:T(8,128)(2,1)S(1)}, bf16[288,576]{1,0:T(8,128)(2,1)S(1)}, u32[]{:S(2)}, u32[]{:S(2)}) collective-permute-start(bf16[288,576]{1,0:T(8,128)(2,1)S(1)} %pad_maximum_fusion.2), channel_id=1, source_target_pairs={{0,0},{1,16},{2,2},{3,18},{4,4},{5,20},{6,6},{7,22},{8,8},{9,24},{... | collective-permute-start | bytes 995336 | tf_op jit(solution)/shard_map/ppermute | solution.py:1171
  280.4 7.1 %outer.1 = f32[1152,3456]{1,0:T(8,128)} custom-call(bf16[32,1152]{1,0:T(8,128)(2,1)} %bitcast.185, bf16[32,3456]{1,0:T(8,128)(2,1)} %pad_maximum_fusion.3.right_ref), custom_call_target="tpu_custom_call" | custom-call | flops 1 | bytes 1 | tf_op jit(solution)/shard_map/outer/pallas_call | solution.py:652
  288.3 12.9 %collective-permute-done.57 = bf16[288,576]{1,0:T(8,128)(2,1)S(1)} collective-permute-done((bf16[288,576]{1,0:T(8,128)(2,1)S(1)}, bf16[288,576]{1,0:T(8,128)(2,1)S(1)}, u32[]{:S(2)}, u32[]{:S(2)}) %collective-permute-start.57) | collective-permute-done | bytes 331808 | tf_op jit(solution)/shard_map/ppermute | solution.py:1171
  (327 shorter events, 105.5 us)
Async XLA Ops:
  4.6 16.7 %collective-permute-start.1 = (bf16[144,2304]{1,0:T(8,128)(2,1)S(1)}, bf16[144,2304]{1,0:T(8,128)(2,1)S(1)}, u32[]{:S(2)}, u32[]{:S(2)}) collective-permute-start(bf16[144,2304]{1,0:T(8,128)(2,1)S(1)} %pad_maximum_fusion), channel_id=1, source_target_pairs={{0,1},{1,0},{2,3},{3,2},{4,5},{5,4},{6,7},{7,6},{8,9},{9,8},{10,11... | collective-permute-start | bytes 1990664 | tf_op jit(solution)/shard_map/ppermute | solution.py:739
  7.9 30.8 %all-to-all-start = ((bf16[16,8,2432]{2,1,0:T(8,128)(2,1)}), bf16[16,8,2432]{2,1,0:T(8,128)(2,1)S(1)}, u32[]{:S(2)}, u32[]{:S(2)}) async-start(bf16[16,8,2432]{2,1,0:T(8,128)(2,1)} %fusion.2), calls=%async_computation | async-start | bytes 1245184 | tf_op jit(solution)/shard_map/all_to_all | solution.py:753
  23.7 17.2 %collective-permute-start.6 = (bf16[144,2304]{1,0:T(8,128)(2,1)S(1)}, bf16[144,2304]{1,0:T(8,128)(2,1)S(1)}, u32[]{:S(2)}, u32[]{:S(2)}) collective-permute-start(bf16[144,2304]{1,0:T(8,128)(2,1)S(1)} %collective-permute-done.1.refs_5_.refs_1_), channel_id=1, source_target_pairs={{0,4},{2,6},{4,0},{6,2},{8,12},{10,14},{12,8},{14,10},{16,20},{18,... | collective-permute-start | bytes 1990664 | tf_op jit(solution)/shard_map/ppermute | solution.py:736
  29.0 19.8 %collective-permute-start.3 = (bf16[288,1152]{1,0:T(8,128)(2,1)}, bf16[288,1152]{1,0:T(8,128)(2,1)S(1)}, u32[]{:S(2)}, u32[]{:S(2)}) collective-permute-start(bf16[288,1152]{1,0:T(8,128)(2,1)} %constant_dynamic-slice_fusion.1), channel_id=1, source_target_pairs={{0,1},{1,0},{2,3},{3,2},{4,5},{5,4},{6,7},{7,6},{8,9},{9,8},{10,11... | collective-permute-start | bytes 1990664 | tf_op jit(solution)/shard_map/ppermute | solution.py:739
  37.2 13.7 %collective-permute-start.10 = (bf16[144,1152]{1,0:T(8,128)(2,1)}, bf16[144,1152]{1,0:T(8,128)(2,1)}, u32[]{:S(2)}, u32[]{:S(2)}) collective-permute-start(bf16[144,1152]{1,0:T(8,128)(2,1)} %collective-permute-done.8.refs_9_), channel_id=1, source_target_pairs={{0,8},{2,10},{4,12},{6,14},{8,0},{10,2},{12,4},{14,6},{16,24},{18,... | collective-permute-start | bytes 995336 | tf_op jit(solution)/shard_map/ppermute | solution.py:736
  43.4 13.0 %collective-permute-start.13 = (bf16[128,1152]{1,0:T(8,128)(2,1)}, bf16[128,1152]{1,0:T(8,128)(2,1)}, u32[]{:S(2)}, u32[]{:S(2)}) collective-permute-start(bf16[128,1152]{1,0:T(8,128)(2,1)} %get-tuple-element.90.refs_13_.refs_15_), channel_id=1, source_target_pairs={{0,4},{2,6},{4,12},{6,14},{12,8},{14,10},{8,16},{10,18},{16,20},{1... | collective-permute-start | bytes 884744 | tf_op jit(solution)/shard_map/ppermute | solution.py:745
  56.5 20.0 %collective-permute-start.17 = (bf16[144,2304]{1,0:T(8,128)(2,1)S(1)}, bf16[144,2304]{1,0:T(8,128)(2,1)}, u32[]{:S(2)}, u32[]{:S(2)}) collective-permute-start(bf16[144,2304]{1,0:T(8,128)(2,1)S(1)} %dynamic_slice.85), channel_id=1, source_target_pairs={{0,1},{1,0},{2,3},{3,2},{4,5},{5,4},{6,7},{7,6},{8,9},{9,8},{10,11... | collective-permute-start | bytes 1990664 | tf_op jit(solution)/shard_map/ppermute | solution.py:739
  76.5 19.5 %collective-permute-start.19 = (bf16[144,2304]{1,0:T(8,128)(2,1)}, bf16[144,2304]{1,0:T(8,128)(2,1)S(1)}, u32[]{:S(2)}, u32[]{:S(2)}) collective-permute-start(bf16[144,2304]{1,0:T(8,128)(2,1)} %collective-permute-done.17.refs_1_), channel_id=1, source_target_pairs={{0,4},{2,6},{4,0},{6,2},{8,12},{10,14},{12,8},{14,10},{16,20},{18,... | collective-permute-start | bytes 1990664 | tf_op jit(solution)/shard_map/ppermute | solution.py:736
  111.9 15.8 %collective-permute-start.25 = (bf16[128,2304]{1,0:T(8,128)(2,1)}, bf16[128,2304]{1,0:T(8,128)(2,1)S(1)}, u32[]{:S(2)}, u32[]{:S(2)}) collective-permute-start(bf16[128,2304]{1,0:T(8,128)(2,1)} %get-tuple-element.110), channel_id=1, source_target_pairs={{0,1},{1,0},{2,3},{3,2},{4,5},{5,4},{6,7},{7,6},{8,9},{9,8},{10,11... | collective-permute-start | bytes 1769480 | tf_op jit(solution)/shard_map/ppermute | solution.py:739
  112.7 26.0 %collective-permute-start.27 = (bf16[256,2304]{1,0:T(8,128)(2,1)}, bf16[256,2304]{1,0:T(8,128)(2,1)S(1)}, u32[]{:S(2)}, u32[]{:S(2)}) collective-permute-start(bf16[256,2304]{1,0:T(8,128)(2,1)} %get-tuple-element.117.refs_0_), channel_id=1, source_target_pairs={{0,2},{2,0},{4,6},{6,4},{8,10},{10,8},{12,14},{14,12},{16,18},{18,... | collective-permute-start | bytes 3538952 | tf_op jit(solution)/shard_map/ppermute | solution.py:736
  122.4 28.9 %collective-permute-start.31 = (bf16[4,40,2304]{2,1,0:T(8,128)(2,1)}, bf16[4,40,2304]{2,1,0:T(8,128)(2,1)S(1)}, u32[]{:S(2)}, u32[]{:S(2)}) collective-permute-start(bf16[4,40,2304]{2,1,0:T(8,128)(2,1)} %get-tuple-element.106), channel_id=1, source_target_pairs={{0,8},{2,10},{4,12},{6,14},{8,0},{10,2},{12,4},{14,6},{16,24},{18,... | collective-permute-start | bytes 2211848 | tf_op jit(solution)/shard_map/ppermute | solution.py:736
  135.5 15.7 %collective-permute-start.30 = (bf16[4,32,2304]{2,1,0:T(8,128)(2,1)S(1)}, bf16[4,32,2304]{2,1,0:T(8,128)(2,1)S(1)}, u32[]{:S(2)}, u32[]{:S(2)}) collective-permute-start(bf16[4,32,2304]{2,1,0:T(8,128)(2,1)S(1)} %copy-done.51), channel_id=1, source_target_pairs={{0,4},{2,6},{4,0},{6,2},{8,12},{10,14},{12,8},{14,10},{16,20},{18,... | collective-permute-start | bytes 1769480 | tf_op jit(solution)/shard_map/ppermute | solution.py:736
  137.9 15.6 %collective-permute-start.36 = (bf16[128,2304]{1,0:T(8,128)(2,1)}, bf16[128,2304]{1,0:T(8,128)(2,1)S(1)}, u32[]{:S(2)}, u32[]{:S(2)}) collective-permute-start(bf16[128,2304]{1,0:T(8,128)(2,1)} %get-tuple-element.115), channel_id=1, source_target_pairs={{0,1},{1,0},{2,3},{3,2},{4,5},{5,4},{6,7},{7,6},{8,9},{9,8},{10,11... | collective-permute-start | bytes 1769480 | tf_op jit(solution)/shard_map/ppermute | solution.py:739
  151.3 24.9 %collective-permute-start.35 = (bf16[128,2304]{1,0:T(8,128)(2,1)}, bf16[128,2304]{1,0:T(8,128)(2,1)S(1)}, u32[]{:S(2)}, u32[]{:S(2)}) collective-permute-start(bf16[128,2304]{1,0:T(8,128)(2,1)} %get-tuple-element.130), channel_id=1, source_target_pairs={{0,2},{2,0},{4,6},{6,4},{8,10},{10,8},{12,14},{14,12},{16,18},{18,... | collective-permute-start | bytes 1769480 | tf_op jit(solution)/shard_map/ppermute | solution.py:736
  156.3 29.3 %collective-permute-start.40 = (bf16[128,2304]{1,0:T(8,128)(2,1)}, bf16[128,2304]{1,0:T(8,128)(2,1)S(1)}, u32[]{:S(2)}, u32[]{:S(2)}) collective-permute-start(bf16[128,2304]{1,0:T(8,128)(2,1)} %get-tuple-element.165), channel_id=1, source_target_pairs={{0,4},{2,6},{4,12},{6,14},{12,8},{14,10},{8,16},{10,18},{16,20},{1... | collective-permute-start | bytes 1769480 | tf_op jit(solution)/shard_map/ppermute | solution.py:745
  159.8 25.9 %collective-permute-start.39 = (bf16[128,2304]{1,0:T(8,128)(2,1)}, bf16[128,2304]{1,0:T(8,128)(2,1)}, u32[]{:S(2)}, u32[]{:S(2)}) collective-permute-start(bf16[128,2304]{1,0:T(8,128)(2,1)} %get-tuple-element.166), channel_id=1, source_target_pairs={{4,0},{6,2},{12,4},{14,6},{8,12},{10,14},{16,8},{18,10},{20,16},{2... | collective-permute-start | bytes 1769480 | tf_op jit(solution)/shard_map/ppermute | solution.py:745
  162.2 22.9 %collective-permute-start.34 = (bf16[2,40,2304]{2,1,0:T(8,128)(2,1)}, bf16[2,40,2304]{2,1,0:T(8,128)(2,1)}, u32[]{:S(2)}, u32[]{:S(2)}) collective-permute-start(bf16[2,40,2304]{2,1,0:T(8,128)(2,1)} %dynamic-slice_bitcast_fusion.2), channel_id=1, source_target_pairs={{0,4},{2,6},{4,0},{6,2},{8,12},{10,14},{12,8},{14,10},{16,20},{18,... | collective-permute-start | bytes 1105928 | tf_op jit(solution)/shard_map/ppermute | solution.py:736
  176.2 26.0 %collective-permute-start.43 = (bf16[128,1152]{1,0:T(8,128)(2,1)S(1)}, bf16[128,1152]{1,0:T(8,128)(2,1)S(1)}, u32[]{:S(2)}, u32[]{:S(2)}) collective-permute-start(bf16[128,1152]{1,0:T(8,128)(2,1)S(1)} %copy-done.21), channel_id=1, source_target_pairs={{0,1},{1,0},{2,3},{3,2},{4,5},{5,4},{6,7},{7,6},{8,9},{9,8},{10,11... | collective-permute-start | bytes 884744 | tf_op jit(solution)/shard_map/ppermute | solution.py:739
  177.4 31.5 %collective-permute-start.41 = (bf16[4,216,576]{2,1,0:T(8,128)(2,1)}, bf16[4,216,576]{2,1,0:T(8,128)(2,1)S(1)}, u32[]{:S(2)}, u32[]{:S(2)}) collective-permute-start(bf16[4,216,576]{2,1,0:T(8,128)(2,1)} %get-tuple-element.131), channel_id=1, source_target_pairs={{0,4},{2,6},{4,0},{6,2},{8,12},{10,14},{12,8},{14,10},{16,20},{18,... | collective-permute-start | bytes 2985992 | tf_op jit(solution)/shard_map/ppermute | solution.py:736
  185.2 21.2 %collective-permute-start.42 = (bf16[4,144,576]{2,1,0:T(8,128)(2,1)}, bf16[4,144,576]{2,1,0:T(8,128)(2,1)S(1)}, u32[]{:S(2)}, u32[]{:S(2)}) collective-permute-start(bf16[4,144,576]{2,1,0:T(8,128)(2,1)} %get-tuple-element.133), channel_id=1, source_target_pairs={{0,8},{2,10},{4,12},{6,14},{8,0},{10,2},{12,4},{14,6},{16,24},{18,... | collective-permute-start | bytes 1990664 | tf_op jit(solution)/shard_map/ppermute | solution.py:736
  187.9 14.3 %collective-permute-start.44 = (bf16[128,2304]{1,0:T(8,128)(2,1)}, bf16[128,2304]{1,0:T(8,128)(2,1)}, u32[]{:S(2)}, u32[]{:S(2)}) collective-permute-start(bf16[128,2304]{1,0:T(8,128)(2,1)} %add_convert_fusion.3.refs_14_.refs_1_), channel_id=1, source_target_pairs={{0,1},{1,0},{2,3},{3,2},{4,5},{5,4},{6,7},{7,6},{8,9},{9,8},{10,11... | collective-permute-start | bytes 1769480 | tf_op jit(solution)/shard_map/ppermute | solution.py:739
  198.9 31.6 %collective-permute-start.55 = (bf16[72,2304]{1,0:T(8,128)(2,1)}, bf16[72,2304]{1,0:T(8,128)(2,1)}, u32[]{:S(2)}, u32[]{:S(2)}) collective-permute-start(bf16[72,2304]{1,0:T(8,128)(2,1)} %fusion.26), channel_id=1, source_target_pairs={{0,16},{2,18},{4,20},{6,22},{8,24},{10,26},{12,28},{14,30},{16,0},... | collective-permute-start | bytes 995336 | tf_op jit(solution)/shard_map/ppermute | solution.py:736
  202.1 17.6 %collective-permute-start.47 = (bf16[128,2304]{1,0:T(8,128)(2,1)}, bf16[128,2304]{1,0:T(8,128)(2,1)}, u32[]{:S(2)}, u32[]{:S(2)}) collective-permute-start(bf16[128,2304]{1,0:T(8,128)(2,1)} %collective-permute-done.44.refs_3_), channel_id=1, source_target_pairs={{0,2},{2,0},{4,6},{6,4},{8,10},{10,8},{12,14},{14,12},{16,18},{18,... | collective-permute-start | bytes 1769480 | tf_op jit(solution)/shard_map/ppermute | solution.py:736
  210.6 22.5 %collective-permute-start.53 = (bf16[2,216,576]{2,1,0:T(8,128)(2,1)}, bf16[2,216,576]{2,1,0:T(8,128)(2,1)S(1)}, u32[]{:S(2)}, u32[]{:S(2)}) collective-permute-start(bf16[2,216,576]{2,1,0:T(8,128)(2,1)} %dynamic-slice_bitcast_fusion), channel_id=1, source_target_pairs={{0,8},{2,10},{4,12},{6,14},{8,0},{10,2},{12,4},{14,6},{16,24},{18,... | collective-permute-start | bytes 1493000 | tf_op jit(solution)/shard_map/ppermute | solution.py:736
  212.0 18.5 %collective-permute-start.54 = (bf16[2,144,576]{2,1,0:T(8,128)(2,1)S(1)}, bf16[2,144,576]{2,1,0:T(8,128)(2,1)}, u32[]{:S(2)}, u32[]{:S(2)}) collective-permute-start(bf16[2,144,576]{2,1,0:T(8,128)(2,1)S(1)} %dynamic-slice_bitcast_fusion.1), channel_id=1, source_target_pairs={{0,4},{2,6},{4,0},{6,2},{8,12},{10,14},{12,8},{14,10},{16,20},{18,... | collective-permute-start | bytes 995336 | tf_op jit(solution)/shard_map/ppermute | solution.py:736
  213.8 45.2 %all-to-all-start.1 = ((bf16[16,8,2304]{2,1,0:T(8,128)(2,1)}), bf16[16,8,2304]{2,1,0:T(8,128)(2,1)}, u32[]{:S(2)}, u32[]{:S(2)}) async-start(bf16[16,8,2304]{2,1,0:T(8,128)(2,1)} %bitcast.186), calls=%async_computation.1 | async-start | bytes 1179648 | tf_op jit(solution)/shard_map/all_to_all | solution.py:757
  227.0 26.0 %collective-permute-start.48 = (bf16[4,104,576]{2,1,0:T(8,128)(2,1)}, bf16[4,104,576]{2,1,0:T(8,128)(2,1)S(1)}, u32[]{:S(2)}, u32[]{:S(2)}) collective-permute-start(bf16[4,104,576]{2,1,0:T(8,128)(2,1)} %get-tuple-element.144), channel_id=1, source_target_pairs={{0,4},{2,6},{4,0},{6,2},{8,12},{10,14},{12,8},{14,10},{16,20},{18,... | collective-permute-start | bytes 1437704 | tf_op jit(solution)/shard_map/ppermute | solution.py:736
  229.1 29.7 %collective-permute-start.49 = (bf16[4,112,576]{2,1,0:T(8,128)(2,1)}, bf16[4,112,576]{2,1,0:T(8,128)(2,1)S(1)}, u32[]{:S(2)}, u32[]{:S(2)}) collective-permute-start(bf16[4,112,576]{2,1,0:T(8,128)(2,1)} %get-tuple-element.146), channel_id=1, source_target_pairs={{0,8},{2,10},{4,12},{6,14},{8,0},{10,2},{12,4},{14,6},{16,24},{18,... | collective-permute-start | bytes 1548296 | tf_op jit(solution)/shard_map/ppermute | solution.py:736
  239.2 34.3 %collective-permute-start.56 = (bf16[360,576]{1,0:T(8,128)(2,1)}, bf16[360,576]{1,0:T(8,128)(2,1)S(1)}, u32[]{:S(2)}, u32[]{:S(2)}) collective-permute-start(bf16[360,576]{1,0:T(8,128)(2,1)} %fusion.20), channel_id=1, source_target_pairs={{0,16},{2,18},{4,20},{6,22},{8,24},{10,26},{12,28},{14,30},{16,0},... | collective-permute-start | bytes 1244168 | tf_op jit(solution)/shard_map/ppermute | solution.py:736
  254.0 16.2 %collective-permute-start.50 = (bf16[2,104,576]{2,1,0:T(8,128)(2,1)}, bf16[2,104,576]{2,1,0:T(8,128)(2,1)}, u32[]{:S(2)}, u32[]{:S(2)}) collective-permute-start(bf16[2,104,576]{2,1,0:T(8,128)(2,1)} %dynamic-slice_bitcast_fusion.5), channel_id=1, source_target_pairs={{0,8},{2,10},{4,12},{6,14},{8,0},{10,2},{12,4},{14,6},{16,24},{18,... | collective-permute-start | bytes 718856 | tf_op jit(solution)/shard_map/ppermute | solution.py:736
  271.4 16.1 %collective-permute-start.52 = (bf16[216,576]{1,0:T(8,128)(2,1)S(1)}, bf16[216,576]{1,0:T(8,128)(2,1)S(1)}, u32[]{:S(2)}, u32[]{:S(2)}) collective-permute-start(bf16[216,576]{1,0:T(8,128)(2,1)S(1)} %fusion.29), channel_id=1, source_target_pairs={{0,16},{2,18},{4,20},{6,22},{8,24},{10,26},{12,28},{14,30},{16,0},... | collective-permute-start | bytes 746504 | tf_op jit(solution)/shard_map/ppermute | solution.py:736
  274.0 27.3 %collective-permute-start.57 = (bf16[288,576]{1,0:T(8,128)(2,1)S(1)}, bf16[288,576]{1,0:T(8,128)(2,1)S(1)}, u32[]{:S(2)}, u32[]{:S(2)}) collective-permute-start(bf16[288,576]{1,0:T(8,128)(2,1)S(1)} %pad_maximum_fusion.2), channel_id=1, source_target_pairs={{0,0},{1,16},{2,2},{3,18},{4,4},{5,20},{6,6},{7,22},{8,8},{9,24},{... | collective-permute-start | bytes 995336 | tf_op jit(solution)/shard_map/ppermute | solution.py:1171
  (92 other events, 681.0 us)

commit v7 on v6

--- a/solution.py
+++ b/solution.py
@@ -382,11 +382,11 @@
     fill(weight_ref, place_ref, refs[:count], parts)
     root = 0.7978845608028654
     pre_acc[...] = dot_nn(mid_all[...], weight_ref[...])
-    back_acc[...] = dot_nt(grad_all[...], down_ref[...])
-    for group, start in [(g, t) for g in range(groups) for t in range(0, tokens, PERIOD)]:
+    blocks = [(g, t) for g in range(groups) for t in range(0, tokens, PERIOD)]
+    for group, start in blocks:
         span = pl.ds(group * tokens + start, PERIOD)
         channels = channel_ref[group]
-        pre, grad_act = pre_acc[span, :], back_acc[span, :]
+        pre = pre_acc[span, :]
         square = pre * pre
         inner = jnp.tanh(root * (pre + 0.044715 * (square * pre)))
         half_sum = 0.5 + 0.5 * inner
@@ -394,9 +394,13 @@
         slope = half_sum + (0.5 * pre) * (1.0 - inner * inner) * (
             root + (3.0 * 0.044715 * root) * square
         )
-        pre_ref[span, :] = (grad_act * channels * slope).astype(bf16)
+        pre_acc[span, :] = channels * slope
+    back_acc[...] = dot_nt(grad_all[...], down_ref[...])
+    out_acc[...] += dot_nn(act_ref[...], down_ref[...])
+    for group, start in blocks:
+        span = pl.ds(group * tokens + start, PERIOD)
+        pre_ref[span, :] = (back_acc[span, :] * pre_acc[span, :]).astype(bf16)
     grad_acc[...] += dot_nt(pre_ref[...], weight_ref[...])
-    out_acc[...] += dot_nn(act_ref[...], down_ref[...])
 
     @pl.when(step == steps - 1)
     def _():
@@ -522,7 +526,7 @@
     count = len(parts)
     dq_ref, dkv_ref, tokens_ref, mod_own, mod_other = refs[count : count + 5]
     grad_mid_ref, block_ref = refs[count + 5 : count + 7]
-    both_ref, sums_ref, weight_ref, grad_ref, sems = refs[count + 7 :]
+    both_ref, sums_ref, weight_ref, grad_ref, normed_ref, inverse_ref, sems = refs[count + 7 :]
     tokens = dq_ref.shape[0]
     copies = copies_in(weight_ref, place_ref, refs[:count], parts, sems)
     for column in (D, 2 * D, 0):
@@ -530,6 +534,11 @@
             if at == column:
                 copy.start()
     both_ref[:, pl.ds(0, D)] = block_ref[...]
+    for start in range(0, tokens, PERIOD):
+        rows = pl.ds(start, PERIOD)
+        normed, inverse = normalized(tokens_ref[rows, pl.ds(0, D)].astype(f32))
+        normed_ref[rows, :] = normed
+        inverse_ref[rows, :] = jnp.broadcast_to(inverse, (PERIOD, 128))
     wait_for(copies, D)
     grad_ref[...] = dot_nt(dkv_ref[:, pl.ds(0, D)], weight_ref[:, pl.ds(D, D)])
     wait_for(copies, 2 * D)
@@ -541,7 +550,7 @@
     scale_sum = jnp.zeros((PERIOD, D), f32)
     for start in range(0, tokens, PERIOD):
         rows = pl.ds(start, PERIOD)
-        normed, inverse = normalized(tokens_ref[rows, pl.ds(0, D)].astype(f32))
+        normed, inverse = normed_ref[rows, :], inverse_ref[rows, :][:, :1]
         grad = grad_ref[rows, :]
         back = normalized_back(grad * scale, normed, inverse)
         both_ref[rows, pl.ds(D, D)] = (grad_mid_ref[rows, :] + back).astype(bf16)
@@ -559,7 +568,12 @@
         sources,
         inputs,
         [shaped(tokens, 2 * D, dtype=bf16), shaped(2, PERIOD, D)],
-        [pltpu.VMEM((D, 3 * D), bf16), pltpu.VMEM((tokens, D), f32)],
+        [
+            pltpu.VMEM((D, 3 * D), bf16),
+            pltpu.VMEM((tokens, D), f32),
+            pltpu.VMEM((tokens, D), f32),
+            pltpu.VMEM((tokens, 128), f32),
+        ],
         "in_back",
     )
 

time: 307 us -> 307 us (level)
  no operation moved by 1% of the time
where the time goes in v7:
time: 307 us; the launch traced here: 302 us
  Pallas kernels  89.8 us (29%)
  starting transfers between devices  83.5 us (27%)
  waiting for transfers between devices  74.5 us (24%)
  other arithmetic  25.3 us (8%)
  local copies, waits for them, and re-layouts  19 us (6%)
  matrix products  8.19 us (3%)
    ppermute x46, starting transfers between devices, flip(): return lax.ppermute(value, 'seq', [(i, i ^ bit) for i in range(seq)])  45.2 us
    ppermute x46, waiting for transfers between devices, flip(): return lax.ppermute(value, 'seq', [(i, i ^ bit) for i in range(seq)])  35.2 us
    pallas_call x4, Pallas kernels, staged_call(): pl.pallas_call(functools.partial(kernel, parts=parts), out_shape=out_shap...  33.2 us
    pallas_call x3, Pallas kernels, term(): pl.pallas_call(functools.partial(term_kernel, layout=layout, outputs=2),...  23.5 us
    ppermute x13, waiting for transfers between devices, cross(): return lax.ppermute(value, 'fsdp', [(0, 1), (1, 0)])  21.9 us
    ppermute x13, starting transfers between devices, cross(): return lax.ppermute(value, 'fsdp', [(0, 1), (1, 0)])  13.5 us
    ppermute x1, waiting for transfers between devices, local(): lax.ppermute(up_mine, ('seq', 'fsdp'), pairs)  12.9 us
    pallas_call x1, Pallas kernels, feed(): pl.pallas_call(functools.partial(feed_kernel, parts=parts, arrays=len(mid...  12.6 us
  transfers between devices with their start and end apart: 66, of which 27 were waited for; matrix products, arithmetic and copies ran while one was open for 14% of the time, Pallas kernels for 26%

profile of v7, /device:TPU:2, one launch (start us, length us, event | category | flops | bytes accessed | tf_op | source)
XLA Modules:
  0.0 302.3 jit_solution(6018074215214929346)
XLA Ops:
  7.9 5.9 %all-to-all-start = ((bf16[16,8,2432]{2,1,0:T(8,128)(2,1)}), bf16[16,8,2432]{2,1,0:T(8,128)(2,1)S(1)}, u32[]{:S(2)}, u32[]{:S(2)}) async-start(bf16[16,8,2432]{2,1,0:T(8,128)(2,1)} %fusion.2), calls=%async_computation | async-start | bytes 1245184 | tf_op jit(solution)/shard_map/all_to_all | solution.py:767
  15.8 4.6 %fusion = f32[2,16,3456]{2,1,0:T(8,128)S(1)} fusion(bf16[2,16,1152]{2,1,0:T(8,128)(2,1)S(1)} %fusion.32, bf16[1152,3456]{1,0:T(8,128)(2,1)} %param.25), kind=kOutput, calls=%fused_computation | convolution fusion | flops 254803968 | bytes 8478720 | tf_op jit(solution)/shard_map/dot_general | solution.py:823
  30.6 6.6 %collective-permute-done.8.refs_9_ = bf16[144,1152]{1,0:T(8,128)(2,1)} collective-permute-done((bf16[144,1152]{1,0:T(8,128)(2,1)S(1)}, bf16[144,1152]{1,0:T(8,128)(2,1)}, u32[]{:S(2)}, u32[]{:S(2)}) %collective-permute-start.8) | collective-permute-done | bytes 331808 | tf_op jit(solution)/shard_map/ppermute | solution.py:753
  40.9 2.5 norm_in.1
  43.4 3.7 %collective-permute-start.13 = (bf16[128,1152]{1,0:T(8,128)(2,1)}, bf16[128,1152]{1,0:T(8,128)(2,1)}, u32[]{:S(2)}, u32[]{:S(2)}) collective-permute-start(bf16[128,1152]{1,0:T(8,128)(2,1)} %get-tuple-element.90.refs_13_.refs_15_), channel_id=1, source_target_pairs={{0,4},{2,6},{4,12},{6,14},{12,8},{14,10},{8,16},{10,18},{16,20},{1... | collective-permute-start | bytes 884744 | tf_op jit(solution)/shard_map/ppermute | solution.py:759
  52.0 4.4 %collective-permute-done.14.refs_16_ = bf16[128,1152]{1,0:T(8,128)(2,1)} collective-permute-done((bf16[128,1152]{1,0:T(8,128)(2,1)}, bf16[128,1152]{1,0:T(8,128)(2,1)}, u32[]{:S(2)}, u32[]{:S(2)}) %collective-permute-start.14) | collective-permute-done | bytes 294944 | tf_op jit(solution)/shard_map/ppermute | solution.py:759
  65.8 10.7 %project.1 = (bf16[128,1152]{1,0:T(8,128)(2,1)}, bf16[640,2304]{1,0:T(8,128)(2,1)}) custom-call(s32[8]{0:T(128)} %stack.77.place_ref, bf16[576,3456]{1,0:T(8,128)(2,1)} %refs_2_.3, bf16[576,3456]{1,0:T(8,128)(2,1)} %refs_2_.3, bf16[576,3456]{1,0:T(8,128)(2,1)} %refs_2_.3, bf16[288,1152]{1,0:T(8,128)(2,1)} %copy-done.8, bf16[288,1152]{1,0:T(8,128)(2,1)} %copy-done.9, ...), custom_call_target="tpu_custom_call" | custom-call | flops 1 | bytes 1 | tf_op jit(solution)/shard_map/project/pallas_call | solution.py:106
  79.5 7.5 %attend.1 = (bf16[128,1152]{1,0:T(8,128)(2,1)}, f32[128,1152]{1,0:T(8,128)}, f32[128,1152]{1,0:T(8,128)}, bf16[128,1152]{1,0:T(8,128)(2,1)}) custom-call(s32[8]{0:T(128)} %stack.77.place_ref, bf16[576,1152]{1,0:T(8,128)(2,1)} %refs_0_.8, bf16[144,2304]{1,0:T(8,128)(2,1)} %copy-done.1, bf16[144,2304]{1,0:T(8,128)(2,1)} %copy-done.3, ...), custom_call_target="tpu_custom_call" | custom-call | flops 1 | bytes 1 | tf_op jit(solution)/shard_map/attend/pallas_call | solution.py:106
  87.8 8.2 %collective-permute-done.20.refs_6_.refs_3_ = bf16[128,1152]{1,0:T(8,128)(2,1)S(1)} collective-permute-done((bf16[128,1152]{1,0:T(8,128)(2,1)}, bf16[128,1152]{1,0:T(8,128)(2,1)S(1)}, u32[]{:S(2)}, u32[]{:S(2)}) %collective-permute-start.20) | collective-permute-done | bytes 294944 | tf_op jit(solution)/shard_map/ppermute | solution.py:753
  99.1 12.6 %feed.1 = (bf16[256,2304]{1,0:T(8,128)(2,1)}, bf16[256,2304]{1,0:T(8,128)(2,1)}, f32[128,1152]{1,0:T(8,128)}, f32[128,1152]{1,0:T(8,128)}, bf16[128,2304]{1,0:T(8,128)(2,1)}) custom-call(s32[8]{0:T(128)} %stack.77.place_ref, bf16[576,4608]{1,0:T(8,128)(2,1)} %refs_0_.7, bf16[144,2304]{1,0:T(8,128)(2,1)} %collective-permute-done.17.refs_1_, ...), custom_call_target="tpu_custom_call" | custom-call | flops 1 | bytes 1 | tf_op jit(solution)/shard_map/feed/pallas_call | solution.py:420
  115.8 6.6 %term.3 = (bf16[4,32,2304]{2,1,0:T(8,128)(2,1)}, bf16[4,32,2304]{2,1,0:T(8,128)(2,1)}, bf16[4,40,2304]{2,1,0:T(8,128)(2,1)}, bf16[4,40,2304]{2,1,0:T(8,128)(2,1)}) custom-call(s32[8]{0:T(128)} %stack.77.place_ref, bf16[128,1152]{1,0:T(8,128)(2,1)} %get-tuple-element.92.refs_7_.refs_0_, bf16[128,1152]{1,0:T(8,128)(2,1)} %copy-done.24, ...), custom_call_target="tpu_custom_call" | custom-call | flops 1 | bytes 1 | tf_op jit(solution)/shard_map/term/pallas_call | solution.py:638
  123.9 3.8 %collective-permute-done.25.refs_7_ = bf16[128,2304]{1,0:T(8,128)(2,1)S(1)} collective-permute-done((bf16[128,2304]{1,0:T(8,128)(2,1)}, bf16[128,2304]{1,0:T(8,128)(2,1)S(1)}, u32[]{:S(2)}, u32[]{:S(2)}) %collective-permute-start.25) | collective-permute-done | bytes 589856 | tf_op jit(solution)/shard_map/ppermute | solution.py:753
  128.5 6.9 %mid_back.1 = (f32[128,1152]{1,0:T(8,128)}, bf16[128,2304]{1,0:T(8,128)(2,1)}, bf16[128,2304]{1,0:T(8,128)(2,1)}, bf16[128,1152]{1,0:T(8,128)(2,1)}, bf16[128,1152]{1,0:T(8,128)(2,1)}, /*index=5*/f32[4,16,1152]{2,1,0:T(8,128)}) custom-call(s32[8]{0:T(128)} %stack.77.place_ref, bf16[576,1152]{1,0:T(8,128)(2,1)} %refs_0_.8, bf16[144,2304]{1,0:T(8,128)(2,1)} %copy-done.1, ...), custom_call_target="tpu_custom_call" | custom-call | flops 1 | bytes 1 | tf_op jit(solution)/shard_map/mid_back/pallas_call | solution.py:106
  138.7 10.9 %attend_back.1 = (bf16[128,1152]{1,0:T(8,128)(2,1)}, bf16[128,2304]{1,0:T(8,128)(2,1)}, bf16[128,2304]{1,0:T(8,128)(2,1)}, bf16[128,2304]{1,0:T(8,128)(2,1)}, bf...) custom-call(bf16[128,1152]{1,0:T(8,128)(2,1)} %get-tuple-element.94.refs_5_.q_ref, ...), custom_call_target="tpu_custom_call" | custom-call | flops 1 | bytes 1 | tf_op jit(solution)/shard_map/attend_back/pallas_call | solution.py:344
  153.6 2.7 select_add_fusion
  156.3 3.4 %collective-permute-start.40 = (bf16[128,2304]{1,0:T(8,128)(2,1)}, bf16[128,2304]{1,0:T(8,128)(2,1)S(1)}, u32[]{:S(2)}, u32[]{:S(2)}) collective-permute-start(bf16[128,2304]{1,0:T(8,128)(2,1)} %get-tuple-element.165), channel_id=1, source_target_pairs={{0,4},{2,6},{4,12},{6,14},{12,8},{14,10},{8,16},{10,18},{16,20},{1... | collective-permute-start | bytes 1769480 | tf_op jit(solution)/shard_map/ppermute | solution.py:759
  162.2 2.6 collective-permute-start.34
  166.5 9.7 %term.4 = (bf16[4,216,576]{2,1,0:T(8,128)(2,1)}, bf16[4,216,576]{2,1,0:T(8,128)(2,1)}, bf16[4,144,576]{2,1,0:T(8,128)(2,1)}, bf16[4,144,576]{2,1,0:T(8,128)(2,1)}) custom-call(s32[8]{0:T(128)} %stack.77.place_ref, bf16[256,2304]{1,0:T(8,128)(2,1)} %get-tuple-element.117.refs_0_, bf16[256,2304]{1,0:T(8,128)(2,1)} %copy-done.15, ...), custom_call_target="tpu_custom_call" | custom-call | flops 1 | bytes 1 | tf_op jit(solution)/shard_map/term/pallas_call | solution.py:638
  177.4 7.6 %collective-permute-start.41 = (bf16[4,216,576]{2,1,0:T(8,128)(2,1)}, bf16[4,216,576]{2,1,0:T(8,128)(2,1)S(1)}, u32[]{:S(2)}, u32[]{:S(2)}) collective-permute-start(bf16[4,216,576]{2,1,0:T(8,128)(2,1)} %get-tuple-element.131), channel_id=1, source_target_pairs={{0,4},{2,6},{4,0},{6,2},{8,12},{10,14},{12,8},{14,10},{16,20},{18,... | collective-permute-start | bytes 2985992 | tf_op jit(solution)/shard_map/ppermute | solution.py:750
  188.8 8.1 %in_back.1 = (bf16[128,2304]{1,0:T(8,128)(2,1)}, f32[2,16,1152]{2,1,0:T(8,128)}) custom-call(s32[8]{0:T(128)} %stack.77.place_ref, bf16[576,3456]{1,0:T(8,128)(2,1)} %refs_2_.3, bf16[576,3456]{1,0:T(8,128)(2,1)} %refs_2_.3, bf16[576,3456]{1,0:T(8,128)(2,1)} %refs_2_.3, bf16[288,1152]{1,0:T(8,128)(2,1)} %copy-done.8, bf16[288,1152]{1,0:T(8,128)(2,1)} %copy-done.9, ...), custom_call_target="tpu_custom_call" | custom-call | flops 1 | bytes 1 | tf_op jit(solution)/shard_map/in_back/pallas_call | solution.py:106
  202.1 4.3 %collective-permute-done.42 = bf16[4,144,576]{2,1,0:T(8,128)(2,1)S(1)} collective-permute-done((bf16[4,144,576]{2,1,0:T(8,128)(2,1)}, bf16[4,144,576]{2,1,0:T(8,128)(2,1)S(1)}, u32[]{:S(2)}, u32[]{:S(2)}) %collective-permute-start.42) | collective-permute-done | bytes 663584 | tf_op jit(solution)/shard_map/ppermute | solution.py:750
  206.5 2.4 collective-permute-done.41
  213.7 4.9 %all-to-all-start.1 = ((bf16[16,8,2304]{2,1,0:T(8,128)(2,1)}), bf16[16,8,2304]{2,1,0:T(8,128)(2,1)}, u32[]{:S(2)}, u32[]{:S(2)}) async-start(bf16[16,8,2304]{2,1,0:T(8,128)(2,1)} %bitcast.186), calls=%async_computation.1 | async-start | bytes 1179648 | tf_op jit(solution)/shard_map/all_to_all | solution.py:771
  219.7 7.3 %term.5 = (bf16[4,104,576]{2,1,0:T(8,128)(2,1)}, bf16[4,104,576]{2,1,0:T(8,128)(2,1)}, bf16[4,112,576]{2,1,0:T(8,128)(2,1)}, bf16[4,112,576]{2,1,0:T(8,128)(2,1)}) custom-call(s32[8]{0:T(128)} %stack.77.place_ref, bf16[128,1152]{1,0:T(8,128)(2,1)} %get-tuple-element.128.refs_13_.refs_0_, bf16[128,2304]{1,0:T(8,128)(2,1)} %add_convert_fusion.3.refs_14_.refs_1_, ...), custom_call_target="tpu_custom_call" | custom-call | flops 1 | bytes 1 | tf_op jit(solution)/shard_map/term/pallas_call | solution.py:638
  230.5 2.5 collective-permute-done.53
  240.9 7.1 %collective-permute-done.59 = bf16[2,16,1728]{2,1,0:T(8,128)(2,1)S(1)} collective-permute-done((bf16[2,16,1728]{2,1,0:T(8,128)(2,1)S(1)}, bf16[2,16,1728]{2,1,0:T(8,128)(2,1)S(1)}, u32[]{:S(2)}, u32[]{:S(2)}) %collective-permute-start.59) | collective-permute-done | bytes 110624 | tf_op jit(solution)/shard_map/ppermute | solution.py:750
  248.1 2.2 collective-permute-start.60
  254.0 4.8 %collective-permute-start.50 = (bf16[2,104,576]{2,1,0:T(8,128)(2,1)}, bf16[2,104,576]{2,1,0:T(8,128)(2,1)}, u32[]{:S(2)}, u32[]{:S(2)}) collective-permute-start(bf16[2,104,576]{2,1,0:T(8,128)(2,1)} %dynamic-slice_bitcast_fusion.5), channel_id=1, source_target_pairs={{0,8},{2,10},{4,12},{6,14},{8,0},{10,2},{12,4},{14,6},{16,24},{18,... | collective-permute-start | bytes 718856 | tf_op jit(solution)/shard_map/ppermute | solution.py:750
  264.2 6.0 %collective-permute-done.61 = bf16[2,16,1728]{2,1,0:T(8,128)(2,1)S(1)} collective-permute-done((bf16[2,16,1728]{2,1,0:T(8,128)(2,1)S(1)}, bf16[2,16,1728]{2,1,0:T(8,128)(2,1)S(1)}, u32[]{:S(2)}, u32[]{:S(2)}) %collective-permute-start.61) | collective-permute-done | bytes 110624 | tf_op jit(solution)/shard_map/ppermute | solution.py:750
  273.9 4.1 %collective-permute-start.57 = (bf16[288,576]{1,0:T(8,128)(2,1)S(1)}, bf16[288,576]{1,0:T(8,128)(2,1)S(1)}, u32[]{:S(2)}, u32[]{:S(2)}) collective-permute-start(bf16[288,576]{1,0:T(8,128)(2,1)S(1)} %pad_maximum_fusion.2), channel_id=1, source_target_pairs={{0,0},{1,16},{2,2},{3,18},{4,4},{5,20},{6,6},{7,22},{8,8},{9,24},{... | collective-permute-start | bytes 995336 | tf_op jit(solution)/shard_map/ppermute | solution.py:1185
  280.3 7.1 %outer.1 = f32[1152,3456]{1,0:T(8,128)} custom-call(bf16[32,1152]{1,0:T(8,128)(2,1)} %bitcast.185, bf16[32,3456]{1,0:T(8,128)(2,1)} %pad_maximum_fusion.3.right_ref), custom_call_target="tpu_custom_call" | custom-call | flops 1 | bytes 1 | tf_op jit(solution)/shard_map/outer/pallas_call | solution.py:666
  288.3 12.9 %collective-permute-done.57 = bf16[288,576]{1,0:T(8,128)(2,1)S(1)} collective-permute-done((bf16[288,576]{1,0:T(8,128)(2,1)S(1)}, bf16[288,576]{1,0:T(8,128)(2,1)S(1)}, u32[]{:S(2)}, u32[]{:S(2)}) %collective-permute-start.57) | collective-permute-done | bytes 331808 | tf_op jit(solution)/shard_map/ppermute | solution.py:1185
  (327 shorter events, 105.6 us)
Async XLA Ops:
  4.6 16.7 %collective-permute-start.1 = (bf16[144,2304]{1,0:T(8,128)(2,1)S(1)}, bf16[144,2304]{1,0:T(8,128)(2,1)S(1)}, u32[]{:S(2)}, u32[]{:S(2)}) collective-permute-start(bf16[144,2304]{1,0:T(8,128)(2,1)S(1)} %pad_maximum_fusion), channel_id=1, source_target_pairs={{0,1},{1,0},{2,3},{3,2},{4,5},{5,4},{6,7},{7,6},{8,9},{9,8},{10,11... | collective-permute-start | bytes 1990664 | tf_op jit(solution)/shard_map/ppermute | solution.py:753
  7.9 30.8 %all-to-all-start = ((bf16[16,8,2432]{2,1,0:T(8,128)(2,1)}), bf16[16,8,2432]{2,1,0:T(8,128)(2,1)S(1)}, u32[]{:S(2)}, u32[]{:S(2)}) async-start(bf16[16,8,2432]{2,1,0:T(8,128)(2,1)} %fusion.2), calls=%async_computation | async-start | bytes 1245184 | tf_op jit(solution)/shard_map/all_to_all | solution.py:767
  23.7 17.2 %collective-permute-start.6 = (bf16[144,2304]{1,0:T(8,128)(2,1)S(1)}, bf16[144,2304]{1,0:T(8,128)(2,1)S(1)}, u32[]{:S(2)}, u32[]{:S(2)}) collective-permute-start(bf16[144,2304]{1,0:T(8,128)(2,1)S(1)} %collective-permute-done.1.refs_5_.refs_1_), channel_id=1, source_target_pairs={{0,4},{2,6},{4,0},{6,2},{8,12},{10,14},{12,8},{14,10},{16,20},{18,... | collective-permute-start | bytes 1990664 | tf_op jit(solution)/shard_map/ppermute | solution.py:750
  29.0 19.8 %collective-permute-start.3 = (bf16[288,1152]{1,0:T(8,128)(2,1)}, bf16[288,1152]{1,0:T(8,128)(2,1)S(1)}, u32[]{:S(2)}, u32[]{:S(2)}) collective-permute-start(bf16[288,1152]{1,0:T(8,128)(2,1)} %constant_dynamic-slice_fusion.1), channel_id=1, source_target_pairs={{0,1},{1,0},{2,3},{3,2},{4,5},{5,4},{6,7},{7,6},{8,9},{9,8},{10,11... | collective-permute-start | bytes 1990664 | tf_op jit(solution)/shard_map/ppermute | solution.py:753
  37.2 13.7 %collective-permute-start.10 = (bf16[144,1152]{1,0:T(8,128)(2,1)}, bf16[144,1152]{1,0:T(8,128)(2,1)}, u32[]{:S(2)}, u32[]{:S(2)}) collective-permute-start(bf16[144,1152]{1,0:T(8,128)(2,1)} %collective-permute-done.8.refs_9_), channel_id=1, source_target_pairs={{0,8},{2,10},{4,12},{6,14},{8,0},{10,2},{12,4},{14,6},{16,24},{18,... | collective-permute-start | bytes 995336 | tf_op jit(solution)/shard_map/ppermute | solution.py:750
  43.4 13.0 %collective-permute-start.13 = (bf16[128,1152]{1,0:T(8,128)(2,1)}, bf16[128,1152]{1,0:T(8,128)(2,1)}, u32[]{:S(2)}, u32[]{:S(2)}) collective-permute-start(bf16[128,1152]{1,0:T(8,128)(2,1)} %get-tuple-element.90.refs_13_.refs_15_), channel_id=1, source_target_pairs={{0,4},{2,6},{4,12},{6,14},{12,8},{14,10},{8,16},{10,18},{16,20},{1... | collective-permute-start | bytes 884744 | tf_op jit(solution)/shard_map/ppermute | solution.py:759
  56.5 20.0 %collective-permute-start.17 = (bf16[144,2304]{1,0:T(8,128)(2,1)S(1)}, bf16[144,2304]{1,0:T(8,128)(2,1)}, u32[]{:S(2)}, u32[]{:S(2)}) collective-permute-start(bf16[144,2304]{1,0:T(8,128)(2,1)S(1)} %dynamic_slice.85), channel_id=1, source_target_pairs={{0,1},{1,0},{2,3},{3,2},{4,5},{5,4},{6,7},{7,6},{8,9},{9,8},{10,11... | collective-permute-start | bytes 1990664 | tf_op jit(solution)/shard_map/ppermute | solution.py:753
  76.5 19.5 %collective-permute-start.19 = (bf16[144,2304]{1,0:T(8,128)(2,1)}, bf16[144,2304]{1,0:T(8,128)(2,1)S(1)}, u32[]{:S(2)}, u32[]{:S(2)}) collective-permute-start(bf16[144,2304]{1,0:T(8,128)(2,1)} %collective-permute-done.17.refs_1_), channel_id=1, source_target_pairs={{0,4},{2,6},{4,0},{6,2},{8,12},{10,14},{12,8},{14,10},{16,20},{18,... | collective-permute-start | bytes 1990664 | tf_op jit(solution)/shard_map/ppermute | solution.py:750
  111.9 15.8 %collective-permute-start.25 = (bf16[128,2304]{1,0:T(8,128)(2,1)}, bf16[128,2304]{1,0:T(8,128)(2,1)S(1)}, u32[]{:S(2)}, u32[]{:S(2)}) collective-permute-start(bf16[128,2304]{1,0:T(8,128)(2,1)} %get-tuple-element.110), channel_id=1, source_target_pairs={{0,1},{1,0},{2,3},{3,2},{4,5},{5,4},{6,7},{7,6},{8,9},{9,8},{10,11... | collective-permute-start | bytes 1769480 | tf_op jit(solution)/shard_map/ppermute | solution.py:753
  112.7 26.0 %collective-permute-start.27 = (bf16[256,2304]{1,0:T(8,128)(2,1)}, bf16[256,2304]{1,0:T(8,128)(2,1)S(1)}, u32[]{:S(2)}, u32[]{:S(2)}) collective-permute-start(bf16[256,2304]{1,0:T(8,128)(2,1)} %get-tuple-element.117.refs_0_), channel_id=1, source_target_pairs={{0,2},{2,0},{4,6},{6,4},{8,10},{10,8},{12,14},{14,12},{16,18},{18,... | collective-permute-start | bytes 3538952 | tf_op jit(solution)/shard_map/ppermute | solution.py:750
  122.4 28.9 %collective-permute-start.31 = (bf16[4,40,2304]{2,1,0:T(8,128)(2,1)}, bf16[4,40,2304]{2,1,0:T(8,128)(2,1)S(1)}, u32[]{:S(2)}, u32[]{:S(2)}) collective-permute-start(bf16[4,40,2304]{2,1,0:T(8,128)(2,1)} %get-tuple-element.106), channel_id=1, source_target_pairs={{0,8},{2,10},{4,12},{6,14},{8,0},{10,2},{12,4},{14,6},{16,24},{18,... | collective-permute-start | bytes 2211848 | tf_op jit(solution)/shard_map/ppermute | solution.py:750
  135.5 15.7 %collective-permute-start.30 = (bf16[4,32,2304]{2,1,0:T(8,128)(2,1)S(1)}, bf16[4,32,2304]{2,1,0:T(8,128)(2,1)S(1)}, u32[]{:S(2)}, u32[]{:S(2)}) collective-permute-start(bf16[4,32,2304]{2,1,0:T(8,128)(2,1)S(1)} %copy-done.51), channel_id=1, source_target_pairs={{0,4},{2,6},{4,0},{6,2},{8,12},{10,14},{12,8},{14,10},{16,20},{18,... | collective-permute-start | bytes 1769480 | tf_op jit(solution)/shard_map/ppermute | solution.py:750
  137.9 15.6 %collective-permute-start.36 = (bf16[128,2304]{1,0:T(8,128)(2,1)}, bf16[128,2304]{1,0:T(8,128)(2,1)S(1)}, u32[]{:S(2)}, u32[]{:S(2)}) collective-permute-start(bf16[128,2304]{1,0:T(8,128)(2,1)} %get-tuple-element.115), channel_id=1, source_target_pairs={{0,1},{1,0},{2,3},{3,2},{4,5},{5,4},{6,7},{7,6},{8,9},{9,8},{10,11... | collective-permute-start | bytes 1769480 | tf_op jit(solution)/shard_map/ppermute | solution.py:753
  151.3 24.9 %collective-permute-start.35 = (bf16[128,2304]{1,0:T(8,128)(2,1)}, bf16[128,2304]{1,0:T(8,128)(2,1)S(1)}, u32[]{:S(2)}, u32[]{:S(2)}) collective-permute-start(bf16[128,2304]{1,0:T(8,128)(2,1)} %get-tuple-element.130), channel_id=1, source_target_pairs={{0,2},{2,0},{4,6},{6,4},{8,10},{10,8},{12,14},{14,12},{16,18},{18,... | collective-permute-start | bytes 1769480 | tf_op jit(solution)/shard_map/ppermute | solution.py:750
  156.3 29.3 %collective-permute-start.40 = (bf16[128,2304]{1,0:T(8,128)(2,1)}, bf16[128,2304]{1,0:T(8,128)(2,1)S(1)}, u32[]{:S(2)}, u32[]{:S(2)}) collective-permute-start(bf16[128,2304]{1,0:T(8,128)(2,1)} %get-tuple-element.165), channel_id=1, source_target_pairs={{0,4},{2,6},{4,12},{6,14},{12,8},{14,10},{8,16},{10,18},{16,20},{1... | collective-permute-start | bytes 1769480 | tf_op jit(solution)/shard_map/ppermute | solution.py:759
  159.8 25.9 %collective-permute-start.39 = (bf16[128,2304]{1,0:T(8,128)(2,1)}, bf16[128,2304]{1,0:T(8,128)(2,1)}, u32[]{:S(2)}, u32[]{:S(2)}) collective-permute-start(bf16[128,2304]{1,0:T(8,128)(2,1)} %get-tuple-element.166), channel_id=1, source_target_pairs={{4,0},{6,2},{12,4},{14,6},{8,12},{10,14},{16,8},{18,10},{20,16},{2... | collective-permute-start | bytes 1769480 | tf_op jit(solution)/shard_map/ppermute | solution.py:759
  162.2 22.9 %collective-permute-start.34 = (bf16[2,40,2304]{2,1,0:T(8,128)(2,1)}, bf16[2,40,2304]{2,1,0:T(8,128)(2,1)}, u32[]{:S(2)}, u32[]{:S(2)}) collective-permute-start(bf16[2,40,2304]{2,1,0:T(8,128)(2,1)} %dynamic-slice_bitcast_fusion.2), channel_id=1, source_target_pairs={{0,4},{2,6},{4,0},{6,2},{8,12},{10,14},{12,8},{14,10},{16,20},{18,... | collective-permute-start | bytes 1105928 | tf_op jit(solution)/shard_map/ppermute | solution.py:750
  176.2 26.0 %collective-permute-start.43 = (bf16[128,1152]{1,0:T(8,128)(2,1)S(1)}, bf16[128,1152]{1,0:T(8,128)(2,1)S(1)}, u32[]{:S(2)}, u32[]{:S(2)}) collective-permute-start(bf16[128,1152]{1,0:T(8,128)(2,1)S(1)} %copy-done.21), channel_id=1, source_target_pairs={{0,1},{1,0},{2,3},{3,2},{4,5},{5,4},{6,7},{7,6},{8,9},{9,8},{10,11... | collective-permute-start | bytes 884744 | tf_op jit(solution)/shard_map/ppermute | solution.py:753
  177.4 31.5 %collective-permute-start.41 = (bf16[4,216,576]{2,1,0:T(8,128)(2,1)}, bf16[4,216,576]{2,1,0:T(8,128)(2,1)S(1)}, u32[]{:S(2)}, u32[]{:S(2)}) collective-permute-start(bf16[4,216,576]{2,1,0:T(8,128)(2,1)} %get-tuple-element.131), channel_id=1, source_target_pairs={{0,4},{2,6},{4,0},{6,2},{8,12},{10,14},{12,8},{14,10},{16,20},{18,... | collective-permute-start | bytes 2985992 | tf_op jit(solution)/shard_map/ppermute | solution.py:750
  185.2 21.3 %collective-permute-start.42 = (bf16[4,144,576]{2,1,0:T(8,128)(2,1)}, bf16[4,144,576]{2,1,0:T(8,128)(2,1)S(1)}, u32[]{:S(2)}, u32[]{:S(2)}) collective-permute-start(bf16[4,144,576]{2,1,0:T(8,128)(2,1)} %get-tuple-element.133), channel_id=1, source_target_pairs={{0,8},{2,10},{4,12},{6,14},{8,0},{10,2},{12,4},{14,6},{16,24},{18,... | collective-permute-start | bytes 1990664 | tf_op jit(solution)/shard_map/ppermute | solution.py:750
  187.9 14.3 %collective-permute-start.44 = (bf16[128,2304]{1,0:T(8,128)(2,1)}, bf16[128,2304]{1,0:T(8,128)(2,1)}, u32[]{:S(2)}, u32[]{:S(2)}) collective-permute-start(bf16[128,2304]{1,0:T(8,128)(2,1)} %add_convert_fusion.3.refs_14_.refs_1_), channel_id=1, source_target_pairs={{0,1},{1,0},{2,3},{3,2},{4,5},{5,4},{6,7},{7,6},{8,9},{9,8},{10,11... | collective-permute-start | bytes 1769480 | tf_op jit(solution)/shard_map/ppermute | solution.py:753
  198.9 31.6 %collective-permute-start.55 = (bf16[72,2304]{1,0:T(8,128)(2,1)}, bf16[72,2304]{1,0:T(8,128)(2,1)}, u32[]{:S(2)}, u32[]{:S(2)}) collective-permute-start(bf16[72,2304]{1,0:T(8,128)(2,1)} %fusion.26), channel_id=1, source_target_pairs={{0,16},{2,18},{4,20},{6,22},{8,24},{10,26},{12,28},{14,30},{16,0},... | collective-permute-start | bytes 995336 | tf_op jit(solution)/shard_map/ppermute | solution.py:750
  202.1 17.6 %collective-permute-start.47 = (bf16[128,2304]{1,0:T(8,128)(2,1)}, bf16[128,2304]{1,0:T(8,128)(2,1)}, u32[]{:S(2)}, u32[]{:S(2)}) collective-permute-start(bf16[128,2304]{1,0:T(8,128)(2,1)} %collective-permute-done.44.refs_3_), channel_id=1, source_target_pairs={{0,2},{2,0},{4,6},{6,4},{8,10},{10,8},{12,14},{14,12},{16,18},{18,... | collective-permute-start | bytes 1769480 | tf_op jit(solution)/shard_map/ppermute | solution.py:750
  210.6 22.4 %collective-permute-start.53 = (bf16[2,216,576]{2,1,0:T(8,128)(2,1)}, bf16[2,216,576]{2,1,0:T(8,128)(2,1)S(1)}, u32[]{:S(2)}, u32[]{:S(2)}) collective-permute-start(bf16[2,216,576]{2,1,0:T(8,128)(2,1)} %dynamic-slice_bitcast_fusion), channel_id=1, source_target_pairs={{0,8},{2,10},{4,12},{6,14},{8,0},{10,2},{12,4},{14,6},{16,24},{18,... | collective-permute-start | bytes 1493000 | tf_op jit(solution)/shard_map/ppermute | solution.py:750
  212.0 18.5 %collective-permute-start.54 = (bf16[2,144,576]{2,1,0:T(8,128)(2,1)S(1)}, bf16[2,144,576]{2,1,0:T(8,128)(2,1)}, u32[]{:S(2)}, u32[]{:S(2)}) collective-permute-start(bf16[2,144,576]{2,1,0:T(8,128)(2,1)S(1)} %dynamic-slice_bitcast_fusion.1), channel_id=1, source_target_pairs={{0,4},{2,6},{4,0},{6,2},{8,12},{10,14},{12,8},{14,10},{16,20},{18,... | collective-permute-start | bytes 995336 | tf_op jit(solution)/shard_map/ppermute | solution.py:750
  213.7 45.2 %all-to-all-start.1 = ((bf16[16,8,2304]{2,1,0:T(8,128)(2,1)}), bf16[16,8,2304]{2,1,0:T(8,128)(2,1)}, u32[]{:S(2)}, u32[]{:S(2)}) async-start(bf16[16,8,2304]{2,1,0:T(8,128)(2,1)} %bitcast.186), calls=%async_computation.1 | async-start | bytes 1179648 | tf_op jit(solution)/shard_map/all_to_all | solution.py:771
  227.0 26.0 %collective-permute-start.48 = (bf16[4,104,576]{2,1,0:T(8,128)(2,1)}, bf16[4,104,576]{2,1,0:T(8,128)(2,1)S(1)}, u32[]{:S(2)}, u32[]{:S(2)}) collective-permute-start(bf16[4,104,576]{2,1,0:T(8,128)(2,1)} %get-tuple-element.144), channel_id=1, source_target_pairs={{0,4},{2,6},{4,0},{6,2},{8,12},{10,14},{12,8},{14,10},{16,20},{18,... | collective-permute-start | bytes 1437704 | tf_op jit(solution)/shard_map/ppermute | solution.py:750
  229.0 29.7 %collective-permute-start.49 = (bf16[4,112,576]{2,1,0:T(8,128)(2,1)}, bf16[4,112,576]{2,1,0:T(8,128)(2,1)S(1)}, u32[]{:S(2)}, u32[]{:S(2)}) collective-permute-start(bf16[4,112,576]{2,1,0:T(8,128)(2,1)} %get-tuple-element.146), channel_id=1, source_target_pairs={{0,8},{2,10},{4,12},{6,14},{8,0},{10,2},{12,4},{14,6},{16,24},{18,... | collective-permute-start | bytes 1548296 | tf_op jit(solution)/shard_map/ppermute | solution.py:750
  239.1 34.3 %collective-permute-start.56 = (bf16[360,576]{1,0:T(8,128)(2,1)}, bf16[360,576]{1,0:T(8,128)(2,1)S(1)}, u32[]{:S(2)}, u32[]{:S(2)}) collective-permute-start(bf16[360,576]{1,0:T(8,128)(2,1)} %fusion.20), channel_id=1, source_target_pairs={{0,16},{2,18},{4,20},{6,22},{8,24},{10,26},{12,28},{14,30},{16,0},... | collective-permute-start | bytes 1244168 | tf_op jit(solution)/shard_map/ppermute | solution.py:750
  254.0 16.2 %collective-permute-start.50 = (bf16[2,104,576]{2,1,0:T(8,128)(2,1)}, bf16[2,104,576]{2,1,0:T(8,128)(2,1)}, u32[]{:S(2)}, u32[]{:S(2)}) collective-permute-start(bf16[2,104,576]{2,1,0:T(8,128)(2,1)} %dynamic-slice_bitcast_fusion.5), channel_id=1, source_target_pairs={{0,8},{2,10},{4,12},{6,14},{8,0},{10,2},{12,4},{14,6},{16,24},{18,... | collective-permute-start | bytes 718856 | tf_op jit(solution)/shard_map/ppermute | solution.py:750
  271.3 16.1 %collective-permute-start.52 = (bf16[216,576]{1,0:T(8,128)(2,1)S(1)}, bf16[216,576]{1,0:T(8,128)(2,1)S(1)}, u32[]{:S(2)}, u32[]{:S(2)}) collective-permute-start(bf16[216,576]{1,0:T(8,128)(2,1)S(1)} %fusion.29), channel_id=1, source_target_pairs={{0,16},{2,18},{4,20},{6,22},{8,24},{10,26},{12,28},{14,30},{16,0},... | collective-permute-start | bytes 746504 | tf_op jit(solution)/shard_map/ppermute | solution.py:750
  273.9 27.3 %collective-permute-start.57 = (bf16[288,576]{1,0:T(8,128)(2,1)S(1)}, bf16[288,576]{1,0:T(8,128)(2,1)S(1)}, u32[]{:S(2)}, u32[]{:S(2)}) collective-permute-start(bf16[288,576]{1,0:T(8,128)(2,1)S(1)} %pad_maximum_fusion.2), channel_id=1, source_target_pairs={{0,0},{1,16},{2,2},{3,18},{4,4},{5,20},{6,6},{7,22},{8,8},{9,24},{... | collective-permute-start | bytes 995336 | tf_op jit(solution)/shard_map/ppermute | solution.py:1185
  (92 other events, 681.0 us)
